TPU v7x, 32 devices: a whole 2x2x4 slice. The times are simulated.
32 devices in a mesh: ctx: 16 (over z, y, x), wsh: 2 (over core).
Axes of the slice: x: 2, y: 2, z: 4, core: 2. Of those that a mesh axis runs over, the one named last changes fastest.
Arguments:
- tokens: bfloat16 [8, 2048, 512], P('wsh', 'ctx'), may hold values from -6 to 6
- routes: int32 [8, 2048, 2], P('wsh', 'ctx'), may hold values from 0 to 7, all different within a row
- block_order: int32 [16], replicated, may hold values from 0 to 15, each once
- norm_gain1: bfloat16 [512], P('wsh'), may hold values from 0.5 to 1.5
- router_w: bfloat16 [512, 8], P('wsh'), may hold values from -0.1875 to 0.1875
- query_w: bfloat16 [512, 512], P('wsh'), may hold values from -0.25 to 0.25
- kv_w: bfloat16 [512, 128], P('wsh'), may hold values from -0.25 to 0.25
- out_w: bfloat16 [512, 512], P('wsh'), may hold values from -6 to 6
- norm_gain2: bfloat16 [512], P('wsh'), may hold values from 0.5 to 1.5
- up_w: bfloat16 [512, 2048], P('wsh'), may hold values from -0.25 to 0.25
- down_w: bfloat16 [2048, 512], P('wsh'), may hold values from -0.125 to 0.125
- cotangent: bfloat16 [8, 2048, 512], P('wsh', 'ctx'), may hold values from -6 to 6
Outputs:
- layer_out: float32 [8, 2048, 512], P('wsh', 'ctx')
- input_grad: float32 [8, 2048, 512], P('wsh', 'ctx')
- grad_gain1: float32 [512], P('wsh')
- grad_router: float32 [512, 8], P('wsh')
- grad_query: float32 [512, 512], P('wsh')
- grad_kv: float32 [512, 128], P('wsh')
- grad_out: float32 [512, 512], P('wsh')
- grad_gain2: float32 [512], P('wsh')
- grad_up: float32 [512, 2048], P('wsh')
- grad_down: float32 [2048, 512], P('wsh')
Inputs may be any that keep to these rules, and one draw needn't show every extreme that they name: `routes`: each token names 2 different experts. A permutation: index p of ctx holds, of every sequence, block block_order[p] and block 31 - block_order[p], as the first step says.
All inputs are finite; a program needn't handle non-finite values.
Results may differ from a plain program's by a relative error of at most 0.013.
Values may be sent and summed in bfloat16 or wider, within the bound.
No kernel may reach another device: no remote copies, remote signals or barrier semaphores. Data moves between devices by JAX's collectives and lax.ppermute only.
A program may use at most 192 MiB of HBM per device.

v0:
```python
import math

import jax
import jax.numpy as jnp
from jax import lax
from jax.sharding import PartitionSpec as P

MB = 4


HIGHEST = lax.Precision.HIGHEST


def smooth_unit(values_in):
    return jax.nn.gelu(values_in, approximate=False)


def normalize(inputs, gain_vec):
    centre = inputs - jnp.mean(inputs, axis=-1, keepdims=True)
    spread = jnp.mean(centre * centre, axis=-1, keepdims=True)
    return centre * lax.rsqrt(spread + 1e-05) * gain_vec


def gating(logits, expert_hot):
    chosen = jnp.sum(expert_hot * logits[..., None, :], axis=-1)
    return jax.nn.softmax(chosen, axis=-1)


def tile_scores(queries, kv_all, query_places, key_places, first_row, width):
    head = queries.shape[-1]
    tile = lax.dynamic_slice_in_dim(kv_all, first_row, width, 1)
    places = lax.dynamic_slice_in_dim(key_places, first_row, width, 0)
    keys_tile = tile[..., :head]
    values_tile = tile[..., head:]
    scores = jnp.einsum("btsh,bkh->btsk", queries, keys_tile, preferred_element_type=jnp.float32)
    allowed = places[None, None, None, :] <= query_places[None, :, None, None]
    return (keys_tile, values_tile, scores, allowed)


def log_totals(queries, kv_all, query_places, key_places):
    rows = kv_all.shape[1]
    width = math.gcd(rows, 2048)

    def log_advance(carry, index):
        top_score, total = carry
        unused_keys, unused_values, scores, allowed = tile_scores(
            queries, kv_all, query_places, key_places, index * width, width
        )
        fresh = jnp.maximum(top_score, jnp.max(jnp.where(allowed, scores, -1e30), axis=-1))
        shares = jnp.where(allowed, jnp.exp(scores - fresh[..., None]), 0.0)
        total = total * jnp.exp(top_score - fresh) + jnp.sum(shares, axis=-1)
        return ((fresh, total), None)

    shape = queries.shape[:-1]
    initial = (jnp.full(shape, -1e30, jnp.float32), jnp.zeros(shape, jnp.float32))
    carry, unused = lax.scan(log_advance, initial, jnp.arange(rows // width, dtype=jnp.int32))
    return carry[0] + jnp.log(carry[1])


def attend(queries, kv_all, query_places, key_places, log_total):
    rows = kv_all.shape[1]
    width = math.gcd(rows, 2048)

    def attend_advance(carry, index):
        unused_keys, values_tile, scores, allowed = tile_scores(
            queries, kv_all, query_places, key_places, index * width, width
        )
        shares = jnp.where(allowed, jnp.exp(scores - log_total[..., None]), 0.0).astype(
            jnp.bfloat16
        )
        return (
            carry
            + jnp.einsum("btsk,bkh->btsh", shares, values_tile, preferred_element_type=jnp.float32),
            None,
        )

    summed, unused = lax.scan(
        attend_advance,
        jnp.zeros(queries.shape, jnp.float32),
        jnp.arange(rows // width, dtype=jnp.int32),
    )
    return summed


def key_range_grads(
    queries, back_attended, kv_all, query_places, key_places, log_total, row_delta, begin, row_count
):
    width = math.gcd(row_count, 2048)

    def key_advance(carry, index):
        back_query, back_kv = carry
        keys_tile, values_tile, scores, allowed = tile_scores(
            queries, kv_all, query_places, key_places, begin + index * width, width
        )
        shares = jnp.where(allowed, jnp.exp(scores - log_total[..., None]), 0.0)
        back_shares = jnp.einsum(
            "btsh,bkh->btsk", back_attended, values_tile, preferred_element_type=jnp.float32
        )
        back_scores = (shares * (back_shares - row_delta[..., None])).astype(jnp.bfloat16)
        back_query = back_query + jnp.einsum(
            "btsk,bkh->btsh", back_scores, keys_tile, preferred_element_type=jnp.float32
        )
        back_keys = jnp.einsum(
            "btsk,btsh->bkh", back_scores, queries, preferred_element_type=jnp.float32
        )
        back_values = jnp.einsum(
            "btsk,btsh->bkh",
            shares.astype(jnp.bfloat16),
            back_attended,
            preferred_element_type=jnp.float32,
        )
        back_kv = lax.dynamic_update_slice_in_dim(
            back_kv, jnp.concatenate([back_keys, back_values], axis=-1), index * width, 1
        )
        return ((back_query, back_kv), None)

    head = queries.shape[-1]
    kv_start = jnp.zeros((queries.shape[0], row_count, 2 * head), jnp.float32)
    carry, unused = lax.scan(
        key_advance,
        (jnp.zeros(queries.shape, jnp.float32), kv_start),
        jnp.arange(row_count // width, dtype=jnp.int32),
    )
    return carry


def on_device(
    tokens,
    routes,
    block_order,
    norm_gain1,
    router_w,
    query_w,
    kv_w,
    out_w,
    norm_gain2,
    up_w,
    down_w,
    cotangent,
):
    gathered = (
        lax.all_gather(norm_gain1, "wsh", axis=0, tiled=True),
        lax.all_gather(router_w, "wsh", axis=0, tiled=True),
        lax.all_gather(query_w, "wsh", axis=0, tiled=True),
        lax.all_gather(kv_w, "wsh", axis=0, tiled=True),
        lax.all_gather(out_w, "wsh", axis=0, tiled=True),
        lax.all_gather(norm_gain2, "wsh", axis=0, tiled=True),
        lax.all_gather(up_w, "wsh", axis=0, tiled=True),
        lax.all_gather(down_w, "wsh", axis=0, tiled=True),
    )
    gain_one, router, query_mat, kv_mat, out_mat, gain_two, up_mat, down_mat = gathered
    gain_one_f = gain_one.astype(jnp.float32)
    gain_two_f = gain_two.astype(jnp.float32)
    router_f = router.astype(jnp.float32)
    experts = router.shape[1]
    head = kv_mat.shape[1] // 2
    pairs = lax.axis_size("ctx")
    local = tokens.shape[1]
    block = local // 2
    offsets = jnp.arange(block, dtype=jnp.int32)
    front_rows = block_order[:, None] * block + offsets[None, :]
    back_rows = (2 * pairs - 1 - block_order)[:, None] * block + offsets[None, :]
    key_places = jnp.concatenate([front_rows, back_rows], axis=1).reshape(-1)
    length = key_places.shape[0]
    query_places = lax.dynamic_slice_in_dim(key_places, lax.axis_index("ctx") * local, local, 0)
    group = tokens.shape[0] // MB
    totals = [jnp.zeros(w.shape, jnp.float32) for w in gathered]
    layer_parts = []
    input_parts = []
    for batch in range(MB):
        inputs = tokens[batch * group : (batch + 1) * group].astype(jnp.float32)
        seq_routes = routes[batch * group : (batch + 1) * group]
        seq_cotangent = cotangent[batch * group : (batch + 1) * group]
        seqs = inputs.shape[0]
        expert_hot = (seq_routes[..., None] == jnp.arange(experts, dtype=jnp.int32)).astype(
            jnp.float32
        )
        normed, norm_pull_one = jax.vjp(normalize, inputs, gain_one_f)
        normed_low = normed.astype(jnp.bfloat16)
        logits = jnp.dot(normed_low, router, preferred_element_type=jnp.float32)
        gate_values, gate_pull = jax.vjp(lambda values_in: gating(values_in, expert_hot), logits)
        query_all = jnp.dot(normed_low, query_mat, preferred_element_type=jnp.float32).reshape(
            seqs, local, experts, head
        )
        queries = (
            jnp.einsum("btse,bteh->btsh", expert_hot, query_all, precision=HIGHEST) * 0.125
        ).astype(jnp.bfloat16)
        keyval = jnp.dot(normed_low, kv_mat, preferred_element_type=jnp.float32).astype(
            jnp.bfloat16
        )
        kv_all = lax.all_gather(keyval, "ctx", axis=1, tiled=True)
        log_total = log_totals(queries, kv_all, query_places, key_places)
        attended = attend(queries, kv_all, query_places, key_places, log_total)
        weighted = gate_values[..., None] * attended
        mixed_heads = (
            jnp.einsum("btse,btsh->bteh", expert_hot, weighted, precision=HIGHEST)
            .reshape(seqs, local, experts * head)
            .astype(jnp.bfloat16)
        )
        hidden = inputs + jnp.dot(mixed_heads, out_mat, preferred_element_type=jnp.float32)
        normed_two, norm_pull_two = jax.vjp(normalize, hidden, gain_two_f)
        normed_two_low = normed_two.astype(jnp.bfloat16)
        pre_act = jnp.dot(normed_two_low, up_mat, preferred_element_type=jnp.float32)
        act_values, act_pull = jax.vjp(smooth_unit, pre_act)
        activated = act_values.astype(jnp.bfloat16)
        layer_parts.append(
            hidden + jnp.dot(activated, down_mat, preferred_element_type=jnp.float32)
        )
        totals[7] = totals[7] + jnp.einsum(
            "btf,btd->fd", activated, seq_cotangent, preferred_element_type=jnp.float32
        )
        back_act = jnp.einsum(
            "btd,fd->btf", seq_cotangent, down_mat, preferred_element_type=jnp.float32
        )
        (back_pre_f,) = act_pull(back_act)
        back_pre = back_pre_f.astype(jnp.bfloat16)
        totals[6] = totals[6] + jnp.einsum(
            "btd,btf->df", normed_two_low, back_pre, preferred_element_type=jnp.float32
        )
        back_normed_two = jnp.einsum(
            "btf,df->btd", back_pre, up_mat, preferred_element_type=jnp.float32
        )
        hidden_part, gain_two_grad = norm_pull_two(back_normed_two)
        back_hidden = seq_cotangent.astype(jnp.float32) + hidden_part
        totals[5] = totals[5] + gain_two_grad
        back_branch = back_hidden.astype(jnp.bfloat16)
        totals[4] = totals[4] + jnp.einsum(
            "btk,btd->kd", mixed_heads, back_branch, preferred_element_type=jnp.float32
        )
        back_mixed = jnp.einsum(
            "btd,kd->btk", back_branch, out_mat, preferred_element_type=jnp.float32
        ).reshape(seqs, local, experts, head)
        back_slots = jnp.einsum("btse,bteh->btsh", expert_hot, back_mixed, precision=HIGHEST)
        back_gates = jnp.sum(back_slots * attended, axis=-1)
        back_attended = (gate_values[..., None] * back_slots).astype(jnp.bfloat16)
        row_delta = jnp.sum(back_attended.astype(jnp.float32) * attended, axis=-1)
        (back_logits,) = gate_pull(back_gates)
        back_query, full_kv = key_range_grads(
            queries,
            back_attended,
            kv_all,
            query_places,
            key_places,
            log_total,
            row_delta,
            0,
            length,
        )
        own_kv = lax.psum_scatter(full_kv, "ctx", scatter_dimension=1, tiled=True)
        back_kv_low = own_kv.astype(jnp.bfloat16)
        back_query_low = back_query.astype(jnp.bfloat16)
        back_qall = (
            (
                jnp.einsum(
                    "btse,btsh->bteh",
                    expert_hot.astype(jnp.bfloat16),
                    back_query_low,
                    preferred_element_type=jnp.float32,
                )
                * 0.125
            )
            .reshape(seqs, local, experts * head)
            .astype(jnp.bfloat16)
        )
        totals[2] = totals[2] + jnp.einsum(
            "btd,btk->dk", normed_low, back_qall, preferred_element_type=jnp.float32
        )
        totals[3] = totals[3] + jnp.einsum(
            "btd,btk->dk", normed_low, back_kv_low, preferred_element_type=jnp.float32
        )
        totals[1] = totals[1] + jnp.einsum(
            "btd,bte->de", normed_low.astype(jnp.float32), back_logits, precision=HIGHEST
        )
        back_normed = jnp.einsum(
            "btk,dk->btd", back_qall, query_mat, preferred_element_type=jnp.float32
        )
        back_normed = back_normed + jnp.einsum(
            "btk,dk->btd", back_kv_low, kv_mat, preferred_element_type=jnp.float32
        )
        back_normed = back_normed + jnp.einsum(
            "bte,de->btd", back_logits, router_f, precision=HIGHEST
        )
        input_part, gain_one_grad = norm_pull_one(back_normed)
        totals[0] = totals[0] + gain_one_grad
        input_parts.append(back_hidden + input_part)
    layer_out = jnp.concatenate(layer_parts, axis=0)
    input_grad = jnp.concatenate(input_parts, axis=0)
    owned = (
        lax.psum_scatter(
            totals[0].astype(jnp.bfloat16), "wsh", scatter_dimension=0, tiled=True
        ).astype(jnp.float32),
        lax.psum_scatter(
            totals[1].astype(jnp.bfloat16), "wsh", scatter_dimension=0, tiled=True
        ).astype(jnp.float32),
        lax.psum_scatter(
            totals[2].astype(jnp.bfloat16), "wsh", scatter_dimension=0, tiled=True
        ).astype(jnp.float32),
        lax.psum_scatter(
            totals[3].astype(jnp.bfloat16), "wsh", scatter_dimension=0, tiled=True
        ).astype(jnp.float32),
        lax.psum_scatter(
            totals[4].astype(jnp.bfloat16), "wsh", scatter_dimension=0, tiled=True
        ).astype(jnp.float32),
        lax.psum_scatter(
            totals[5].astype(jnp.bfloat16), "wsh", scatter_dimension=0, tiled=True
        ).astype(jnp.float32),
        lax.psum_scatter(
            totals[6].astype(jnp.bfloat16), "wsh", scatter_dimension=0, tiled=True
        ).astype(jnp.float32),
        lax.psum_scatter(
            totals[7].astype(jnp.bfloat16), "wsh", scatter_dimension=0, tiled=True
        ).astype(jnp.float32),
    )
    summed = lax.psum(
        (owned[0], owned[1], owned[2], owned[3], owned[4], owned[5], owned[6], owned[7]), "ctx"
    )
    return (
        layer_out,
        input_grad,
        summed[0],
        summed[1],
        summed[2],
        summed[3],
        summed[4],
        summed[5],
        summed[6],
        summed[7],
    )


def solution(mesh):
    placed = (
        P("wsh", "ctx", None),
        P("wsh", "ctx", None),
        P(),
        P("wsh"),
        P("wsh", None),
        P("wsh", None),
        P("wsh", None),
        P("wsh", None),
        P("wsh"),
        P("wsh", None),
        P("wsh", None),
        P("wsh", "ctx", None),
    )
    return jax.shard_map(
        on_device,
        mesh=mesh,
        in_specs=placed,
        out_specs=(
            P("wsh", "ctx", None),
            P("wsh", "ctx", None),
            P("wsh"),
            P("wsh", None),
            P("wsh", None),
            P("wsh", None),
            P("wsh", None),
            P("wsh"),
            P("wsh", None),
            P("wsh", None),
        ),
        check_vma=False,
    )
```

profile of v0, /device:TPU:0, one launch (start us, length us, event | category | flops | bytes accessed | tf_op | source)
XLA Modules:
  0.0 953.8 jit_solution(5892758774405874934)
XLA Ops:
  20.5 2.6 all_gather.38
  30.5 45.1 %all-gather.3 = bf16[2048,128]{1,0:T(8,128)(2,1)S(1)} all-gather(bf16[128,128]{1,0:T(8,128)(2,1)S(1)} %convolution_convert_fusion.8), channel_id=5, replica_groups=mesh['ctx'=16,'wsh'=2] {'ctx'}, dimensions={0}, use_global_device_ids=true | all-gather | bytes 557056 | tf_op jit(solution)/shard_map/all_gather | solution.py:191
  75.7 38.7 %all-gather.2 = bf16[2048,128]{1,0:T(8,128)(2,1)S(1)} all-gather(bf16[128,128]{1,0:T(8,128)(2,1)S(1)} %convolution_convert_fusion.9), channel_id=4, replica_groups=mesh['ctx'=16,'wsh'=2] {'ctx'}, dimensions={0}, use_global_device_ids=true | all-gather | bytes 557056 | tf_op jit(solution)/shard_map/all_gather | solution.py:191
  114.3 40.8 %all-gather.1 = bf16[2048,128]{1,0:T(8,128)(2,1)S(1)} all-gather(bf16[128,128]{1,0:T(8,128)(2,1)S(1)} %convolution_convert_fusion.10), channel_id=3, replica_groups=mesh['ctx'=16,'wsh'=2] {'ctx'}, dimensions={0}, use_global_device_ids=true | all-gather | bytes 557056 | tf_op jit(solution)/shard_map/all_gather | solution.py:191
  167.1 3.2 broadcast_multiply_fusion.1
  171.9 2.6 convolution_convert_fusion.1
  176.3 2.5 broadcast_multiply_fusion.2
  189.0 5.5 multiply_convert_fusion
  194.6 3.2 add_convert_fusion.2
  198.8 3.7 multiply_convert_fusion.1
  202.5 4.2 multiply_convert_fusion.2
  221.8 3.0 convolution_bitcast_fusion
  252.6 2.6 fusion.5
  258.8 2.7 fusion.6
  301.2 3.5 fusion.286
  304.7 2.8 fusion.282
  307.5 15.8 %reduce-scatter.17.cloned.1.call-done = f32[1,128,128]{1,2,0:T(8,128)} async-done(((f32[1,2048,128]{1,2,0:T(8,128)}), f32[1,128,128]{1,2,0:T(8,128)}) %reduce-scatter.17.cloned.1.call-update) | async-done | bytes 65552 | tf_op jit(solution)/shard_map/reduce_scatter | solution.py:249
  325.3 75.0 %reduce-scatter.15.cloned.1.call-done = f32[1,128,128]{1,2,0:T(8,128)} async-done(((f32[1,2048,128]{1,2,0:T(8,128)}), f32[1,128,128]{1,2,0:T(8,128)}) %reduce-scatter.15.cloned.1.call-update) | async-done | bytes 65552 | tf_op jit(solution)/shard_map/reduce_scatter | solution.py:249
  402.3 75.0 %reduce-scatter.13.cloned.1.call-done = f32[1,128,128]{1,2,0:T(8,128)} async-done(((f32[1,2048,128]{1,2,0:T(8,128)}), f32[1,128,128]{1,2,0:T(8,128)}) %reduce-scatter.13.cloned.1.call-update) | async-done | bytes 65552 | tf_op jit(solution)/shard_map/reduce_scatter | solution.py:249
  477.3 3.0 fusion.99
  497.1 39.5 %all-gather = bf16[2048,128]{1,0:T(8,128)(2,1)S(1)} all-gather(bf16[128,128]{1,0:T(8,128)(2,1)} %convolution_convert_fusion.11), channel_id=2, replica_groups=mesh['ctx'=16,'wsh'=2] {'ctx'}, dimensions={0}, use_global_device_ids=true | all-gather | bytes 557056 | tf_op jit(solution)/shard_map/all_gather | solution.py:191
  541.7 2.6 convolution_convert_fusion.3
  547.6 5.0 multiply_convert_fusion.3
  559.6 2.4 fusion.197
  589.3 3.8 fusion.290
  593.2 53.5 %reduce-scatter.11.cloned.1.call-done = f32[1,128,128]{1,2,0:T(8,128)} async-done(((f32[1,2048,128]{1,2,0:T(8,128)}), f32[1,128,128]{1,2,0:T(8,128)}) %reduce-scatter.11.cloned.1.call-update) | async-done | bytes 65552 | tf_op jit(solution)/shard_map/reduce_scatter | solution.py:249
  651.8 7.0 add_convert_fusion.1
  678.4 2.5 all-reduce.3
  683.6 3.4 reduce-scatter.23.cloned.1.call-done
  687.0 13.6 %reduce-scatter.27.cloned.1.call-done = bf16[256,2048]{1,0:T(8,128)(2,1)} async-done(((bf16[512,2048]{1,0:T(8,128)(2,1)}), bf16[256,2048]{1,0:T(8,128)(2,1)}) %reduce-scatter.27.cloned.1.call-update) | async-done | bytes 1048592 | tf_op jit(solution)/shard_map/reduce_scatter | solution.py:307
  700.7 13.6 %reduce-scatter.29.cloned.1.call-done = bf16[1024,512]{1,0:T(8,128)(2,1)} async-done(((bf16[2048,512]{1,0:T(8,128)(2,1)}), bf16[1024,512]{1,0:T(8,128)(2,1)}) %reduce-scatter.29.cloned.1.call-update) | async-done | bytes 1048592 | tf_op jit(solution)/shard_map/reduce_scatter | solution.py:310
  714.2 232.3 %all-reduce.5 = (f32[256]{0:T(256)}, f32[256,8]{0,1:T(8,128)}, f32[256,512]{1,0:T(8,128)}, f32[256,128]{1,0:T(8,128)}, f32[256,512]{1,0:T(8,128)}, /*index=5*/f3...) all-reduce(f32[256]{0:T(256)S(1)} %dynamic-slice_convert_fusion.1, ...), channel_id=1, replica_groups=mesh['ctx'=16,'wsh'=2] {'ctx'}, use_global_device_ids=true, to_apply=%region_77.78 | all-reduce | flops 1346048 | bytes 8077312 | tf_op jit(solution)/shard_map/psum | solution.py:314
  (703 shorter events, 221.0 us)
Async XLA Ops:
  7.2 181.7 %all-gather.9.cloned.1.call-start = ((), (), s32[]{:S(2)}) async-start(), calls=%async_computation.10 | async-start | bytes 3145728 | tf_op jit(solution)/shard_map/all_gather | solution.py:148
  8.0 12.4 %copy-start.98 = (bf16[256,512]{1,0:T(8,128)(2,1)S(1)}, bf16[256,512]{1,0:T(8,128)(2,1)}, u32[]{:S(2)}) copy-start(bf16[256,512]{1,0:T(8,128)(2,1)} %param.17) | copy-start | bytes 786436
  8.0 186.6 %all-gather.11.cloned.1.call-start = ((), (), s32[]{:S(2)}) async-start(), calls=%async_computation.11 | async-start | bytes 3145728 | tf_op jit(solution)/shard_map/all_gather | solution.py:149
  8.7 314.6 %reduce-scatter.17.cloned.1.call-start = ((), (), s32[]{:S(2)}) async-start(), calls=%async_computation.15 | async-start | bytes 1114112 | tf_op jit(solution)/shard_map/reduce_scatter | solution.py:249
  11.7 11.7 %copy-start.180 = (f32[128]{0:T(128)}, f32[128]{0:T(128)S(1)}, u32[]{:S(2)}) copy-start(f32[128]{0:T(128)S(1)} %fusion.249) | copy-start | bytes 1540
  12.1 11.3 %copy-start.136 = (f32[128]{0:T(128)}, f32[128]{0:T(128)S(1)}, u32[]{:S(2)}) copy-start(f32[128]{0:T(128)S(1)} %fusion.251) | copy-start | bytes 1540
  12.2 11.2 %copy-start.183 = (f32[128]{0:T(128)}, f32[128]{0:T(128)S(1)}, u32[]{:S(2)}) copy-start(f32[128]{0:T(128)S(1)} %fusion.253) | copy-start | bytes 1540
  12.8 11.8 %copy-start.118 = (s32[128,2]{0,1:T(2,128)}, s32[128,2]{0,1:T(2,128)S(1)}, u32[]{:S(2)}) copy-start(s32[128,2]{0,1:T(2,128)S(1)} %get-tuple-element.385) | copy-start | bytes 3076
  14.8 11.8 %copy-start.104 = (s32[128,2]{1,0:T(8,128)}, s32[128,2]{1,0:T(8,128)S(1)}, u32[]{:S(2)}) copy-start(s32[128,2]{1,0:T(8,128)S(1)} %copy.269) | copy-start | bytes 3076
  16.4 11.2 %copy-start.105 = (s32[128,2]{1,0:T(8,128)}, s32[128,2]{1,0:T(8,128)S(1)}, u32[]{:S(2)}) copy-start(s32[128,2]{1,0:T(8,128)S(1)} %copy.276) | copy-start | bytes 3076
  27.3 130.2 %copy-start.91 = (f32[128,2,64]{0,2,1:T(8,128)}, f32[128,2,64]{0,2,1:T(8,128)S(1)}, u32[]{:S(2)}) copy-start(f32[128,2,64]{0,2,1:T(8,128)S(1)} %copy.271) | copy-start | bytes 196612
  28.2 126.9 %copy-start.95 = (bf16[256,512]{1,0:T(8,128)(2,1)S(1)}, bf16[256,512]{1,0:T(8,128)(2,1)}, u32[]{:S(2)}) copy-start(bf16[256,512]{1,0:T(8,128)(2,1)} %param.19) | copy-start | bytes 786436
  75.7 86.4 %copy-start.44 = (bf16[2048,128]{1,0:T(8,128)(2,1)}, bf16[2048,128]{1,0:T(8,128)(2,1)S(1)}, u32[]{:S(2)}) copy-start(bf16[2048,128]{1,0:T(8,128)(2,1)S(1)} %all-gather.3) | copy-start | bytes 1572868
  114.3 44.3 %copy-start.40 = (bf16[2048,128]{1,0:T(8,128)(2,1)}, bf16[2048,128]{1,0:T(8,128)(2,1)S(1)}, u32[]{:S(2)}) copy-start(bf16[2048,128]{1,0:T(8,128)(2,1)S(1)} %all-gather.2) | copy-start | bytes 1572868
  114.3 43.8 %copy-start.93 = (f32[128,2,64]{0,2,1:T(8,128)S(1)}, f32[128,2,64]{0,2,1:T(8,128)}, u32[]{:S(2)}) copy-start(f32[128,2,64]{0,2,1:T(8,128)} %copy.285) | copy-start | bytes 196612
  183.1 11.4 %copy-start.18 = (f32[1,128,512]{2,1,0:T(8,128)}, f32[1,128,512]{2,1,0:T(8,128)S(1)}, u32[]{:S(2)}) copy-start(f32[1,128,512]{2,1,0:T(8,128)S(1)} %get-tuple-element.413) | copy-start | bytes 786436
  183.5 15.2 %copy-start.22 = (f32[1,128,512]{2,1,0:T(8,128)}, f32[1,128,512]{2,1,0:T(8,128)S(1)}, u32[]{:S(2)}) copy-start(f32[1,128,512]{2,1,0:T(8,128)S(1)} %get-tuple-element.408) | copy-start | bytes 786436
  183.5 15.2 %copy-start.145 = (f32[128]{0:T(128)}, f32[128]{0:T(128)S(1)}, u32[]{:S(2)}) copy-start(f32[128]{0:T(128)S(1)} %broadcast_multiply_fusion.7) | copy-start | bytes 1540
  183.9 10.6 %copy-start.15 = (f32[1,128,512]{2,1,0:T(8,128)}, f32[1,128,512]{2,1,0:T(8,128)S(1)}, u32[]{:S(2)}) copy-start(f32[1,128,512]{2,1,0:T(8,128)S(1)} %get-tuple-element.403) | copy-start | bytes 786436
  249.5 150.9 %reduce-scatter.15.cloned.1.call-start = ((), (), s32[]{:S(2)}) async-start(), calls=%async_computation.14 | async-start | bytes 1114112 | tf_op jit(solution)/shard_map/reduce_scatter | solution.py:249
  276.7 200.6 %reduce-scatter.13.cloned.1.call-start = ((), (), s32[]{:S(2)}) async-start(), calls=%async_computation.13 | async-start | bytes 1114112 | tf_op jit(solution)/shard_map/reduce_scatter | solution.py:249
  294.6 352.0 %reduce-scatter.11.cloned.1.call-start = ((), (), s32[]{:S(2)}) async-start(), calls=%async_computation.12 | async-start | bytes 1114112 | tf_op jit(solution)/shard_map/reduce_scatter | solution.py:249
  571.8 103.9 %reduce-scatter.19.cloned.1.call-start = ((), (), s32[]{:S(2)}) async-start(), calls=%async_computation.16 | async-start | bytes 12288 | tf_op jit(solution)/shard_map/reduce_scatter | solution.py:292
  582.1 93.6 %reduce-scatter.25.cloned.1.call-start = ((), (), s32[]{:S(2)}) async-start(), calls=%async_computation.19 | async-start | bytes 786432 | tf_op jit(solution)/shard_map/reduce_scatter | solution.py:301
  585.8 90.5 %reduce-scatter.21.cloned.1.call-start = ((), (), s32[]{:S(2)}) async-start(), calls=%async_computation.17 | async-start | bytes 786432 | tf_op jit(solution)/shard_map/reduce_scatter | solution.py:295
  589.2 97.8 %reduce-scatter.23.cloned.1.call-start = ((), (), s32[]{:S(2)}) async-start(), calls=%async_computation.18 | async-start | bytes 196608 | tf_op jit(solution)/shard_map/reduce_scatter | solution.py:298
  593.2 58.6 %copy-start.17 = (f32[1,128,512]{2,1,0:T(8,128)S(1)}, f32[1,128,512]{2,1,0:T(8,128)}, u32[]{:S(2)}) copy-start(f32[1,128,512]{2,1,0:T(8,128)} %copy-done.15) | copy-start | bytes 786436
  651.7 48.9 %reduce-scatter.27.cloned.1.call-start = ((), (), s32[]{:S(2)}) async-start(), calls=%async_computation.20 | async-start | bytes 3145728 | tf_op jit(solution)/shard_map/reduce_scatter | solution.py:307
  658.8 55.4 %reduce-scatter.29.cloned.1.call-start = ((), (), s32[]{:S(2)}) async-start(), calls=%async_computation.21 | async-start | bytes 3145728 | tf_op jit(solution)/shard_map/reduce_scatter | solution.py:310
  682.2 32.0 %copy-start.96 = (bf16[256,512]{1,0:T(8,128)(2,1)S(1)}, bf16[256,512]{1,0:T(8,128)(2,1)}, u32[]{:S(2)}) copy-start(bf16[256,512]{1,0:T(8,128)(2,1)} %reduce-scatter.25.cloned.1.call-done) | copy-start | bytes 786436
  682.2 32.0 %copy-start.97 = (bf16[256,512]{1,0:T(8,128)(2,1)S(1)}, bf16[256,512]{1,0:T(8,128)(2,1)}, u32[]{:S(2)}) copy-start(bf16[256,512]{1,0:T(8,128)(2,1)} %reduce-scatter.21.cloned.1.call-done) | copy-start | bytes 786436
  682.2 32.0 %copy-start.167 = (bf16[256,8]{0,1:T(8,128)(2,1)S(1)}, bf16[256,8]{0,1:T(8,128)(2,1)}, u32[]{:S(2)}) copy-start(bf16[256,8]{0,1:T(8,128)(2,1)} %reduce-scatter.19.cloned.1.call-done) | copy-start | bytes 12292
  (191 other events, 738.3 us)
Sparse Core Ops, SparseCore 0:
  9.6 13.6 all-gather.8
  24.8 11.3 all-gather.10
  249.6 73.6 reduce-scatter.16
  326.1 74.1 reduce-scatter.14
  403.0 74.2 reduce-scatter.12
  571.9 74.7 reduce-scatter.10
  649.4 3.9 reduce-scatter.18
  655.6 9.1 reduce-scatter.24
  667.2 9.0 reduce-scatter.20
  678.4 8.6 reduce-scatter.22
  689.9 10.7 reduce-scatter.26
  703.4 10.7 reduce-scatter.28
where the time goes:
time: 961 us; the launch traced here: 954 us
  blocking collectives  411 us (43%)
  waiting for transfers between devices  252 us (26%)
  matrix products  171 us (18%)
  local copies, waits for them, and re-layouts  55.3 us (6%)
  other arithmetic  44.9 us (5%)
  between operations  18.1 us (2%)
    psum x1, blocking collectives, on_device(): lax.psum((owned[0], owned[1], owned[2], owned[3], owned[4], owned[5], own...  232 us
    reduce_scatter x4, waiting for transfers between devices, on_device(): own_kv = lax.psum_scatter(full_kv, 'ctx', scatter_dimension=1, tiled=True)  219 us
    all_gather x4, blocking collectives, on_device(): kv_all = lax.all_gather(keyval, 'ctx', axis=1, tiled=True)  164 us
  transfers between devices with their start and end apart: 12, of which 8 were waited for; matrix products, arithmetic and copies ran while one was open for 16% of the time, Pallas kernels for 0%

commit v1 on v0

v1 whole, which is shorter than its diff:
```python
import math

import jax
import jax.numpy as jnp
from jax import lax
from jax.sharding import PartitionSpec as P

HIGHEST = lax.Precision.HIGHEST
BF = jnp.bfloat16
F32 = jnp.float32


def factors(size):
    out = []
    while size > 1:
        step = 4 if size % 4 == 0 else 2
        out.append(step)
        size //= step
    return out


def swap(values, mask, size):
    return lax.ppermute(values, "ctx", [(i, i ^ mask) for i in range(size)])


def smooth_unit(values_in):
    return jax.nn.gelu(values_in, approximate=False)


def normalize(inputs, gain_vec):
    centre = inputs - jnp.mean(inputs, axis=-1, keepdims=True)
    spread = jnp.mean(centre * centre, axis=-1, keepdims=True)
    return centre * lax.rsqrt(spread + 1e-05) * gain_vec


def gating(logits, expert_hot):
    chosen = jnp.sum(expert_hot * logits[..., None, :], axis=-1)
    return jax.nn.softmax(chosen, axis=-1)


def tile_scores(queries, kv_all, query_places, key_places, first_row, width):
    head = queries.shape[-1]
    tile = lax.dynamic_slice_in_dim(kv_all, first_row, width, 1)
    places = lax.dynamic_slice_in_dim(key_places, first_row, width, 0)
    keys_tile = tile[..., :head]
    values_tile = tile[..., head:]
    scores = jnp.einsum("btsh,bkh->btsk", queries, keys_tile, preferred_element_type=jnp.float32)
    allowed = places[None, None, None, :] <= query_places[None, :, None, None]
    return (keys_tile, values_tile, scores, allowed)


def log_totals(queries, kv_all, query_places, key_places):
    rows = kv_all.shape[1]
    width = math.gcd(rows, 2048)

    def log_advance(carry, index):
        top_score, total = carry
        unused_keys, unused_values, scores, allowed = tile_scores(
            queries, kv_all, query_places, key_places, index * width, width
        )
        fresh = jnp.maximum(top_score, jnp.max(jnp.where(allowed, scores, -1e30), axis=-1))
        shares = jnp.where(allowed, jnp.exp(scores - fresh[..., None]), 0.0)
        total = total * jnp.exp(top_score - fresh) + jnp.sum(shares, axis=-1)
        return ((fresh, total), None)

    shape = queries.shape[:-1]
    initial = (jnp.full(shape, -1e30, jnp.float32), jnp.zeros(shape, jnp.float32))
    carry, unused = lax.scan(log_advance, initial, jnp.arange(rows // width, dtype=jnp.int32))
    return carry[0] + jnp.log(carry[1])


def attend(queries, kv_all, query_places, key_places, log_total):
    rows = kv_all.shape[1]
    width = math.gcd(rows, 2048)

    def attend_advance(carry, index):
        unused_keys, values_tile, scores, allowed = tile_scores(
            queries, kv_all, query_places, key_places, index * width, width
        )
        shares = jnp.where(allowed, jnp.exp(scores - log_total[..., None]), 0.0).astype(
            jnp.bfloat16
        )
        return (
            carry
            + jnp.einsum("btsk,bkh->btsh", shares, values_tile, preferred_element_type=jnp.float32),
            None,
        )

    summed, unused = lax.scan(
        attend_advance,
        jnp.zeros(queries.shape, jnp.float32),
        jnp.arange(rows // width, dtype=jnp.int32),
    )
    return summed


def key_range_grads(
    queries, back_attended, kv_all, query_places, key_places, log_total, row_delta, begin, row_count
):
    width = math.gcd(row_count, 2048)

    def key_advance(carry, index):
        back_query, back_kv = carry
        keys_tile, values_tile, scores, allowed = tile_scores(
            queries, kv_all, query_places, key_places, begin + index * width, width
        )
        shares = jnp.where(allowed, jnp.exp(scores - log_total[..., None]), 0.0)
        back_shares = jnp.einsum(
            "btsh,bkh->btsk", back_attended, values_tile, preferred_element_type=jnp.float32
        )
        back_scores = (shares * (back_shares - row_delta[..., None])).astype(jnp.bfloat16)
        back_query = back_query + jnp.einsum(
            "btsk,bkh->btsh", back_scores, keys_tile, preferred_element_type=jnp.float32
        )
        back_keys = jnp.einsum(
            "btsk,btsh->bkh", back_scores, queries, preferred_element_type=jnp.float32
        )
        back_values = jnp.einsum(
            "btsk,btsh->bkh",
            shares.astype(jnp.bfloat16),
            back_attended,
            preferred_element_type=jnp.float32,
        )
        back_kv = lax.dynamic_update_slice_in_dim(
            back_kv, jnp.concatenate([back_keys, back_values], axis=-1), index * width, 1
        )
        return ((back_query, back_kv), None)

    head = queries.shape[-1]
    kv_start = jnp.zeros((queries.shape[0], row_count, 2 * head), jnp.float32)
    carry, unused = lax.scan(
        key_advance,
        (jnp.zeros(queries.shape, jnp.float32), kv_start),
        jnp.arange(row_count // width, dtype=jnp.int32),
    )
    return carry


def pick(parts, index):
    return lax.dynamic_index_in_dim(parts, index, 0, False)


def spread_out(parts, place, stride, size):
    count = parts.shape[0]
    slots = [pick(parts, place)]
    for k in range(1, count):
        slots.append(swap(pick(parts, place ^ k), k * stride, size))
    return jnp.stack(slots)


def bring_back(slots, place, stride, size):
    count = slots.shape[0]
    out = jnp.zeros(slots.shape, slots.dtype)
    for k in range(count):
        got = slots[0] if k == 0 else swap(slots[k], k * stride, size)
        out = lax.dynamic_update_index_in_dim(out, got, place ^ k, 0)
    return out


def gather_masked(rows, span, size):
    stride = 1
    for step in factors(span):
        rows = jnp.concatenate(
            [rows] + [swap(rows, j * stride, size) for j in range(1, step)], axis=0
        )
        stride *= step
    return rows


def scatter_masked(rows, span, size):
    steps = factors(span)
    stride = span
    for step in reversed(steps):
        stride //= step
        parts = rows.reshape((step, rows.shape[0] // step) + rows.shape[1:])
        total = parts[0]
        for j in range(1, step):
            total = total + swap(parts[j].astype(BF), j * stride, size).astype(F32)
        rows = total
    return rows


def reduce_all(rows, size):
    here = lax.axis_index("ctx")
    stride = 1
    for step in factors(size):
        digit = (here // stride) % step
        parts = rows.reshape(step, rows.shape[0] // step, rows.shape[1])
        total = pick(parts, digit).astype(F32)
        for j in range(1, step):
            total = total + swap(pick(parts, digit ^ j), j * stride, size).astype(F32)
        rows = total.astype(BF)
        stride *= step
    for step in reversed(factors(size)):
        stride //= step
        digit = (here // stride) % step
        out = jnp.zeros((step,) + rows.shape, rows.dtype)
        for j in range(step):
            got = rows if j == 0 else swap(rows, j * stride, size)
            out = lax.dynamic_update_index_in_dim(out, got, digit ^ j, 0)
        rows = out.reshape(step * rows.shape[0], rows.shape[1])
    return rows


def total_grads(grads, size, width=512):
    core = lax.axis_index("wsh")
    halves = [g.reshape(2, -1, width) if g.size >= 2 * width else g.reshape(2, 1, -1) for g in grads]
    mine = [pick(h, core) for h in halves]
    theirs = [pick(h, 1 - core).astype(BF) for h in halves]
    mine = [jnp.pad(h, ((0, 0), (0, width - h.shape[1]))) for h in mine]
    theirs = [jnp.pad(h, ((0, 0), (0, width - h.shape[1]))) for h in theirs]
    packed = jnp.concatenate(theirs, axis=0)
    own = jnp.concatenate(mine, axis=0)
    rows = own.shape[0]
    unit = 16 * size
    extra = -rows % unit
    packed = jnp.pad(packed, ((0, extra), (0, 0)))
    own = jnp.pad(own, ((0, extra), (0, 0)))
    own = own + lax.ppermute(packed, "wsh", [(0, 1), (1, 0)]).astype(F32)
    done = reduce_all(own.astype(BF), size)
    out = []
    at = 0
    for g, h in zip(grads, halves):
        count, wide = h.shape[1:]
        piece = done[at : at + count, :wide].astype(F32)
        at += count
        out.append(piece.reshape((g.shape[0] // 2,) + g.shape[1:]))
    return out


def whole(half):
    core = lax.axis_index("wsh")
    other = lax.ppermute(half, "wsh", [(0, 1), (1, 0)])
    both = jnp.stack([half, other])
    return jnp.concatenate([pick(both, core), pick(both, 1 - core)], axis=0)


def on_device(
    tokens,
    routes,
    block_order,
    norm_gain1,
    router_w,
    query_w,
    kv_w,
    out_w,
    norm_gain2,
    up_w,
    down_w,
    cotangent,
):
    size = lax.axis_size("ctx")
    count, local, width = tokens.shape
    rest = size // count
    here = lax.axis_index("ctx")
    place, other = here // rest, here % rest
    router, query_mat, kv_mat, out_mat, up_mat, down_mat = (
        whole(w) for w in (router_w, query_w, kv_w, out_w, up_w, down_w)
    )
    gain_one = whole(norm_gain1).astype(F32)
    gain_two = whole(norm_gain2).astype(F32)
    experts = router.shape[1]
    head = kv_mat.shape[1] // 2
    block = local // 2

    inputs = spread_out(tokens, place, rest, size).reshape(count * local, width).astype(F32)
    my_routes = spread_out(routes, place, rest, size).reshape(count * local, 2)
    my_cot = spread_out(cotangent, place, rest, size).reshape(count * local, width)

    slots = jnp.arange(count, dtype=jnp.int32)
    masks = jnp.arange(rest, dtype=jnp.int32)
    pair = (place ^ slots)[None, :] * rest + (other ^ masks)[:, None]
    first = block_order[pair.reshape(-1)]
    offsets = jnp.arange(block, dtype=jnp.int32)
    front = first[:, None] * block + offsets[None, :]
    back = (2 * size - 1 - first)[:, None] * block + offsets[None, :]
    key_places = jnp.concatenate([front, back], axis=1).reshape(-1)
    query_places = key_places[: count * local]

    expert_hot = (my_routes[..., None] == jnp.arange(experts, dtype=jnp.int32)).astype(F32)
    normed, norm_pull_one = jax.vjp(normalize, inputs, gain_one)
    normed_low = normed.astype(BF)
    logits = jnp.dot(normed_low, router, preferred_element_type=F32)
    gate_values, gate_pull = jax.vjp(lambda v: gating(v, expert_hot), logits)
    query_all = jnp.dot(normed_low, query_mat, preferred_element_type=F32).reshape(-1, experts, head)
    queries = (jnp.einsum("tse,teh->tsh", expert_hot, query_all, precision=HIGHEST) * 0.125).astype(BF)
    keyval = jnp.dot(normed_low, kv_mat, preferred_element_type=F32).astype(BF)
    kv_all = gather_masked(keyval, rest, size)
    queries, kv_all = queries[None], kv_all[None]
    log_total = log_totals(queries, kv_all, query_places, key_places)
    attended = attend(queries, kv_all, query_places, key_places, log_total)[0]
    weighted = gate_values[..., None] * attended
    mixed = (
        jnp.einsum("tse,tsh->teh", expert_hot, weighted, precision=HIGHEST)
        .reshape(-1, experts * head)
        .astype(BF)
    )
    hidden = inputs + jnp.dot(mixed, out_mat, preferred_element_type=F32)
    normed_two, norm_pull_two = jax.vjp(normalize, hidden, gain_two)
    two_low = normed_two.astype(BF)
    pre_act = jnp.dot(two_low, up_mat, preferred_element_type=F32)
    act_values, act_pull = jax.vjp(smooth_unit, pre_act)
    activated = act_values.astype(BF)
    layer_part = hidden + jnp.dot(activated, down_mat, preferred_element_type=F32)
    grad_down = jnp.einsum("tf,td->fd", activated, my_cot, preferred_element_type=F32)
    back_act = jnp.einsum("td,fd->tf", my_cot, down_mat, preferred_element_type=F32)
    (back_pre_f,) = act_pull(back_act)
    back_pre = back_pre_f.astype(BF)
    grad_up = jnp.einsum("td,tf->df", two_low, back_pre, preferred_element_type=F32)
    back_two = jnp.einsum("tf,df->td", back_pre, up_mat, preferred_element_type=F32)
    hidden_part, grad_gain2 = norm_pull_two(back_two)
    back_hidden = my_cot.astype(F32) + hidden_part
    back_branch = back_hidden.astype(BF)
    grad_out = jnp.einsum("tk,td->kd", mixed, back_branch, preferred_element_type=F32)
    early = total_grads([grad_up, grad_down, grad_out, grad_gain2], size)

    back_mixed = jnp.einsum("td,kd->tk", back_branch, out_mat, preferred_element_type=F32).reshape(
        -1, experts, head
    )
    back_slots = jnp.einsum("tse,teh->tsh", expert_hot, back_mixed, precision=HIGHEST)
    back_gates = jnp.sum(back_slots * attended, axis=-1)
    back_attended = (gate_values[..., None] * back_slots).astype(BF)
    (back_logits,) = gate_pull(back_gates)
    row_delta = jnp.sum(back_attended.astype(F32) * attended, axis=-1)
    back_query, full_kv = key_range_grads(
        queries,
        back_attended[None],
        kv_all,
        query_places,
        key_places,
        log_total,
        row_delta[None],
        0,
        kv_all.shape[1],
    )
    back_query = back_query[0].astype(BF)
    back_kv = scatter_masked(full_kv[0], rest, size).astype(BF)
    back_qall = (
        (jnp.einsum("tse,tsh->teh", expert_hot.astype(BF), back_query, preferred_element_type=F32) * 0.125)
        .reshape(-1, experts * head)
        .astype(BF)
    )
    grad_query = jnp.einsum("td,tk->dk", normed_low, back_qall, preferred_element_type=F32)
    grad_kv = jnp.einsum("td,tk->dk", normed_low, back_kv, preferred_element_type=F32)
    grad_router = jnp.einsum("td,te->de", normed_low.astype(F32), back_logits, precision=HIGHEST)
    back_normed = jnp.einsum("tk,dk->td", back_qall, query_mat, preferred_element_type=F32)
    back_normed = back_normed + jnp.einsum("tk,dk->td", back_kv, kv_mat, preferred_element_type=F32)
    back_normed = back_normed + jnp.einsum(
        "te,de->td", back_logits, router.astype(F32), precision=HIGHEST
    )
    input_part, grad_gain1 = norm_pull_one(back_normed)
    input_part = back_hidden + input_part
    late = total_grads([grad_query, grad_kv, grad_router, grad_gain1], size)

    layer_out = bring_back(layer_part.reshape(count, local, width).astype(BF), place, rest, size)
    input_grad = bring_back(input_part.reshape(count, local, width).astype(BF), place, rest, size)
    return (
        layer_out.astype(F32),
        input_grad.astype(F32),
        late[3],
        late[2],
        late[0],
        late[1],
        early[2],
        early[3],
        early[0],
        early[1],
    )


def solution(mesh):
    placed = (
        P("wsh", "ctx", None),
        P("wsh", "ctx", None),
        P(),
        P("wsh"),
        P("wsh", None),
        P("wsh", None),
        P("wsh", None),
        P("wsh", None),
        P("wsh"),
        P("wsh", None),
        P("wsh", None),
        P("wsh", "ctx", None),
    )
    return jax.shard_map(
        on_device,
        mesh=mesh,
        in_specs=placed,
        out_specs=(
            P("wsh", "ctx", None),
            P("wsh", "ctx", None),
            P("wsh"),
            P("wsh", None),
            P("wsh", None),
            P("wsh", None),
            P("wsh", None),
            P("wsh"),
            P("wsh", None),
            P("wsh", None),
        ),
        check_vma=False,
    )
```

time: 961 us -> 373 us (0.39)
  blocking collectives: 411 us -> 0 us
  waiting for transfers between devices: 252 us -> 80.9 us
  matrix products: 171 us -> 75 us
  starting transfers between devices: 0.92 us -> 65.7 us
  other arithmetic: 44.9 us -> 70.6 us
  local copies, waits for them, and re-layouts: 55.3 us -> 71.9 us
  between operations: 18.1 us -> 2.52 us
    reduce_scatter x10 -> x0, waiting for transfers between devices: 251 us -> none  [the longest x4 219 us: on_device(): own_kv = lax.psum_scatter(full_kv, 'ctx', scatter_dimension=1, tiled=True)]
    psum x1 -> x0, blocking collectives: 232 us -> none  [on_device(): lax.psum((owned[0], owned[1], owned[2], owned[3], owned[4], owned[5], own...]
    all_gather x10 -> x0, blocking collectives: 177 us -> none  [the longest x4 164 us: on_device(): kv_all = lax.all_gather(keyval, 'ctx', axis=1, tiled=True)]
    ppermute x0 -> x55, waiting for transfers between devices: none -> 80.9 us  [the longest x45 80.2 us: swap(): return lax.ppermute(values, 'ctx', [(i, i ^ mask) for i in range(size)])]
    dot_general x88 -> x22, matrix products: 135 us -> 56 us  [the longest x1 10.1 us: on_device(): pre_act = jnp.dot(two_low, up_mat, preferred_element_type=F32)]
    ppermute x0 -> x55, starting transfers between devices: none -> 65.7 us  [the longest x45 64.3 us: swap(): return lax.ppermute(values, 'ctx', [(i, i ^ mask) for i in range(size)])]
    convert_element_type x9 -> x18, other arithmetic: 2.32 us -> 27.2 us  [the longest x1 9.76 us: on_device(): activated = act_values.astype(BF)]
    reshape x0 -> x8, local copies, waits for them, and re-layouts: none -> 14.2 us  [the longest x3 7.01 us: total_grads(): g.reshape(2, -1, width)]
  transfers between devices with their start and end apart: 12 -> 55, of which waited for: 8 -> 16; matrix products, arithmetic and copies ran while one was open for 16% -> 31% of each run, Pallas kernels for 0% -> 0%
where the time goes in v1:
time: 373 us; the launch traced here: 367 us
  waiting for transfers between devices  80.9 us (22%)
  matrix products  75 us (20%)
  local copies, waits for them, and re-layouts  71.9 us (19%)
  other arithmetic  70.6 us (19%)
  starting transfers between devices  65.7 us (18%)
    ppermute x45, waiting for transfers between devices, swap(): return lax.ppermute(values, 'ctx', [(i, i ^ mask) for i in range(size)])  80.2 us
    ppermute x45, starting transfers between devices, swap(): return lax.ppermute(values, 'ctx', [(i, i ^ mask) for i in range(size)])  64.3 us
    reduce_sum x2, other arithmetic, gating(): chosen = jnp.sum(expert_hot * logits[..., None, :], axis=-1)  11.7 us
    dot_general x1, matrix products, on_device(): pre_act = jnp.dot(two_low, up_mat, preferred_element_type=F32)  10.1 us
    convert_element_type x1, other arithmetic, on_device(): activated = act_values.astype(BF)  9.76 us
  transfers between devices with their start and end apart: 55, of which 16 were waited for; matrix products, arithmetic and copies ran while one was open for 31% of the time, Pallas kernels for 0%

profile of v1, /device:TPU:0, one launch (start us, length us, event | category | flops | bytes accessed | tf_op | source)
XLA Modules:
  0.0 366.6 jit_solution(1502359864812905458)
XLA Ops:
  1.9 5.1 %collective-permute-start.2 = (bf16[128,512]{1,0:T(8,128)(2,1)S(1)}, bf16[128,512]{1,0:T(8,128)(2,1)S(1)}, u32[]{:S(2)}, u32[]{:S(2)}) collective-permute-start(bf16[128,512]{1,0:T(8,128)(2,1)S(1)} %get-tuple-element.175), channel_id=1, source_target_pairs={{0,24},{2,26},{4,28},{6,30},{8,16},{10,18},{12,20},{14,22},{16,8},... | collective-permute-start | bytes 393224 | tf_op jit(solution)/shard_map/ppermute | solution.py:23
  32.7 7.5 %select_reduce_fusion.3 = f32[512,2]{1,0:T(8,128)S(1)} fusion(f32[512,8]{1,0:T(8,128)S(1)} %fusion.95, s32[512,2]{1,0:T(8,128)S(1)} %copy.164), kind=kLoop, calls=%fused_computation.150 | loop fusion | flops 23552 | bytes 24576 | tf_op jit(solution)/shard_map/jvp()/reduce_sum | solution.py:37
  61.0 3.2 copy.169
  64.2 4.4 %fusion.53 = f32[512,2,64]{2,1,0:T(2,128)} fusion(f32[512,8,64]{2,1,0:T(8,128)} %copy.169, s32[512,2]{1,0:T(8,128)S(1)} %copy.164), kind=kOutput, calls=%fused_computation.153 | convolution fusion | flops 6299648 | bytes 1314816 | tf_op jit(solution)/shard_map/tse,teh->tsh/dot_general | solution.py:286
  72.8 2.6 select_reduce_fusion
  76.1 2.9 broadcast_multiply_fusion
  81.0 3.9 %convolution_convert_fusion = bf16[512,8,64]{2,1,0:T(8,128)(2,1)S(1)} fusion(f32[512,2,64]{2,1,0:T(2,128)} %copy.173, s32[512,2]{1,0:T(8,128)} %copy-done.23), kind=kOutput, calls=%fused_computation.72 | convolution fusion | flops 6561792 | bytes 790528 | tf_op jit(solution)/shard_map/tse,tsh->teh/dot_general | solution.py:294
  93.6 10.1 %fusion.2 = (f32[512,2048]{1,0:T(8,128)S(1)}, f32[512,2048]{1,0:T(8,128)S(1)}) fusion(bf16[256,2048]{1,0:T(8,128)(2,1)S(1)} %get-tuple-element.145, bf16[256,2048]{1,0:T(8,128)(2,1)S(1)} %get-tuple-element.144, f32[512,512]{0,1:T(8,128)S(1)} %get-tuple-element.197, f32[512]{0:T(512)S(1)} %maximum_convert_fusion.1, f32[512]{0:T(512)S(1)} %fusion.103, ...), kind=kOutput, calls=%fused_computation.12 | convolution fusion | flops 1143996416 | bytes 11540480 | tf_op jit(solution)/shard_map/dot_general | solution.py:301
  105.8 4.6 %add_convert_fusion.1 = bf16[512,2048]{1,0:T(8,128)(2,1)S(1)} fusion(f32[512,2048]{1,0:T(8,128)S(1)} %get-tuple-element.198, f32[512,2048]{1,0:T(8,128)S(1)} %get-tuple-element.199, bf16[512,512]{1,0:T(8,128)(2,1)S(1)} %bitcast.375, bf16[1024,512]{1,0:T(8,128)(2,1)S(1)} %get-tuple-element.147, bf16[1024,512]{1,0:T(8,128)(2,1)S(1)} %get-tuple-element.146), kind=kOutput, calls=%fused_computation.33 | convolution fusion | flops 1092616192 | bytes 13107200 | tf_op jit(solution)/shard_map/td,fd->tf/dot_general | solution.py:306
  115.4 3.2 copy.181
  118.7 4.4 %fusion.52 = f32[512,2,64]{2,1,0:T(2,128)} fusion(f32[512,8,64]{2,1,0:T(8,128)} %copy.181, s32[512,2]{1,0:T(8,128)} %copy-done.23), kind=kOutput, calls=%fused_computation.152 | convolution fusion | flops 6299648 | bytes 1314816 | tf_op jit(solution)/shard_map/tse,teh->tsh/dot_general | solution.py:320
  126.2 5.8 %multiply_convert_fusion = bf16[512,2,2048]{2,0,1:T(8,128)(2,1)S(1)} fusion(f32[512,2,2048]{2,0,1:T(8,128)} %copy-done.2, bf16[512,2,64]{0,2,1:T(8,128)(2,1)S(1)} %get-tuple-element.136, f32[512,2]{0,1:T(2,128)S(1)} %get-tuple-element.126, f32[512,2]{0,1:T(2,128)S(1)} %log_add_fusion, pred[512,2048]{1,0:T(8,128)(4,1)} %copy-done.8, ...), kind=kOutput, calls=%fused_computation.1 | convolution fusion | flops 278921216 | bytes 14295040 | tf_op jit(solution)/shard_map/while/body/eval_jaxpr/btsh,bkh->btsk/dot_general | solution.py:108
  134.3 6.3 %convolution_bitcast_fusion = f32[1,2048,64]{1,2,0:T(8,128)} fusion(bf16[512,2,64]{0,2,1:T(8,128)(2,1)S(1)} %get-tuple-element.136, f32[512,2,2048]{2,0,1:T(8,128)} %copy-done.2, f32[512,2]{0,1:T(2,128)S(1)} %copy-done.70, pred[512,2048]{1,0:T(8,128)(4,1)S(1)} %copy-done.9), kind=kOutput, calls=%fused_computation.58 | convolution fusion | flops 274726912 | bytes 10096640 | tf_op jit(solution)/shard_map/while/body/eval_jaxpr/btsk,btsh->bkh/dot_general | solution.py:118
  142.8 4.2 %select_reduce_fusion.2 = f32[512,8]{1,0:T(8,128)S(1)} fusion(f32[512,2]{1,0:T(8,128)} %copy.188, s32[512,2]{1,0:T(8,128)S(1)} %copy-done.24), kind=kLoop, calls=%fused_computation.148 | loop fusion | flops 20480 | bytes 24576 | tf_op jit(solution)/shard_map/transpose(jvp())/reduce_sum | solution.py:37
  153.5 4.9 %fusion.141 = f32[512,2048]{1,0:T(8,128)} fusion(bf16[512,2048]{1,0:T(8,128)(2,1)} %copy-done.27, f32[512,512]{0,1:T(8,128)S(1)} %get-tuple-element.197, f32[512]{0:T(512)S(1)} %maximum_convert_fusion.1, f32[512]{0:T(512)} %copy-done.55, f32[512]{0:T(512)S(1)} %broadcast_multiply_fusion.1), kind=kOutput, calls=%fused_computation.357 | convolution fusion | flops 1074790400 | bytes 7346176 | tf_op jit(solution)/shard_map/td,tf->df/dot_general | solution.py:309
  158.4 9.8 %fusion.5 = bf16[2048,512]{0,1:T(8,128)(2,1)} fusion(f32[512,2048]{1,0:T(8,128)S(1)} %copy-done.4), kind=kLoop, calls=%fused_computation.15 | loop fusion | flops 68157440 | bytes 6291456 | tf_op jit(solution)/shard_map/convert_element_type | solution.py:303
  168.2 5.3 %reshape.615 = f32[2,1024,512]{2,1,0:T(8,128)} reshape(f32[512,2048]{1,0:T(8,128)} %fusion.141) | data formatting | bytes 8388608 | tf_op jit(solution)/shard_map/reshape | solution.py:207
  173.5 4.0 %copy.216 = bf16[2048,512]{1,0:T(8,128)(2,1)} copy(bf16[2048,512]{0,1:T(8,128)(2,1)} %fusion.5) | data formatting | bytes 4194304 | tf_op jit(solution)/shard_map/tf,td->fd/dot_general | solution.py:305
  177.4 3.0 fusion.154
  189.8 3.7 %multiply_convert_fusion.3 = bf16[512,8,64]{2,1,0:T(8,128)(2,1)} fusion(bf16[512,2,64]{2,1,0:T(2,128)(2,1)} %copy.185, s32[512,2]{1,0:T(8,128)S(1)} %copy-done.24), kind=kOutput, calls=%fused_computation.67 | convolution fusion | flops 1597440 | bytes 659456 | tf_op jit(solution)/shard_map/tse,tsh->teh/dot_general | solution.py:339
  193.5 2.6 copy.186
  205.5 2.7 select_maximum_fusion
  233.3 2.9 collective-permute-start.27
  257.8 3.1 collective-permute-done.38
  262.5 4.0 %add_convert_fusion = bf16[2560,512]{1,0:T(8,128)(2,1)S(1)} fusion(bf16[2560,512]{1,0:T(8,128)(2,1)} %collective-permute-done.42, f32[2305,512]{1,0:T(8,128)} %select_maximum_fusion), kind=kLoop, calls=%fused_computation.8 | loop fusion | flops 3932160 | bytes 9963520 | tf_op jit(solution)/shard_map/convert_element_type | solution.py:220
  273.4 26.7 %collective-permute-done.40 = bf16[128,512]{1,0:T(8,128)(2,1)S(1)} collective-permute-done((bf16[128,512]{1,0:T(8,128)(2,1)S(1)}, bf16[128,512]{1,0:T(8,128)(2,1)S(1)}, u32[]{:S(2)}, u32[]{:S(2)}) %collective-permute-start.40) | collective-permute-done | bytes 131104 | tf_op jit(solution)/shard_map/ppermute | solution.py:23
  300.5 3.3 collective-permute-start.48
  305.0 4.5 %collective-permute-done.48 = bf16[160,512]{1,0:T(8,128)(2,1)S(1)} collective-permute-done((bf16[160,512]{1,0:T(8,128)(2,1)S(1)}, bf16[160,512]{1,0:T(8,128)(2,1)S(1)}, u32[]{:S(2)}, u32[]{:S(2)}) %collective-permute-start.48) | collective-permute-done | bytes 163872 | tf_op jit(solution)/shard_map/ppermute | solution.py:23
  309.6 7.3 %collective-permute-done.47 = bf16[160,512]{1,0:T(8,128)(2,1)S(1)} collective-permute-done((bf16[160,512]{1,0:T(8,128)(2,1)S(1)}, bf16[160,512]{1,0:T(8,128)(2,1)S(1)}, u32[]{:S(2)}, u32[]{:S(2)}) %collective-permute-start.47) | collective-permute-done | bytes 163872 | tf_op jit(solution)/shard_map/ppermute | solution.py:23
  323.7 8.8 %collective-permute-done.50 = bf16[160,512]{1,0:T(8,128)(2,1)S(1)} collective-permute-done((bf16[160,512]{1,0:T(8,128)(2,1)S(1)}, bf16[160,512]{1,0:T(8,128)(2,1)S(1)}, u32[]{:S(2)}, u32[]{:S(2)}) %collective-permute-start.50) | collective-permute-done | bytes 163872 | tf_op jit(solution)/shard_map/ppermute | solution.py:23
  338.5 11.8 %collective-permute-done.52 = bf16[640,512]{1,0:T(8,128)(2,1)S(1)} collective-permute-done((bf16[640,512]{1,0:T(8,128)(2,1)S(1)}, bf16[640,512]{1,0:T(8,128)(2,1)S(1)}, u32[]{:S(2)}, u32[]{:S(2)}) %collective-permute-start.52) | collective-permute-done | bytes 655392 | tf_op jit(solution)/shard_map/ppermute | solution.py:23
  350.4 10.5 %collective-permute-done.53 = bf16[640,512]{1,0:T(8,128)(2,1)S(1)} collective-permute-done((bf16[640,512]{1,0:T(8,128)(2,1)S(1)}, bf16[640,512]{1,0:T(8,128)(2,1)S(1)}, u32[]{:S(2)}, u32[]{:S(2)}) %collective-permute-start.53) | collective-permute-done | bytes 655392 | tf_op jit(solution)/shard_map/ppermute | solution.py:23
  (419 shorter events, 176.9 us)
Async XLA Ops:
  1.9 20.2 %collective-permute-start.2 = (bf16[128,512]{1,0:T(8,128)(2,1)S(1)}, bf16[128,512]{1,0:T(8,128)(2,1)S(1)}, u32[]{:S(2)}, u32[]{:S(2)}) collective-permute-start(bf16[128,512]{1,0:T(8,128)(2,1)S(1)} %get-tuple-element.175), channel_id=1, source_target_pairs={{0,24},{2,26},{4,28},{6,30},{8,16},{10,18},{12,20},{14,22},{16,8},... | collective-permute-start | bytes 393224 | tf_op jit(solution)/shard_map/ppermute | solution.py:23
  7.0 17.5 %collective-permute-start.1 = (bf16[128,512]{1,0:T(8,128)(2,1)S(1)}, bf16[128,512]{1,0:T(8,128)(2,1)S(1)}, u32[]{:S(2)}, u32[]{:S(2)}) collective-permute-start(bf16[128,512]{1,0:T(8,128)(2,1)S(1)} %get-tuple-element.176), channel_id=1, source_target_pairs={{0,16},{2,18},{4,20},{6,22},{8,24},{10,26},{12,28},{14,30},{16,0},... | collective-permute-start | bytes 393224 | tf_op jit(solution)/shard_map/ppermute | solution.py:23
  20.9 30.5 %collective-permute-start.8 = (bf16[256,512]{1,0:T(8,128)(2,1)}, bf16[256,512]{1,0:T(8,128)(2,1)}, u32[]{:S(2)}, u32[]{:S(2)}) collective-permute-start(bf16[256,512]{1,0:T(8,128)(2,1)} %param.17), channel_id=1, source_target_pairs={{0,1},{1,0},{2,3},{3,2},{4,5},{5,4},{6,7},{7,6},{8,9},{9,8},{10,11... | collective-permute-start | bytes 786440 | tf_op jit(solution)/shard_map/ppermute | solution.py:233
  21.6 64.7 %collective-permute-start.13 = (bf16[256,512]{1,0:T(8,128)(2,1)}, bf16[256,512]{1,0:T(8,128)(2,1)}, u32[]{:S(2)}, u32[]{:S(2)}) collective-permute-start(bf16[256,512]{1,0:T(8,128)(2,1)} %param.19), channel_id=1, source_target_pairs={{0,1},{1,0},{2,3},{3,2},{4,5},{5,4},{6,7},{7,6},{8,9},{9,8},{10,11... | collective-permute-start | bytes 786440 | tf_op jit(solution)/shard_map/ppermute | solution.py:233
  22.1 20.7 %collective-permute-start.22 = (bf16[128,512]{1,0:T(8,128)(2,1)}, bf16[128,512]{1,0:T(8,128)(2,1)}, u32[]{:S(2)}, u32[]{:S(2)}) collective-permute-start(bf16[128,512]{1,0:T(8,128)(2,1)} %get-tuple-element.163), channel_id=1, source_target_pairs={{0,24},{2,26},{4,28},{6,30},{8,16},{10,18},{12,20},{14,22},{16,8},... | collective-permute-start | bytes 393224 | tf_op jit(solution)/shard_map/ppermute | solution.py:23
  24.5 18.3 %collective-permute-start.21 = (bf16[128,512]{1,0:T(8,128)(2,1)}, bf16[128,512]{1,0:T(8,128)(2,1)}, u32[]{:S(2)}, u32[]{:S(2)}) collective-permute-start(bf16[128,512]{1,0:T(8,128)(2,1)} %get-tuple-element.164), channel_id=1, source_target_pairs={{0,16},{2,18},{4,20},{6,22},{8,24},{10,26},{12,28},{14,30},{16,0},... | collective-permute-start | bytes 393224 | tf_op jit(solution)/shard_map/ppermute | solution.py:23
  25.2 20.1 %collective-permute-start.20 = (bf16[128,512]{1,0:T(8,128)(2,1)}, bf16[128,512]{1,0:T(8,128)(2,1)}, u32[]{:S(2)}, u32[]{:S(2)}) collective-permute-start(bf16[128,512]{1,0:T(8,128)(2,1)} %get-tuple-element.162), channel_id=1, source_target_pairs={{0,8},{2,10},{4,12},{6,14},{8,0},{10,2},{12,4},{14,6},{16,24},{18,... | collective-permute-start | bytes 393224 | tf_op jit(solution)/shard_map/ppermute | solution.py:23
  42.8 46.8 %collective-permute-start.16 = (bf16[1024,512]{1,0:T(8,128)(2,1)}, bf16[1024,512]{1,0:T(8,128)(2,1)}, u32[]{:S(2)}, u32[]{:S(2)}) collective-permute-start(bf16[1024,512]{1,0:T(8,128)(2,1)} %param.22), channel_id=1, source_target_pairs={{0,1},{1,0},{2,3},{3,2},{4,5},{5,4},{6,7},{7,6},{8,9},{9,8},{10,11... | collective-permute-start | bytes 3145736 | tf_op jit(solution)/shard_map/ppermute | solution.py:233
  42.8 27.0 %collective-permute-start.12 = (bf16[512,128]{1,0:T(8,128)(2,1)}, bf16[512,128]{1,0:T(8,128)(2,1)}, u32[]{:S(2)}, u32[]{:S(2)}) collective-permute-start(bf16[512,128]{1,0:T(8,128)(2,1)} %convolution_convert_fusion.2), channel_id=1, source_target_pairs={{0,6},{2,4},{4,2},{6,0},{8,14},{10,12},{12,10},{14,8},{16,22},{18,... | collective-permute-start | bytes 393224 | tf_op jit(solution)/shard_map/ppermute | solution.py:23
  45.3 24.6 %collective-permute-start.11 = (bf16[512,128]{1,0:T(8,128)(2,1)}, bf16[512,128]{1,0:T(8,128)(2,1)}, u32[]{:S(2)}, u32[]{:S(2)}) collective-permute-start(bf16[512,128]{1,0:T(8,128)(2,1)} %convolution_convert_fusion.2), channel_id=1, source_target_pairs={{0,4},{2,6},{4,0},{6,2},{8,12},{10,14},{12,8},{14,10},{16,20},{18,... | collective-permute-start | bytes 393224 | tf_op jit(solution)/shard_map/ppermute | solution.py:23
  51.3 18.6 %collective-permute-start.10 = (bf16[512,128]{1,0:T(8,128)(2,1)}, bf16[512,128]{1,0:T(8,128)(2,1)}, u32[]{:S(2)}, u32[]{:S(2)}) collective-permute-start(bf16[512,128]{1,0:T(8,128)(2,1)} %convolution_convert_fusion.2), channel_id=1, source_target_pairs={{0,2},{2,0},{4,6},{6,4},{8,10},{10,8},{12,14},{14,12},{16,18},{18,... | collective-permute-start | bytes 393224 | tf_op jit(solution)/shard_map/ppermute | solution.py:23
  69.8 21.7 %collective-permute-start.15 = (bf16[256,2048]{1,0:T(8,128)(2,1)}, bf16[256,2048]{1,0:T(8,128)(2,1)}, u32[]{:S(2)}, u32[]{:S(2)}) collective-permute-start(bf16[256,2048]{1,0:T(8,128)(2,1)} %param.21), channel_id=1, source_target_pairs={{0,1},{1,0},{2,3},{3,2},{4,5},{5,4},{6,7},{7,6},{8,9},{9,8},{10,11... | collective-permute-start | bytes 3145736 | tf_op jit(solution)/shard_map/ppermute | solution.py:233
  186.1 32.2 %collective-permute-start.17 = (bf16[128,512]{0,1:T(8,128)(2,1)}, bf16[128,512]{0,1:T(8,128)(2,1)}, u32[]{:S(2)}, u32[]{:S(2)}) collective-permute-start(bf16[128,512]{0,1:T(8,128)(2,1)} %get-tuple-element.167), channel_id=1, source_target_pairs={{0,8},{2,10},{4,12},{6,14},{8,0},{10,2},{12,4},{14,6},{16,24},{18,... | collective-permute-start | bytes 393224 | tf_op jit(solution)/shard_map/ppermute | solution.py:23
  186.7 33.2 %collective-permute-start.18 = (bf16[128,512]{0,1:T(8,128)(2,1)}, bf16[128,512]{0,1:T(8,128)(2,1)}, u32[]{:S(2)}, u32[]{:S(2)}) collective-permute-start(bf16[128,512]{0,1:T(8,128)(2,1)} %get-tuple-element.166), channel_id=1, source_target_pairs={{0,16},{2,18},{4,20},{6,22},{8,24},{10,26},{12,28},{14,30},{16,0},... | collective-permute-start | bytes 393224 | tf_op jit(solution)/shard_map/ppermute | solution.py:23
  199.1 10.6 %collective-permute-start.25 = (bf16[512,128]{0,1:T(8,128)(2,1)S(1)}, bf16[512,128]{0,1:T(8,128)(2,1)S(1)}, u32[]{:S(2)}, u32[]{:S(2)}) collective-permute-start(bf16[512,128]{0,1:T(8,128)(2,1)S(1)} %get-tuple-element.159), channel_id=1, source_target_pairs={{0,6},{2,4},{4,2},{6,0},{8,14},{10,12},{12,10},{14,8},{16,22},{18,... | collective-permute-start | bytes 393224 | tf_op jit(solution)/shard_map/ppermute | solution.py:23
  209.8 11.9 %collective-permute-start.19 = (bf16[128,512]{0,1:T(8,128)(2,1)}, bf16[128,512]{0,1:T(8,128)(2,1)S(1)}, u32[]{:S(2)}, u32[]{:S(2)}) collective-permute-start(bf16[128,512]{0,1:T(8,128)(2,1)} %get-tuple-element.165), channel_id=1, source_target_pairs={{0,24},{2,26},{4,28},{6,30},{8,16},{10,18},{12,20},{14,22},{16,8},... | collective-permute-start | bytes 393224 | tf_op jit(solution)/shard_map/ppermute | solution.py:23
  216.1 10.4 %collective-permute-start.29 = (bf16[512,512]{1,0:T(8,128)(2,1)}, bf16[512,512]{1,0:T(8,128)(2,1)}, u32[]{:S(2)}, u32[]{:S(2)}) collective-permute-start(bf16[512,512]{1,0:T(8,128)(2,1)} %pad.33), channel_id=1, source_target_pairs={{0,1},{1,0},{2,3},{3,2},{4,5},{5,4},{6,7},{7,6},{8,9},{9,8},{10,11... | collective-permute-start | bytes 1572872 | tf_op jit(solution)/shard_map/ppermute | solution.py:219
  217.7 44.7 %collective-permute-start.42 = (bf16[2560,512]{1,0:T(8,128)(2,1)S(1)}, bf16[2560,512]{1,0:T(8,128)(2,1)}, u32[]{:S(2)}, u32[]{:S(2)}) collective-permute-start(bf16[2560,512]{1,0:T(8,128)(2,1)S(1)} %pad.37), channel_id=1, source_target_pairs={{0,1},{1,0},{2,3},{3,2},{4,5},{5,4},{6,7},{7,6},{8,9},{9,8},{10,11... | collective-permute-start | bytes 7864328 | tf_op jit(solution)/shard_map/ppermute | solution.py:219
  233.3 11.0 %collective-permute-start.27 = (bf16[128,512]{0,1:T(8,128)(2,1)}, bf16[128,512]{0,1:T(8,128)(2,1)S(1)}, u32[]{:S(2)}, u32[]{:S(2)}) collective-permute-start(bf16[128,512]{0,1:T(8,128)(2,1)} %get-tuple-element.155), channel_id=1, source_target_pairs={{0,16},{2,18},{4,20},{6,22},{8,24},{10,26},{12,28},{14,30},{16,0},... | collective-permute-start | bytes 393224 | tf_op jit(solution)/shard_map/ppermute | solution.py:23
  261.0 10.9 %collective-permute-start.39 = (bf16[128,512]{1,0:T(8,128)(2,1)S(1)}, bf16[128,512]{1,0:T(8,128)(2,1)S(1)}, u32[]{:S(2)}, u32[]{:S(2)}) collective-permute-start(bf16[128,512]{1,0:T(8,128)(2,1)S(1)} %bitcast.410), channel_id=1, source_target_pairs={{0,2},{2,0},{4,6},{6,4},{8,10},{10,8},{12,14},{14,12},{16,18},{18,... | collective-permute-start | bytes 393224 | tf_op jit(solution)/shard_map/ppermute | solution.py:23
  266.6 33.5 %collective-permute-start.45 = (bf16[640,512]{1,0:T(8,128)(2,1)S(1)}, bf16[640,512]{1,0:T(8,128)(2,1)S(1)}, u32[]{:S(2)}, u32[]{:S(2)}) collective-permute-start(bf16[640,512]{1,0:T(8,128)(2,1)S(1)} %get-tuple-element.142), channel_id=1, source_target_pairs={{0,6},{2,4},{4,2},{6,0},{8,14},{10,12},{12,10},{14,8},{16,22},{18,... | collective-permute-start | bytes 1966088 | tf_op jit(solution)/shard_map/ppermute | solution.py:23
  268.1 32.0 %collective-permute-start.44 = (bf16[640,512]{1,0:T(8,128)(2,1)S(1)}, bf16[640,512]{1,0:T(8,128)(2,1)S(1)}, u32[]{:S(2)}, u32[]{:S(2)}) collective-permute-start(bf16[640,512]{1,0:T(8,128)(2,1)S(1)} %get-tuple-element.143), channel_id=1, source_target_pairs={{0,4},{2,6},{4,0},{6,2},{8,12},{10,14},{12,8},{14,10},{16,20},{18,... | collective-permute-start | bytes 1966088 | tf_op jit(solution)/shard_map/ppermute | solution.py:23
  268.7 31.5 %collective-permute-start.43 = (bf16[640,512]{1,0:T(8,128)(2,1)S(1)}, bf16[640,512]{1,0:T(8,128)(2,1)S(1)}, u32[]{:S(2)}, u32[]{:S(2)}) collective-permute-start(bf16[640,512]{1,0:T(8,128)(2,1)S(1)} %get-tuple-element.141), channel_id=1, source_target_pairs={{0,2},{2,0},{4,6},{6,4},{8,10},{10,8},{12,14},{14,12},{16,18},{18,... | collective-permute-start | bytes 1966088 | tf_op jit(solution)/shard_map/ppermute | solution.py:23
  271.3 28.8 %collective-permute-start.40 = (bf16[128,512]{1,0:T(8,128)(2,1)S(1)}, bf16[128,512]{1,0:T(8,128)(2,1)S(1)}, u32[]{:S(2)}, u32[]{:S(2)}) collective-permute-start(bf16[128,512]{1,0:T(8,128)(2,1)S(1)} %bitcast.411), channel_id=1, source_target_pairs={{0,4},{2,6},{4,0},{6,2},{8,12},{10,14},{12,8},{14,10},{16,20},{18,... | collective-permute-start | bytes 393224 | tf_op jit(solution)/shard_map/ppermute | solution.py:23
  271.9 33.1 %collective-permute-start.41 = (bf16[128,512]{1,0:T(8,128)(2,1)S(1)}, bf16[128,512]{1,0:T(8,128)(2,1)S(1)}, u32[]{:S(2)}, u32[]{:S(2)}) collective-permute-start(bf16[128,512]{1,0:T(8,128)(2,1)S(1)} %bitcast.413), channel_id=1, source_target_pairs={{0,6},{2,4},{4,2},{6,0},{8,14},{10,12},{12,10},{14,8},{16,22},{18,... | collective-permute-start | bytes 393224 | tf_op jit(solution)/shard_map/ppermute | solution.py:23
  303.8 13.0 %collective-permute-start.47 = (bf16[160,512]{1,0:T(8,128)(2,1)S(1)}, bf16[160,512]{1,0:T(8,128)(2,1)S(1)}, u32[]{:S(2)}, u32[]{:S(2)}) collective-permute-start(bf16[160,512]{1,0:T(8,128)(2,1)S(1)} %get-tuple-element.150), channel_id=1, source_target_pairs={{0,16},{2,18},{4,20},{6,22},{8,24},{10,26},{12,28},{14,30},{16,0},... | collective-permute-start | bytes 491528 | tf_op jit(solution)/shard_map/ppermute | solution.py:23
  303.8 13.0 %collective-permute-start.46 = (bf16[160,512]{1,0:T(8,128)(2,1)S(1)}, bf16[160,512]{1,0:T(8,128)(2,1)S(1)}, u32[]{:S(2)}, u32[]{:S(2)}) collective-permute-start(bf16[160,512]{1,0:T(8,128)(2,1)S(1)} %get-tuple-element.148), channel_id=1, source_target_pairs={{0,8},{2,10},{4,12},{6,14},{8,0},{10,2},{12,4},{14,6},{16,24},{18,... | collective-permute-start | bytes 491528 | tf_op jit(solution)/shard_map/ppermute | solution.py:23
  318.2 14.4 %collective-permute-start.50 = (bf16[160,512]{1,0:T(8,128)(2,1)S(1)}, bf16[160,512]{1,0:T(8,128)(2,1)S(1)}, u32[]{:S(2)}, u32[]{:S(2)}) collective-permute-start(bf16[160,512]{1,0:T(8,128)(2,1)S(1)} %get-tuple-element.133), channel_id=1, source_target_pairs={{0,16},{2,18},{4,20},{6,22},{8,24},{10,26},{12,28},{14,30},{16,0},... | collective-permute-start | bytes 491528 | tf_op jit(solution)/shard_map/ppermute | solution.py:23
  319.7 12.9 %collective-permute-start.51 = (bf16[160,512]{1,0:T(8,128)(2,1)S(1)}, bf16[160,512]{1,0:T(8,128)(2,1)S(1)}, u32[]{:S(2)}, u32[]{:S(2)}) collective-permute-start(bf16[160,512]{1,0:T(8,128)(2,1)S(1)} %get-tuple-element.133), channel_id=1, source_target_pairs={{0,24},{2,26},{4,28},{6,30},{8,16},{10,18},{12,20},{14,22},{16,8},... | collective-permute-start | bytes 491528 | tf_op jit(solution)/shard_map/ppermute | solution.py:23
  332.6 17.7 %collective-permute-start.52 = (bf16[640,512]{1,0:T(8,128)(2,1)S(1)}, bf16[640,512]{1,0:T(8,128)(2,1)S(1)}, u32[]{:S(2)}, u32[]{:S(2)}) collective-permute-start(bf16[640,512]{1,0:T(8,128)(2,1)S(1)} %bitcast.380), channel_id=1, source_target_pairs={{0,2},{2,0},{4,6},{6,4},{8,10},{10,8},{12,14},{14,12},{16,18},{18,... | collective-permute-start | bytes 1966088 | tf_op jit(solution)/shard_map/ppermute | solution.py:23
  333.3 27.7 %collective-permute-start.53 = (bf16[640,512]{1,0:T(8,128)(2,1)S(1)}, bf16[640,512]{1,0:T(8,128)(2,1)S(1)}, u32[]{:S(2)}, u32[]{:S(2)}) collective-permute-start(bf16[640,512]{1,0:T(8,128)(2,1)S(1)} %bitcast.381), channel_id=1, source_target_pairs={{0,4},{2,6},{4,0},{6,2},{8,12},{10,14},{12,8},{14,10},{16,20},{18,... | collective-permute-start | bytes 1966088 | tf_op jit(solution)/shard_map/ppermute | solution.py:23
  334.8 26.2 %collective-permute-start.54 = (bf16[640,512]{1,0:T(8,128)(2,1)S(1)}, bf16[640,512]{1,0:T(8,128)(2,1)S(1)}, u32[]{:S(2)}, u32[]{:S(2)}) collective-permute-start(bf16[640,512]{1,0:T(8,128)(2,1)S(1)} %bitcast.382), channel_id=1, source_target_pairs={{0,6},{2,4},{4,2},{6,0},{8,14},{10,12},{12,10},{14,8},{16,22},{18,... | collective-permute-start | bytes 1966088 | tf_op jit(solution)/shard_map/ppermute | solution.py:23
  (95 other events, 815.1 us)

commit v2 on v1

v2 whole, which is shorter than its diff:
```python
import functools
import math

import jax
import jax.numpy as jnp
from jax import lax
from jax.experimental import pallas as pl
from jax.experimental.pallas import tpu as pltpu
from jax.sharding import PartitionSpec as P

BF = jnp.bfloat16
F32 = jnp.float32
I32 = jnp.int32
NONE = -1e30
TWO = 2


def factors(size):
    out = []
    while size > 1:
        step = 4 if size % 4 == 0 else 2
        out.append(step)
        size //= step
    return out


def swap(values, mask, size):
    return lax.ppermute(values, "ctx", [(i, i ^ mask) for i in range(size)])


def trade(values):
    return lax.ppermute(values, "wsh", [(0, 1), (1, 0)])


def pick(parts, index):
    return lax.dynamic_index_in_dim(parts, index, 0, False)


def mm(a, b, left=1, right=0):
    return lax.dot_general(a, b, (((left,), (right,)), ((), ())), preferred_element_type=F32)


def call(body, outs, args, scratch=(), smem=(), flops=0, mib=40):
    whole = pl.BlockSpec(memory_space=pltpu.VMEM)
    scalars = pl.BlockSpec(memory_space=pltpu.SMEM)
    moved = sum(math.prod(s) * jnp.dtype(d).itemsize for s, d in outs)
    moved += sum(a.size * a.dtype.itemsize for a in args)
    return pl.pallas_call(
        body,
        out_shape=[jax.ShapeDtypeStruct(s, d) for s, d in outs],
        in_specs=[scalars if i in smem else whole for i in range(len(args))],
        out_specs=[whole] * len(outs),
        scratch_shapes=[pltpu.VMEM(s, d) for s, d in scratch],
        compiler_params=pltpu.CompilerParams(vmem_limit_bytes=mib << 20),
        cost_estimate=pl.CostEstimate(flops=int(flops), bytes_accessed=int(moved), transcendentals=0),
    )(*args)


def join(slots):
    half = slots[0].shape[0] // 2
    return jnp.concatenate([s[:half] for s in slots] + [s[half:] for s in slots], axis=0)


def slot_rows(rows, k, count):
    half = rows.shape[0] // (2 * count)
    low = k * half
    high = rows.shape[0] // 2 + k * half
    return jnp.concatenate([rows[low : low + half], rows[high : high + half]], axis=0)


def centred(rows):
    centre = rows - jnp.mean(rows, axis=-1, keepdims=True)
    scale = lax.rsqrt(jnp.mean(centre * centre, axis=-1, keepdims=True) + 1e-05)
    return centre * scale, scale


def fill(scratch, own, other, core):
    half = own.shape[0]
    scratch[pl.ds(pl.multiple_of(core * half, half), half), :] = own[...]
    scratch[pl.ds(pl.multiple_of((1 - core) * half, half), half), :] = other[...]


def gain_row(own, other, core):
    part = core.astype(F32)
    a, b = own[...].astype(F32), other[...].astype(F32)
    return jnp.concatenate([a + part * (b - a), b + part * (a - b)], axis=1)


def pick_gain(own, other, core):
    a, b = own[...].astype(F32), other[...].astype(F32)
    first = jnp.where(core == 0, a, b)
    second = jnp.where(core == 0, b, a)
    return jnp.concatenate([first, second], axis=1)


def route_rows(pieces):
    lane = lax.broadcasted_iota(I32, (8, 128), 1)
    low = lane < 64
    rolled = [pltpu.roll(p, 64, 1) for p in pieces]
    count = len(pieces)
    front = [jnp.where(low, pieces[i], rolled[i + 1]) for i in range(0, count, 2)]
    back = [jnp.where(low, rolled[i], pieces[i + 1]) for i in range(0, count, 2)]
    return jnp.concatenate(front + back, axis=1)


def project_body(count, rest, experts, head, *refs):
    tok, others = refs[0], refs[1:count]
    (routes0, *routes_x) = refs[count : 2 * count]
    g_own, g_other, q_own, q_other, k_own, k_other, r_own, r_other = refs[2 * count : 2 * count + 8]
    kv_out, qt_out, nt_out, gate_out, route_out, wq, wk, wr = refs[2 * count + 8 :]
    core = lax.axis_index("wsh")
    place = lax.axis_index("ctx") // rest
    fill(wq, q_own, q_other, core)
    fill(wk, k_own, k_other, core)
    wr[...] = jnp.zeros_like(wr)
    half = r_own.shape[0]
    wr[pl.ds(pl.multiple_of(core * half, half), half), :experts] = r_own[...].astype(F32)
    wr[pl.ds(pl.multiple_of((1 - core) * half, half), half), :experts] = r_other[...].astype(F32)
    rows = join([tok[place]] + [o[...] for o in others]).astype(F32)
    unit, _ = centred(rows)
    normed = (unit * pick_gain(g_own, g_other, core)).astype(BF)
    nt_out[...] = normed.T
    kv_out[...] = mm(normed, wk[...]).astype(BF)
    routes = route_rows([routes0[place]] + [r[...] for r in routes_x])
    route_out[...] = routes
    logits = mm(normed, wr[...].astype(BF)).T
    queries = (mm(normed, wq[...]) * 0.125).T
    chosen = []
    for s in range(TWO):
        route = routes[s : s + 1]
        total = jnp.zeros((head, rows.shape[0]), F32)
        value = jnp.zeros((1, rows.shape[0]), F32)
        for e in range(experts):
            here = route == e
            total = jnp.where(here, queries[e * head : (e + 1) * head], total)
            value = jnp.where(here, logits[e : e + 1], value)
        qt_out[s * head : (s + 1) * head, :] = total.astype(BF)
        chosen.append(value)
    top = jnp.maximum(chosen[0], chosen[1])
    raised = [jnp.exp(c - top) for c in chosen]
    total = raised[0] + raised[1]
    gate_out[...] = jnp.concatenate([r / total for r in raised], axis=0)


def places(order, count, rest, block, width, part):
    me = lax.axis_index("ctx")
    place, other = me // rest, me % rest
    size = count * rest
    lane = lax.broadcasted_iota(I32, (1, width), 1)
    out = jnp.zeros((1, width), I32)
    for k in range(count):
        first = order[(place ^ k) * rest + other]
        base = jnp.where(part == 0, first, 2 * size - 1 - first) * block
        out = jnp.where(lane // block == k, lane - k * block + base, out)
    return out


def key_bases(order, count, rest, block, chunk, part):
    me = lax.axis_index("ctx")
    place, other = me // rest, me % rest
    size = count * rest
    out = []
    for k in range(count):
        first = order[(place ^ k) * rest + (other ^ chunk)]
        out.append((first if part == 0 else 2 * size - 1 - first) * block)
    return out


def masked(scores, gap, bases, block):
    parts = [
        jnp.where(gap <= -base, scores[k * block : (k + 1) * block], NONE)
        for k, base in enumerate(bases)
    ]
    return jnp.concatenate(parts, axis=0)


def scored(kv, side, h, gap, order, count, rest, block, chunk, half):
    first = mm(kv[:half], side)
    if h == 0:
        return masked(first, gap, key_bases(order, count, rest, block, chunk, 0), block)
    second = mm(kv[half:], side)
    second = masked(second, gap, key_bases(order, count, rest, block, chunk, 1), block)
    return jnp.concatenate([first, second], axis=0)


def load_keys(kv_refs, kv_all, kv_turned):
    rows = kv_refs[0].shape[0]
    for c, ref in enumerate(kv_refs):
        kv_all[c * rows : (c + 1) * rows, :] = ref[...]
        kv_turned[:, c * rows : (c + 1) * rows] = ref[...].T


def attend_body(count, rest, experts, head, pieces, *refs):
    order = refs[0]
    kv_refs = refs[1 : 1 + pieces]
    qt, gates, routes, tok = refs[1 + pieces : 5 + pieces]
    others = refs[5 + pieces : 4 + pieces + count]
    g_own, g_other, o_own, o_other = refs[4 + pieces + count : 8 + pieces + count]
    att_out, log_out, mixed_out, hidden_out, two_out, turned_out, kv_all, kv_turned, wo = refs[
        8 + pieces + count :
    ]
    core = lax.axis_index("wsh")
    place = lax.axis_index("ctx") // rest
    total = qt.shape[1]
    half = total // 2
    block = half // count
    load_keys(kv_refs, kv_all, kv_turned)
    fill(wo, o_own, o_other, core)
    for h in range(2):
        gap = lax.broadcasted_iota(I32, (block, half), 0) - places(order, count, rest, block, half, h)
        for s in range(TWO):
            side = qt[s * head : (s + 1) * head, h * half : (h + 1) * half]
            side = jnp.concatenate([side, jnp.zeros_like(side)], axis=0)
            reach = half * (h + 1)

            def step(chunk, carry, side=side, h=h, gap=gap, reach=reach):
                top, norm, summed = carry
                at = pl.multiple_of(chunk * total, total)
                kv = kv_all[pl.ds(at, total), :]
                scores = scored(kv, side, h, gap, order, count, rest, block, chunk, half)
                fresh = jnp.maximum(top, jnp.max(scores, axis=0, keepdims=True))
                shares = jnp.exp(scores - fresh)
                fade = jnp.exp(top - fresh)
                norm = norm * fade + jnp.sum(shares, axis=0, keepdims=True)
                values = kv_turned[head:, pl.ds(at, reach)]
                summed = summed * fade + mm(values, shares.astype(BF))
                return fresh, norm, summed

            start = (
                jnp.full((1, half), NONE, F32),
                jnp.zeros((1, half), F32),
                jnp.zeros((head, half), F32),
            )
            top, norm, summed = lax.fori_loop(0, rest, step, start, unroll=rest <= 4)
            log_out[s : s + 1, h * half : (h + 1) * half] = top + jnp.log(norm)
            att_out[s * head : (s + 1) * head, h * half : (h + 1) * half] = summed / norm
    for e in range(experts):
        part = jnp.zeros((head, total), F32)
        for s in range(TWO):
            gate = jnp.where(routes[s : s + 1] == e, gates[s : s + 1], 0.0)
            part = part + gate * att_out[s * head : (s + 1) * head, :]
        mixed_out[e * head : (e + 1) * head, :] = part.astype(BF)
    rows = join([tok[place]] + [o[...] for o in others]).astype(F32)
    hidden = rows + mm(mixed_out[...].T, wo[...])
    hidden_out[...] = hidden
    unit, _ = centred(hidden)
    two = (unit * pick_gain(g_own, g_other, core)).astype(BF)
    two_out[...] = two
    turned_out[...] = two.T


def feed_body(count, rest, first, tile, *refs):
    two, turned, cot = refs[:3]
    others = refs[3 : 2 + count]
    u_own, u_other, down, layer_in = refs[2 + count : 6 + count]
    at = 6 + count
    back_in = None
    if not first:
        back_in = refs[at]
        at += 1
    if first:
        layer_out, back_out, send, keep = refs[at : at + 4]
        up, cots = refs[at + 4 :]
    else:
        outs = refs[at : at + count + 4]
        layer_pieces, back_out, keep_down, keep, send = outs[:count], *outs[count:]
        up, cots, layer_out = refs[at + count + 4 :]
    core = lax.axis_index("wsh")
    place = lax.axis_index("ctx") // rest
    side = (1 - core) if first else core
    width = down.shape[0]
    half = u_own.shape[0]
    lanes = pl.ds(pl.multiple_of(side * width, width), width)
    up[pl.ds(pl.multiple_of(core * half, half), half), :] = u_own[:, lanes]
    up[pl.ds(pl.multiple_of((1 - core) * half, half), half), :] = u_other[:, lanes]
    cots[...] = join([cot[place]] + [o[...] for o in others])
    layer_out[...] = layer_in[...]
    if first:
        back_out[...] = jnp.zeros_like(back_out)
    else:
        back_out[...] = back_in[...]
    mine = pl.ds(pl.multiple_of(core * half, half), half)
    theirs = pl.ds(pl.multiple_of((1 - core) * half, half), half)
    dim = up.shape[0]
    per = dim // tile

    def step(j, carry):
        cols = pl.ds(pl.multiple_of(j * tile, tile), tile)
        up_j = up[:, cols]
        down_j = down[cols, :]
        pre = mm(two[...], up_j)
        back = mm(cots[...], down_j, 1, 1)
        phi = 0.5 * (1.0 + lax.erf(pre * math.sqrt(0.5)))
        bell = jnp.exp(pre * pre * -0.5) * (1.0 / math.sqrt(2.0 * math.pi))
        act = (pre * phi).astype(BF)
        back_pre = (back * (phi + pre * bell)).astype(BF)
        layer_out[...] += mm(act, down_j)
        back_out[...] += mm(back_pre, up_j, 1, 1)
        grad = mm(act.T, cots[...]).astype(BF)
        grad_mine = mm(turned[mine, :], back_pre).astype(BF)
        grad_theirs = mm(turned[theirs, :], back_pre).astype(BF)
        rows = pl.ds(pl.multiple_of((j // per) * half, half), half)
        lane = pl.ds(pl.multiple_of((j % per) * tile, tile), tile)
        keep[rows, lane] = grad_mine
        if first:
            send[cols, :] = grad
            lower = pl.ds(pl.multiple_of(width + (j // per) * half, half), half)
            send[lower, lane] = grad_theirs
        else:
            keep_down[cols, :] = grad
            send[rows, lane] = grad_theirs
        return carry

    lax.fori_loop(0, width // tile, step, 0)
    if not first:
        for k in range(count):
            layer_pieces[k][...] = slot_rows(layer_out[...], k, count).astype(layer_pieces[k].dtype)


def turn_body(count, rest, experts, head, *refs):
    hidden, back_two, cot = refs[:3]
    others = refs[3 : 2 + count]
    mixed, o_own, o_other, g_own, g_other, gates, routes, att = refs[2 + count : 10 + count]
    back_hidden_out, keep, send, grad_att_out, delta_out, logit_out, gain_out, wo = refs[10 + count :]
    core = lax.axis_index("wsh")
    place = lax.axis_index("ctx") // rest
    fill(wo, o_own, o_other, core)
    half = o_own.shape[0]
    unit, scale = centred(hidden[...])
    back = back_two[...]
    side = back * pick_gain(g_own, g_other, core)
    part = scale * (
        side
        - jnp.mean(side, axis=-1, keepdims=True)
        - unit * jnp.mean(side * unit, axis=-1, keepdims=True)
    )
    gain_out[...] = jnp.broadcast_to(jnp.sum(back * unit, axis=0, keepdims=True), gain_out.shape)
    cots = join([cot[place]] + [o[...] for o in others]).astype(F32)
    back_hidden = cots + part
    back_hidden_out[...] = back_hidden
    branch = back_hidden.astype(BF)
    keep[...] = mm(mixed[pl.ds(pl.multiple_of(core * half, half), half), :], branch).astype(BF)
    send[...] = mm(mixed[pl.ds(pl.multiple_of((1 - core) * half, half), half), :], branch).astype(BF)
    back_mixed = mm(wo[...], branch, 1, 1)
    grads = []
    for s in range(TWO):
        total = jnp.zeros((head, branch.shape[0]), F32)
        for e in range(experts):
            total = jnp.where(routes[s : s + 1] == e, back_mixed[e * head : (e + 1) * head], total)
        att_s = att[s * head : (s + 1) * head, :]
        grads.append(jnp.sum(total * att_s, axis=0, keepdims=True))
        low = (gates[s : s + 1] * total).astype(BF)
        grad_att_out[s * head : (s + 1) * head, :] = low
        delta_out[s : s + 1, :] = jnp.sum(low.astype(F32) * att_s, axis=0, keepdims=True)
    mean = gates[0:1] * grads[0] + gates[1:2] * grads[1]
    row = lax.broadcasted_iota(I32, logit_out.shape, 0)
    logit = jnp.zeros(logit_out.shape, F32)
    for s in range(TWO):
        value = gates[s : s + 1] * (grads[s] - mean)
        logit = logit + jnp.where(row == routes[s : s + 1], value, 0.0)
    logit_out[...] = logit


def attend_back_body(count, rest, head, pieces, split, *refs):
    order = refs[0]
    kv_refs = refs[1 : 1 + pieces]
    qt, grad_att, logs, delta = refs[1 + pieces : 5 + pieces]
    grad_q_out = refs[5 + pieces]
    outs = refs[6 + pieces : 6 + pieces + split]
    kv_all, kv_turned, sides, turned, grad_kv, grad_q = refs[6 + pieces + split :]
    total = qt.shape[1]
    half = total // 2
    block = half // count
    load_keys(kv_refs, kv_all, kv_turned)
    blank = jnp.zeros((head, total), BF)
    for s in range(TWO):
        q_side = jnp.concatenate([qt[s * head : (s + 1) * head, :], blank], axis=0)
        g_side = jnp.concatenate([blank, grad_att[s * head : (s + 1) * head, :]], axis=0)
        sides[2 * s], sides[2 * s + 1] = q_side, g_side
        turned[2 * s], turned[2 * s + 1] = q_side.T, g_side.T
    grad_q[...] = jnp.zeros_like(grad_q)
    gaps = [
        lax.broadcasted_iota(I32, (block, half), 0) - places(order, count, rest, block, half, h)
        for h in range(2)
    ]

    def step(chunk, carry):
        at = pl.multiple_of(chunk * total, total)
        kv = kv_all[pl.ds(at, total), :]
        front = jnp.zeros((half, 2 * head), F32)
        back = jnp.zeros((half, 2 * head), F32)
        for h in range(2):
            cols = slice(h * half, (h + 1) * half)
            reach = half * (h + 1)
            for s in range(TWO):
                scores = scored(
                    kv, sides[2 * s, :, cols], h, gaps[h], order, count, rest, block, chunk, half
                )
                shares = jnp.exp(scores - logs[s : s + 1, cols])
                back_shares = mm(kv[:reach], sides[2 * s + 1, :, cols])
                back_scores = (shares * (back_shares - delta[s : s + 1, cols])).astype(BF)
                grad = mm(back_scores, turned[2 * s, cols, :]) + mm(
                    shares.astype(BF), turned[2 * s + 1, cols, :]
                )
                front = front + grad[:half]
                if h == 1:
                    back = back + grad[half:]
                rows = slice(s * head, (s + 1) * head)
                grad_q[rows, cols] += mm(kv_turned[:head, pl.ds(at, reach)], back_scores)
        grad_kv[pl.ds(at, half), :] = front
        grad_kv[pl.ds(at + half, half), :] = back
        return carry

    lax.fori_loop(0, rest, step, 0)
    grad_q_out[...] = grad_q[...].astype(BF)
    rows = outs[0].shape[0]
    for i, out in enumerate(outs):
        out[...] = grad_kv[i * rows : (i + 1) * rows, :].astype(out.dtype)


def unproject_body(count, rest, experts, head, terms, *refs):
    kv_terms = refs[:terms]
    grad_q, normed_t, routes, logit, tok = refs[terms : terms + 5]
    others = refs[terms + 5 : terms + 4 + count]
    at = terms + 4 + count
    back_hidden, q_own, q_other, k_own, k_other, r_own, r_other, g_own, g_other, gain_two = refs[
        at : at + 10
    ]
    at += 10
    pieces = refs[at : at + count]
    keep, send, wq, wk, wr, bqt, gains, routers = refs[at + count :]
    core = lax.axis_index("wsh")
    place = lax.axis_index("ctx") // rest
    fill(wq, q_own, q_other, core)
    fill(wk, k_own, k_other, core)
    wr[...] = jnp.zeros_like(wr)
    half = r_own.shape[0]
    wr[pl.ds(pl.multiple_of(core * half, half), half), :experts] = r_own[...].astype(F32)
    wr[pl.ds(pl.multiple_of((1 - core) * half, half), half), :experts] = r_other[...].astype(F32)
    back_kv = kv_terms[0][...].astype(F32)
    for term in kv_terms[1:]:
        back_kv = back_kv + term[...].astype(F32)
    back_kv = back_kv.astype(BF)
    total = back_kv.shape[0]
    for e in range(experts):
        part = jnp.zeros((head, total), F32)
        for s in range(TWO):
            value = grad_q[s * head : (s + 1) * head, :].astype(F32) * 0.125
            part = jnp.where(routes[s : s + 1] == e, value, part)
        bqt[e * head : (e + 1) * head, :] = part.astype(BF)
    back_q = bqt[...].T
    logits = logit[...]
    parts = []
    left = logits
    for _ in range(3):
        low = left.astype(BF)
        parts.append(low)
        left = left - low.astype(F32)
    router = parts_dot(parts, normed_t[...])
    routers[...] = router
    back = mm(back_q, wq[...], 1, 1) + mm(back_kv, wk[...], 1, 1)
    wr_turned = wr[...].T.astype(BF)
    for low in parts:
        padded = jnp.concatenate([low.astype(F32), jnp.zeros((120, total), F32)], axis=0)
        back = back + mm(padded.T.astype(BF), wr_turned)
    rows = join([tok[place]] + [o[...] for o in others]).astype(F32)
    unit, scale = centred(rows)
    side = back * pick_gain(g_own, g_other, core)
    grad = back_hidden[...] + scale * (
        side
        - jnp.mean(side, axis=-1, keepdims=True)
        - unit * jnp.mean(side * unit, axis=-1, keepdims=True)
    )
    for k in range(count):
        pieces[k][...] = slot_rows(grad, k, count).astype(pieces[k].dtype)
    gains[0:1, :] = jnp.sum(back * unit, axis=0, keepdims=True)
    gains[1:2, :] = gain_two[0:1, :]
    for out, which in ((keep, core), (send, 1 - core)):
        mine = pl.ds(pl.multiple_of(which * half, half), half)
        turned = normed_t[mine, :]
        out[:half, :] = mm(turned, back_q).astype(out.dtype)
        grad_k = mm(turned, back_kv).astype(out.dtype)
        step = half // 4
        for j in range(4):
            out[half : half + step, j * 128 : (j + 1) * 128] = grad_k[j * step : (j + 1) * step]
        at = half + step
        blank = jnp.zeros((experts, half), F32)
        out[at : at + 8, :] = jnp.concatenate([routers[:, mine], blank], axis=1).astype(out.dtype)
        gain = jnp.concatenate([gains[0:1, mine], gains[1:2, mine]], axis=1)
        out[at + 8 : at + 16, :] = jnp.broadcast_to(gain, (8, 2 * half)).astype(out.dtype)
        out[at + 16 :, :] = jnp.zeros((out.shape[0] - at - 16, 2 * half), out.dtype)


def parts_dot(parts, normed_t):
    out = None
    for low in parts:
        value = mm(low, normed_t, 1, 1)
        out = value if out is None else out + value
    return out


def place_of(strides):
    me = lax.axis_index("ctx")
    return [(me // stride) % step for stride, step in strides]


def first_body(layout, rows, stride, step, n_in, *refs):
    ins, outs, total = refs[:n_in], refs[n_in : n_in + step], refs[n_in + step]
    at = 0
    for terms in layout:
        height = terms[0][2]
        value = None
        for index, begin, count in terms:
            part = ins[index][begin : begin + count, :].astype(F32)
            value = part if value is None else value + part
        total[at : at + height, :] = value
        at += height
    if at < total.shape[0]:
        total[at:, :] = jnp.zeros((total.shape[0] - at, total.shape[1]), F32)
    digit = (lax.axis_index("ctx") // stride) % step
    for j in range(step):
        begin = pl.multiple_of((digit ^ j) * rows, 8)
        outs[j][...] = total[pl.ds(begin, rows), :].astype(outs[j].dtype)


def final_body(strides, dest, n_in, *refs):
    ins = refs[:n_in]
    outs, total = refs[n_in:-1], refs[-1]
    me = lax.axis_index("ctx")
    shift = 0
    blocks = 1
    for stride, step in strides:
        shift = shift * step + (me // stride) % step
        blocks *= step
    rows = total.shape[0] // blocks
    per = blocks // n_in
    for i, ref in enumerate(ins):
        for b in range(per):
            begin = pl.multiple_of(((i * per + b) ^ shift) * rows, 8)
            total[pl.ds(begin, rows), :] = ref[b * rows : (b + 1) * rows, :].astype(F32)
    dest(total, outs)


def reduce_rows(args, layout, height, size, dest, outs):
    strides = []
    stride = 1
    for step in factors(size):
        strides.append((stride, step))
        stride *= step
    width = 512
    unit = 8 * size
    height = -(-height // unit) * unit
    rows = height
    terms = None
    for i, (stride, step) in enumerate(strides):
        full, rows = rows, rows // step
        if i > 0:
            args = terms
            layout = [[(index, 0, full) for index in range(len(terms))]]
        pieces = call(
            functools.partial(first_body, layout, rows, stride, step, len(args)),
            [((rows, width), F32)] + [((rows, width), BF)] * (step - 1),
            args,
            scratch=[((full, width), F32)],
        )
        terms = [pieces[0]] + [swap(pieces[j], j * stride, size) for j in range(1, step)]
    done = functools.reduce(lambda a, b: a + b.astype(F32), terms).astype(BF)
    for i, (stride, step) in reversed(list(enumerate(strides))):
        got = [done] + [swap(done, j * stride, size) for j in range(1, step)]
        if i > 0:
            done = jnp.concatenate(got, axis=0)
    return call(
        functools.partial(final_body, strides, dest, len(got)),
        outs,
        got,
        scratch=[((height, width), F32)],
    )


def down_dest(total, outs):
    outs[0][...] = total[: outs[0].shape[0], :]


def up_dest(total, outs):
    up, out = outs
    half = up.shape[0]
    core = lax.axis_index("wsh")
    tiles = up.shape[1] // 512
    for i in range(tiles):
        side, inner = i // (tiles // 2), i % (tiles // 2)
        tile = (core if side == 0 else 1 - core) * (tiles // 2) + inner
        up[:, pl.ds(pl.multiple_of(tile * 512, 512), 512)] = total[i * half : (i + 1) * half, :]
    out[...] = total[tiles * half : tiles * half + out.shape[0], :]


def late_dest(total, outs):
    query, kv, router, gains = outs
    half = query.shape[0]
    step = half // 4
    query[...] = total[:half, :]
    for j in range(4):
        kv[j * step : (j + 1) * step, :] = total[half : half + step, j * 128 : (j + 1) * 128]
    at = half + step
    experts = router.shape[1]
    block = jnp.concatenate([total[at : at + 8, :half], jnp.zeros((120, half), F32)], axis=0)
    router[...] = block.T[:, :experts]
    gains[0:1, :] = total[at + 8 : at + 9, :half]
    gains[1:2, :] = total[at + 8 : at + 9, half:]


def place_body(rest, *refs):
    place = lax.axis_index("ctx") // rest
    for k, ref in enumerate(refs[:-1]):
        refs[-1][place ^ k] = ref[...].astype(F32)


def on_device(
    tokens,
    routes,
    block_order,
    norm_gain1,
    router_w,
    query_w,
    kv_w,
    out_w,
    norm_gain2,
    up_w,
    down_w,
    cotangent,
):
    size = lax.axis_size("ctx")
    count, local, dim = tokens.shape
    rest = size // count
    place = lax.axis_index("ctx") // rest
    total = count * local
    experts = router_w.shape[1]
    head = kv_w.shape[1] // 2
    feed = up_w.shape[1]

    def away(parts):
        return [swap(pick(parts, place ^ k), k * rest, size) for k in range(1, count)]

    tok_x = away(tokens)
    routes_all = jnp.pad(routes.transpose(0, 2, 1), ((0, 0), (0, 6), (0, 0)))
    routes_x = away(routes_all)
    gains = jnp.stack([norm_gain1, norm_gain2])
    gains_x = trade(gains)
    g1, g2 = gains[0:1], gains[1:2]
    g1x, g2x = gains_x[0:1], gains_x[1:2]
    query_x, kv_x, router_x = trade(query_w), trade(kv_w), trade(router_w)
    cot_x = away(cotangent)
    out_x, up_x, down_x = trade(out_w), trade(up_w), trade(down_w)

    kv, qt, normed_t, gates, route = call(
        functools.partial(project_body, count, rest, experts, head),
        [
            ((total, 2 * head), BF),
            ((TWO * head, total), BF),
            ((dim, total), BF),
            ((TWO, total), F32),
            ((8, total), I32),
        ],
        [tokens, *tok_x, routes_all, *routes_x, g1, g1x, query_w, query_x, kv_w, kv_x, router_w, router_x],
        scratch=[((dim, experts * head), BF), ((dim, 2 * head), BF), ((dim, 128), F32)],
        flops=2 * total * dim * (experts * head + 256),
    )

    steps = factors(rest)
    stride = 1
    have = kv
    for i, step in enumerate(steps):
        kv_pieces = [have] + [swap(have, j * stride, size) for j in range(1, step)]
        stride *= step
        if i + 1 < len(steps):
            have = jnp.concatenate(kv_pieces, axis=0)
    span = rest * total
    att, logs, mixed, hidden, two, two_t = call(
        functools.partial(attend_body, count, rest, experts, head, len(kv_pieces)),
        [
            ((TWO * head, total), F32),
            ((TWO, total), F32),
            ((experts * head, total), BF),
            ((total, dim), F32),
            ((total, dim), BF),
            ((dim, total), BF),
        ],
        [block_order, *kv_pieces, qt, gates, route, tokens, *tok_x, g2, g2x, out_w, out_x],
        scratch=[((span, 2 * head), BF), ((2 * head, span), BF), ((experts * head, dim), BF)],
        smem=(0,),
        flops=8 * total * span * head,
    )

    tile = 256
    wide = feed // 2
    tall = dim // 2
    upper = wide * tall // dim
    flops = 12 * total * dim * wide
    feed_scratch = [((dim, wide), BF), ((total, dim), BF)]
    layer, back_two, send_one, keep_one = call(
        functools.partial(feed_body, count, rest, True, tile),
        [
            ((total, dim), F32),
            ((total, dim), F32),
            ((wide + upper, dim), BF),
            ((upper, dim), BF),
        ],
        [two, two_t, cotangent, *cot_x, up_w, up_x, down_x, hidden],
        scratch=feed_scratch,
        flops=flops,
    )
    recv_one = trade(send_one)
    *layer_pieces, back_two, keep_down, keep_two, send_two = call(
        functools.partial(feed_body, count, rest, False, tile),
        [((local, dim), F32)]
        + [((local, dim), BF)] * (count - 1)
        + [
            ((total, dim), F32),
            ((wide, dim), BF),
            ((upper, dim), BF),
            ((upper, dim), BF),
        ],
        [two, two_t, cotangent, *cot_x, up_w, up_x, down_w, layer, back_two],
        scratch=feed_scratch + [((total, dim), F32)],
        flops=flops,
    )
    recv_two = trade(send_two)
    (grad_down,) = reduce_rows(
        [keep_down, recv_one],
        [[(0, 0, wide), (1, 0, wide)]],
        wide,
        size,
        down_dest,
        [((wide, dim), F32)],
    )
    layer_got = layer_pieces[:1] + [swap(layer_pieces[k], k * rest, size) for k in range(1, count)]
    (layer_out,) = call(
        functools.partial(place_body, rest), [((count, local, dim), F32)], layer_got
    )

    back_hidden, keep_out, send_out, grad_att, delta, logit, gain_two = call(
        functools.partial(turn_body, count, rest, experts, head),
        [
            ((total, dim), F32),
            ((tall, dim), BF),
            ((tall, dim), BF),
            ((TWO * head, total), BF),
            ((TWO, total), F32),
            ((experts, total), F32),
            ((8, dim), F32),
        ],
        [hidden, back_two, cotangent, *cot_x, mixed, out_w, out_x, g2, g2x, gates, route, att],
        scratch=[((experts * head, dim), BF)],
        flops=6 * total * dim * dim,
    )
    recv_out = trade(send_out)
    grad_up, grad_out = reduce_rows(
        [keep_two, recv_one, keep_one, recv_two, keep_out, recv_out],
        [
            [(0, 0, upper), (1, wide, upper)],
            [(2, 0, upper), (3, 0, upper)],
            [(4, 0, tall), (5, 0, tall)],
        ],
        2 * upper + tall,
        size,
        up_dest,
        [((tall, feed), F32), ((tall, dim), F32)],
    )

    split = steps[-1]
    share = span // split
    grad_q, *kv_terms = call(
        functools.partial(attend_back_body, count, rest, head, len(kv_pieces), split),
        [((TWO * head, total), BF), ((share, 2 * head), F32)] + [((share, 2 * head), BF)] * (split - 1),
        [block_order, *kv_pieces, qt, grad_att, logs, delta],
        scratch=[
            ((span, 2 * head), BF),
            ((2 * head, span), BF),
            ((2 * TWO, 2 * head, total), BF),
            ((2 * TWO, total, 2 * head), BF),
            ((span, 2 * head), F32),
            ((TWO * head, total), F32),
        ],
        smem=(0,),
        flops=20 * total * span * head,
    )
    stride = rest
    for i, step in reversed(list(enumerate(steps))):
        stride //= step
        if i + 1 < len(steps):
            summed = functools.reduce(lambda a, b: a + b.astype(F32), terms)
            kv_terms = jnp.split(summed, step, axis=0)
        terms = [kv_terms[0]] + [
            swap(kv_terms[j].astype(BF), j * stride, size) for j in range(1, step)
        ]

    height = -(-(tall + tall // 4 + 16) // (8 * size)) * 8 * size
    *input_pieces, keep_late, send_late = call(
        functools.partial(unproject_body, count, rest, experts, head, len(terms)),
        [((local, dim), F32)]
        + [((local, dim), BF)] * (count - 1)
        + [((height, dim), F32), ((height, dim), BF)],
        [
            *terms,
            grad_q,
            normed_t,
            route,
            logit,
            tokens,
            *tok_x,
            back_hidden,
            query_w,
            query_x,
            kv_w,
            kv_x,
            router_w,
            router_x,
            g1,
            g1x,
            gain_two,
        ],
        scratch=[
            ((dim, experts * head), BF),
            ((dim, 2 * head), BF),
            ((dim, 128), F32),
            ((experts * head, total), BF),
            ((8, dim), F32),
            ((8, dim), F32),
        ],
        flops=8 * total * dim * dim,
    )
    recv_late = trade(send_late)
    grad_query, grad_kv, grad_router, grad_gains = reduce_rows(
        [keep_late, recv_late],
        [[(0, 0, height), (1, 0, height)]],
        height,
        size,
        late_dest,
        [((tall, experts * head), F32), ((tall, 2 * head), F32), ((tall, experts), F32), ((2, tall), F32)],
    )
    input_got = input_pieces[:1] + [swap(input_pieces[k], k * rest, size) for k in range(1, count)]
    (input_grad,) = call(
        functools.partial(place_body, rest), [((count, local, dim), F32)], input_got
    )
    return (
        layer_out,
        input_grad,
        grad_gains[0],
        grad_router,
        grad_query,
        grad_kv,
        grad_out,
        grad_gains[1],
        grad_up,
        grad_down,
    )


def solution(mesh):
    placed = (
        P("wsh", "ctx", None),
        P("wsh", "ctx", None),
        P(),
        P("wsh"),
        P("wsh", None),
        P("wsh", None),
        P("wsh", None),
        P("wsh", None),
        P("wsh"),
        P("wsh", None),
        P("wsh", None),
        P("wsh", "ctx", None),
    )
    return jax.shard_map(
        on_device,
        mesh=mesh,
        in_specs=placed,
        out_specs=(
            P("wsh", "ctx", None),
            P("wsh", "ctx", None),
            P("wsh"),
            P("wsh", None),
            P("wsh", None),
            P("wsh", None),
            P("wsh", None),
            P("wsh"),
            P("wsh", None),
            P("wsh", None),
        ),
        check_vma=False,
    )
```

time: 373 us -> 202 us (0.54); the launches traced: 367 us -> 202 us
  matrix products: 75 us -> 0 us
  other arithmetic: 70.6 us -> 0.16 us
  local copies, waits for them, and re-layouts: 71.9 us -> 9.38 us
  Pallas kernels: 0 us -> 36 us
  starting transfers between devices: 65.7 us -> 89.6 us
  waiting for transfers between devices: 80.9 us -> 66 us
    dot_general x28 -> x0, matrix products: 75 us -> none  [the longest x1 10.1 us: on_device(): pre_act = jnp.dot(two_low, up_mat, preferred_element_type=F32)]
    pallas_call x0 -> x18, Pallas kernels: none -> 36 us  [call(): pl.pallas_call(body, out_shape=[jax.ShapeDtypeStruct(s, d) for s, d in ou...]
    convert_element_type x18 -> x3, other arithmetic: 27.2 us -> 0.1 us  [reduce_rows(): done = functools.reduce(lambda a, b: a + b.astype(F32), terms).astype(BF)]
    ppermute x45 -> x57, starting transfers between devices: 64.3 us -> 87.6 us  [swap(): return lax.ppermute(values, 'ctx', [(i, i ^ mask) for i in range(size)])]
    reduce_sum x11 -> x0, other arithmetic: 16.9 us -> none  [the longest x2 11.7 us: gating(): chosen = jnp.sum(expert_hot * logits[..., None, :], axis=-1)]
    ppermute x45 -> x57, waiting for transfers between devices: 80.2 us -> 63.4 us  [swap(): return lax.ppermute(values, 'ctx', [(i, i ^ mask) for i in range(size)])]
    reshape x8 -> x0, local copies, waits for them, and re-layouts: 14.2 us -> none  [the longest x3 7.01 us: total_grads(): g.reshape(2, -1, width)]
    convert_element_type x10 -> x0, local copies, waits for them, and re-layouts: 10.6 us -> none  [the longest x5 3.96 us: total_grads(): theirs = [pick(h, 1 - core).astype(BF) for h in halves]]
  transfers between devices with their start and end apart: 55 -> 68, of which waited for: 16 -> 25; matrix products, arithmetic and copies ran while one was open for 31% -> 3% of each run, Pallas kernels for 0% -> 14%
where the time goes in v2:
time: 202 us
  starting transfers between devices  89.6 us (44%)
  waiting for transfers between devices  66 us (33%)
  Pallas kernels  36 us (18%)
  local copies, waits for them, and re-layouts  9.38 us (5%)
    ppermute x57, starting transfers between devices, swap(): return lax.ppermute(values, 'ctx', [(i, i ^ mask) for i in range(size)])  87.6 us
    ppermute x57, waiting for transfers between devices, swap(): return lax.ppermute(values, 'ctx', [(i, i ^ mask) for i in range(size)])  63.4 us
    pallas_call x18, Pallas kernels, call(): pl.pallas_call(body, out_shape=[jax.ShapeDtypeStruct(s, d) for s, d in ou...  36 us
    unnamed x24, local copies, waits for them, and re-layouts  4.35 us
  transfers between devices with their start and end apart: 68, of which 25 were waited for; matrix products, arithmetic and copies ran while one was open for 3% of the time, Pallas kernels for 14%

profile of v2, /device:TPU:0, one launch (start us, length us, event | category | flops | bytes accessed | tf_op | source)
XLA Modules:
  0.0 202.1 jit_solution(12340077193198620474)
XLA Ops:
  4.8 4.7 %collective-permute-start.2 = (bf16[128,512]{1,0:T(8,128)(2,1)}, bf16[128,512]{1,0:T(8,128)(2,1)S(1)}, u32[]{:S(2)}, u32[]{:S(2)}) collective-permute-start(bf16[128,512]{1,0:T(8,128)(2,1)} %get-tuple-element.165), channel_id=1, source_target_pairs={{0,24},{2,26},{4,28},{6,30},{8,16},{10,18},{12,20},{14,22},{16,8},... | collective-permute-start | bytes 393224 | tf_op jit(solution)/shard_map/ppermute | solution.py:28
  12.1 4.7 %collective-permute-done.5.refs_7_ = s32[8,128]{1,0:T(8,128)S(1)} collective-permute-done((s32[8,128]{1,0:T(8,128)S(1)}, s32[8,128]{1,0:T(8,128)S(1)}, u32[]{:S(2)}, u32[]{:S(2)}) %collective-permute-start.5) | collective-permute-done | bytes 4128 | tf_op jit(solution)/shard_map/ppermute | solution.py:28
  16.8 5.3 %collective-permute-start.3 = (s32[8,128]{1,0:T(8,128)S(1)}, s32[8,128]{1,0:T(8,128)S(1)}, u32[]{:S(2)}, u32[]{:S(2)}) collective-permute-start(s32[8,128]{1,0:T(8,128)S(1)} %get-tuple-element.169), channel_id=1, source_target_pairs={{0,8},{2,10},{4,12},{6,14},{8,0},{10,2},{12,4},{14,6},{16,24},{18,... | collective-permute-start | bytes 12296 | tf_op jit(solution)/shard_map/ppermute | solution.py:28
  23.7 3.0 %collective-permute-start.4 = (s32[8,128]{1,0:T(8,128)S(1)}, s32[8,128]{1,0:T(8,128)S(1)}, u32[]{:S(2)}, u32[]{:S(2)}) collective-permute-start(s32[8,128]{1,0:T(8,128)S(1)} %get-tuple-element.170), channel_id=1, source_target_pairs={{0,16},{2,18},{4,20},{6,22},{8,24},{10,26},{12,28},{14,30},{16,0},... | collective-permute-start | bytes 12296 | tf_op jit(solution)/shard_map/ppermute | solution.py:28
  34.2 3.8 %collective-permute-done.refs_1_.refs_9_ = bf16[128,512]{1,0:T(8,128)(2,1)S(1)} collective-permute-done((bf16[128,512]{1,0:T(8,128)(2,1)S(1)}, bf16[128,512]{1,0:T(8,128)(2,1)S(1)}, u32[]{:S(2)}, u32[]{:S(2)}) %collective-permute-start) | collective-permute-done | bytes 131104 | tf_op jit(solution)/shard_map/ppermute | solution.py:28
  42.0 2.5 %collective-permute-start.12 = (bf16[512,128]{1,0:T(8,128)(2,1)S(1)}, bf16[512,128]{1,0:T(8,128)(2,1)S(1)}, u32[]{:S(2)}, u32[]{:S(2)}) collective-permute-start(bf16[512,128]{1,0:T(8,128)(2,1)S(1)} %get-tuple-element.81.refs_1_), channel_id=1, source_target_pairs={{0,6},{2,4},{4,2},{6,0},{8,14},{10,12},{12,10},{14,8},{16,22},{18,... | collective-permute-start | bytes 393224 | tf_op jit(solution)/shard_map/ppermute | solution.py:28
  45.6 2.9 %collective-permute-done.12.refs_4_ = bf16[512,128]{1,0:T(8,128)(2,1)S(1)} collective-permute-done((bf16[512,128]{1,0:T(8,128)(2,1)S(1)}, bf16[512,128]{1,0:T(8,128)(2,1)S(1)}, u32[]{:S(2)}, u32[]{:S(2)}) %collective-permute-start.12) | collective-permute-done | bytes 131104 | tf_op jit(solution)/shard_map/ppermute | solution.py:28
  48.4 2.5 %collective-permute-start.16 = (bf16[128,512]{1,0:T(8,128)(2,1)S(1)}, bf16[128,512]{1,0:T(8,128)(2,1)S(1)}, u32[]{:S(2)}, u32[]{:S(2)}) collective-permute-start(bf16[128,512]{1,0:T(8,128)(2,1)S(1)} %get-tuple-element.162), channel_id=1, source_target_pairs={{0,24},{2,26},{4,28},{6,30},{8,16},{10,18},{12,20},{14,22},{16,8},... | collective-permute-start | bytes 393224 | tf_op jit(solution)/shard_map/ppermute | solution.py:28
  50.9 2.4 %collective-permute-start.15 = (bf16[128,512]{1,0:T(8,128)(2,1)S(1)}, bf16[128,512]{1,0:T(8,128)(2,1)S(1)}, u32[]{:S(2)}, u32[]{:S(2)}) collective-permute-start(bf16[128,512]{1,0:T(8,128)(2,1)S(1)} %get-tuple-element.163), channel_id=1, source_target_pairs={{0,16},{2,18},{4,20},{6,22},{8,24},{10,26},{12,28},{14,30},{16,0},... | collective-permute-start | bytes 393224 | tf_op jit(solution)/shard_map/ppermute | solution.py:28
  53.9 6.3 %shard_map.196 = (f32[128,512]{1,0:T(8,128)S(1)}, f32[2,512]{1,0:T(2,128)S(1)}, bf16[512,512]{1,0:T(8,128)(2,1)S(1)}, f32[512,512]{1,0:T(8,128)S(1)}, bf16[512,5...) custom-call(s32[16]{0:T(128)S(1)} %copy-done.8, bf16[512,128]{1,0:T(8,128)(2,1)S(1)} %get-tuple-element.81.refs_1_, ...), custom_call_target="tpu_custom_call" | custom-call | flops 536870912 | bytes 5006400 | tf_op jit(solution)/shard_map/pallas_call | solution.py:48
  61.7 5.0 %shard_map.197 = (f32[512,512]{1,0:T(8,128)S(1)}, f32[512,512]{1,0:T(8,128)S(1)}, bf16[1536,512]{1,0:T(8,128)(2,1)S(1)}, bf16[512,512]{1,0:T(8,128)(2,1)S(1)}) custom-call(bf16[512,512]{1,0:T(8,128)(2,1)S(1)} %get-tuple-element.85.refs_0_, bf16[512,512]{1,0:T(8,128)(2,1)S(1)} %get-tuple-element.86.refs_1_, bf16[4,128,512]{2,1,0:T(8,128)(2,1)S(1)} %copy-done.2, ...), custom_call_target="tpu_custom_call" | custom-call | flops 3221225472 | bytes 10354688 | tf_op jit(solution)/shard_map/pallas_call | solution.py:48
  66.8 4.8 %shard_map.198 = (f32[128,512]{1,0:T(8,128)S(1)}, bf16[128,512]{1,0:T(8,128)(2,1)S(1)}, bf16[128,512]{1,0:T(8,128)(2,1)S(1)}, bf16[128,512]{1,0:T(8,128)(2,1)S(1...) custom-call(bf16[512,512]{1,0:T(8,128)(2,1)S(1)} %get-tuple-element., ...), custom_call_target="tpu_custom_call" | custom-call | flops 3221225472 | bytes 11010048 | tf_op jit(solution)/shard_map/pallas_call | solution.py:48
  73.1 6.9 %shard_map.201 = (bf16[128,512]{1,0:T(8,128)(2,1)S(1)}, f32[512,128]{1,0:T(8,128)S(1)}, bf16[512,128]{1,0:T(8,128)(2,1)S(1)}, bf16[512,128]{1,0:T(8,128)(2,1)S(1)}, bf16[512,128]{1,0:T(8,128)(2,1)S(1)}) custom-call(s32[16]{0:T(128)S(1)} %copy-done.8, bf16[512,128]{1,0:T(8,128)(2,1)S(1)} %get-tuple-element.81.refs_1_, ...), custom_call_target="tpu_custom_call" | custom-call | flops 1342177280 | bytes 1581120 | tf_op jit(solution)/shard_map/pallas_call | solution.py:48
  80.1 2.2 %collective-permute-start.22 = (bf16[512,128]{1,0:T(8,128)(2,1)S(1)}, bf16[512,128]{1,0:T(8,128)(2,1)S(1)}, u32[]{:S(2)}, u32[]{:S(2)}) collective-permute-start(bf16[512,128]{1,0:T(8,128)(2,1)S(1)} %get-tuple-element.101), channel_id=1, source_target_pairs={{0,2},{2,0},{4,6},{6,4},{8,10},{10,8},{12,14},{14,12},{16,18},{18,... | collective-permute-start | bytes 393224 | tf_op jit(solution)/shard_map/ppermute | solution.py:28
  83.9 2.7 %collective-permute-done.22.refs_1_ = bf16[512,128]{1,0:T(8,128)(2,1)S(1)} collective-permute-done((bf16[512,128]{1,0:T(8,128)(2,1)S(1)}, bf16[512,128]{1,0:T(8,128)(2,1)S(1)}, u32[]{:S(2)}, u32[]{:S(2)}) %collective-permute-start.22) | collective-permute-done | bytes 131104 | tf_op jit(solution)/shard_map/ppermute | solution.py:28
  86.6 4.2 %collective-permute-done.23.refs_2_ = bf16[512,128]{1,0:T(8,128)(2,1)S(1)} collective-permute-done((bf16[512,128]{1,0:T(8,128)(2,1)S(1)}, bf16[512,128]{1,0:T(8,128)(2,1)S(1)}, u32[]{:S(2)}, u32[]{:S(2)}) %collective-permute-start.23) | collective-permute-done | bytes 131104 | tf_op jit(solution)/shard_map/ppermute | solution.py:28
  90.8 2.2 %shard_map.202 = (f32[128,512]{1,0:T(8,128)S(1)}, bf16[128,512]{1,0:T(8,128)(2,1)S(1)}, bf16[128,512]{1,0:T(8,128)(2,1)S(1)}, bf16[128,512]{1,0:T(8,128)(2,1)S(1...) custom-call(f32[512,128]{1,0:T(8,128)S(1)} %get-tuple-element.100.refs_0_, ...), custom_call_target="tpu_custom_call" | custom-call | flops 1073741824 | bytes 5825536 | tf_op jit(solution)/shard_map/pallas_call | solution.py:48
  97.3 5.4 %collective-permute-done.56.refs_1_ = bf16[256,512]{1,0:T(8,128)(2,1)S(1)} collective-permute-done((bf16[256,512]{1,0:T(8,128)(2,1)S(1)}, bf16[256,512]{1,0:T(8,128)(2,1)S(1)}, u32[]{:S(2)}, u32[]{:S(2)}) %collective-permute-start.56) | collective-permute-done | bytes 262176 | tf_op jit(solution)/shard_map/ppermute | solution.py:28
  103.1 5.0 %collective-permute-done.57.refs_2_ = bf16[256,512]{1,0:T(8,128)(2,1)S(1)} collective-permute-done((bf16[256,512]{1,0:T(8,128)(2,1)S(1)}, bf16[256,512]{1,0:T(8,128)(2,1)S(1)}, u32[]{:S(2)}, u32[]{:S(2)}) %collective-permute-start.57) | collective-permute-done | bytes 262176 | tf_op jit(solution)/shard_map/ppermute | solution.py:28
  113.2 3.0 %collective-permute-start.45 = (bf16[320,512]{1,0:T(8,128)(2,1)S(1)}, bf16[320,512]{1,0:T(8,128)(2,1)S(1)}, u32[]{:S(2)}, u32[]{:S(2)}) collective-permute-start(bf16[320,512]{1,0:T(8,128)(2,1)S(1)} %get-tuple-element.135), channel_id=1, source_target_pairs={{0,4},{2,6},{4,0},{6,2},{8,12},{10,14},{12,8},{14,10},{16,20},{18,... | collective-permute-start | bytes 983048 | tf_op jit(solution)/shard_map/ppermute | solution.py:28
  118.0 3.8 %collective-permute-done.32 = bf16[24,512]{1,0:T(8,128)(2,1)S(1)} collective-permute-done((bf16[24,512]{1,0:T(8,128)(2,1)S(1)}, bf16[24,512]{1,0:T(8,128)(2,1)S(1)}, u32[]{:S(2)}, u32[]{:S(2)}) %collective-permute-start.32) | collective-permute-done | bytes 24608 | tf_op jit(solution)/shard_map/ppermute | solution.py:28
  124.5 3.5 %collective-permute-done.60 = bf16[64,512]{1,0:T(8,128)(2,1)S(1)} collective-permute-done((bf16[64,512]{1,0:T(8,128)(2,1)S(1)}, bf16[64,512]{1,0:T(8,128)(2,1)S(1)}, u32[]{:S(2)}, u32[]{:S(2)}) %collective-permute-start.60) | collective-permute-done | bytes 65568 | tf_op jit(solution)/shard_map/ppermute | solution.py:28
  129.5 2.6 %collective-permute-start.34 = (bf16[24,512]{1,0:T(8,128)(2,1)S(1)}, bf16[24,512]{1,0:T(8,128)(2,1)S(1)}, u32[]{:S(2)}, u32[]{:S(2)}) collective-permute-start(bf16[24,512]{1,0:T(8,128)(2,1)S(1)} %get-tuple-element.122), channel_id=1, source_target_pairs={{0,24},{2,26},{4,28},{6,30},{8,16},{10,18},{12,20},{14,22},{16,8},... | collective-permute-start | bytes 73736 | tf_op jit(solution)/shard_map/ppermute | solution.py:28
  132.2 3.4 %collective-permute-done.33 = bf16[24,512]{1,0:T(8,128)(2,1)S(1)} collective-permute-done((bf16[24,512]{1,0:T(8,128)(2,1)S(1)}, bf16[24,512]{1,0:T(8,128)(2,1)S(1)}, u32[]{:S(2)}, u32[]{:S(2)}) %collective-permute-start.33) | collective-permute-done | bytes 24608 | tf_op jit(solution)/shard_map/ppermute | solution.py:28
  135.8 2.9 %collective-permute-start.21 = (bf16[128,512]{1,0:T(8,128)(2,1)S(1)}, bf16[128,512]{1,0:T(8,128)(2,1)S(1)}, u32[]{:S(2)}, u32[]{:S(2)}) collective-permute-start(bf16[128,512]{1,0:T(8,128)(2,1)S(1)} %get-tuple-element.93), channel_id=1, source_target_pairs={{0,24},{2,26},{4,28},{6,30},{8,16},{10,18},{12,20},{14,22},{16,8},... | collective-permute-start | bytes 393224 | tf_op jit(solution)/shard_map/ppermute | solution.py:28
  139.7 2.2 %collective-permute-start.63 = (bf16[64,512]{1,0:T(8,128)(2,1)S(1)}, bf16[64,512]{1,0:T(8,128)(2,1)S(1)}, u32[]{:S(2)}, u32[]{:S(2)}) collective-permute-start(bf16[64,512]{1,0:T(8,128)(2,1)S(1)} %add_convert_fusion.1), channel_id=1, source_target_pairs={{0,16},{2,18},{4,20},{6,22},{8,24},{10,26},{12,28},{14,30},{16,0},... | collective-permute-start | bytes 196616 | tf_op jit(solution)/shard_map/ppermute | solution.py:28
  143.5 3.4 %collective-permute-done.64 = bf16[64,512]{1,0:T(8,128)(2,1)S(1)} collective-permute-done((bf16[64,512]{1,0:T(8,128)(2,1)S(1)}, bf16[64,512]{1,0:T(8,128)(2,1)S(1)}, u32[]{:S(2)}, u32[]{:S(2)}) %collective-permute-start.64) | collective-permute-done | bytes 65568 | tf_op jit(solution)/shard_map/ppermute | solution.py:28
  146.8 7.7 %collective-permute-start.47 = (bf16[80,512]{1,0:T(8,128)(2,1)S(1)}, bf16[80,512]{1,0:T(8,128)(2,1)S(1)}, u32[]{:S(2)}, u32[]{:S(2)}) collective-permute-start(bf16[80,512]{1,0:T(8,128)(2,1)S(1)} %get-tuple-element.138), channel_id=1, source_target_pairs={{0,8},{2,10},{4,12},{6,14},{8,0},{10,2},{12,4},{14,6},{16,24},{18,... | collective-permute-start | bytes 245768 | tf_op jit(solution)/shard_map/ppermute | solution.py:28
  161.5 2.9 %collective-permute-done.48 = bf16[80,512]{1,0:T(8,128)(2,1)S(1)} collective-permute-done((bf16[80,512]{1,0:T(8,128)(2,1)S(1)}, bf16[80,512]{1,0:T(8,128)(2,1)S(1)}, u32[]{:S(2)}, u32[]{:S(2)}) %collective-permute-start.48) | collective-permute-done | bytes 81952 | tf_op jit(solution)/shard_map/ppermute | solution.py:28
  164.3 4.3 %collective-permute-start.35 = (bf16[24,512]{1,0:T(8,128)(2,1)S(1)}, bf16[24,512]{1,0:T(8,128)(2,1)S(1)}, u32[]{:S(2)}, u32[]{:S(2)}) collective-permute-start(bf16[24,512]{1,0:T(8,128)(2,1)S(1)} %add_convert_fusion.2), channel_id=1, source_target_pairs={{0,8},{2,10},{4,12},{6,14},{8,0},{10,2},{12,4},{14,6},{16,24},{18,... | collective-permute-start | bytes 73736 | tf_op jit(solution)/shard_map/ppermute | solution.py:28
  171.1 2.9 %collective-permute-start.52 = (bf16[80,512]{1,0:T(8,128)(2,1)S(1)}, bf16[80,512]{1,0:T(8,128)(2,1)S(1)}, u32[]{:S(2)}, u32[]{:S(2)}) collective-permute-start(bf16[80,512]{1,0:T(8,128)(2,1)S(1)} %add_convert_fusion), channel_id=1, source_target_pairs={{0,24},{2,26},{4,28},{6,30},{8,16},{10,18},{12,20},{14,22},{16,8},... | collective-permute-start | bytes 245768 | tf_op jit(solution)/shard_map/ppermute | solution.py:28
  192.4 6.3 %collective-permute-done.66.refs_2_ = bf16[256,512]{1,0:T(8,128)(2,1)S(1)} collective-permute-done((bf16[256,512]{1,0:T(8,128)(2,1)S(1)}, bf16[256,512]{1,0:T(8,128)(2,1)S(1)}, u32[]{:S(2)}, u32[]{:S(2)}) %collective-permute-start.66) | collective-permute-done | bytes 262176 | tf_op jit(solution)/shard_map/ppermute | solution.py:28
  (161 shorter events, 75.9 us)
Async XLA Ops:
  0.7 61.0 %collective-permute-start.18 = (bf16[1024,512]{1,0:T(8,128)(2,1)}, bf16[1024,512]{1,0:T(8,128)(2,1)S(1)}, u32[]{:S(2)}, u32[]{:S(2)}) collective-permute-start(bf16[1024,512]{1,0:T(8,128)(2,1)} %refs_8_.4), channel_id=1, source_target_pairs={{0,1},{1,0},{2,3},{3,2},{4,5},{5,4},{6,7},{7,6},{8,9},{9,8},{10,11... | collective-permute-start | bytes 3145736 | tf_op jit(solution)/shard_map/ppermute | solution.py:32
  1.2 60.5 %collective-permute-start.17 = (bf16[256,2048]{1,0:T(8,128)(2,1)}, bf16[256,2048]{1,0:T(8,128)(2,1)S(1)}, u32[]{:S(2)}, u32[]{:S(2)}) collective-permute-start(bf16[256,2048]{1,0:T(8,128)(2,1)} %refs_6_.3), channel_id=1, source_target_pairs={{0,1},{1,0},{2,3},{3,2},{4,5},{5,4},{6,7},{7,6},{8,9},{9,8},{10,11... | collective-permute-start | bytes 3145736 | tf_op jit(solution)/shard_map/ppermute | solution.py:32
  4.8 27.1 %collective-permute-start.2 = (bf16[128,512]{1,0:T(8,128)(2,1)}, bf16[128,512]{1,0:T(8,128)(2,1)S(1)}, u32[]{:S(2)}, u32[]{:S(2)}) collective-permute-start(bf16[128,512]{1,0:T(8,128)(2,1)} %get-tuple-element.165), channel_id=1, source_target_pairs={{0,24},{2,26},{4,28},{6,30},{8,16},{10,18},{12,20},{14,22},{16,8},... | collective-permute-start | bytes 393224 | tf_op jit(solution)/shard_map/ppermute | solution.py:28
  9.5 22.8 %collective-permute-start.1 = (bf16[128,512]{1,0:T(8,128)(2,1)S(1)}, bf16[128,512]{1,0:T(8,128)(2,1)S(1)}, u32[]{:S(2)}, u32[]{:S(2)}) collective-permute-start(bf16[128,512]{1,0:T(8,128)(2,1)S(1)} %get-tuple-element.166), channel_id=1, source_target_pairs={{0,16},{2,18},{4,20},{6,22},{8,24},{10,26},{12,28},{14,30},{16,0},... | collective-permute-start | bytes 393224 | tf_op jit(solution)/shard_map/ppermute | solution.py:28
  31.9 13.1 %collective-permute-start.13 = (bf16[256,512]{1,0:T(8,128)(2,1)}, bf16[256,512]{1,0:T(8,128)(2,1)S(1)}, u32[]{:S(2)}, u32[]{:S(2)}) collective-permute-start(bf16[256,512]{1,0:T(8,128)(2,1)} %refs_7_.1), channel_id=1, source_target_pairs={{0,1},{1,0},{2,3},{3,2},{4,5},{5,4},{6,7},{7,6},{8,9},{9,8},{10,11... | collective-permute-start | bytes 786440 | tf_op jit(solution)/shard_map/ppermute | solution.py:32
  48.4 11.7 %collective-permute-start.16 = (bf16[128,512]{1,0:T(8,128)(2,1)S(1)}, bf16[128,512]{1,0:T(8,128)(2,1)S(1)}, u32[]{:S(2)}, u32[]{:S(2)}) collective-permute-start(bf16[128,512]{1,0:T(8,128)(2,1)S(1)} %get-tuple-element.162), channel_id=1, source_target_pairs={{0,24},{2,26},{4,28},{6,30},{8,16},{10,18},{12,20},{14,22},{16,8},... | collective-permute-start | bytes 393224 | tf_op jit(solution)/shard_map/ppermute | solution.py:28
  50.9 10.8 %collective-permute-start.15 = (bf16[128,512]{1,0:T(8,128)(2,1)S(1)}, bf16[128,512]{1,0:T(8,128)(2,1)S(1)}, u32[]{:S(2)}, u32[]{:S(2)}) collective-permute-start(bf16[128,512]{1,0:T(8,128)(2,1)S(1)} %get-tuple-element.163), channel_id=1, source_target_pairs={{0,16},{2,18},{4,20},{6,22},{8,24},{10,26},{12,28},{14,30},{16,0},... | collective-permute-start | bytes 393224 | tf_op jit(solution)/shard_map/ppermute | solution.py:28
  66.7 26.4 %collective-permute-start.41 = (bf16[1536,512]{1,0:T(8,128)(2,1)S(1)}, bf16[1536,512]{1,0:T(8,128)(2,1)S(1)}, u32[]{:S(2)}, u32[]{:S(2)}) collective-permute-start(bf16[1536,512]{1,0:T(8,128)(2,1)S(1)} %get-tuple-element.128), channel_id=1, source_target_pairs={{0,1},{1,0},{2,3},{3,2},{4,5},{5,4},{6,7},{7,6},{8,9},{9,8},{10,11... | collective-permute-start | bytes 4718600 | tf_op jit(solution)/shard_map/ppermute | solution.py:32
  83.9 11.8 %collective-permute-start.43 = (bf16[256,512]{1,0:T(8,128)(2,1)S(1)}, bf16[256,512]{1,0:T(8,128)(2,1)S(1)}, u32[]{:S(2)}, u32[]{:S(2)}) collective-permute-start(bf16[256,512]{1,0:T(8,128)(2,1)S(1)} %get-tuple-element.132), channel_id=1, source_target_pairs={{0,1},{1,0},{2,3},{3,2},{4,5},{5,4},{6,7},{7,6},{8,9},{9,8},{10,11... | collective-permute-start | bytes 786440 | tf_op jit(solution)/shard_map/ppermute | solution.py:32
  86.6 24.9 %collective-permute-start.42 = (bf16[512,512]{1,0:T(8,128)(2,1)S(1)}, bf16[512,512]{1,0:T(8,128)(2,1)S(1)}, u32[]{:S(2)}, u32[]{:S(2)}) collective-permute-start(bf16[512,512]{1,0:T(8,128)(2,1)S(1)} %get-tuple-element.130), channel_id=1, source_target_pairs={{0,1},{1,0},{2,3},{3,2},{4,5},{5,4},{6,7},{7,6},{8,9},{9,8},{10,11... | collective-permute-start | bytes 1572872 | tf_op jit(solution)/shard_map/ppermute | solution.py:32
  94.0 14.1 %collective-permute-start.57 = (bf16[256,512]{1,0:T(8,128)(2,1)S(1)}, bf16[256,512]{1,0:T(8,128)(2,1)S(1)}, u32[]{:S(2)}, u32[]{:S(2)}) collective-permute-start(bf16[256,512]{1,0:T(8,128)(2,1)S(1)} %get-tuple-element.146), channel_id=1, source_target_pairs={{0,4},{2,6},{4,0},{6,2},{8,12},{10,14},{12,8},{14,10},{16,20},{18,... | collective-permute-start | bytes 786440 | tf_op jit(solution)/shard_map/ppermute | solution.py:28
  95.6 14.0 %collective-permute-start.58 = (bf16[256,512]{1,0:T(8,128)(2,1)S(1)}, bf16[256,512]{1,0:T(8,128)(2,1)S(1)}, u32[]{:S(2)}, u32[]{:S(2)}) collective-permute-start(bf16[256,512]{1,0:T(8,128)(2,1)S(1)} %get-tuple-element.147), channel_id=1, source_target_pairs={{0,6},{2,4},{4,2},{6,0},{8,14},{10,12},{12,10},{14,8},{16,22},{18,... | collective-permute-start | bytes 786440 | tf_op jit(solution)/shard_map/ppermute | solution.py:28
  97.1 20.8 %collective-permute-start.19 = (bf16[128,512]{1,0:T(8,128)(2,1)S(1)}, bf16[128,512]{1,0:T(8,128)(2,1)S(1)}, u32[]{:S(2)}, u32[]{:S(2)}) collective-permute-start(bf16[128,512]{1,0:T(8,128)(2,1)S(1)} %get-tuple-element.91), channel_id=1, source_target_pairs={{0,8},{2,10},{4,12},{6,14},{8,0},{10,2},{12,4},{14,6},{16,24},{18,... | collective-permute-start | bytes 393224 | tf_op jit(solution)/shard_map/ppermute | solution.py:28
  111.5 11.6 %collective-permute-start.59 = (bf16[64,512]{1,0:T(8,128)(2,1)S(1)}, bf16[64,512]{1,0:T(8,128)(2,1)S(1)}, u32[]{:S(2)}, u32[]{:S(2)}) collective-permute-start(bf16[64,512]{1,0:T(8,128)(2,1)S(1)} %get-tuple-element.149), channel_id=1, source_target_pairs={{0,8},{2,10},{4,12},{6,14},{8,0},{10,2},{12,4},{14,6},{16,24},{18,... | collective-permute-start | bytes 196616 | tf_op jit(solution)/shard_map/ppermute | solution.py:28
  112.1 26.7 %collective-permute-start.44 = (bf16[320,512]{1,0:T(8,128)(2,1)S(1)}, bf16[320,512]{1,0:T(8,128)(2,1)S(1)}, u32[]{:S(2)}, u32[]{:S(2)}) collective-permute-start(bf16[320,512]{1,0:T(8,128)(2,1)S(1)} %get-tuple-element.134), channel_id=1, source_target_pairs={{0,2},{2,0},{4,6},{6,4},{8,10},{10,8},{12,14},{14,12},{16,18},{18,... | collective-permute-start | bytes 983048 | tf_op jit(solution)/shard_map/ppermute | solution.py:28
  113.2 26.4 %collective-permute-start.45 = (bf16[320,512]{1,0:T(8,128)(2,1)S(1)}, bf16[320,512]{1,0:T(8,128)(2,1)S(1)}, u32[]{:S(2)}, u32[]{:S(2)}) collective-permute-start(bf16[320,512]{1,0:T(8,128)(2,1)S(1)} %get-tuple-element.135), channel_id=1, source_target_pairs={{0,4},{2,6},{4,0},{6,2},{8,12},{10,14},{12,8},{14,10},{16,20},{18,... | collective-permute-start | bytes 983048 | tf_op jit(solution)/shard_map/ppermute | solution.py:28
  116.2 25.7 %collective-permute-start.46 = (bf16[320,512]{1,0:T(8,128)(2,1)S(1)}, bf16[320,512]{1,0:T(8,128)(2,1)S(1)}, u32[]{:S(2)}, u32[]{:S(2)}) collective-permute-start(bf16[320,512]{1,0:T(8,128)(2,1)S(1)} %get-tuple-element.136), channel_id=1, source_target_pairs={{0,6},{2,4},{4,2},{6,0},{8,14},{10,12},{12,10},{14,8},{16,22},{18,... | collective-permute-start | bytes 983048 | tf_op jit(solution)/shard_map/ppermute | solution.py:28
  135.6 21.3 %collective-permute-start.20 = (bf16[128,512]{1,0:T(8,128)(2,1)S(1)}, bf16[128,512]{1,0:T(8,128)(2,1)S(1)}, u32[]{:S(2)}, u32[]{:S(2)}) collective-permute-start(bf16[128,512]{1,0:T(8,128)(2,1)S(1)} %get-tuple-element.92), channel_id=1, source_target_pairs={{0,16},{2,18},{4,20},{6,22},{8,24},{10,26},{12,28},{14,30},{16,0},... | collective-permute-start | bytes 393224 | tf_op jit(solution)/shard_map/ppermute | solution.py:28
  135.8 23.2 %collective-permute-start.21 = (bf16[128,512]{1,0:T(8,128)(2,1)S(1)}, bf16[128,512]{1,0:T(8,128)(2,1)S(1)}, u32[]{:S(2)}, u32[]{:S(2)}) collective-permute-start(bf16[128,512]{1,0:T(8,128)(2,1)S(1)} %get-tuple-element.93), channel_id=1, source_target_pairs={{0,24},{2,26},{4,28},{6,30},{8,16},{10,18},{12,20},{14,22},{16,8},... | collective-permute-start | bytes 393224 | tf_op jit(solution)/shard_map/ppermute | solution.py:28
  139.7 15.7 %collective-permute-start.63 = (bf16[64,512]{1,0:T(8,128)(2,1)S(1)}, bf16[64,512]{1,0:T(8,128)(2,1)S(1)}, u32[]{:S(2)}, u32[]{:S(2)}) collective-permute-start(bf16[64,512]{1,0:T(8,128)(2,1)S(1)} %add_convert_fusion.1), channel_id=1, source_target_pairs={{0,16},{2,18},{4,20},{6,22},{8,24},{10,26},{12,28},{14,30},{16,0},... | collective-permute-start | bytes 196616 | tf_op jit(solution)/shard_map/ppermute | solution.py:28
  141.9 13.5 %collective-permute-start.62 = (bf16[64,512]{1,0:T(8,128)(2,1)S(1)}, bf16[64,512]{1,0:T(8,128)(2,1)S(1)}, u32[]{:S(2)}, u32[]{:S(2)}) collective-permute-start(bf16[64,512]{1,0:T(8,128)(2,1)S(1)} %add_convert_fusion.1), channel_id=1, source_target_pairs={{0,8},{2,10},{4,12},{6,14},{8,0},{10,2},{12,4},{14,6},{16,24},{18,... | collective-permute-start | bytes 196616 | tf_op jit(solution)/shard_map/ppermute | solution.py:28
  146.8 13.1 %collective-permute-start.47 = (bf16[80,512]{1,0:T(8,128)(2,1)S(1)}, bf16[80,512]{1,0:T(8,128)(2,1)S(1)}, u32[]{:S(2)}, u32[]{:S(2)}) collective-permute-start(bf16[80,512]{1,0:T(8,128)(2,1)S(1)} %get-tuple-element.138), channel_id=1, source_target_pairs={{0,8},{2,10},{4,12},{6,14},{8,0},{10,2},{12,4},{14,6},{16,24},{18,... | collective-permute-start | bytes 245768 | tf_op jit(solution)/shard_map/ppermute | solution.py:28
  156.9 11.8 %collective-permute-start.25 = (bf16[128,512]{1,0:T(8,128)(2,1)S(1)}, bf16[128,512]{1,0:T(8,128)(2,1)S(1)}, u32[]{:S(2)}, u32[]{:S(2)}) collective-permute-start(bf16[128,512]{1,0:T(8,128)(2,1)S(1)} %get-tuple-element.110), channel_id=1, source_target_pairs={{0,8},{2,10},{4,12},{6,14},{8,0},{10,2},{12,4},{14,6},{16,24},{18,... | collective-permute-start | bytes 393224 | tf_op jit(solution)/shard_map/ppermute | solution.py:28
  159.0 10.8 %collective-permute-start.26 = (bf16[128,512]{1,0:T(8,128)(2,1)S(1)}, bf16[128,512]{1,0:T(8,128)(2,1)S(1)}, u32[]{:S(2)}, u32[]{:S(2)}) collective-permute-start(bf16[128,512]{1,0:T(8,128)(2,1)S(1)} %get-tuple-element.111), channel_id=1, source_target_pairs={{0,16},{2,18},{4,20},{6,22},{8,24},{10,26},{12,28},{14,30},{16,0},... | collective-permute-start | bytes 393224 | tf_op jit(solution)/shard_map/ppermute | solution.py:28
  159.9 11.2 %collective-permute-start.37 = (bf16[24,512]{1,0:T(8,128)(2,1)S(1)}, bf16[24,512]{1,0:T(8,128)(2,1)S(1)}, u32[]{:S(2)}, u32[]{:S(2)}) collective-permute-start(bf16[24,512]{1,0:T(8,128)(2,1)S(1)} %add_convert_fusion.2), channel_id=1, source_target_pairs={{0,24},{2,26},{4,28},{6,30},{8,16},{10,18},{12,20},{14,22},{16,8},... | collective-permute-start | bytes 73736 | tf_op jit(solution)/shard_map/ppermute | solution.py:28
  168.7 12.8 %collective-permute-start.27 = (bf16[128,512]{1,0:T(8,128)(2,1)S(1)}, bf16[128,512]{1,0:T(8,128)(2,1)S(1)}, u32[]{:S(2)}, u32[]{:S(2)}) collective-permute-start(bf16[128,512]{1,0:T(8,128)(2,1)S(1)} %get-tuple-element.112), channel_id=1, source_target_pairs={{0,24},{2,26},{4,28},{6,30},{8,16},{10,18},{12,20},{14,22},{16,8},... | collective-permute-start | bytes 393224 | tf_op jit(solution)/shard_map/ppermute | solution.py:28
  169.8 18.0 %collective-permute-start.67 = (bf16[256,512]{1,0:T(8,128)(2,1)S(1)}, bf16[256,512]{1,0:T(8,128)(2,1)S(1)}, u32[]{:S(2)}, u32[]{:S(2)}) collective-permute-start(bf16[256,512]{1,0:T(8,128)(2,1)S(1)} %pad_maximum_fusion.1.refs_0_), channel_id=1, source_target_pairs={{0,6},{2,4},{4,2},{6,0},{8,14},{10,12},{12,10},{14,8},{16,22},{18,... | collective-permute-start | bytes 786440 | tf_op jit(solution)/shard_map/ppermute | solution.py:28
  181.5 18.8 %collective-permute-start.55 = (bf16[320,512]{1,0:T(8,128)(2,1)S(1)}, bf16[320,512]{1,0:T(8,128)(2,1)S(1)}, u32[]{:S(2)}, u32[]{:S(2)}) collective-permute-start(bf16[320,512]{1,0:T(8,128)(2,1)S(1)} %pad_maximum_fusion.refs_0_), channel_id=1, source_target_pairs={{0,6},{2,4},{4,2},{6,0},{8,14},{10,12},{12,10},{14,8},{16,22},{18,... | collective-permute-start | bytes 983048 | tf_op jit(solution)/shard_map/ppermute | solution.py:28
  184.0 16.3 %collective-permute-start.54 = (bf16[320,512]{1,0:T(8,128)(2,1)S(1)}, bf16[320,512]{1,0:T(8,128)(2,1)S(1)}, u32[]{:S(2)}, u32[]{:S(2)}) collective-permute-start(bf16[320,512]{1,0:T(8,128)(2,1)S(1)} %pad_maximum_fusion.refs_0_), channel_id=1, source_target_pairs={{0,4},{2,6},{4,0},{6,2},{8,12},{10,14},{12,8},{14,10},{16,20},{18,... | collective-permute-start | bytes 983048 | tf_op jit(solution)/shard_map/ppermute | solution.py:28
  185.6 14.6 %collective-permute-start.53 = (bf16[320,512]{1,0:T(8,128)(2,1)S(1)}, bf16[320,512]{1,0:T(8,128)(2,1)S(1)}, u32[]{:S(2)}, u32[]{:S(2)}) collective-permute-start(bf16[320,512]{1,0:T(8,128)(2,1)S(1)} %pad_maximum_fusion.refs_0_), channel_id=1, source_target_pairs={{0,2},{2,0},{4,6},{6,4},{8,10},{10,8},{12,14},{14,12},{16,18},{18,... | collective-permute-start | bytes 983048 | tf_op jit(solution)/shard_map/ppermute | solution.py:28
  186.2 12.4 %collective-permute-start.66 = (bf16[256,512]{1,0:T(8,128)(2,1)S(1)}, bf16[256,512]{1,0:T(8,128)(2,1)S(1)}, u32[]{:S(2)}, u32[]{:S(2)}) collective-permute-start(bf16[256,512]{1,0:T(8,128)(2,1)S(1)} %pad_maximum_fusion.1.refs_0_), channel_id=1, source_target_pairs={{0,4},{2,6},{4,0},{6,2},{8,12},{10,14},{12,8},{14,10},{16,20},{18,... | collective-permute-start | bytes 786440 | tf_op jit(solution)/shard_map/ppermute | solution.py:28
  187.8 10.9 %collective-permute-start.65 = (bf16[256,512]{1,0:T(8,128)(2,1)S(1)}, bf16[256,512]{1,0:T(8,128)(2,1)S(1)}, u32[]{:S(2)}, u32[]{:S(2)}) collective-permute-start(bf16[256,512]{1,0:T(8,128)(2,1)S(1)} %pad_maximum_fusion.1.refs_0_), channel_id=1, source_target_pairs={{0,2},{2,0},{4,6},{6,4},{8,10},{10,8},{12,14},{14,12},{16,18},{18,... | collective-permute-start | bytes 786440 | tf_op jit(solution)/shard_map/ppermute | solution.py:28
  (47 other events, 473.3 us)

commit v3 on v2

v3 whole, which is shorter than its diff:
```python
import functools
import math

import jax
import jax.numpy as jnp
from jax import lax
from jax.experimental import pallas as pl
from jax.experimental.pallas import tpu as pltpu
from jax.sharding import PartitionSpec as P

BF = jnp.bfloat16
F32 = jnp.float32
I32 = jnp.int32
NONE = -1e30
TWO = 2


def factors(size):
    out = []
    while size > 1:
        step = 4 if size % 4 == 0 else 2
        out.append(step)
        size //= step
    return out


def swap(values, mask, size):
    return lax.ppermute(values, "ctx", [(i, i ^ mask) for i in range(size)])


def groups_of(stride, step, size):
    out = []
    for i in range(size):
        if (i // stride) % step == 0:
            out.append([i + j * stride for j in range(step)])
    return out


def exchange(parts, stride, size):
    step = parts.shape[0]
    groups = groups_of(stride, step, size)
    return lax.all_to_all(parts, "ctx", 0, 0, tiled=True, axis_index_groups=groups)


def trade(values):
    return lax.ppermute(values, "wsh", [(0, 1), (1, 0)])


def pick(parts, index):
    return lax.dynamic_index_in_dim(parts, index, 0, False)


def mm(a, b, left=1, right=0):
    return lax.dot_general(a, b, (((left,), (right,)), ((), ())), preferred_element_type=F32)


class Order:
    last = None
    rest = None
    leave = None


def after(value, *earlier):
    return lax.optimization_barrier((value, *earlier))[0]


class Far:
    def __init__(self, value):
        self.value = value


class Ahead:
    def __init__(self, value, shape=None, view=None):
        self.value, self.view = value, view
        self.shape = value.shape if shape is None else shape


def loading_body(body, plan, n_out, far_out, late, views, n_scratch, *refs):
    n_in, n_pre = len(plan), len(views)
    ins, pre_in = list(refs[:n_in]), refs[n_in : n_in + n_pre]
    at = n_in + n_pre
    outs, pre_out = list(refs[at : at + n_out]), refs[at + n_out : at + n_out + n_pre]
    at += n_out + n_pre
    own = refs[at : at + n_scratch]
    held, sems = refs[at + n_scratch : -1], refs[-1]
    first, second, ahead, slot = [], [], [], 0
    for i in range(n_in):
        if plan[i]:
            copy = pltpu.make_async_copy(ins[i], held[slot], sems.at[slot])
            (second if i in late else first).append(copy)
            ins[i] = held[slot]
            slot += 1
    leaving = {}
    for i in range(n_out):
        if far_out[i]:
            leaving[i] = pltpu.make_async_copy(held[slot], outs[i], sems.at[slot])
            outs[i] = held[slot]
            slot += 1
    for view, source, target in zip(views, pre_in, pre_out):
        source = source if view is None else view(source)
        ahead.append(pltpu.make_async_copy(source, target, sems.at[slot]))
        slot += 1
    for copy in first + second + ahead:
        copy.start()
    for copy in first:
        copy.wait()

    def rest():
        for copy in second:
            copy.wait()

    gone = []

    def leave(*which):
        for i in which:
            if far_out[i]:
                gone.append(i)
                leaving[i].start()

    Order.rest, Order.leave = rest, leave
    body(*ins, *outs, *own)
    leave(*[i for i in range(n_out) if i not in gone])
    for i in gone:
        leaving[i].wait()
    for copy in ahead:
        copy.wait()


def call(body, outs, args, scratch=(), smem=(), late=(), ahead=(), mib=14):
    whole = pl.BlockSpec(memory_space=pltpu.VMEM)
    scalars = pl.BlockSpec(memory_space=pltpu.SMEM)
    distant = pl.BlockSpec(memory_space=pltpu.HBM)
    plan = [isinstance(a, Far) for a in args]
    args = [
        pltpu.with_memory_space_constraint(a.value, pltpu.HBM) if isinstance(a, Far) else a
        for a in args
    ]
    far_out = [len(o) > 2 for o in outs]
    if Order.last is not None:
        args[0] = after(args[0], Order.last)
    held = [(a.shape, a.dtype) for a, far in zip(args, plan) if far]
    held += [o[:2] for o, far in zip(outs, far_out) if far]
    need = sum(math.prod(s) * jnp.dtype(d).itemsize for s, d in [*held, *scratch])
    run = pl.pallas_call(
        functools.partial(
            loading_body,
            body,
            plan,
            len(outs),
            far_out,
            late,
            [a.view for a in ahead],
            len(scratch),
        ),
        out_shape=[
            pltpu.HBM(o[0], o[1]) if far else jax.ShapeDtypeStruct(o[0], o[1])
            for o, far in zip(outs, far_out)
        ]
        + [jax.ShapeDtypeStruct(a.shape, a.value.dtype) for a in ahead],
        in_specs=[
            scalars if i in smem else distant if plan[i] else whole for i in range(len(args))
        ]
        + [distant] * len(ahead),
        out_specs=[distant if far else whole for far in far_out] + [whole] * len(ahead),
        scratch_shapes=[pltpu.VMEM(s, d) for s, d in [*scratch, *held]]
        + [pltpu.SemaphoreType.DMA((max(len(held) + len(ahead), 1),))],
        compiler_params=pltpu.CompilerParams(vmem_limit_bytes=(mib << 20) + need),
        cost_estimate=pl.CostEstimate(flops=1, bytes_accessed=1, transcendentals=0),
    )
    moved = [pltpu.with_memory_space_constraint(a.value, pltpu.HBM) for a in ahead]
    got = list(run(*args, *moved))
    Order.last = got[0]
    return got


def far(values):
    return [Far(v) for v in values]


def join(slots):
    half = slots[0].shape[0] // 2
    return jnp.concatenate([s[:half] for s in slots] + [s[half:] for s in slots], axis=0)


def slot_rows(rows, k, count):
    half = rows.shape[0] // (2 * count)
    low = k * half
    high = rows.shape[0] // 2 + k * half
    return jnp.concatenate([rows[low : low + half], rows[high : high + half]], axis=0)


def centred(rows):
    centre = rows - jnp.mean(rows, axis=-1, keepdims=True)
    scale = lax.rsqrt(jnp.mean(centre * centre, axis=-1, keepdims=True) + 1e-05)
    return centre * scale, scale


def fill(scratch, own, other, core):
    half = own.shape[0]
    scratch[pl.ds(pl.multiple_of(core * half, half), half), :] = own[...]
    scratch[pl.ds(pl.multiple_of((1 - core) * half, half), half), :] = other[...]


def pick_gain(own, other, which, core):
    a = own[which : which + 1, :].astype(F32)
    b = other[which : which + 1, :].astype(F32)
    first = jnp.where(core == 0, a, b)
    second = jnp.where(core == 0, b, a)
    return jnp.concatenate([first, second], axis=1)


def route_rows(pieces):
    lane = lax.broadcasted_iota(I32, (8, 128), 1)
    low = lane < 64
    rolled = [pltpu.roll(p, 64, 1) for p in pieces]
    count = len(pieces)
    front = [jnp.where(low, pieces[i], rolled[i + 1]) for i in range(0, count, 2)]
    back = [jnp.where(low, rolled[i], pieces[i + 1]) for i in range(0, count, 2)]
    return jnp.concatenate(front + back, axis=1)


def pack_body(count, rest, *refs):
    tok, routes = refs[:2]
    place = lax.axis_index("ctx") // rest
    local, dim = tok.shape[1:]
    for k, out in enumerate(refs[2:]):
        out[:local, :] = tok[place ^ (k + 1)]
        out[local:, :] = jnp.zeros((8, dim), BF)
        out[local : local + TWO, :128] = routes[place ^ (k + 1)].astype(F32).astype(BF)


def pack_weights_body(query, kv, router, packed):
    half, cols = query.shape
    packed[half:, :] = jnp.zeros((8, packed.shape[1]), BF)
    packed[:half, :cols] = query[...]
    packed[:half, cols:] = kv[...]
    packed[half:, :half] = router[...]


def fill_router(wr, own, packed, core):
    half = own.shape[1]
    wr[...] = jnp.zeros_like(wr)
    experts = own.shape[0]
    mine = pl.ds(pl.multiple_of(core * half, half), half)
    theirs = pl.ds(pl.multiple_of((1 - core) * half, half), half)
    wr[:experts, mine] = own[...].astype(F32)
    wr[:experts, theirs] = packed[half:, :half].astype(F32)


def keys_body(count, rest, *refs):
    toks = refs[:count]
    routes, g_own, g_other, k_own, packed = refs[count : count + 5]
    kv_out, normed_out, tok_out, gain_out, wk, tail_out = refs[count + 5 :]
    core = lax.axis_index("wsh")
    place = lax.axis_index("ctx") // rest
    half = k_own.shape[0]
    local = toks[0].shape[0]
    keys = k_own.shape[1]
    fill(wk, k_own, packed.at[:half, packed.shape[1] - keys :], core)
    rows = join([t[:local] for t in toks])
    tok_out[...] = rows
    Order.leave(2, 4)
    tail_out[...] = jnp.zeros_like(tail_out)
    tail_out[:TWO, :] = routes[place].astype(F32)
    for k in range(1, count):
        tail_out[8 * k : 8 * k + 8, :] = toks[k][local : local + 8, :128].astype(F32)
    rows = rows.astype(F32)
    unit, _ = centred(rows)
    gain_out[...] = jnp.zeros_like(gain_out)
    for which in range(TWO):
        gain_out[which : which + 1, :] = pick_gain(g_own, g_other, which, core)
    normed = (unit * gain_out[0:1, :]).astype(BF)
    normed_out[...] = normed
    kv = mm(normed, wk[...]).astype(BF)
    for i in range(kv_out.shape[0]):
        kv_out[i] = kv


def project_body(count, experts, head, *refs):
    normed_ref, tails, q_own, r_own, packed = refs[:5]
    qt_out, qt_far, nt_out, gate_out, gate_far, route_out, route_far, wq, wr = refs[5:]
    core = lax.axis_index("wsh")
    half, cols = q_own.shape
    fill(wq, q_own, packed.at[:half, :cols], core)
    fill_router(wr, r_own, packed, core)
    normed = normed_ref[...]
    nt_out[...] = normed.T
    Order.leave(2, 7, 8)
    routes = route_rows([tails[8 * k : 8 * k + 8, :] for k in range(count)])
    route_out[...] = routes
    route_far[...] = routes
    logits = mm(wr[...].astype(BF), normed, 1, 1)
    queries = (mm(normed, wq[...]) * 0.125).T
    chosen = []
    for s in range(TWO):
        route = routes[s : s + 1]
        total = jnp.zeros((head, normed.shape[0]), F32)
        value = jnp.zeros((1, normed.shape[0]), F32)
        for e in range(experts):
            here = route == e
            total = jnp.where(here, queries[e * head : (e + 1) * head], total)
            value = jnp.where(here, logits[e : e + 1], value)
        qt_out[s * head : (s + 1) * head, :] = total.astype(BF)
        chosen.append(value)
    qt_far[...] = qt_out[...]
    top = jnp.maximum(chosen[0], chosen[1])
    raised = [jnp.exp(c - top) for c in chosen]
    total = raised[0] + raised[1]
    gate_out[...] = jnp.concatenate([r / total for r in raised], axis=0)
    gate_far[...] = gate_out[...]


def places(order, count, rest, block, width, part):
    me = lax.axis_index("ctx")
    place, other = me // rest, me % rest
    size = count * rest
    lane = lax.broadcasted_iota(I32, (1, width), 1)
    out = jnp.zeros((1, width), I32)
    for k in range(count):
        first = order[(place ^ k) * rest + other]
        base = jnp.where(part == 0, first, 2 * size - 1 - first) * block
        out = jnp.where(lane // block == k, lane - k * block + base, out)
    return out


def key_bases(order, count, rest, block, chunk, part):
    me = lax.axis_index("ctx")
    place = me // rest
    size = count * rest
    out = []
    for k in range(count):
        first = order[(place ^ k) * rest + chunk]
        out.append((first if part == 0 else 2 * size - 1 - first) * block)
    return out


def masked(scores, gap, bases, block):
    parts = [
        jnp.where(gap <= -base, scores[k * block : (k + 1) * block], NONE)
        for k, base in enumerate(bases)
    ]
    return jnp.concatenate(parts, axis=0)


def scored(kv, side, h, gap, order, count, rest, block, chunk, half):
    first = mm(kv[:half], side)
    if h == 0:
        return masked(first, gap, key_bases(order, count, rest, block, chunk, 0), block)
    second = mm(kv[half:], side)
    second = masked(second, gap, key_bases(order, count, rest, block, chunk, 1), block)
    return jnp.concatenate([first, second], axis=0)


def turn_keys(kv, kv_turned):
    rows = kv.shape[1]
    for c in range(kv.shape[0]):
        kv_turned[:, c * rows : (c + 1) * rows] = kv[c].T


def attend_body(count, rest, experts, head, *refs):
    order, kv_ref, qt, gates, routes = refs[:5]
    tok, gains, o_own, o_other = refs[5:9]
    att_out, log_out, mixed_out, hidden_out, two_out, turned_out, kv_out, wo_out, kv_turned = refs[9:]
    kv_out[...] = kv_ref[...]
    Order.leave(6)
    core = lax.axis_index("wsh")
    other = lax.axis_index("ctx") % rest
    total = qt.shape[1]
    half = total // 2
    block = half // count
    turn_keys(kv_ref, kv_turned)
    for h in range(2):
        gap = lax.broadcasted_iota(I32, (block, half), 0) - places(order, count, rest, block, half, h)
        for s in range(TWO):
            side = qt[s * head : (s + 1) * head, h * half : (h + 1) * half]
            side = jnp.concatenate([side, jnp.zeros_like(side)], axis=0)
            reach = half * (h + 1)

            def step(turn, carry, side=side, h=h, gap=gap, reach=reach):
                top, norm, summed = carry
                chunk = turn ^ other
                at = pl.multiple_of(chunk * total, total)
                kv = kv_ref[chunk]
                scores = scored(kv, side, h, gap, order, count, rest, block, chunk, half)
                fresh = jnp.maximum(top, jnp.max(scores, axis=0, keepdims=True))
                shares = jnp.exp(scores - fresh)
                fade = jnp.exp(top - fresh)
                norm = norm * fade + jnp.sum(shares, axis=0, keepdims=True)
                values = kv_turned[head:, pl.ds(at, reach)]
                summed = summed * fade + mm(values, shares.astype(BF))
                return fresh, norm, summed

            start = (
                jnp.full((1, half), NONE, F32),
                jnp.zeros((1, half), F32),
                jnp.zeros((head, half), F32),
            )
            top, norm, summed = lax.fori_loop(0, rest, step, start, unroll=rest <= 4)
            log_out[s : s + 1, h * half : (h + 1) * half] = top + jnp.log(norm)
            att_out[s * head : (s + 1) * head, h * half : (h + 1) * half] = summed / norm
    Order.rest()
    fill(wo_out, o_own, o_other, core)
    Order.leave(0, 1, 7)
    for e in range(experts):
        part = jnp.zeros((head, total), F32)
        for s in range(TWO):
            gate = jnp.where(routes[s : s + 1] == e, gates[s : s + 1], 0.0)
            part = part + gate * att_out[s * head : (s + 1) * head, :]
        mixed_out[e * head : (e + 1) * head, :] = part.astype(BF)
    Order.leave(2)
    hidden = tok[...].astype(F32) + mm(mixed_out[...].T, wo_out[...])
    hidden_out[...] = hidden
    unit, _ = centred(hidden)
    two = (unit * gains[1:2, :]).astype(BF)
    two_out[...] = two
    turned_out[...] = two.T


def feed_body(count, rest, first, tile, *refs):
    two, turned = refs[:2]
    if first:
        slots = refs[2 : 2 + count]
        u_own, u_other, down, layer_in = refs[2 + count : 6 + count]
        layer_out, back_out, send, keep, cots, cot_far, send_up, up = refs[6 + count :]
    else:
        cots, u_own, u_other, down, layer_in, back_in = refs[2:8]
        outs = refs[8 : 12 + count]
        layer_pieces, back_out, keep_down, keep, send = outs[:count], *outs[count:]
        up, layer_out = refs[12 + count :]
    core = lax.axis_index("wsh")
    side = (1 - core) if first else core
    width = down.shape[0]
    half = u_own.shape[0]
    lanes = pl.ds(pl.multiple_of(side * width, width), width)
    up[pl.ds(pl.multiple_of(core * half, half), half), :] = u_own[...]
    up[pl.ds(pl.multiple_of((1 - core) * half, half), half), :] = u_other[:, lanes]
    if first:
        cots[...] = join([o[...] for o in slots])
        cot_far[...] = cots[...]
        Order.leave(5)
    layer_out[...] = layer_in[...]
    if first:
        back_out[...] = jnp.zeros_like(back_out)
    else:
        back_out[...] = back_in[...]
    mine = pl.ds(pl.multiple_of(core * half, half), half)
    theirs = pl.ds(pl.multiple_of((1 - core) * half, half), half)
    dim = up.shape[0]
    per = dim // tile

    def step(j, carry):
        cols = pl.ds(pl.multiple_of(j * tile, tile), tile)
        up_j = up[:, cols]
        down_j = down[cols, :]
        pre = mm(two[...], up_j)
        back = mm(cots[...], down_j, 1, 1)
        phi = 0.5 * (1.0 + lax.erf(pre * math.sqrt(0.5)))
        bell = jnp.exp(pre * pre * -0.5) * (1.0 / math.sqrt(2.0 * math.pi))
        act = (pre * phi).astype(BF)
        back_pre = (back * (phi + pre * bell)).astype(BF)
        layer_out[...] += mm(act, down_j)
        back_out[...] += mm(back_pre, up_j, 1, 1)
        grad = mm(act.T, cots[...]).astype(BF)
        grad_mine = mm(turned[mine, :], back_pre).astype(BF)
        grad_theirs = mm(turned[theirs, :], back_pre).astype(BF)
        rows = pl.ds(pl.multiple_of((j // per) * half, half), half)
        lane = pl.ds(pl.multiple_of((j % per) * tile, tile), tile)
        keep[rows, lane] = grad_mine
        if first:
            send[cols, :] = grad
            send_up[rows, lane] = grad_theirs
        else:
            keep_down[cols, :] = grad
            send[rows, lane] = grad_theirs
        return carry

    lax.fori_loop(0, width // tile, step, 0)
    if not first:
        for k in range(count):
            layer_pieces[k][...] = slot_rows(layer_out[...], k, count).astype(layer_pieces[k].dtype)


def turn_body(count, rest, experts, head, *refs):
    hidden, back_two, cot, wo, gain, gates, routes, att = refs[:8]
    back_hidden_out, branch_out, grad_att_out, delta_out, logit_out, gain_out = refs[8:]
    unit, scale = centred(hidden[...])
    back = back_two[...]
    side = back * gain[1:2, :]
    part = scale * (
        side
        - jnp.mean(side, axis=-1, keepdims=True)
        - unit * jnp.mean(side * unit, axis=-1, keepdims=True)
    )
    gain_out[...] = jnp.broadcast_to(jnp.sum(back * unit, axis=0, keepdims=True), gain_out.shape)
    back_hidden = cot[...].astype(F32) + part
    back_hidden_out[...] = back_hidden
    branch = back_hidden.astype(BF)
    branch_out[...] = branch
    Order.leave(0, 1, 5)
    back_mixed = mm(wo[...], branch, 1, 1)
    grads = []
    for s in range(TWO):
        total = jnp.zeros((head, branch.shape[0]), F32)
        for e in range(experts):
            total = jnp.where(routes[s : s + 1] == e, back_mixed[e * head : (e + 1) * head], total)
        att_s = att[s * head : (s + 1) * head, :]
        grads.append(jnp.sum(total * att_s, axis=0, keepdims=True))
        low = (gates[s : s + 1] * total).astype(BF)
        grad_att_out[s * head : (s + 1) * head, :] = low
        delta_out[s : s + 1, :] = jnp.sum(low.astype(F32) * att_s, axis=0, keepdims=True)
    mean = gates[0:1] * grads[0] + gates[1:2] * grads[1]
    row = lax.broadcasted_iota(I32, logit_out.shape, 0)
    logit = jnp.zeros(logit_out.shape, F32)
    for s in range(TWO):
        value = gates[s : s + 1] * (grads[s] - mean)
        logit = logit + jnp.where(row.astype(F32) == routes[s : s + 1], value, 0.0)
    logit_out[...] = logit


def attend_back_body(count, rest, head, split, *refs):
    order, kv_ref, qt, grad_att, logs, delta, grad_q_out = refs[:7]
    outs = refs[7 : 7 + split]
    kv_turned, sides, turned, grad_kv, grad_q = refs[7 + split :]
    total = qt.shape[1]
    half = total // 2
    block = half // count
    turn_keys(kv_ref, kv_turned)
    blank = jnp.zeros((head, total), BF)
    for s in range(TWO):
        q_side = jnp.concatenate([qt[s * head : (s + 1) * head, :], blank], axis=0)
        g_side = jnp.concatenate([blank, grad_att[s * head : (s + 1) * head, :]], axis=0)
        sides[2 * s], sides[2 * s + 1] = q_side, g_side
        turned[2 * s], turned[2 * s + 1] = q_side.T, g_side.T
    grad_q[...] = jnp.zeros_like(grad_q)
    gaps = [
        lax.broadcasted_iota(I32, (block, half), 0) - places(order, count, rest, block, half, h)
        for h in range(2)
    ]

    def step(chunk, carry):
        at = pl.multiple_of(chunk * total, total)
        kv = kv_ref[chunk]
        front = jnp.zeros((half, 2 * head), F32)
        back = jnp.zeros((half, 2 * head), F32)
        for h in range(2):
            cols = slice(h * half, (h + 1) * half)
            reach = half * (h + 1)
            for s in range(TWO):
                scores = scored(
                    kv, sides[2 * s, :, cols], h, gaps[h], order, count, rest, block, chunk, half
                )
                shares = jnp.exp(scores - logs[s : s + 1, cols])
                back_shares = mm(kv[:reach], sides[2 * s + 1, :, cols])
                back_scores = (shares * (back_shares - delta[s : s + 1, cols])).astype(BF)
                grad = mm(back_scores, turned[2 * s, cols, :]) + mm(
                    shares.astype(BF), turned[2 * s + 1, cols, :]
                )
                front = front + grad[:half]
                if h == 1:
                    back = back + grad[half:]
                rows = slice(s * head, (s + 1) * head)
                grad_q[rows, cols] += mm(kv_turned[:head, pl.ds(at, reach)], back_scores)
        grad_kv[pl.ds(at, half), :] = front
        grad_kv[pl.ds(at + half, half), :] = back
        return carry

    lax.fori_loop(0, rest, step, 0)
    grad_q_out[...] = grad_q[...].astype(BF)
    rows = outs[0].shape[0]
    digit = (lax.axis_index("ctx") % rest) // (rest // split)
    for i, out in enumerate(outs):
        begin = pl.multiple_of((digit ^ i) * rows, rows)
        out[...] = grad_kv[pl.ds(begin, rows), :].astype(out.dtype)


def query_body(experts, head, *refs):
    grad_q, normed_t, routes, mixed, branch, wq, wr, logit, tok = refs[:9]
    keep_out, keep, send, back_out, unit_out, scale_out, routers, bqt = refs[9:]
    core = lax.axis_index("wsh")
    total = grad_q.shape[1]
    for e in range(experts):
        part = jnp.zeros((head, total), F32)
        for s in range(TWO):
            value = grad_q[s * head : (s + 1) * head, :].astype(F32) * 0.125
            part = jnp.where(routes[s : s + 1] == e, value, part)
        bqt[e * head : (e + 1) * head, :] = part.astype(BF)
    back_q = bqt[...].T
    half = keep.shape[0]
    mine = pl.ds(pl.multiple_of(core * half, half), half)
    theirs = pl.ds(pl.multiple_of((1 - core) * half, half), half)
    send[:half, :] = mm(mixed[theirs, :], branch[...]).astype(BF)
    send[half:, :] = mm(normed_t[theirs, :], back_q).astype(BF)
    keep_out[...] = mm(mixed[mine, :], branch[...]).astype(BF)
    keep[...] = mm(normed_t[mine, :], back_q).astype(BF)
    parts = []
    left = logit[...]
    for _ in range(3):
        low = left.astype(BF)
        parts.append(low)
        left = left - low.astype(F32)
    routers[...] = parts_dot(parts, normed_t[...])
    back = mm(back_q, wq[...], 1, 1)
    wr_turned = wr[...].astype(BF)
    for low in parts:
        padded = jnp.concatenate([low.astype(F32), jnp.zeros((120, total), F32)], axis=0)
        back = back + mm(padded.T.astype(BF), wr_turned)
    back_out[...] = back
    unit, scale = centred(tok[...].astype(F32))
    unit_out[...] = unit
    scale_out[...] = jnp.broadcast_to(scale, scale_out.shape)


def unproject_body(count, terms, *refs):
    kv_terms = refs[:terms]
    back_part, unit_ref, scale_ref, routers, normed_t, back_hidden, wk, gain, gain_two, sent = refs[
        terms : terms + 10
    ]
    at = terms + 10
    pieces = refs[at : at + count]
    keep, send, gains = refs[at + count :]
    core = lax.axis_index("wsh")
    half = back_part.shape[1] // 2
    back_kv = kv_terms[0][...].astype(F32)
    for term in kv_terms[1:]:
        back_kv = back_kv + term[...].astype(F32)
    back_kv = back_kv.astype(BF)
    back = back_part[...] + mm(back_kv, wk[...], 1, 1)
    unit, scale = unit_ref[...], scale_ref[:, 0:1]
    side = back * gain[0:1, :]
    grad = back_hidden[...] + scale * (
        side
        - jnp.mean(side, axis=-1, keepdims=True)
        - unit * jnp.mean(side * unit, axis=-1, keepdims=True)
    )
    gains[0:1, :] = jnp.sum(back * unit, axis=0, keepdims=True)
    gains[1:2, :] = gain_two[0:1, :]
    step = half // 4
    experts = routers.shape[0]
    high = sent.shape[0]
    send[:high, :] = sent[...]
    for out, which in ((keep, core), (send.at[high:, :], 1 - core)):
        mine = pl.ds(pl.multiple_of(which * half, half), half)
        grad_k = mm(normed_t[mine, :], back_kv).astype(out.dtype)
        for j in range(4):
            out[:step, j * 128 : (j + 1) * 128] = grad_k[j * step : (j + 1) * step]
        blank = jnp.zeros((experts, half), F32)
        out[step : step + 8, :] = jnp.concatenate([routers[:, mine], blank], axis=1).astype(out.dtype)
        gain_pair = jnp.concatenate([gains[0:1, mine], gains[1:2, mine]], axis=1)
        out[step + 8 :, :] = jnp.broadcast_to(gain_pair, (8, 2 * half)).astype(out.dtype)
    for k in range(count):
        pieces[k][...] = slot_rows(grad, k, count).astype(pieces[k].dtype)


def parts_dot(parts, normed_t):
    out = None
    for low in parts:
        value = mm(low, normed_t, 1, 1)
        out = value if out is None else out + value
    return out


def sum_layout(layout, ins, total):
    at = 0
    for terms in layout:
        height = terms[0][2]
        value = None
        for index, begin, count in terms:
            part = ins[index][begin : begin + count, :].astype(F32)
            value = part if value is None else value + part
        total[at : at + height, :] = value
        at += height
    if at < total.shape[0]:
        total[at:, :] = jnp.zeros((total.shape[0] - at, total.shape[1]), F32)


def cut_rows(total, outs, stride, step):
    rows = outs[0].shape[0]
    digit = (lax.axis_index("ctx") // stride) % step
    for j in range(step):
        begin = pl.multiple_of((digit ^ j) * rows, 8)
        outs[j][...] = total[pl.ds(begin, rows), :].astype(outs[j].dtype)


def start_body(layout, whole, stride, step, n_in, *refs):
    ins, outs, total = refs[:n_in], refs[n_in:-1], refs[-1]
    sum_layout(layout, ins, total)
    if whole:
        rows = total.shape[0] // step
        for j in range(step):
            outs[0][j] = total[j * rows : (j + 1) * rows, :].astype(BF)
    else:
        cut_rows(total, outs, stride, step)


def terms_of(ref):
    return [ref.at[j] for j in range(ref.shape[0])] if len(ref.shape) == 3 else [ref]


def middle_body(chunks, stride, step, n_in, riders, *refs):
    ins, riding = refs[:n_in], refs[n_in : n_in + riders]
    refs = refs[n_in + riders :]
    outs, totals = refs[:step], refs[step:]
    digit = (lax.axis_index("ctx") // stride) % step
    at, low = 0, 0
    for count, total in zip(chunks, totals):
        value = None
        for ref in ins[at : at + count]:
            for term in terms_of(ref):
                part = term[...].astype(F32)
                value = part if value is None else value + part
        total[...] = value
        rows = total.shape[0] // step
        for j in range(step):
            begin = pl.multiple_of((digit ^ j) * rows, 8)
            outs[j][low : low + rows, :] = total[pl.ds(begin, rows), :].astype(outs[j].dtype)
        low += rows
        at += count
    for j in range(1, step if riders else 1):
        outs[j][low:, :] = riding[j - 1][...]


def copies_body(slices, n_in, *refs):
    ins, out = refs[:n_in], refs[-1]
    for j in range(out.shape[0]):
        at = 0
        for begin, rows in slices:
            for ref in ins:
                out[j, at : at + rows, :] = ref[begin : begin + rows, :]
                at += rows


def final_body(strides, parts, dests, n_out, *refs):
    got, outs, totals = refs[0], refs[1 : 1 + n_out], refs[1 + n_out :]
    me = lax.axis_index("ctx")
    shift, per = 0, 1
    for stride, step in strides[1:]:
        shift = shift * step + (me // stride) % step
        per *= step
    at, used = 0, 0
    for height, total, (dest, many) in zip(parts, totals, dests):
        rows = height // per
        for i in range(got.shape[0]):
            for b in range(per):
                begin = pl.multiple_of((i * per + (b ^ shift)) * rows, 8)
                piece = got[i, at + b * rows : at + (b + 1) * rows, :]
                total[pl.ds(begin, rows), :] = piece.astype(F32)
        at += height
        dest(total, outs[used : used + many])
        used += many


WIDTH = 512


def cut_up(chunks, heights, strides, at, size, riders=()):
    stride, step = strides[at]
    total = sum(heights) // step
    more = riders[0].shape[0] if riders else 0
    n_in = sum(len(c) for c in chunks)
    pieces = call(
        functools.partial(middle_body, [len(c) for c in chunks], stride, step, n_in, len(riders)),
        [((total, WIDTH), F32)] + [((total + more, WIDTH), BF)] * (step - 1),
        [t for c in chunks for t in c] + far(riders),
        scratch=[((h, WIDTH), F32) for h in heights],
    )
    return pieces[:1] + [swap(pieces[j], j * stride, size) for j in range(1, step)]


def spread(done, strides, at, size):
    stride, step = strides[at]
    return [done] + [swap(done, j * stride, size) for j in range(1, step)]


def settle(terms):
    return call(add_body, [(terms[0].shape, BF)], terms)[0]


def add_body(*refs):
    rows = refs[-1].shape[0]
    value = refs[0][:rows, :].astype(F32)
    for ref in refs[1:-1]:
        value = value + ref[:rows, :].astype(F32)
    refs[-1][...] = value.astype(refs[-1].dtype)


def early_dest(total, outs):
    down, tile = outs
    wide = down.shape[0]
    down[...] = total[:wide, :]
    tile[...] = total[wide : wide + tile.shape[0], :]


def both_final_body(strides, parts, got, tile, *refs):
    outs, totals = refs[:7], refs[7:]

    def main(total, outs):
        (up,) = outs
        half = up.shape[0]
        core = lax.axis_index("wsh")
        tiles = up.shape[1] // WIDTH
        for i in range(tiles):
            side, inner = i // (tiles // 2), i % (tiles // 2)
            at = (core if side == 0 else 1 - core) * (tiles // 2) + inner
            rows = tile[...] if i == 0 else total[(i - 1) * half : i * half, :]
            up[:, pl.ds(pl.multiple_of(at * WIDTH, WIDTH), WIDTH)] = rows

    dests = [(main, 1), (late_dest, 6)]
    final_body(strides, parts, dests, 7, got, *outs, *totals)


def late_dest(total, outs):
    out, query, kv, router, one, two = outs
    half = kv.shape[0]
    out[...] = total[:half, :]
    query[...] = total[half : 2 * half, :]
    step = half // 4
    at = 2 * half
    for j in range(4):
        kv[j * step : (j + 1) * step, :] = total[at : at + step, j * 128 : (j + 1) * 128]
    at += step
    router[...] = total[at : at + router.shape[0], :half]
    one[...] = total[at + 8 : at + 9, :half]
    two[...] = total[at + 8 : at + 9, half:]


def place_body(rest, *refs):
    place = lax.axis_index("ctx") // rest
    out = refs[-1]
    local = out.shape[1]
    for k, ref in enumerate(refs[:-1]):
        begin = ref.shape[0] - local
        out[place ^ k] = ref[begin:, :].astype(F32)


def on_device(
    tokens,
    routes,
    block_order,
    norm_gain1,
    router_w,
    query_w,
    kv_w,
    out_w,
    norm_gain2,
    up_w,
    down_w,
    cotangent,
):
    size = lax.axis_size("ctx")
    count, local, dim = tokens.shape
    rest = size // count
    place = lax.axis_index("ctx") // rest
    total = count * local
    experts = router_w.shape[1]
    head = kv_w.shape[1] // 2
    feed = up_w.shape[1]

    Order.last = None
    tall = dim // 2
    keys = 2 * head
    router_t = router_w.T
    routes_t = routes.transpose(0, 2, 1)

    def core():
        return lax.axis_index("wsh")

    def here():
        return lax.axis_index("ctx") // rest

    tok_pieces = call(
        functools.partial(pack_body, count, rest),
        [((local + 8, dim), BF)] * (count - 1),
        far([tokens, routes_t]),
    )
    tok_x = [swap(tok_pieces[k - 1], k * rest, size) for k in range(1, count)]
    packed, tok_own, kv_own = call(
        pack_weights_body,
        [((tall + 8, experts * head + keys), BF)],
        far([query_w, kv_w, router_t]),
        ahead=[Ahead(tokens, (local, dim), lambda r: r.at[here()]), Ahead(kv_w)],
    )
    packed_x = trade(packed)
    gain_one, gain_two = after((norm_gain1, norm_gain2), packed)
    gains = jnp.stack([gain_one, gain_two])
    gains_x = trade(gains)

    steps = factors(rest)
    kv, normed, tok, gain_rows, wk, tails, query_own, router_own, *cot_pieces = call(
        functools.partial(keys_body, count, rest),
        [
            ((steps[0], total, keys), BF),
            ((total, dim), BF),
            ((total, dim), BF, 1),
            ((8, dim), F32, 1),
            ((dim, keys), BF, 1),
            ((8 * count, 128), F32),
        ],
        [tok_own, *tok_x, Far(routes_t), gains, gains_x, kv_own, packed_x],
        ahead=[Ahead(query_w), Ahead(router_t)]
        + [
            Ahead(cotangent, (local, dim), lambda r, k=k: r.at[here() ^ k])
            for k in range(1, count)
        ],
    )
    stride = 1
    for i, step in enumerate(steps):
        if i > 0:
            kv = jnp.broadcast_to(kv[None], (step,) + kv.shape)
        kv = exchange(kv, stride, size).reshape(-1, total, keys)
        stride *= step
    cot_x = [swap(cot_pieces[k - 1], k * rest, size) for k in range(1, count)]
    qt, qt_far, normed_t, gates, gates_far, route, route_far, wq, wr = call(
        functools.partial(project_body, count, experts, head),
        [
            ((TWO * head, total), BF),
            ((TWO * head, total), BF, 1),
            ((dim, total), BF, 1),
            ((TWO, total), F32),
            ((TWO, total), F32, 1),
            ((8, total), F32),
            ((8, total), F32, 1),
            ((dim, experts * head), BF, 1),
            ((128, dim), F32, 1),
        ],
        [normed, tails, query_own, router_own, packed_x],
    )
    up_w2, down_w2, out_w2, _ = lax.optimization_barrier((up_w, down_w, out_w, normed))
    out_x, up_x, down_x = trade(out_w2), trade(up_w2), trade(down_w2)
    span = rest * total
    wide = feed // 2

    def lanes(which):
        def view(ref):
            side = which()
            return ref.at[:, pl.ds(pl.multiple_of(side * wide, wide), wide)]

        return view

    att, logs, mixed, hidden, two, two_t, kv_far, wo, cot_own, up_first = call(
        functools.partial(attend_body, count, rest, experts, head),
        [
            ((TWO * head, total), F32, 1),
            ((TWO, total), F32, 1),
            ((experts * head, total), BF, 1),
            ((total, dim), F32),
            ((total, dim), BF),
            ((dim, total), BF),
            ((rest, total, keys), BF, 1),
            ((experts * head, dim), BF, 1),
        ],
        [block_order, kv, qt, gates, route, *far([tok, gain_rows, out_w]), out_x],
        scratch=[((keys, span), BF)],
        smem=(0,),
        late=(5, 6, 7),
        ahead=[
            Ahead(cotangent, (local, dim), lambda r: r.at[here()]),
            Ahead(up_w, (tall, wide), lanes(lambda: 1 - core())),
        ],
    )

    tile = 256
    upper = wide * tall // dim
    layer, back_two, send_one, keep_one, cots, cots_far, send_up, up_second, down_own = call(
        functools.partial(feed_body, count, rest, True, tile),
        [
            ((total, dim), F32),
            ((total, dim), F32),
            ((wide, dim), BF),
            ((upper, dim), BF, 1),
            ((total, dim), BF),
            ((total, dim), BF, 1),
            ((upper, dim), BF),
        ],
        [two, two_t, cot_own, *cot_x, up_first, up_x, down_x, hidden],
        scratch=[((dim, wide), BF)],
        ahead=[Ahead(up_w, (tall, wide), lanes(core)), Ahead(down_w)],
    )
    recv_down, recv_up = trade(send_one), trade(send_up)
    *layer_pieces, back_two, keep_down, keep_two, send_two, cots, wo, gain_near, gates, route, att = call(
        functools.partial(feed_body, count, rest, False, tile),
        [((local, dim), F32, 1)]
        + [((local, dim), BF, 1)] * (count - 1)
        + [
            ((total, dim), F32),
            ((wide, dim), BF, 1),
            ((upper, dim), BF, 1),
            ((upper, dim), BF, 1),
        ],
        [two, two_t, cots, up_second, up_x, down_own, layer, back_two],
        scratch=[((dim, wide), BF), ((total, dim), F32)],
        ahead=[
            Ahead(a)
            for a in (cots_far, wo, gain_rows, gates_far, route_far, att)
        ],
    )
    recv_two = trade(send_two)
    layer_got = [layer_pieces[0]] + [swap(layer_pieces[k], k * rest, size) for k in range(1, count)]

    strides = []
    stride = 1
    for step in [*steps, count]:
        strides.append((stride, step))
        stride *= step
    last = len(strides) - 1
    unit = 8 * size
    first = strides[0][1]
    early_rows = -(-(wide + tall) // unit) * unit
    main_rows = -(-(2 * upper - tall) // unit) * unit
    small = tall // 4 + 16
    late_rows = -(-(small + 2 * tall) // unit) * unit

    def bulk(args, layout, height, ahead=()):
        pieces, *near = call(
            functools.partial(start_body, layout, True, 1, first, len(args)),
            [((first, height // first, WIDTH), BF)],
            args,
            scratch=[((height, WIDTH), F32)],
            ahead=ahead,
        )
        return exchange(pieces, 1, size), near

    def inner(terms, height, riders=()):
        height //= first
        for at in range(1, last + 1):
            more = riders if at == last else ()
            terms = cut_up([terms], [height], strides, at, size, more)
            height //= strides[at][1]
        return terms

    def outer(got):
        for at in reversed(range(1, last)):
            got = spread(jnp.concatenate(got, axis=0), strides, at, size)
        return got

    def ready(got, ahead=()):
        rows = got[0].shape[0]
        copies, *near = call(
            functools.partial(copies_body, [(0, rows)], len(got)),
            [((first, rows * len(got), WIDTH), BF)],
            got,
            ahead=ahead,
        )
        return exchange(copies, 1, size), near

    back_hidden, branch, grad_att, delta, logit, gain_two = call(
        functools.partial(turn_body, count, rest, experts, head),
        [
            ((total, dim), F32, 1),
            ((total, dim), BF, 1),
            ((TWO * head, total), BF, 1),
            ((TWO, total), F32, 1),
            ((experts, total), F32, 1),
            ((8, dim), F32, 1),
        ],
        [hidden, back_two, cots, wo, gain_near, gates, route, att],
    )
    early, (kv_near, qt_near, logs_near, grad_att, delta) = bulk(
        [Far(keep_down), recv_down, Far(keep_two), recv_up],
        [[(0, 0, wide), (1, 0, wide)], [(2, 0, tall), (3, 0, tall)]],
        early_rows,
        [Ahead(a) for a in (kv_far, qt_far, logs, grad_att, delta)],
    )
    split = steps[-1]
    share = span // split
    grad_q, *kv_terms = call(
        functools.partial(attend_back_body, count, rest, head, split),
        [((TWO * head, total), BF), ((share, keys), F32, 1)] + [((share, keys), BF, 1)] * (split - 1),
        [block_order, kv_near, qt_near, grad_att, logs_near, delta],
        scratch=[
            ((keys, span), BF),
            ((2 * TWO, keys, total), BF),
            ((2 * TWO, total, keys), BF),
            ((span, keys), F32),
            ((TWO * head, total), F32),
        ],
        smem=(0,),
        ahead=[Ahead(a) for a in (normed_t, route_far, mixed, branch, wq, wr, logit, tok)],
    )
    kv_terms, ahead = kv_terms[:split], kv_terms[split:]
    stride = rest
    for i, step in reversed(list(enumerate(steps))):
        stride //= step
        if i + 1 < len(steps):
            summed = functools.reduce(lambda a, b: a + b.astype(F32), terms)
            parts = summed.reshape(step, -1, keys)
            digit = (lax.axis_index("ctx") // stride) % step
            kv_terms = [pick(parts, digit ^ j) for j in range(step)]
        terms = [kv_terms[0]] + [
            swap(kv_terms[j].astype(BF), j * stride, size) for j in range(1, step)
        ]
    grad_q = after(grad_q, *layer_got[1:])
    keep_out, keep_query, send_main, back_part, unit_rows, scale_rows, routers, *near = call(
        functools.partial(query_body, experts, head),
        [
            ((tall, dim), BF, 1),
            ((tall, dim), BF, 1),
            ((2 * tall, dim), BF, 1),
            ((total, dim), F32),
            ((total, dim), F32),
            ((total, 128), F32),
            ((experts, dim), F32),
        ],
        [grad_q, *ahead],
        scratch=[((experts * head, total), BF)],
        ahead=[Ahead(a) for a in (normed_t, back_hidden, wk, gain_rows, gain_two, terms[0])],
    )
    *near, term = near
    *input_pieces, keep_late, send_late = call(
        functools.partial(unproject_body, count, len(terms)),
        [((local, dim), F32, 1)]
        + [((local, dim), BF, 1)] * (count - 1)
        + [((small, dim), F32, 1), ((small + 2 * tall, dim), BF)],
        [term, *terms[1:], back_part, unit_rows, scale_rows, routers, *near, Far(send_main)],
        scratch=[((8, dim), F32)],
    )
    recv_late = trade(send_late)
    main, _ = bulk(
        [*far([keep_two]), recv_up, *far([keep_one]), recv_two],
        [
            [(0, tall, upper - tall), (1, tall, upper - tall)],
            [(2, 0, upper), (3, 0, upper)],
        ],
        main_rows,
    )
    early_terms = inner([early], early_rows)
    pieces = call(
        functools.partial(
            start_body,
            [
                [(0, 0, tall), (1, 0, tall)],
                [(0, tall, tall), (2, 0, tall)],
                [(0, 2 * tall, small), (3, 0, small)],
            ],
            False,
            1,
            first,
            4,
        ),
        [((late_rows // first, WIDTH), F32)] + [((late_rows // first, WIDTH), BF)] * (first - 1),
        [recv_late, *far([keep_out, keep_query, keep_late])],
        scratch=[((late_rows, WIDTH), F32)],
    )
    late = pieces[:1] + [swap(pieces[j], j, size) for j in range(1, first)]
    early_got = outer(spread(settle(early_terms), strides, last, size))
    heights = [main_rows // first, late_rows // first]
    chunks = [[main], late]
    for at in range(1, last):
        chunks = [cut_up([c], [h], strides, at, size) for c, h in zip(chunks, heights)]
        heights = [h // strides[at][1] for h in heights]
    both_terms = cut_up(chunks, heights, strides, last, size)
    heights = [h // count for h in heights]
    early_last, _ = ready(early_got)
    both_got = spread(settle(both_terms), strides, last, size)
    slices = [(0, heights[0]), (heights[0], heights[1])]
    for stage in reversed(range(1, last)):
        moved = []
        for begin, h in slices:
            piece = jnp.concatenate([g[begin : begin + h] for g in both_got], axis=0)
            moved.append(spread(piece, strides, stage, size))
        both_got = [jnp.concatenate([m[j] for m in moved], axis=0) for j in range(strides[stage][1])]
        tops = [m[0].shape[0] for m in moved]
        slices = [(0, tops[0]), (tops[0], tops[1])]
    tall_rows = sum(h for _, h in slices) * len(both_got)
    (copies,) = call(
        functools.partial(copies_body, slices, len(both_got)),
        [((first, tall_rows, WIDTH), BF)],
        both_got,
    )
    both_last = exchange(copies, 1, size)
    input_pieces = after(tuple(input_pieces), both_got[0])
    input_got = [input_pieces[0]] + [swap(input_pieces[k], k * rest, size) for k in range(1, count)]
    (layer_out,) = call(
        functools.partial(place_body, rest),
        [((count, local, dim), F32, 1)],
        [Far(layer_got[0]), *layer_got[1:]],
    )
    grad_down, up_tile = call(
        functools.partial(final_body, strides, [early_rows // first], [(early_dest, 2)], 2),
        [((wide, dim), F32, 1), ((tall, WIDTH), F32)],
        [early_last],
        scratch=[((early_rows, WIDTH), F32)],
    )
    (input_grad,) = call(
        functools.partial(place_body, rest),
        [((count, local, dim), F32, 1)],
        [Far(input_got[0]), *input_got[1:]],
    )
    grad_up, grad_out, grad_query, grad_kv, grad_router, grad_one, grad_two = call(
        functools.partial(both_final_body, strides, [main_rows // first, late_rows // first]),
        [
            ((tall, feed), F32, 1),
            ((tall, dim), F32, 1),
            ((tall, experts * head), F32, 1),
            ((tall, keys), F32, 1),
            ((experts, tall), F32, 1),
            ((1, tall), F32, 1),
            ((1, tall), F32, 1),
        ],
        [both_last, up_tile],
        scratch=[((main_rows, WIDTH), F32), ((late_rows, WIDTH), F32)],
    )
    return (
        layer_out,
        input_grad,
        grad_one.reshape(tall),
        grad_router.T,
        grad_query,
        grad_kv,
        grad_out,
        grad_two.reshape(tall),
        grad_up,
        grad_down,
    )


def solution(mesh):
    placed = (
        P("wsh", "ctx", None),
        P("wsh", "ctx", None),
        P(),
        P("wsh"),
        P("wsh", None),
        P("wsh", None),
        P("wsh", None),
        P("wsh", None),
        P("wsh"),
        P("wsh", None),
        P("wsh", None),
        P("wsh", "ctx", None),
    )
    return jax.shard_map(
        on_device,
        mesh=mesh,
        in_specs=placed,
        out_specs=(
            P("wsh", "ctx", None),
            P("wsh", "ctx", None),
            P("wsh"),
            P("wsh", None),
            P("wsh", None),
            P("wsh", None),
            P("wsh", None),
            P("wsh"),
            P("wsh", None),
            P("wsh", None),
        ),
        check_vma=False,
    )
```

time: 202 us -> 176 us (0.87)
  Pallas kernels: 36 us -> 60.8 us
  waiting for transfers between devices: 66 us -> 41.5 us
  starting transfers between devices: 89.6 us -> 65.4 us
  local copies, waits for them, and re-layouts: 9.38 us -> 5.8 us
    ppermute x57 -> x30, starting transfers between devices: 87.6 us -> 44.8 us  [swap(): return lax.ppermute(values, 'ctx', [(i, i ^ mask) for i in range(size)])]
    ppermute x57 -> x30, waiting for transfers between devices: 63.4 us -> 37.1 us  [swap(): return lax.ppermute(values, 'ctx', [(i, i ^ mask) for i in range(size)])]
    pallas_call x18 -> x24, Pallas kernels: 36 us -> 60.8 us  [call(): got = list(run(*args, *moved))]
    all_to_all x0 -> x5, starting transfers between devices: none -> 18.9 us  [exchange(): lax.all_to_all(parts, 'ctx', 0, 0, tiled=True, axis_index_groups=groups)]
    all_to_all x0 -> x5, waiting for transfers between devices: none -> 3.29 us  [exchange(): lax.all_to_all(parts, 'ctx', 0, 0, tiled=True, axis_index_groups=groups)]
    squeeze x3 -> x0, local copies, waits for them, and re-layouts: 2.45 us -> none  [pick(): return lax.dynamic_index_in_dim(parts, index, 0, False)]
    unnamed x24 -> x34, local copies, waits for them, and re-layouts: 4.35 us -> 5.79 us
  transfers between devices with their start and end apart: 68 -> 44, of which waited for: 25 -> 16; matrix products, arithmetic and copies ran while one was open for 3% -> 0% of each run, Pallas kernels for 14% -> 25%
where the time goes in v3:
time: 176 us; the launch traced here: 175 us
  starting transfers between devices  65.4 us (37%)
  Pallas kernels  60.8 us (35%)
  waiting for transfers between devices  41.5 us (24%)
  local copies, waits for them, and re-layouts  5.8 us (3%)
    pallas_call x24, Pallas kernels, call(): got = list(run(*args, *moved))  60.8 us
    ppermute x30, starting transfers between devices, swap(): return lax.ppermute(values, 'ctx', [(i, i ^ mask) for i in range(size)])  44.8 us
    ppermute x30, waiting for transfers between devices, swap(): return lax.ppermute(values, 'ctx', [(i, i ^ mask) for i in range(size)])  37.1 us
    all_to_all x5, starting transfers between devices, exchange(): lax.all_to_all(parts, 'ctx', 0, 0, tiled=True, axis_index_groups=groups)  18.9 us
    unnamed x34, local copies, waits for them, and re-layouts  5.79 us
  transfers between devices with their start and end apart: 44, of which 16 were waited for; matrix products, arithmetic and copies ran while one was open for 0% of the time, Pallas kernels for 25%

profile of v3, /device:TPU:0, one launch (start us, length us, event | category | flops | bytes accessed | tf_op | source)
XLA Modules:
  0.0 174.8 jit_solution(10503891113338031701)
XLA Ops:
  3.4 3.7 %collective-permute-start.1 = (bf16[136,512]{1,0:T(8,128)(2,1)S(1)}, bf16[136,512]{1,0:T(8,128)(2,1)S(1)}, u32[]{:S(2)}, u32[]{:S(2)}) collective-permute-start(bf16[136,512]{1,0:T(8,128)(2,1)S(1)} %get-tuple-element.172), channel_id=1, source_target_pairs={{0,16},{2,18},{4,20},{6,22},{8,24},{10,26},{12,28},{14,30},{16,0},... | collective-permute-start | bytes 417800 | tf_op jit(solution)/shard_map/ppermute | solution.py:28
  9.9 7.7 %collective-permute-done.1.refs_2_ = bf16[136,512]{1,0:T(8,128)(2,1)S(1)} collective-permute-done((bf16[136,512]{1,0:T(8,128)(2,1)S(1)}, bf16[136,512]{1,0:T(8,128)(2,1)S(1)}, u32[]{:S(2)}, u32[]{:S(2)}) %collective-permute-start.1) | collective-permute-done | bytes 139296 | tf_op jit(solution)/shard_map/ppermute | solution.py:28
  18.6 2.1 %shard_map.197 = (bf16[4,512,128]{2,1,0:T(8,128)(2,1)S(1)}, bf16[512,512]{1,0:T(8,128)(2,1)S(1)}, bf16[512,512]{1,0:T(8,128)(2,1)}, f32[8,512]{1,0:T(8,128)}, bf...) custom-call(bf16[128,512]{1,0:T(8,128)(2,1)S(1)} %get-tuple-element., ...), custom_call_target="tpu_custom_call" | custom-call | flops 1 | bytes 1 | tf_op jit(solution)/shard_map/pallas_call | solution.py:171
  22.8 3.8 %all-to-all-start = ((bf16[4,512,128]{2,1,0:T(8,128)(2,1)}), bf16[4,512,128]{2,1,0:T(8,128)(2,1)S(1)}, u32[]{:S(2)}, u32[]{:S(2)}) async-start(bf16[4,512,128]{2,1,0:T(8,128)(2,1)} %copy-done), calls=%async_computation | async-start | bytes 1048576 | tf_op jit(solution)/shard_map/all_to_all | solution.py:42
  26.6 2.4 %collective-permute-start.6 = (bf16[128,512]{1,0:T(8,128)(2,1)}, bf16[128,512]{1,0:T(8,128)(2,1)}, u32[]{:S(2)}, u32[]{:S(2)}) collective-permute-start(bf16[128,512]{1,0:T(8,128)(2,1)} %copy-done.10), channel_id=1, source_target_pairs={{0,8},{2,10},{4,12},{6,14},{8,0},{10,2},{12,4},{14,6},{16,24},{18,... | collective-permute-start | bytes 393224 | tf_op jit(solution)/shard_map/ppermute | solution.py:28
  38.1 8.0 %shard_map.199 = (f32[128,512]{1,0:T(8,128)}, f32[2,512]{1,0:T(2,128)}, bf16[512,512]{1,0:T(8,128)(2,1)}, f32[512,512]{1,0:T(8,128)S(1)}, bf16[512,512]{1,0:T(8,...) custom-call(s32[16]{0:T(128)S(1)} %copy-done.7, ...), custom_call_target="tpu_custom_call" | custom-call | flops 1 | bytes 1 | tf_op jit(solution)/shard_map/pallas_call | solution.py:171
  46.2 6.7 %shard_map.200 = (f32[512,512]{1,0:T(8,128)S(1)}, f32[512,512]{1,0:T(8,128)S(1)}, bf16[1024,512]{1,0:T(8,128)(2,1)S(1)}, bf16[512,512]{1,0:T(8,128)(2,1)}, bf16[...) custom-call(bf16[512,512]{1,0:T(8,128)(2,1)S(1)} %get-tuple-element., ...), custom_call_target="tpu_custom_call" | custom-call | flops 1 | bytes 1 | tf_op jit(solution)/shard_map/pallas_call | solution.py:171
  53.5 6.4 %shard_map.201 = (f32[128,512]{1,0:T(8,128)}, bf16[128,512]{1,0:T(8,128)(2,1)}, bf16[128,512]{1,0:T(8,128)(2,1)}, bf16[128,512]{1,0:T(8,128)(2,1)}, f32[512,512]...) custom-call(bf16[512,512]{1,0:T(8,128)(2,1)S(1)} %get-tuple-element., ...), custom_call_target="tpu_custom_call" | custom-call | flops 1 | bytes 1 | tf_op jit(solution)/shard_map/pallas_call | solution.py:171
  59.9 2.1 %shard_map.202 = (f32[512,512]{1,0:T(8,128)}, bf16[512,512]{1,0:T(8,128)(2,1)}, bf16[128,512]{1,0:T(8,128)(2,1)}, f32[2,512]{1,0:T(2,128)}, f32[8,512]{1,0:T(8,128)}, /*index=5*/f32[8,512]{1,0:T(8,128)}) custom-call(f32[512,512]{1,0:T(8,128)S(1)} %get-tuple-element.215.refs_9_.refs_0_, f32[512,512]{1,0:T(8,128)S(1)} %get-tuple-element.216.refs_1_, ...), custom_call_target="tpu_custom_call" | custom-call | flops 1 | bytes 1 | tf_op jit(solution)/shard_map/pallas_call | solution.py:171
  62.0 2.8 %shard_map.203 = (bf16[4,320,512]{2,1,0:T(8,128)(2,1)}, bf16[4,512,128]{2,1,0:T(8,128)(2,1)S(1)}, bf16[128,512]{1,0:T(8,128)(2,1)S(1)}, f32[2,512]{1,0:T(2,128)S...) custom-call(bf16[1024,512]{1,0:T(8,128)(2,1)} %get-tuple-element.224.refs_0_, ...), custom_call_target="tpu_custom_call" | custom-call | flops 1 | bytes 1 | tf_op jit(solution)/shard_map/pallas_call | solution.py:171
  64.8 4.4 %all-to-all-start.2 = ((bf16[4,320,512]{2,1,0:T(8,128)(2,1)}), bf16[4,320,512]{2,1,0:T(8,128)(2,1)S(1)}, u32[]{:S(2)}, u32[]{:S(2)}) async-start(bf16[4,320,512]{2,1,0:T(8,128)(2,1)} %get-tuple-element.232), calls=%async_computation.2 | async-start | bytes 2621440 | tf_op jit(solution)/shard_map/all_to_all | solution.py:42
  70.0 2.1 %collective-permute-start.14 = (bf16[128,512]{1,0:T(8,128)(2,1)S(1)}, bf16[128,512]{1,0:T(8,128)(2,1)S(1)}, u32[]{:S(2)}, u32[]{:S(2)}) collective-permute-start(bf16[128,512]{1,0:T(8,128)(2,1)S(1)} %copy-done.14), channel_id=1, source_target_pairs={{0,16},{2,18},{4,20},{6,22},{8,24},{10,26},{12,28},{14,30},{16,0},... | collective-permute-start | bytes 393224 | tf_op jit(solution)/shard_map/ppermute | solution.py:28
  73.6 7.6 %shard_map.204 = (bf16[128,512]{1,0:T(8,128)(2,1)S(1)}, f32[512,128]{1,0:T(8,128)}, bf16[512,128]{1,0:T(8,128)(2,1)}, bf16[512,128]{1,0:T(8,128)(2,1)}, bf16[512...) custom-call(s32[16]{0:T(128)S(1)} %copy-done.7, ...), custom_call_target="tpu_custom_call" | custom-call | flops 1 | bytes 1 | tf_op jit(solution)/shard_map/pallas_call | solution.py:171
  81.2 2.1 %collective-permute-start.16 = (bf16[512,128]{1,0:T(8,128)(2,1)}, bf16[512,128]{1,0:T(8,128)(2,1)S(1)}, u32[]{:S(2)}, u32[]{:S(2)}) collective-permute-start(bf16[512,128]{1,0:T(8,128)(2,1)} %get-tuple-element.265), channel_id=1, source_target_pairs={{0,2},{2,0},{4,6},{6,4},{8,10},{10,8},{12,14},{14,12},{16,18},{18,... | collective-permute-start | bytes 393224 | tf_op jit(solution)/shard_map/ppermute | solution.py:28
  84.8 3.6 %shard_map.205 = (bf16[256,512]{1,0:T(8,128)(2,1)}, bf16[256,512]{1,0:T(8,128)(2,1)}, bf16[512,512]{1,0:T(8,128)(2,1)}, f32[512,512]{1,0:T(8,128)S(1)}, f32[512,...) custom-call(bf16[128,512]{1,0:T(8,128)(2,1)S(1)} %get-tuple-element., ...), custom_call_target="tpu_custom_call" | custom-call | flops 1 | bytes 1 | tf_op jit(solution)/shard_map/pallas_call | solution.py:171
  89.8 2.6 %collective-permute-done.18.refs_3_ = bf16[512,128]{1,0:T(8,128)(2,1)S(1)} collective-permute-done((bf16[512,128]{1,0:T(8,128)(2,1)}, bf16[512,128]{1,0:T(8,128)(2,1)S(1)}, u32[]{:S(2)}, u32[]{:S(2)}) %collective-permute-start.18) | collective-permute-done | bytes 131104 | tf_op jit(solution)/shard_map/ppermute | solution.py:28
  92.4 3.4 %shard_map.206 = (f32[128,512]{1,0:T(8,128)}, bf16[128,512]{1,0:T(8,128)(2,1)}, bf16[128,512]{1,0:T(8,128)(2,1)}, bf16[128,512]{1,0:T(8,128)(2,1)}, f32[80,512]{1,0:T(8,128)}, /*index=5*/bf16[592,512]{1,0:T(8,128)(2,1)}) custom-call(f32[512,128]{1,0:T(8,128)S(1)} %get-tuple-element.264.refs_0_, bf16[512,128]{1,0:T(8,128)(2,1)S(1)} %collective-permute-done.16.refs_1_, ...), custom_call_target="tpu_custom_call" | custom-call | flops 1 | bytes 1 | tf_op jit(solution)/shard_map/pallas_call | solution.py:171
  96.0 2.3 %shard_map.207 = bf16[4,192,512]{2,1,0:T(8,128)(2,1)} custom-call(bf16[512,512]{1,0:T(8,128)(2,1)} %get-tuple-element.279.refs_2_.refs_0_, bf16[512,512]{1,0:T(8,128)(2,1)S(1)} %collective-permute-done.12.refs_3_.refs_1_, bf16[512,512]{1,0:T(8,128)(2,1)} %get-tuple-element.280.refs_2_, bf16[512,512]{1,0:T(8,128)(2,1)S(1)} %collective-permute-done.19.refs_3_), custom_call_target="tpu_custom_call" | custom-call | flops 1 | bytes 1 | tf_op jit(solution)/shard_map/pallas_call | solution.py:171
  98.3 3.5 %all-to-all-start.1 = ((bf16[4,192,512]{2,1,0:T(8,128)(2,1)}), bf16[4,192,512]{2,1,0:T(8,128)(2,1)S(1)}, u32[]{:S(2)}, u32[]{:S(2)}) async-start(bf16[4,192,512]{2,1,0:T(8,128)(2,1)} %shard_map.207), calls=%async_computation.1 | async-start | bytes 1572864 | tf_op jit(solution)/shard_map/all_to_all | solution.py:42
  104.3 2.0 %collective-permute-start.24 = (bf16[160,512]{1,0:T(8,128)(2,1)S(1)}, bf16[160,512]{1,0:T(8,128)(2,1)S(1)}, u32[]{:S(2)}, u32[]{:S(2)}) collective-permute-start(bf16[160,512]{1,0:T(8,128)(2,1)S(1)} %get-tuple-element.294), channel_id=1, source_target_pairs={{0,2},{2,0},{4,6},{6,4},{8,10},{10,8},{12,14},{14,12},{16,18},{18,... | collective-permute-start | bytes 491528 | tf_op jit(solution)/shard_map/ppermute | solution.py:28
  106.4 2.1 %collective-permute-start.22 = (bf16[80,512]{1,0:T(8,128)(2,1)S(1)}, bf16[80,512]{1,0:T(8,128)(2,1)S(1)}, u32[]{:S(2)}, u32[]{:S(2)}) collective-permute-start(bf16[80,512]{1,0:T(8,128)(2,1)S(1)} %get-tuple-element.291), channel_id=1, source_target_pairs={{0,16},{2,18},{4,20},{6,22},{8,24},{10,26},{12,28},{14,30},{16,0},... | collective-permute-start | bytes 245768 | tf_op jit(solution)/shard_map/ppermute | solution.py:28
  113.4 3.0 %collective-permute-done.23.refs_3_ = bf16[80,512]{1,0:T(8,128)(2,1)S(1)} collective-permute-done((bf16[80,512]{1,0:T(8,128)(2,1)S(1)}, bf16[80,512]{1,0:T(8,128)(2,1)S(1)}, u32[]{:S(2)}, u32[]{:S(2)}) %collective-permute-start.23) | collective-permute-done | bytes 81952 | tf_op jit(solution)/shard_map/ppermute | solution.py:28
  123.7 2.2 %collective-permute-done.28.refs_2_ = bf16[80,512]{1,0:T(8,128)(2,1)S(1)} collective-permute-done((bf16[80,512]{1,0:T(8,128)(2,1)S(1)}, bf16[80,512]{1,0:T(8,128)(2,1)S(1)}, u32[]{:S(2)}, u32[]{:S(2)}) %collective-permute-start.28) | collective-permute-done | bytes 81952 | tf_op jit(solution)/shard_map/ppermute | solution.py:28
  127.0 3.6 %all-to-all-start.3 = ((bf16[4,320,512]{2,1,0:T(8,128)(2,1)}), bf16[4,320,512]{2,1,0:T(8,128)(2,1)S(1)}, u32[]{:S(2)}, u32[]{:S(2)}) async-start(bf16[4,320,512]{2,1,0:T(8,128)(2,1)} %shard_map.212), calls=%async_computation.3 | async-start | bytes 2621440 | tf_op jit(solution)/shard_map/all_to_all | solution.py:42
  130.6 2.8 %collective-permute-start.31 = (bf16[88,512]{1,0:T(8,128)(2,1)S(1)}, bf16[88,512]{1,0:T(8,128)(2,1)S(1)}, u32[]{:S(2)}, u32[]{:S(2)}) collective-permute-start(bf16[88,512]{1,0:T(8,128)(2,1)S(1)} %get-tuple-element.301), channel_id=1, source_target_pairs={{0,16},{2,18},{4,20},{6,22},{8,24},{10,26},{12,28},{14,30},{16,0},... | collective-permute-start | bytes 270344 | tf_op jit(solution)/shard_map/ppermute | solution.py:28
  135.7 4.7 %collective-permute-done.31.refs_2_ = bf16[88,512]{1,0:T(8,128)(2,1)S(1)} collective-permute-done((bf16[88,512]{1,0:T(8,128)(2,1)S(1)}, bf16[88,512]{1,0:T(8,128)(2,1)S(1)}, u32[]{:S(2)}, u32[]{:S(2)}) %collective-permute-start.31) | collective-permute-done | bytes 90144 | tf_op jit(solution)/shard_map/ppermute | solution.py:28
  145.0 2.1 %collective-permute-done.35.refs_3_ = bf16[88,512]{1,0:T(8,128)(2,1)S(1)} collective-permute-done((bf16[88,512]{1,0:T(8,128)(2,1)S(1)}, bf16[88,512]{1,0:T(8,128)(2,1)S(1)}, u32[]{:S(2)}, u32[]{:S(2)}) %collective-permute-start.35) | collective-permute-done | bytes 90144 | tf_op jit(solution)/shard_map/ppermute | solution.py:28
  147.1 2.9 %collective-permute-done.34.refs_2_ = bf16[88,512]{1,0:T(8,128)(2,1)S(1)} collective-permute-done((bf16[88,512]{1,0:T(8,128)(2,1)S(1)}, bf16[88,512]{1,0:T(8,128)(2,1)S(1)}, u32[]{:S(2)}, u32[]{:S(2)}) %collective-permute-start.34) | collective-permute-done | bytes 90144 | tf_op jit(solution)/shard_map/ppermute | solution.py:28
  151.3 3.7 %all-to-all-start.4 = ((bf16[4,352,512]{2,1,0:T(8,128)(2,1)}), bf16[4,352,512]{2,1,0:T(8,128)(2,1)S(1)}, u32[]{:S(2)}, u32[]{:S(2)}) async-start(bf16[4,352,512]{2,1,0:T(8,128)(2,1)} %shard_map.214), calls=%async_computation.4 | async-start | bytes 2883584 | tf_op jit(solution)/shard_map/all_to_all | solution.py:42
  155.1 2.5 %collective-permute-start.37 = (bf16[128,512]{1,0:T(8,128)(2,1)S(1)}, bf16[128,512]{1,0:T(8,128)(2,1)S(1)}, u32[]{:S(2)}, u32[]{:S(2)}) collective-permute-start(bf16[128,512]{1,0:T(8,128)(2,1)S(1)} %copy-done.12), channel_id=1, source_target_pairs={{0,16},{2,18},{4,20},{6,22},{8,24},{10,26},{12,28},{14,30},{16,0},... | collective-permute-start | bytes 393224 | tf_op jit(solution)/shard_map/ppermute | solution.py:28
  163.1 4.2 %collective-permute-done.37.refs_2_ = bf16[128,512]{1,0:T(8,128)(2,1)S(1)} collective-permute-done((bf16[128,512]{1,0:T(8,128)(2,1)S(1)}, bf16[128,512]{1,0:T(8,128)(2,1)S(1)}, u32[]{:S(2)}, u32[]{:S(2)}) %collective-permute-start.37) | collective-permute-done | bytes 131104 | tf_op jit(solution)/shard_map/ppermute | solution.py:28
  169.3 3.3 %all-to-all-done.4.refs_0_ = bf16[4,352,512]{2,1,0:T(8,128)(2,1)S(1)} async-done(((bf16[4,352,512]{2,1,0:T(8,128)(2,1)}), bf16[4,352,512]{2,1,0:T(8,128)(2,1)S(1)}, u32[]{:S(2)}, u32[]{:S(2)}) %all-to-all-start.4) | async-done | bytes 1441824 | tf_op jit(solution)/shard_map/all_to_all | solution.py:42
  (117 shorter events, 57.4 us)
Async XLA Ops:
  2.9 15.8 %collective-permute-start.4 = (bf16[264,640]{1,0:T(8,128)(2,1)S(1)}, bf16[264,640]{1,0:T(8,128)(2,1)S(1)}, u32[]{:S(2)}, u32[]{:S(2)}) collective-permute-start(bf16[264,640]{1,0:T(8,128)(2,1)S(1)} %get-tuple-element.170), channel_id=1, source_target_pairs={{0,1},{1,0},{2,3},{3,2},{4,5},{5,4},{6,7},{7,6},{8,9},{9,8},{10,11... | collective-permute-start | bytes 1013768 | tf_op jit(solution)/shard_map/ppermute | solution.py:46
  3.4 14.2 %collective-permute-start.1 = (bf16[136,512]{1,0:T(8,128)(2,1)S(1)}, bf16[136,512]{1,0:T(8,128)(2,1)S(1)}, u32[]{:S(2)}, u32[]{:S(2)}) collective-permute-start(bf16[136,512]{1,0:T(8,128)(2,1)S(1)} %get-tuple-element.172), channel_id=1, source_target_pairs={{0,16},{2,18},{4,20},{6,22},{8,24},{10,26},{12,28},{14,30},{16,0},... | collective-permute-start | bytes 417800 | tf_op jit(solution)/shard_map/ppermute | solution.py:28
  7.0 10.5 %collective-permute-start.2 = (bf16[136,512]{1,0:T(8,128)(2,1)S(1)}, bf16[136,512]{1,0:T(8,128)(2,1)S(1)}, u32[]{:S(2)}, u32[]{:S(2)}) collective-permute-start(bf16[136,512]{1,0:T(8,128)(2,1)S(1)} %get-tuple-element.173), channel_id=1, source_target_pairs={{0,24},{2,26},{4,28},{6,30},{8,16},{10,18},{12,20},{14,22},{16,8},... | collective-permute-start | bytes 417800 | tf_op jit(solution)/shard_map/ppermute | solution.py:28
  8.4 10.3 %collective-permute-start = (bf16[136,512]{1,0:T(8,128)(2,1)S(1)}, bf16[136,512]{1,0:T(8,128)(2,1)S(1)}, u32[]{:S(2)}, u32[]{:S(2)}) collective-permute-start(bf16[136,512]{1,0:T(8,128)(2,1)S(1)} %get-tuple-element.167), channel_id=1, source_target_pairs={{0,8},{2,10},{4,12},{6,14},{8,0},{10,2},{12,4},{14,6},{16,24},{18,... | collective-permute-start | bytes 417800 | tf_op jit(solution)/shard_map/ppermute | solution.py:28
  22.3 23.9 %collective-permute-start.9 = (bf16[256,2048]{1,0:T(8,128)(2,1)}, bf16[256,2048]{1,0:T(8,128)(2,1)S(1)}, u32[]{:S(2)}, u32[]{:S(2)}) collective-permute-start(bf16[256,2048]{1,0:T(8,128)(2,1)} %refs_10_.3), channel_id=1, source_target_pairs={{0,1},{1,0},{2,3},{3,2},{4,5},{5,4},{6,7},{7,6},{8,9},{9,8},{10,11... | collective-permute-start | bytes 3145736 | tf_op jit(solution)/shard_map/ppermute | solution.py:46
  22.4 23.8 %collective-permute-start.10 = (bf16[1024,512]{1,0:T(8,128)(2,1)}, bf16[1024,512]{1,0:T(8,128)(2,1)S(1)}, u32[]{:S(2)}, u32[]{:S(2)}) collective-permute-start(bf16[1024,512]{1,0:T(8,128)(2,1)} %refs_11_.3), channel_id=1, source_target_pairs={{0,1},{1,0},{2,3},{3,2},{4,5},{5,4},{6,7},{7,6},{8,9},{9,8},{10,11... | collective-permute-start | bytes 3145736 | tf_op jit(solution)/shard_map/ppermute | solution.py:46
  22.8 13.4 %all-to-all-start = ((bf16[4,512,128]{2,1,0:T(8,128)(2,1)}), bf16[4,512,128]{2,1,0:T(8,128)(2,1)S(1)}, u32[]{:S(2)}, u32[]{:S(2)}) async-start(bf16[4,512,128]{2,1,0:T(8,128)(2,1)} %copy-done), calls=%async_computation | async-start | bytes 1048576 | tf_op jit(solution)/shard_map/all_to_all | solution.py:42
  26.6 19.5 %collective-permute-start.6 = (bf16[128,512]{1,0:T(8,128)(2,1)}, bf16[128,512]{1,0:T(8,128)(2,1)}, u32[]{:S(2)}, u32[]{:S(2)}) collective-permute-start(bf16[128,512]{1,0:T(8,128)(2,1)} %copy-done.10), channel_id=1, source_target_pairs={{0,8},{2,10},{4,12},{6,14},{8,0},{10,2},{12,4},{14,6},{16,24},{18,... | collective-permute-start | bytes 393224 | tf_op jit(solution)/shard_map/ppermute | solution.py:28
  29.0 17.2 %collective-permute-start.7 = (bf16[128,512]{1,0:T(8,128)(2,1)}, bf16[128,512]{1,0:T(8,128)(2,1)}, u32[]{:S(2)}, u32[]{:S(2)}) collective-permute-start(bf16[128,512]{1,0:T(8,128)(2,1)} %copy-done.9), channel_id=1, source_target_pairs={{0,16},{2,18},{4,20},{6,22},{8,24},{10,26},{12,28},{14,30},{16,0},... | collective-permute-start | bytes 393224 | tf_op jit(solution)/shard_map/ppermute | solution.py:28
  31.6 14.5 %collective-permute-start.8 = (bf16[128,512]{1,0:T(8,128)(2,1)}, bf16[128,512]{1,0:T(8,128)(2,1)}, u32[]{:S(2)}, u32[]{:S(2)}) collective-permute-start(bf16[128,512]{1,0:T(8,128)(2,1)} %copy-done.8), channel_id=1, source_target_pairs={{0,24},{2,26},{4,28},{6,30},{8,16},{10,18},{12,20},{14,22},{16,8},... | collective-permute-start | bytes 393224 | tf_op jit(solution)/shard_map/ppermute | solution.py:28
  52.9 9.1 %collective-permute-start.11 = (bf16[1024,512]{1,0:T(8,128)(2,1)S(1)}, bf16[1024,512]{1,0:T(8,128)(2,1)S(1)}, u32[]{:S(2)}, u32[]{:S(2)}) collective-permute-start(bf16[1024,512]{1,0:T(8,128)(2,1)S(1)} %get-tuple-element.225), channel_id=1, source_target_pairs={{0,1},{1,0},{2,3},{3,2},{4,5},{5,4},{6,7},{7,6},{8,9},{9,8},{10,11... | collective-permute-start | bytes 3145736 | tf_op jit(solution)/shard_map/ppermute | solution.py:46
  53.0 9.0 %collective-permute-start.12 = (bf16[512,512]{1,0:T(8,128)(2,1)S(1)}, bf16[512,512]{1,0:T(8,128)(2,1)S(1)}, u32[]{:S(2)}, u32[]{:S(2)}) collective-permute-start(bf16[512,512]{1,0:T(8,128)(2,1)S(1)} %get-tuple-element.226), channel_id=1, source_target_pairs={{0,1},{1,0},{2,3},{3,2},{4,5},{5,4},{6,7},{7,6},{8,9},{9,8},{10,11... | collective-permute-start | bytes 1572872 | tf_op jit(solution)/shard_map/ppermute | solution.py:46
  64.8 33.4 %all-to-all-start.2 = ((bf16[4,320,512]{2,1,0:T(8,128)(2,1)}), bf16[4,320,512]{2,1,0:T(8,128)(2,1)S(1)}, u32[]{:S(2)}, u32[]{:S(2)}) async-start(bf16[4,320,512]{2,1,0:T(8,128)(2,1)} %get-tuple-element.232), calls=%async_computation.2 | async-start | bytes 2621440 | tf_op jit(solution)/shard_map/all_to_all | solution.py:42
  69.2 14.1 %collective-permute-start.13 = (bf16[128,512]{1,0:T(8,128)(2,1)}, bf16[128,512]{1,0:T(8,128)(2,1)S(1)}, u32[]{:S(2)}, u32[]{:S(2)}) collective-permute-start(bf16[128,512]{1,0:T(8,128)(2,1)} %get-tuple-element.246), channel_id=1, source_target_pairs={{0,8},{2,10},{4,12},{6,14},{8,0},{10,2},{12,4},{14,6},{16,24},{18,... | collective-permute-start | bytes 393224 | tf_op jit(solution)/shard_map/ppermute | solution.py:28
  70.0 14.7 %collective-permute-start.14 = (bf16[128,512]{1,0:T(8,128)(2,1)S(1)}, bf16[128,512]{1,0:T(8,128)(2,1)S(1)}, u32[]{:S(2)}, u32[]{:S(2)}) collective-permute-start(bf16[128,512]{1,0:T(8,128)(2,1)S(1)} %copy-done.14), channel_id=1, source_target_pairs={{0,16},{2,18},{4,20},{6,22},{8,24},{10,26},{12,28},{14,30},{16,0},... | collective-permute-start | bytes 393224 | tf_op jit(solution)/shard_map/ppermute | solution.py:28
  72.1 23.9 %collective-permute-start.19 = (bf16[512,512]{1,0:T(8,128)(2,1)}, bf16[512,512]{1,0:T(8,128)(2,1)S(1)}, u32[]{:S(2)}, u32[]{:S(2)}) collective-permute-start(bf16[512,512]{1,0:T(8,128)(2,1)} %get-tuple-element.281), channel_id=1, source_target_pairs={{0,1},{1,0},{2,3},{3,2},{4,5},{5,4},{6,7},{7,6},{8,9},{9,8},{10,11... | collective-permute-start | bytes 1572872 | tf_op jit(solution)/shard_map/ppermute | solution.py:46
  72.1 12.7 %collective-permute-start.15 = (bf16[128,512]{1,0:T(8,128)(2,1)S(1)}, bf16[128,512]{1,0:T(8,128)(2,1)S(1)}, u32[]{:S(2)}, u32[]{:S(2)}) collective-permute-start(bf16[128,512]{1,0:T(8,128)(2,1)S(1)} %copy-done.13), channel_id=1, source_target_pairs={{0,24},{2,26},{4,28},{6,30},{8,16},{10,18},{12,20},{14,22},{16,8},... | collective-permute-start | bytes 393224 | tf_op jit(solution)/shard_map/ppermute | solution.py:28
  81.2 8.7 %collective-permute-start.16 = (bf16[512,128]{1,0:T(8,128)(2,1)}, bf16[512,128]{1,0:T(8,128)(2,1)S(1)}, u32[]{:S(2)}, u32[]{:S(2)}) collective-permute-start(bf16[512,128]{1,0:T(8,128)(2,1)} %get-tuple-element.265), channel_id=1, source_target_pairs={{0,2},{2,0},{4,6},{6,4},{8,10},{10,8},{12,14},{14,12},{16,18},{18,... | collective-permute-start | bytes 393224 | tf_op jit(solution)/shard_map/ppermute | solution.py:28
  84.7 7.7 %collective-permute-start.18 = (bf16[512,128]{1,0:T(8,128)(2,1)}, bf16[512,128]{1,0:T(8,128)(2,1)S(1)}, u32[]{:S(2)}, u32[]{:S(2)}) collective-permute-start(bf16[512,128]{1,0:T(8,128)(2,1)} %get-tuple-element.267), channel_id=1, source_target_pairs={{0,6},{2,4},{4,2},{6,0},{8,14},{10,12},{12,10},{14,8},{16,22},{18,... | collective-permute-start | bytes 393224 | tf_op jit(solution)/shard_map/ppermute | solution.py:28
  98.3 22.6 %all-to-all-start.1 = ((bf16[4,192,512]{2,1,0:T(8,128)(2,1)}), bf16[4,192,512]{2,1,0:T(8,128)(2,1)S(1)}, u32[]{:S(2)}, u32[]{:S(2)}) async-start(bf16[4,192,512]{2,1,0:T(8,128)(2,1)} %shard_map.207), calls=%async_computation.1 | async-start | bytes 1572864 | tf_op jit(solution)/shard_map/all_to_all | solution.py:42
  102.1 7.9 %collective-permute-start.21 = (bf16[80,512]{1,0:T(8,128)(2,1)S(1)}, bf16[80,512]{1,0:T(8,128)(2,1)S(1)}, u32[]{:S(2)}, u32[]{:S(2)}) collective-permute-start(bf16[80,512]{1,0:T(8,128)(2,1)S(1)} %get-tuple-element.290), channel_id=1, source_target_pairs={{0,8},{2,10},{4,12},{6,14},{8,0},{10,2},{12,4},{14,6},{16,24},{18,... | collective-permute-start | bytes 245768 | tf_op jit(solution)/shard_map/ppermute | solution.py:28
  104.3 14.5 %collective-permute-start.24 = (bf16[160,512]{1,0:T(8,128)(2,1)S(1)}, bf16[160,512]{1,0:T(8,128)(2,1)S(1)}, u32[]{:S(2)}, u32[]{:S(2)}) collective-permute-start(bf16[160,512]{1,0:T(8,128)(2,1)S(1)} %get-tuple-element.294), channel_id=1, source_target_pairs={{0,2},{2,0},{4,6},{6,4},{8,10},{10,8},{12,14},{14,12},{16,18},{18,... | collective-permute-start | bytes 491528 | tf_op jit(solution)/shard_map/ppermute | solution.py:28
  108.5 12.4 %collective-permute-start.25 = (bf16[160,512]{1,0:T(8,128)(2,1)S(1)}, bf16[160,512]{1,0:T(8,128)(2,1)S(1)}, u32[]{:S(2)}, u32[]{:S(2)}) collective-permute-start(bf16[160,512]{1,0:T(8,128)(2,1)S(1)} %get-tuple-element.295), channel_id=1, source_target_pairs={{0,4},{2,6},{4,0},{6,2},{8,12},{10,14},{12,8},{14,10},{16,20},{18,... | collective-permute-start | bytes 491528 | tf_op jit(solution)/shard_map/ppermute | solution.py:28
  109.9 11.5 %collective-permute-start.26 = (bf16[160,512]{1,0:T(8,128)(2,1)S(1)}, bf16[160,512]{1,0:T(8,128)(2,1)S(1)}, u32[]{:S(2)}, u32[]{:S(2)}) collective-permute-start(bf16[160,512]{1,0:T(8,128)(2,1)S(1)} %get-tuple-element.296), channel_id=1, source_target_pairs={{0,6},{2,4},{4,2},{6,0},{8,14},{10,12},{12,10},{14,8},{16,22},{18,... | collective-permute-start | bytes 491528 | tf_op jit(solution)/shard_map/ppermute | solution.py:28
  118.4 7.5 %collective-permute-start.28 = (bf16[80,512]{1,0:T(8,128)(2,1)S(1)}, bf16[80,512]{1,0:T(8,128)(2,1)S(1)}, u32[]{:S(2)}, u32[]{:S(2)}) collective-permute-start(bf16[80,512]{1,0:T(8,128)(2,1)S(1)} %shard_map.210.refs_0_), channel_id=1, source_target_pairs={{0,16},{2,18},{4,20},{6,22},{8,24},{10,26},{12,28},{14,30},{16,0},... | collective-permute-start | bytes 245768 | tf_op jit(solution)/shard_map/ppermute | solution.py:28
  127.0 24.3 %all-to-all-start.3 = ((bf16[4,320,512]{2,1,0:T(8,128)(2,1)}), bf16[4,320,512]{2,1,0:T(8,128)(2,1)S(1)}, u32[]{:S(2)}, u32[]{:S(2)}) async-start(bf16[4,320,512]{2,1,0:T(8,128)(2,1)} %shard_map.212), calls=%async_computation.3 | async-start | bytes 2621440 | tf_op jit(solution)/shard_map/all_to_all | solution.py:42
  130.6 9.8 %collective-permute-start.31 = (bf16[88,512]{1,0:T(8,128)(2,1)S(1)}, bf16[88,512]{1,0:T(8,128)(2,1)S(1)}, u32[]{:S(2)}, u32[]{:S(2)}) collective-permute-start(bf16[88,512]{1,0:T(8,128)(2,1)S(1)} %get-tuple-element.301), channel_id=1, source_target_pairs={{0,16},{2,18},{4,20},{6,22},{8,24},{10,26},{12,28},{14,30},{16,0},... | collective-permute-start | bytes 270344 | tf_op jit(solution)/shard_map/ppermute | solution.py:28
  142.2 7.8 %collective-permute-start.34 = (bf16[88,512]{1,0:T(8,128)(2,1)S(1)}, bf16[88,512]{1,0:T(8,128)(2,1)S(1)}, u32[]{:S(2)}, u32[]{:S(2)}) collective-permute-start(bf16[88,512]{1,0:T(8,128)(2,1)S(1)} %shard_map.213.refs_0_), channel_id=1, source_target_pairs={{0,16},{2,18},{4,20},{6,22},{8,24},{10,26},{12,28},{14,30},{16,0},... | collective-permute-start | bytes 270344 | tf_op jit(solution)/shard_map/ppermute | solution.py:28
  151.3 21.3 %all-to-all-start.4 = ((bf16[4,352,512]{2,1,0:T(8,128)(2,1)}), bf16[4,352,512]{2,1,0:T(8,128)(2,1)S(1)}, u32[]{:S(2)}, u32[]{:S(2)}) async-start(bf16[4,352,512]{2,1,0:T(8,128)(2,1)} %shard_map.214), calls=%async_computation.4 | async-start | bytes 2883584 | tf_op jit(solution)/shard_map/all_to_all | solution.py:42
  155.0 8.1 %collective-permute-start.36 = (bf16[128,512]{1,0:T(8,128)(2,1)}, bf16[128,512]{1,0:T(8,128)(2,1)S(1)}, u32[]{:S(2)}, u32[]{:S(2)}) collective-permute-start(bf16[128,512]{1,0:T(8,128)(2,1)} %get-tuple-element.312), channel_id=1, source_target_pairs={{0,8},{2,10},{4,12},{6,14},{8,0},{10,2},{12,4},{14,6},{16,24},{18,... | collective-permute-start | bytes 393224 | tf_op jit(solution)/shard_map/ppermute | solution.py:28
  155.1 12.2 %collective-permute-start.37 = (bf16[128,512]{1,0:T(8,128)(2,1)S(1)}, bf16[128,512]{1,0:T(8,128)(2,1)S(1)}, u32[]{:S(2)}, u32[]{:S(2)}) collective-permute-start(bf16[128,512]{1,0:T(8,128)(2,1)S(1)} %copy-done.12), channel_id=1, source_target_pairs={{0,16},{2,18},{4,20},{6,22},{8,24},{10,26},{12,28},{14,30},{16,0},... | collective-permute-start | bytes 393224 | tf_op jit(solution)/shard_map/ppermute | solution.py:28
  157.6 9.7 %collective-permute-start.38 = (bf16[128,512]{1,0:T(8,128)(2,1)S(1)}, bf16[128,512]{1,0:T(8,128)(2,1)S(1)}, u32[]{:S(2)}, u32[]{:S(2)}) collective-permute-start(bf16[128,512]{1,0:T(8,128)(2,1)S(1)} %copy-done.11), channel_id=1, source_target_pairs={{0,24},{2,26},{4,28},{6,30},{8,16},{10,18},{12,20},{14,22},{16,8},... | collective-permute-start | bytes 393224 | tf_op jit(solution)/shard_map/ppermute | solution.py:28
  (29 other events, 133.8 us)

commit v4 on v3

--- a/solution.py
+++ b/solution.py
@@ -229,11 +229,17 @@
         out[local : local + TWO, :128] = routes[place ^ (k + 1)].astype(F32).astype(BF)
 
 
-def pack_weights_body(query, kv, router, packed):
+def pack_all_body(count, rest, *refs):
+    tok, routes, query, kv, router, out = refs[:6]
+    pieces, packed = refs[6:-1], refs[-1]
+    pack_body(count, rest, tok, routes, *pieces)
+    Order.rest()
     half, cols = query.shape
+    keys = kv.shape[1]
     packed[half:, :] = jnp.zeros((8, packed.shape[1]), BF)
     packed[:half, :cols] = query[...]
-    packed[:half, cols:] = kv[...]
+    packed[:half, cols : cols + keys] = kv[...]
+    packed[:half, cols + keys :] = out[...]
     packed[half:, :half] = router[...]
 
 
@@ -256,7 +262,8 @@
     half = k_own.shape[0]
     local = toks[0].shape[0]
     keys = k_own.shape[1]
-    fill(wk, k_own, packed.at[:half, packed.shape[1] - keys :], core)
+    cols = packed.shape[1] - keys - toks[0].shape[1]
+    fill(wk, k_own, packed.at[:half, cols : cols + keys], core)
     rows = join([t[:local] for t in toks])
     tok_out[...] = rows
     Order.leave(2, 4)
@@ -271,26 +278,30 @@
         gain_out[which : which + 1, :] = pick_gain(g_own, g_other, which, core)
     normed = (unit * gain_out[0:1, :]).astype(BF)
     normed_out[...] = normed
+    Order.leave(1, 3)
     kv = mm(normed, wk[...]).astype(BF)
     for i in range(kv_out.shape[0]):
         kv_out[i] = kv
 
 
 def project_body(count, experts, head, *refs):
-    normed_ref, tails, q_own, r_own, packed = refs[:5]
-    qt_out, qt_far, nt_out, gate_out, gate_far, route_out, route_far, wq, wr = refs[5:]
+    normed_ref, tails, q_own, r_own, o_own, packed = refs[:6]
+    qt_out, nt_out, gate_out, gate_far, route_out, route_far, wq, wr, wo = refs[6:]
     core = lax.axis_index("wsh")
     half, cols = q_own.shape
+    normed = normed_ref[...]
+    nt_out[...] = normed.T
+    Order.leave(1)
+    Order.rest()
     fill(wq, q_own, packed.at[:half, :cols], core)
     fill_router(wr, r_own, packed, core)
-    normed = normed_ref[...]
-    nt_out[...] = normed.T
-    Order.leave(2, 7, 8)
+    fill(wo, o_own, packed.at[:half, packed.shape[1] - o_own.shape[1] :], core)
+    Order.leave(6, 7, 8)
     routes = route_rows([tails[8 * k : 8 * k + 8, :] for k in range(count)])
     route_out[...] = routes
     route_far[...] = routes
     logits = mm(wr[...].astype(BF), normed, 1, 1)
-    queries = (mm(normed, wq[...]) * 0.125).T
+    queries = mm(wq[...], normed, 0, 1) * 0.125
     chosen = []
     for s in range(TWO):
         route = routes[s : s + 1]
@@ -302,7 +313,6 @@
             value = jnp.where(here, logits[e : e + 1], value)
         qt_out[s * head : (s + 1) * head, :] = total.astype(BF)
         chosen.append(value)
-    qt_far[...] = qt_out[...]
     top = jnp.maximum(chosen[0], chosen[1])
     raised = [jnp.exp(c - top) for c in chosen]
     total = raised[0] + raised[1]
@@ -357,50 +367,66 @@
         kv_turned[:, c * rows : (c + 1) * rows] = kv[c].T
 
 
+def both_slots(rows, head, cols):
+    return jnp.concatenate([rows[s * head : (s + 1) * head, cols] for s in range(TWO)], axis=1)
+
+
+def gap_rows(order, count, rest, block, half, h):
+    gap = lax.broadcasted_iota(I32, (block, half), 0) - places(order, count, rest, block, half, h)
+    return jnp.concatenate([gap] * TWO, axis=1)
+
+
 def attend_body(count, rest, experts, head, *refs):
     order, kv_ref, qt, gates, routes = refs[:5]
-    tok, gains, o_own, o_other = refs[5:9]
-    att_out, log_out, mixed_out, hidden_out, two_out, turned_out, kv_out, wo_out, kv_turned = refs[9:]
+    tok, gains, wo = refs[5:8]
+    att_out, log_out, mixed_out, hidden_out, two_out, turned_out, kv_out, kv_turned = refs[8:]
     kv_out[...] = kv_ref[...]
     Order.leave(6)
-    core = lax.axis_index("wsh")
     other = lax.axis_index("ctx") % rest
     total = qt.shape[1]
     half = total // 2
     block = half // count
     turn_keys(kv_ref, kv_turned)
+    sides, gaps = [], []
     for h in range(2):
-        gap = lax.broadcasted_iota(I32, (block, half), 0) - places(order, count, rest, block, half, h)
+        side = both_slots(qt, head, slice(h * half, (h + 1) * half))
+        sides.append(jnp.concatenate([side, jnp.zeros_like(side)], axis=0))
+        gaps.append(gap_rows(order, count, rest, block, half, h))
+
+    def step(turn, carry):
+        chunk = turn ^ other
+        at = pl.multiple_of(chunk * total, total)
+        kv = kv_ref[chunk]
+        scores = [
+            scored(kv, sides[h], h, gaps[h], order, count, rest, block, chunk, half)
+            for h in range(2)
+        ]
+        out = []
+        for h in range(2):
+            top, norm, summed = carry[h]
+            fresh = jnp.maximum(top, jnp.max(scores[h], axis=0, keepdims=True))
+            shares = jnp.exp(scores[h] - fresh)
+            fade = jnp.exp(top - fresh)
+            norm = norm * fade + jnp.sum(shares, axis=0, keepdims=True)
+            values = kv_turned[head:, pl.ds(at, half * (h + 1))]
+            out.append((fresh, norm, summed * fade + mm(values, shares.astype(BF))))
+        return tuple(out)
+
+    start = (
+        jnp.full((1, TWO * half), NONE, F32),
+        jnp.zeros((1, TWO * half), F32),
+        jnp.zeros((head, TWO * half), F32),
+    )
+    done = lax.fori_loop(0, rest, step, (start, start), unroll=rest <= 4)
+    for h in range(2):
+        top, norm, summed = done[h]
+        logs, attended = top + jnp.log(norm), summed / norm
         for s in range(TWO):
-            side = qt[s * head : (s + 1) * head, h * half : (h + 1) * half]
-            side = jnp.concatenate([side, jnp.zeros_like(side)], axis=0)
-            reach = half * (h + 1)
-
-            def step(turn, carry, side=side, h=h, gap=gap, reach=reach):
-                top, norm, summed = carry
-                chunk = turn ^ other
-                at = pl.multiple_of(chunk * total, total)
-                kv = kv_ref[chunk]
-                scores = scored(kv, side, h, gap, order, count, rest, block, chunk, half)
-                fresh = jnp.maximum(top, jnp.max(scores, axis=0, keepdims=True))
-                shares = jnp.exp(scores - fresh)
-                fade = jnp.exp(top - fresh)
-                norm = norm * fade + jnp.sum(shares, axis=0, keepdims=True)
-                values = kv_turned[head:, pl.ds(at, reach)]
-                summed = summed * fade + mm(values, shares.astype(BF))
-                return fresh, norm, summed
-
-            start = (
-                jnp.full((1, half), NONE, F32),
-                jnp.zeros((1, half), F32),
-                jnp.zeros((head, half), F32),
-            )
-            top, norm, summed = lax.fori_loop(0, rest, step, start, unroll=rest <= 4)
-            log_out[s : s + 1, h * half : (h + 1) * half] = top + jnp.log(norm)
-            att_out[s * head : (s + 1) * head, h * half : (h + 1) * half] = summed / norm
+            here, cols = slice(h * half, (h + 1) * half), slice(s * half, (s + 1) * half)
+            log_out[s : s + 1, here] = logs[:, cols]
+            att_out[s * head : (s + 1) * head, here] = attended[:, cols]
     Order.rest()
-    fill(wo_out, o_own, o_other, core)
-    Order.leave(0, 1, 7)
+    Order.leave(0, 1)
     for e in range(experts):
         part = jnp.zeros((head, total), F32)
         for s in range(TWO):
@@ -408,7 +434,7 @@
             part = part + gate * att_out[s * head : (s + 1) * head, :]
         mixed_out[e * head : (e + 1) * head, :] = part.astype(BF)
     Order.leave(2)
-    hidden = tok[...].astype(F32) + mm(mixed_out[...].T, wo_out[...])
+    hidden = tok[...].astype(F32) + mm(mixed_out[...].T, wo[...])
     hidden_out[...] = hidden
     unit, _ = centred(hidden)
     two = (unit * gains[1:2, :]).astype(BF)
@@ -517,6 +543,13 @@
     logit_out[...] = logit
 
 
+def turn_start_body(count, rest, experts, head, layout, step, *refs):
+    ins, early, outs, pieces = refs[:8], refs[8:12], refs[12:18], refs[18]
+    turn_body(count, rest, experts, head, *ins, *outs)
+    Order.rest()
+    start_body(layout, True, 1, step, len(early), *early, pieces, None)
+
+
 def attend_back_body(count, rest, head, split, *refs):
     order, kv_ref, qt, grad_att, logs, delta, grad_q_out = refs[:7]
     outs = refs[7 : 7 + split]
@@ -524,48 +557,44 @@
     total = qt.shape[1]
     half = total // 2
     block = half // count
+    wide = TWO * half
     turn_keys(kv_ref, kv_turned)
-    blank = jnp.zeros((head, total), BF)
-    for s in range(TWO):
-        q_side = jnp.concatenate([qt[s * head : (s + 1) * head, :], blank], axis=0)
-        g_side = jnp.concatenate([blank, grad_att[s * head : (s + 1) * head, :]], axis=0)
-        sides[2 * s], sides[2 * s + 1] = q_side, g_side
-        turned[2 * s], turned[2 * s + 1] = q_side.T, g_side.T
+    blank = jnp.zeros((head, wide), BF)
+    for h in range(2):
+        cols = slice(h * half, (h + 1) * half)
+        q_side = jnp.concatenate([both_slots(qt, head, cols), blank], axis=0)
+        g_side = jnp.concatenate([blank, both_slots(grad_att, head, cols)], axis=0)
+        sides[2 * h], sides[2 * h + 1] = q_side, g_side
+        turned[h, :wide, :], turned[h, wide:, :] = q_side.T, g_side.T
     grad_q[...] = jnp.zeros_like(grad_q)
-    gaps = [
-        lax.broadcasted_iota(I32, (block, half), 0) - places(order, count, rest, block, half, h)
-        for h in range(2)
-    ]
+    gaps = [gap_rows(order, count, rest, block, half, h) for h in range(2)]
+    log_rows = [both_slots(logs, 1, slice(h * half, (h + 1) * half)) for h in range(2)]
+    delta_rows = [both_slots(delta, 1, slice(h * half, (h + 1) * half)) for h in range(2)]
 
     def step(chunk, carry):
         at = pl.multiple_of(chunk * total, total)
         kv = kv_ref[chunk]
-        front = jnp.zeros((half, 2 * head), F32)
-        back = jnp.zeros((half, 2 * head), F32)
+        grads = []
         for h in range(2):
-            cols = slice(h * half, (h + 1) * half)
             reach = half * (h + 1)
-            for s in range(TWO):
-                scores = scored(
-                    kv, sides[2 * s, :, cols], h, gaps[h], order, count, rest, block, chunk, half
-                )
-                shares = jnp.exp(scores - logs[s : s + 1, cols])
-                back_shares = mm(kv[:reach], sides[2 * s + 1, :, cols])
-                back_scores = (shares * (back_shares - delta[s : s + 1, cols])).astype(BF)
-                grad = mm(back_scores, turned[2 * s, cols, :]) + mm(
-                    shares.astype(BF), turned[2 * s + 1, cols, :]
-                )
-                front = front + grad[:half]
-                if h == 1:
-                    back = back + grad[half:]
-                rows = slice(s * head, (s + 1) * head)
-                grad_q[rows, cols] += mm(kv_turned[:head, pl.ds(at, reach)], back_scores)
-        grad_kv[pl.ds(at, half), :] = front
-        grad_kv[pl.ds(at + half, half), :] = back
+            scores = scored(
+                kv, sides[2 * h], h, gaps[h], order, count, rest, block, chunk, half
+            )
+            shares = jnp.exp(scores - log_rows[h])
+            back_shares = mm(kv[:reach], sides[2 * h + 1])
+            back_scores = (shares * (back_shares - delta_rows[h])).astype(BF)
+            both = jnp.concatenate([back_scores, shares.astype(BF)], axis=1)
+            grads.append(mm(both, turned[h]))
+            grad_q[h] += mm(kv_turned[:head, pl.ds(at, reach)], back_scores)
+        grad_kv[pl.ds(at, half), :] = grads[0] + grads[1][:half]
+        grad_kv[pl.ds(at + half, half), :] = grads[1][half:]
         return carry
 
-    lax.fori_loop(0, rest, step, 0)
-    grad_q_out[...] = grad_q[...].astype(BF)
+    lax.fori_loop(0, rest, step, 0, unroll=rest <= 4)
+    for h in range(2):
+        for s in range(TWO):
+            here, cols = slice(h * half, (h + 1) * half), slice(s * half, (s + 1) * half)
+            grad_q_out[s * head : (s + 1) * head, here] = grad_q[h, :, cols].astype(BF)
     rows = outs[0].shape[0]
     digit = (lax.axis_index("ctx") % rest) // (rest // split)
     for i, out in enumerate(outs):
@@ -637,6 +666,7 @@
     step = half // 4
     experts = routers.shape[0]
     high = sent.shape[0]
+    Order.rest()
     send[:high, :] = sent[...]
     for out, which in ((keep, core), (send.at[high:, :], 1 - core)):
         mine = pl.ds(pl.multiple_of(which * half, half), half)
@@ -683,12 +713,27 @@
 
 def start_body(layout, whole, stride, step, n_in, *refs):
     ins, outs, total = refs[:n_in], refs[n_in:-1], refs[-1]
-    sum_layout(layout, ins, total)
     if whole:
-        rows = total.shape[0] // step
-        for j in range(step):
-            outs[0][j] = total[j * rows : (j + 1) * rows, :].astype(BF)
+        rows = outs[0].shape[1]
+        at = 0
+        for terms in layout:
+            height, done = terms[0][2], 0
+            while done < height:
+                j, low = (at + done) // rows, (at + done) % rows
+                take = min(height - done, rows - low)
+                value = None
+                for index, begin, _ in terms:
+                    part = ins[index][begin + done : begin + done + take, :].astype(F32)
+                    value = part if value is None else value + part
+                outs[0][j, low : low + take, :] = value.astype(BF)
+                done += take
+            at += height
+        while at < rows * step:
+            j, low = at // rows, at % rows
+            outs[0][j, low:, :] = jnp.zeros((rows - low, outs[0].shape[2]), BF)
+            at += rows - low
     else:
+        sum_layout(layout, ins, total)
         cut_rows(total, outs, stride, step)
 
 
@@ -746,6 +791,7 @@
                 total[pl.ds(begin, rows), :] = piece.astype(F32)
         at += height
         dest(total, outs[used : used + many])
+        Order.leave(*range(used, used + many))
         used += many
 
 
@@ -867,40 +913,36 @@
     def here():
         return lax.axis_index("ctx") // rest
 
-    tok_pieces = call(
-        functools.partial(pack_body, count, rest),
-        [((local + 8, dim), BF)] * (count - 1),
-        far([tokens, routes_t]),
-    )
+    got = call(
+        functools.partial(pack_all_body, count, rest),
+        [((local + 8, dim), BF)] * (count - 1) + [((tall + 8, experts * head + keys + dim), BF)],
+        far([tokens, routes_t, query_w, kv_w, router_t, out_w]),
+        late=(2, 3, 4, 5),
+        ahead=[Ahead(tokens, (local, dim), lambda r: r.at[here()]), Ahead(kv_w)]
+        + [
+            Ahead(cotangent, (local, dim), lambda r, k=k: r.at[here() ^ k])
+            for k in range(1, count)
+        ],
+    )
+    tok_pieces, (packed, tok_own, kv_own), cot_pieces = got[: count - 1], got[count - 1 : count + 2], got[count + 2 :]
     tok_x = [swap(tok_pieces[k - 1], k * rest, size) for k in range(1, count)]
-    packed, tok_own, kv_own = call(
-        pack_weights_body,
-        [((tall + 8, experts * head + keys), BF)],
-        far([query_w, kv_w, router_t]),
-        ahead=[Ahead(tokens, (local, dim), lambda r: r.at[here()]), Ahead(kv_w)],
-    )
     packed_x = trade(packed)
     gain_one, gain_two = after((norm_gain1, norm_gain2), packed)
     gains = jnp.stack([gain_one, gain_two])
     gains_x = trade(gains)
 
     steps = factors(rest)
-    kv, normed, tok, gain_rows, wk, tails, query_own, router_own, *cot_pieces = call(
+    kv, normed, tok, gain_rows, wk, tails = call(
         functools.partial(keys_body, count, rest),
         [
-            ((steps[0], total, keys), BF),
-            ((total, dim), BF),
+            ((steps[0], total, keys), BF, 1),
+            ((total, dim), BF, 1),
             ((total, dim), BF, 1),
             ((8, dim), F32, 1),
             ((dim, keys), BF, 1),
             ((8 * count, 128), F32),
         ],
         [tok_own, *tok_x, Far(routes_t), gains, gains_x, kv_own, packed_x],
-        ahead=[Ahead(query_w), Ahead(router_t)]
-        + [
-            Ahead(cotangent, (local, dim), lambda r, k=k: r.at[here() ^ k])
-            for k in range(1, count)
-        ],
     )
     stride = 1
     for i, step in enumerate(steps):
@@ -908,11 +950,11 @@
             kv = jnp.broadcast_to(kv[None], (step,) + kv.shape)
         kv = exchange(kv, stride, size).reshape(-1, total, keys)
         stride *= step
+    cot_pieces = after(tuple(cot_pieces), normed)
     cot_x = [swap(cot_pieces[k - 1], k * rest, size) for k in range(1, count)]
-    qt, qt_far, normed_t, gates, gates_far, route, route_far, wq, wr = call(
+    qt, normed_t, gates, gates_far, route, route_far, wq, wr, wo = call(
         functools.partial(project_body, count, experts, head),
         [
-            ((TWO * head, total), BF),
             ((TWO * head, total), BF, 1),
             ((dim, total), BF, 1),
             ((TWO, total), F32),
@@ -921,11 +963,13 @@
             ((8, total), F32, 1),
             ((dim, experts * head), BF, 1),
             ((128, dim), F32, 1),
+            ((experts * head, dim), BF, 1),
         ],
-        [normed, tails, query_own, router_own, packed_x],
-    )
-    up_w2, down_w2, out_w2, _ = lax.optimization_barrier((up_w, down_w, out_w, normed))
-    out_x, up_x, down_x = trade(out_w2), trade(up_w2), trade(down_w2)
+        [Far(normed), tails, *far([query_w, router_t, out_w]), packed_x],
+        late=(2, 3, 4),
+    )
+    up_w2, down_w2, _ = lax.optimization_barrier((up_w, down_w, normed))
+    up_x, down_x = trade(up_w2), trade(down_w2)
     span = rest * total
     wide = feed // 2
 
@@ -936,7 +980,7 @@
 
         return view
 
-    att, logs, mixed, hidden, two, two_t, kv_far, wo, cot_own, up_first = call(
+    att, logs, mixed, hidden, two, two_t, kv_far, cot_own, up_first = call(
         functools.partial(attend_body, count, rest, experts, head),
         [
             ((TWO * head, total), F32, 1),
@@ -946,9 +990,8 @@
             ((total, dim), BF),
             ((dim, total), BF),
             ((rest, total, keys), BF, 1),
-            ((experts * head, dim), BF, 1),
         ],
-        [block_order, kv, qt, gates, route, *far([tok, gain_rows, out_w]), out_x],
+        [block_order, kv, Far(qt), gates, route, *far([tok, gain_rows, wo])],
         scratch=[((keys, span), BF)],
         smem=(0,),
         late=(5, 6, 7),
@@ -1014,7 +1057,7 @@
             functools.partial(start_body, layout, True, 1, first, len(args)),
             [((first, height // first, WIDTH), BF)],
             args,
-            scratch=[((height, WIDTH), F32)],
+            scratch=[((8, WIDTH), F32)],
             ahead=ahead,
         )
         return exchange(pieces, 1, size), near
@@ -1042,24 +1085,43 @@
         )
         return exchange(copies, 1, size), near
 
-    back_hidden, branch, grad_att, delta, logit, gain_two = call(
-        functools.partial(turn_body, count, rest, experts, head),
+    back_hidden, branch, grad_att, delta, logit, gain_two, early, kv_near, qt_near, logs_near = call(
+        functools.partial(
+            turn_start_body,
+            count,
+            rest,
+            experts,
+            head,
+            [[(0, 0, wide), (1, 0, wide)], [(2, 0, tall), (3, 0, tall)]],
+            first,
+        ),
         [
             ((total, dim), F32, 1),
             ((total, dim), BF, 1),
-            ((TWO * head, total), BF, 1),
-            ((TWO, total), F32, 1),
+            ((TWO * head, total), BF),
+            ((TWO, total), F32),
             ((experts, total), F32, 1),
             ((8, dim), F32, 1),
+            ((first, early_rows // first, WIDTH), BF),
         ],
-        [hidden, back_two, cots, wo, gain_near, gates, route, att],
-    )
-    early, (kv_near, qt_near, logs_near, grad_att, delta) = bulk(
-        [Far(keep_down), recv_down, Far(keep_two), recv_up],
-        [[(0, 0, wide), (1, 0, wide)], [(2, 0, tall), (3, 0, tall)]],
-        early_rows,
-        [Ahead(a) for a in (kv_far, qt_far, logs, grad_att, delta)],
-    )
+        [
+            hidden,
+            back_two,
+            cots,
+            wo,
+            gain_near,
+            gates,
+            route,
+            att,
+            Far(keep_down),
+            recv_down,
+            Far(keep_two),
+            recv_up,
+        ],
+        late=(8, 10),
+        ahead=[Ahead(a) for a in (kv_far, qt, logs)],
+    )
+    early = exchange(early, 1, size)
     split = steps[-1]
     share = span // split
     grad_q, *kv_terms = call(
@@ -1068,10 +1130,10 @@
         [block_order, kv_near, qt_near, grad_att, logs_near, delta],
         scratch=[
             ((keys, span), BF),
-            ((2 * TWO, keys, total), BF),
-            ((2 * TWO, total, keys), BF),
+            ((4, keys, total), BF),
+            ((2, 2 * total, keys), BF),
             ((span, keys), F32),
-            ((TWO * head, total), F32),
+            ((2, head, total), F32),
         ],
         smem=(0,),
         ahead=[Ahead(a) for a in (normed_t, route_far, mixed, branch, wq, wr, logit, tok)],
@@ -1105,17 +1167,19 @@
         ahead=[Ahead(a) for a in (normed_t, back_hidden, wk, gain_rows, gain_two, terms[0])],
     )
     *near, term = near
-    *input_pieces, keep_late, send_late = call(
+    *input_pieces, keep_late, send_late, keep_two, keep_one = call(
         functools.partial(unproject_body, count, len(terms)),
         [((local, dim), F32, 1)]
         + [((local, dim), BF, 1)] * (count - 1)
         + [((small, dim), F32, 1), ((small + 2 * tall, dim), BF)],
         [term, *terms[1:], back_part, unit_rows, scale_rows, routers, *near, Far(send_main)],
         scratch=[((8, dim), F32)],
+        late=(len(terms) + 9,),
+        ahead=[Ahead(a) for a in (keep_two, keep_one)],
     )
     recv_late = trade(send_late)
     main, _ = bulk(
-        [*far([keep_two]), recv_up, *far([keep_one]), recv_two],
+        [keep_two, recv_up, keep_one, recv_two],
         [
             [(0, tall, upper - tall), (1, tall, upper - tall)],
             [(2, 0, upper), (3, 0, upper)],

time: 176 us -> 168 us (0.955)
  local copies, waits for them, and re-layouts: 5.8 us -> 0.17 us
  Pallas kernels: 60.8 us -> 56.2 us
  starting transfers between devices: 65.4 us -> 69.7 us
    unnamed x34 -> x18, local copies, waits for them, and re-layouts: 5.79 us -> 0.16 us
    pallas_call x24 -> x22, Pallas kernels: 60.8 us -> 56.2 us  [call(): got = list(run(*args, *moved))]
    ppermute x30, starting transfers between devices: 44.8 us -> 48.8 us  [swap(): return lax.ppermute(values, 'ctx', [(i, i ^ mask) for i in range(size)])]
  transfers between devices with their start and end apart: 44 -> 43, of which waited for: 16 -> 15; matrix products, arithmetic and copies ran while one was open for 0% -> 0% of each run, Pallas kernels for 25% -> 23%
where the time goes in v4:
time: 168 us; the launch traced here: 167 us
  starting transfers between devices  69.7 us (41%)
  Pallas kernels  56.2 us (33%)
  waiting for transfers between devices  40.1 us (24%)
    pallas_call x22, Pallas kernels, call(): got = list(run(*args, *moved))  56.2 us
    ppermute x30, starting transfers between devices, swap(): return lax.ppermute(values, 'ctx', [(i, i ^ mask) for i in range(size)])  48.8 us
    ppermute x30, waiting for transfers between devices, swap(): return lax.ppermute(values, 'ctx', [(i, i ^ mask) for i in range(size)])  36.8 us
    all_to_all x5, starting transfers between devices, exchange(): lax.all_to_all(parts, 'ctx', 0, 0, tiled=True, axis_index_groups=groups)  19 us
  transfers between devices with their start and end apart: 43, of which 15 were waited for; matrix products, arithmetic and copies ran while one was open for 0% of the time, Pallas kernels for 23%

profile of v4, /device:TPU:0, one launch (start us, length us, event | category | flops | bytes accessed | tf_op | source)
XLA Modules:
  0.0 167.5 jit_solution(6999168071009189277)
XLA Ops:
  0.7 2.2 %shard_map.195 = (bf16[136,512]{1,0:T(8,128)(2,1)S(1)}, bf16[136,512]{1,0:T(8,128)(2,1)S(1)}, bf16[136,512]{1,0:T(8,128)(2,1)S(1)}, bf16[264,1152]{1,0:T(8,128)(...) custom-call(bf16[4,128,512]{2,1,0:T(8,128)(2,1)} %refs_6_.1, ...), custom_call_target="tpu_custom_call" | custom-call | flops 1 | bytes 1 | tf_op jit(solution)/shard_map/pallas_call | solution.py:171
  3.5 4.0 %collective-permute-start.1 = (bf16[136,512]{1,0:T(8,128)(2,1)S(1)}, bf16[136,512]{1,0:T(8,128)(2,1)S(1)}, u32[]{:S(2)}, u32[]{:S(2)}) collective-permute-start(bf16[136,512]{1,0:T(8,128)(2,1)S(1)} %get-tuple-element.167), channel_id=1, source_target_pairs={{0,16},{2,18},{4,20},{6,22},{8,24},{10,26},{12,28},{14,30},{16,0},... | collective-permute-start | bytes 417800 | tf_op jit(solution)/shard_map/ppermute | solution.py:28
  10.4 7.7 %collective-permute-done.1.refs_2_ = bf16[136,512]{1,0:T(8,128)(2,1)S(1)} collective-permute-done((bf16[136,512]{1,0:T(8,128)(2,1)S(1)}, bf16[136,512]{1,0:T(8,128)(2,1)S(1)}, u32[]{:S(2)}, u32[]{:S(2)}) %collective-permute-start.1) | collective-permute-done | bytes 139296 | tf_op jit(solution)/shard_map/ppermute | solution.py:28
  18.7 2.4 %shard_map.196 = (bf16[4,512,128]{2,1,0:T(8,128)(2,1)}, bf16[512,512]{1,0:T(8,128)(2,1)}, bf16[512,512]{1,0:T(8,128)(2,1)}, f32[8,512]{1,0:T(8,128)}, bf16[512,128]{1,0:T(8,128)(2,1)}, /*index=5*/f32[32,128]{1,0:T(8,128)S(1)}) custom-call(bf16[128,512]{1,0:T(8,128)(2,1)S(1)} %get-tuple-element.166.refs_0_, ...), custom_call_target="tpu_custom_call" | custom-call | flops 1 | bytes 1 | tf_op jit(solution)/shard_map/pallas_call | solution.py:171
  21.6 3.8 %all-to-all-start = ((bf16[4,512,128]{2,1,0:T(8,128)(2,1)}), bf16[4,512,128]{2,1,0:T(8,128)(2,1)S(1)}, u32[]{:S(2)}, u32[]{:S(2)}) async-start(bf16[4,512,128]{2,1,0:T(8,128)(2,1)} %get-tuple-element.174), calls=%async_computation | async-start | bytes 1048576 | tf_op jit(solution)/shard_map/all_to_all | solution.py:42
  25.4 2.3 %collective-permute-start.5 = (bf16[128,512]{1,0:T(8,128)(2,1)}, bf16[128,512]{1,0:T(8,128)(2,1)S(1)}, u32[]{:S(2)}, u32[]{:S(2)}) collective-permute-start(bf16[128,512]{1,0:T(8,128)(2,1)} %get-tuple-element.192), channel_id=1, source_target_pairs={{0,8},{2,10},{4,12},{6,14},{8,0},{10,2},{12,4},{14,6},{16,24},{18,... | collective-permute-start | bytes 393224 | tf_op jit(solution)/shard_map/ppermute | solution.py:28
  31.1 2.8 %shard_map.197 = (bf16[128,512]{1,0:T(8,128)(2,1)}, bf16[512,512]{1,0:T(8,128)(2,1)}, f32[2,512]{1,0:T(2,128)S(1)}, f32[2,512]{1,0:T(2,128)}, f32[8,512]{1,0:T(8...) custom-call(bf16[512,512]{1,0:T(8,128)(2,1)} %get-tuple-element.175.refs, ...), custom_call_target="tpu_custom_call" | custom-call | flops 1 | bytes 1 | tf_op jit(solution)/shard_map/pallas_call | solution.py:171
  34.0 5.7 %shard_map.198 = (f32[128,512]{1,0:T(8,128)}, f32[2,512]{1,0:T(2,128)}, bf16[512,512]{1,0:T(8,128)(2,1)}, f32[512,512]{1,0:T(8,128)S(1)}, bf16[512,512]{1,0:T(8,...) custom-call(s32[16]{0:T(128)S(1)} %copy-done, ...), custom_call_target="tpu_custom_call" | custom-call | flops 1 | bytes 1 | tf_op jit(solution)/shard_map/pallas_call | solution.py:171
  40.5 6.6 %shard_map.199 = (f32[512,512]{1,0:T(8,128)S(1)}, f32[512,512]{1,0:T(8,128)S(1)}, bf16[1024,512]{1,0:T(8,128)(2,1)S(1)}, bf16[512,512]{1,0:T(8,128)(2,1)}, bf16[...) custom-call(bf16[512,512]{1,0:T(8,128)(2,1)S(1)} %get-tuple-element., ...), custom_call_target="tpu_custom_call" | custom-call | flops 1 | bytes 1 | tf_op jit(solution)/shard_map/pallas_call | solution.py:171
  47.7 6.5 %shard_map.200 = (f32[128,512]{1,0:T(8,128)}, bf16[128,512]{1,0:T(8,128)(2,1)}, bf16[128,512]{1,0:T(8,128)(2,1)}, bf16[128,512]{1,0:T(8,128)(2,1)}, f32[512,512]...) custom-call(bf16[512,512]{1,0:T(8,128)(2,1)S(1)} %get-tuple-element., ...), custom_call_target="tpu_custom_call" | custom-call | flops 1 | bytes 1 | tf_op jit(solution)/shard_map/pallas_call | solution.py:171
  54.2 3.7 %shard_map.201 = (f32[512,512]{1,0:T(8,128)}, bf16[512,512]{1,0:T(8,128)(2,1)}, bf16[128,512]{1,0:T(8,128)(2,1)S(1)}, f32[2,512]{1,0:T(2,128)S(1)}, f32[8,512]{1...) custom-call(f32[512,512]{1,0:T(8,128)S(1)} %get-tuple-element.209.re, ...), custom_call_target="tpu_custom_call" | custom-call | flops 1 | bytes 1 | tf_op jit(solution)/shard_map/pallas_call | solution.py:171
  57.9 4.4 %all-to-all-start.2 = ((bf16[4,320,512]{2,1,0:T(8,128)(2,1)}), bf16[4,320,512]{2,1,0:T(8,128)(2,1)S(1)}, u32[]{:S(2)}, u32[]{:S(2)}) async-start(bf16[4,320,512]{2,1,0:T(8,128)(2,1)} %get-tuple-element.275), calls=%async_computation.2 | async-start | bytes 2621440 | tf_op jit(solution)/shard_map/all_to_all | solution.py:42
  62.3 2.5 %collective-permute-start.12 = (bf16[128,512]{1,0:T(8,128)(2,1)}, bf16[128,512]{1,0:T(8,128)(2,1)S(1)}, u32[]{:S(2)}, u32[]{:S(2)}) collective-permute-start(bf16[128,512]{1,0:T(8,128)(2,1)} %get-tuple-element.237), channel_id=1, source_target_pairs={{0,8},{2,10},{4,12},{6,14},{8,0},{10,2},{12,4},{14,6},{16,24},{18,... | collective-permute-start | bytes 393224 | tf_op jit(solution)/shard_map/ppermute | solution.py:28
  67.7 6.5 %shard_map.202 = (bf16[128,512]{1,0:T(8,128)(2,1)S(1)}, f32[512,128]{1,0:T(8,128)}, bf16[512,128]{1,0:T(8,128)(2,1)}, bf16[512,128]{1,0:T(8,128)(2,1)}, bf16[512...) custom-call(s32[16]{0:T(128)S(1)} %copy-done, ...), custom_call_target="tpu_custom_call" | custom-call | flops 1 | bytes 1 | tf_op jit(solution)/shard_map/pallas_call | solution.py:171
  79.5 3.6 %shard_map.203 = (bf16[256,512]{1,0:T(8,128)(2,1)}, bf16[256,512]{1,0:T(8,128)(2,1)}, bf16[512,512]{1,0:T(8,128)(2,1)}, f32[512,512]{1,0:T(8,128)S(1)}, f32[512,...) custom-call(bf16[128,512]{1,0:T(8,128)(2,1)S(1)} %get-tuple-element., ...), custom_call_target="tpu_custom_call" | custom-call | flops 1 | bytes 1 | tf_op jit(solution)/shard_map/pallas_call | solution.py:171
  83.1 2.4 %collective-permute-done.17.refs_3_ = bf16[512,128]{1,0:T(8,128)(2,1)S(1)} collective-permute-done((bf16[512,128]{1,0:T(8,128)(2,1)}, bf16[512,128]{1,0:T(8,128)(2,1)S(1)}, u32[]{:S(2)}, u32[]{:S(2)}) %collective-permute-start.17) | collective-permute-done | bytes 131104 | tf_op jit(solution)/shard_map/ppermute | solution.py:28
  85.5 3.1 %shard_map.204 = (f32[128,512]{1,0:T(8,128)}, bf16[128,512]{1,0:T(8,128)(2,1)}, bf16[128,512]{1,0:T(8,128)(2,1)}, bf16[128,512]{1,0:T(8,128)(2,1)}, f32[80,512]{...) custom-call(f32[512,128]{1,0:T(8,128)S(1)} %get-tuple-element.255.refs_0_, ...), custom_call_target="tpu_custom_call" | custom-call | flops 1 | bytes 1 | tf_op jit(solution)/shard_map/pallas_call | solution.py:171
  89.8 3.5 %all-to-all-start.1 = ((bf16[4,192,512]{2,1,0:T(8,128)(2,1)}), bf16[4,192,512]{2,1,0:T(8,128)(2,1)S(1)}, u32[]{:S(2)}, u32[]{:S(2)}) async-start(bf16[4,192,512]{2,1,0:T(8,128)(2,1)} %shard_map.205), calls=%async_computation.1 | async-start | bytes 1572864 | tf_op jit(solution)/shard_map/all_to_all | solution.py:42
  93.6 2.5 %collective-permute-start.20 = (bf16[80,512]{1,0:T(8,128)(2,1)S(1)}, bf16[80,512]{1,0:T(8,128)(2,1)S(1)}, u32[]{:S(2)}, u32[]{:S(2)}) collective-permute-start(bf16[80,512]{1,0:T(8,128)(2,1)S(1)} %get-tuple-element.284), channel_id=1, source_target_pairs={{0,8},{2,10},{4,12},{6,14},{8,0},{10,2},{12,4},{14,6},{16,24},{18,... | collective-permute-start | bytes 245768 | tf_op jit(solution)/shard_map/ppermute | solution.py:28
  104.1 3.5 %collective-permute-done.21.refs_2_ = bf16[80,512]{1,0:T(8,128)(2,1)S(1)} collective-permute-done((bf16[80,512]{1,0:T(8,128)(2,1)S(1)}, bf16[80,512]{1,0:T(8,128)(2,1)S(1)}, u32[]{:S(2)}, u32[]{:S(2)}) %collective-permute-start.21) | collective-permute-done | bytes 81952 | tf_op jit(solution)/shard_map/ppermute | solution.py:28
  113.7 2.3 %collective-permute-done.28.refs_3_ = bf16[80,512]{1,0:T(8,128)(2,1)S(1)} collective-permute-done((bf16[80,512]{1,0:T(8,128)(2,1)S(1)}, bf16[80,512]{1,0:T(8,128)(2,1)S(1)}, u32[]{:S(2)}, u32[]{:S(2)}) %collective-permute-start.28) | collective-permute-done | bytes 81952 | tf_op jit(solution)/shard_map/ppermute | solution.py:28
  116.0 2.7 %collective-permute-done.27.refs_2_ = bf16[80,512]{1,0:T(8,128)(2,1)S(1)} collective-permute-done((bf16[80,512]{1,0:T(8,128)(2,1)S(1)}, bf16[80,512]{1,0:T(8,128)(2,1)S(1)}, u32[]{:S(2)}, u32[]{:S(2)}) %collective-permute-start.27) | collective-permute-done | bytes 81952 | tf_op jit(solution)/shard_map/ppermute | solution.py:28
  119.8 3.6 %all-to-all-start.3 = ((bf16[4,320,512]{2,1,0:T(8,128)(2,1)}), bf16[4,320,512]{2,1,0:T(8,128)(2,1)S(1)}, u32[]{:S(2)}, u32[]{:S(2)}) async-start(bf16[4,320,512]{2,1,0:T(8,128)(2,1)} %shard_map.210), calls=%async_computation.3 | async-start | bytes 2621440 | tf_op jit(solution)/shard_map/all_to_all | solution.py:42
  124.0 3.4 %collective-permute-start.30 = (bf16[88,512]{1,0:T(8,128)(2,1)S(1)}, bf16[88,512]{1,0:T(8,128)(2,1)S(1)}, u32[]{:S(2)}, u32[]{:S(2)}) collective-permute-start(bf16[88,512]{1,0:T(8,128)(2,1)S(1)} %get-tuple-element.295), channel_id=1, source_target_pairs={{0,16},{2,18},{4,20},{6,22},{8,24},{10,26},{12,28},{14,30},{16,0},... | collective-permute-start | bytes 270344 | tf_op jit(solution)/shard_map/ppermute | solution.py:28
  128.0 6.6 %collective-permute-done.30.refs_2_ = bf16[88,512]{1,0:T(8,128)(2,1)S(1)} collective-permute-done((bf16[88,512]{1,0:T(8,128)(2,1)S(1)}, bf16[88,512]{1,0:T(8,128)(2,1)S(1)}, u32[]{:S(2)}, u32[]{:S(2)}) %collective-permute-start.30) | collective-permute-done | bytes 90144 | tf_op jit(solution)/shard_map/ppermute | solution.py:28
  134.6 2.6 %collective-permute-start.34 = (bf16[88,512]{1,0:T(8,128)(2,1)S(1)}, bf16[88,512]{1,0:T(8,128)(2,1)S(1)}, u32[]{:S(2)}, u32[]{:S(2)}) collective-permute-start(bf16[88,512]{1,0:T(8,128)(2,1)S(1)} %shard_map.211.refs_0_), channel_id=1, source_target_pairs={{0,24},{2,26},{4,28},{6,30},{8,16},{10,18},{12,20},{14,22},{16,8},... | collective-permute-start | bytes 270344 | tf_op jit(solution)/shard_map/ppermute | solution.py:28
  139.1 2.9 %collective-permute-done.34.refs_3_ = bf16[88,512]{1,0:T(8,128)(2,1)S(1)} collective-permute-done((bf16[88,512]{1,0:T(8,128)(2,1)S(1)}, bf16[88,512]{1,0:T(8,128)(2,1)S(1)}, u32[]{:S(2)}, u32[]{:S(2)}) %collective-permute-start.34) | collective-permute-done | bytes 90144 | tf_op jit(solution)/shard_map/ppermute | solution.py:28
  142.0 2.7 %collective-permute-done.33.refs_2_ = bf16[88,512]{1,0:T(8,128)(2,1)S(1)} collective-permute-done((bf16[88,512]{1,0:T(8,128)(2,1)S(1)}, bf16[88,512]{1,0:T(8,128)(2,1)S(1)}, u32[]{:S(2)}, u32[]{:S(2)}) %collective-permute-start.33) | collective-permute-done | bytes 90144 | tf_op jit(solution)/shard_map/ppermute | solution.py:28
  145.9 3.9 %all-to-all-start.4 = ((bf16[4,352,512]{2,1,0:T(8,128)(2,1)}), bf16[4,352,512]{2,1,0:T(8,128)(2,1)S(1)}, u32[]{:S(2)}, u32[]{:S(2)}) async-start(bf16[4,352,512]{2,1,0:T(8,128)(2,1)} %shard_map.212), calls=%async_computation.4 | async-start | bytes 2883584 | tf_op jit(solution)/shard_map/all_to_all | solution.py:42
  149.8 2.5 %collective-permute-start.36 = (bf16[128,512]{1,0:T(8,128)(2,1)S(1)}, bf16[128,512]{1,0:T(8,128)(2,1)S(1)}, u32[]{:S(2)}, u32[]{:S(2)}) collective-permute-start(bf16[128,512]{1,0:T(8,128)(2,1)S(1)} %copy-done.4), channel_id=1, source_target_pairs={{0,16},{2,18},{4,20},{6,22},{8,24},{10,26},{12,28},{14,30},{16,0},... | collective-permute-start | bytes 393224 | tf_op jit(solution)/shard_map/ppermute | solution.py:28
  157.8 3.2 %collective-permute-done.36.refs_2_ = bf16[128,512]{1,0:T(8,128)(2,1)S(1)} collective-permute-done((bf16[128,512]{1,0:T(8,128)(2,1)S(1)}, bf16[128,512]{1,0:T(8,128)(2,1)S(1)}, u32[]{:S(2)}, u32[]{:S(2)}) %collective-permute-start.36) | collective-permute-done | bytes 131104 | tf_op jit(solution)/shard_map/ppermute | solution.py:28
  163.1 2.2 %all-to-all-done.4.refs_0_ = bf16[4,352,512]{2,1,0:T(8,128)(2,1)S(1)} async-done(((bf16[4,352,512]{2,1,0:T(8,128)(2,1)}), bf16[4,352,512]{2,1,0:T(8,128)(2,1)S(1)}, u32[]{:S(2)}, u32[]{:S(2)}) %all-to-all-start.4) | async-done | bytes 1441824 | tf_op jit(solution)/shard_map/all_to_all | solution.py:42
  (97 shorter events, 48.2 us)
Async XLA Ops:
  2.9 15.8 %collective-permute-start.4 = (bf16[264,1152]{1,0:T(8,128)(2,1)S(1)}, bf16[264,1152]{1,0:T(8,128)(2,1)S(1)}, u32[]{:S(2)}, u32[]{:S(2)}) collective-permute-start(bf16[264,1152]{1,0:T(8,128)(2,1)S(1)} %get-tuple-element.169), channel_id=1, source_target_pairs={{0,1},{1,0},{2,3},{3,2},{4,5},{5,4},{6,7},{7,6},{8,9},{9,8},{10,11... | collective-permute-start | bytes 1824776 | tf_op jit(solution)/shard_map/ppermute | solution.py:46
  3.5 14.5 %collective-permute-start.1 = (bf16[136,512]{1,0:T(8,128)(2,1)S(1)}, bf16[136,512]{1,0:T(8,128)(2,1)S(1)}, u32[]{:S(2)}, u32[]{:S(2)}) collective-permute-start(bf16[136,512]{1,0:T(8,128)(2,1)S(1)} %get-tuple-element.167), channel_id=1, source_target_pairs={{0,16},{2,18},{4,20},{6,22},{8,24},{10,26},{12,28},{14,30},{16,0},... | collective-permute-start | bytes 417800 | tf_op jit(solution)/shard_map/ppermute | solution.py:28
  7.5 10.5 %collective-permute-start.2 = (bf16[136,512]{1,0:T(8,128)(2,1)S(1)}, bf16[136,512]{1,0:T(8,128)(2,1)S(1)}, u32[]{:S(2)}, u32[]{:S(2)}) collective-permute-start(bf16[136,512]{1,0:T(8,128)(2,1)S(1)} %get-tuple-element.168), channel_id=1, source_target_pairs={{0,24},{2,26},{4,28},{6,30},{8,16},{10,18},{12,20},{14,22},{16,8},... | collective-permute-start | bytes 417800 | tf_op jit(solution)/shard_map/ppermute | solution.py:28
  8.9 9.8 %collective-permute-start = (bf16[136,512]{1,0:T(8,128)(2,1)S(1)}, bf16[136,512]{1,0:T(8,128)(2,1)S(1)}, u32[]{:S(2)}, u32[]{:S(2)}) collective-permute-start(bf16[136,512]{1,0:T(8,128)(2,1)S(1)} %get-tuple-element.165), channel_id=1, source_target_pairs={{0,8},{2,10},{4,12},{6,14},{8,0},{10,2},{12,4},{14,6},{16,24},{18,... | collective-permute-start | bytes 417800 | tf_op jit(solution)/shard_map/ppermute | solution.py:28
  21.1 19.4 %collective-permute-start.8 = (bf16[256,2048]{1,0:T(8,128)(2,1)}, bf16[256,2048]{1,0:T(8,128)(2,1)S(1)}, u32[]{:S(2)}, u32[]{:S(2)}) collective-permute-start(bf16[256,2048]{1,0:T(8,128)(2,1)} %refs_10_.3), channel_id=1, source_target_pairs={{0,1},{1,0},{2,3},{3,2},{4,5},{5,4},{6,7},{7,6},{8,9},{9,8},{10,11... | collective-permute-start | bytes 3145736 | tf_op jit(solution)/shard_map/ppermute | solution.py:46
  21.2 19.3 %collective-permute-start.9 = (bf16[1024,512]{1,0:T(8,128)(2,1)}, bf16[1024,512]{1,0:T(8,128)(2,1)S(1)}, u32[]{:S(2)}, u32[]{:S(2)}) collective-permute-start(bf16[1024,512]{1,0:T(8,128)(2,1)} %refs_11_.1), channel_id=1, source_target_pairs={{0,1},{1,0},{2,3},{3,2},{4,5},{5,4},{6,7},{7,6},{8,9},{9,8},{10,11... | collective-permute-start | bytes 3145736 | tf_op jit(solution)/shard_map/ppermute | solution.py:46
  21.6 12.3 %all-to-all-start = ((bf16[4,512,128]{2,1,0:T(8,128)(2,1)}), bf16[4,512,128]{2,1,0:T(8,128)(2,1)S(1)}, u32[]{:S(2)}, u32[]{:S(2)}) async-start(bf16[4,512,128]{2,1,0:T(8,128)(2,1)} %get-tuple-element.174), calls=%async_computation | async-start | bytes 1048576 | tf_op jit(solution)/shard_map/all_to_all | solution.py:42
  25.4 14.3 %collective-permute-start.5 = (bf16[128,512]{1,0:T(8,128)(2,1)}, bf16[128,512]{1,0:T(8,128)(2,1)S(1)}, u32[]{:S(2)}, u32[]{:S(2)}) collective-permute-start(bf16[128,512]{1,0:T(8,128)(2,1)} %get-tuple-element.192), channel_id=1, source_target_pairs={{0,8},{2,10},{4,12},{6,14},{8,0},{10,2},{12,4},{14,6},{16,24},{18,... | collective-permute-start | bytes 393224 | tf_op jit(solution)/shard_map/ppermute | solution.py:28
  27.8 12.0 %collective-permute-start.6 = (bf16[128,512]{1,0:T(8,128)(2,1)}, bf16[128,512]{1,0:T(8,128)(2,1)S(1)}, u32[]{:S(2)}, u32[]{:S(2)}) collective-permute-start(bf16[128,512]{1,0:T(8,128)(2,1)} %copy-done.2), channel_id=1, source_target_pairs={{0,16},{2,18},{4,20},{6,22},{8,24},{10,26},{12,28},{14,30},{16,0},... | collective-permute-start | bytes 393224 | tf_op jit(solution)/shard_map/ppermute | solution.py:28
  29.7 10.8 %collective-permute-start.7 = (bf16[128,512]{1,0:T(8,128)(2,1)}, bf16[128,512]{1,0:T(8,128)(2,1)}, u32[]{:S(2)}, u32[]{:S(2)}) collective-permute-start(bf16[128,512]{1,0:T(8,128)(2,1)} %copy-done.1), channel_id=1, source_target_pairs={{0,24},{2,26},{4,28},{6,30},{8,16},{10,18},{12,20},{14,22},{16,8},... | collective-permute-start | bytes 393224 | tf_op jit(solution)/shard_map/ppermute | solution.py:28
  57.9 31.9 %all-to-all-start.2 = ((bf16[4,320,512]{2,1,0:T(8,128)(2,1)}), bf16[4,320,512]{2,1,0:T(8,128)(2,1)S(1)}, u32[]{:S(2)}, u32[]{:S(2)}) async-start(bf16[4,320,512]{2,1,0:T(8,128)(2,1)} %get-tuple-element.275), calls=%async_computation.2 | async-start | bytes 2621440 | tf_op jit(solution)/shard_map/all_to_all | solution.py:42
  62.3 14.1 %collective-permute-start.12 = (bf16[128,512]{1,0:T(8,128)(2,1)}, bf16[128,512]{1,0:T(8,128)(2,1)S(1)}, u32[]{:S(2)}, u32[]{:S(2)}) collective-permute-start(bf16[128,512]{1,0:T(8,128)(2,1)} %get-tuple-element.237), channel_id=1, source_target_pairs={{0,8},{2,10},{4,12},{6,14},{8,0},{10,2},{12,4},{14,6},{16,24},{18,... | collective-permute-start | bytes 393224 | tf_op jit(solution)/shard_map/ppermute | solution.py:28
  64.7 13.1 %collective-permute-start.13 = (bf16[128,512]{1,0:T(8,128)(2,1)S(1)}, bf16[128,512]{1,0:T(8,128)(2,1)S(1)}, u32[]{:S(2)}, u32[]{:S(2)}) collective-permute-start(bf16[128,512]{1,0:T(8,128)(2,1)S(1)} %copy-done.6), channel_id=1, source_target_pairs={{0,16},{2,18},{4,20},{6,22},{8,24},{10,26},{12,28},{14,30},{16,0},... | collective-permute-start | bytes 393224 | tf_op jit(solution)/shard_map/ppermute | solution.py:28
  66.3 22.5 %collective-permute-start.18 = (bf16[512,512]{1,0:T(8,128)(2,1)}, bf16[512,512]{1,0:T(8,128)(2,1)S(1)}, u32[]{:S(2)}, u32[]{:S(2)}) collective-permute-start(bf16[512,512]{1,0:T(8,128)(2,1)} %get-tuple-element.274), channel_id=1, source_target_pairs={{0,1},{1,0},{2,3},{3,2},{4,5},{5,4},{6,7},{7,6},{8,9},{9,8},{10,11... | collective-permute-start | bytes 1572872 | tf_op jit(solution)/shard_map/ppermute | solution.py:46
  66.3 13.3 %collective-permute-start.14 = (bf16[128,512]{1,0:T(8,128)(2,1)S(1)}, bf16[128,512]{1,0:T(8,128)(2,1)S(1)}, u32[]{:S(2)}, u32[]{:S(2)}) collective-permute-start(bf16[128,512]{1,0:T(8,128)(2,1)S(1)} %copy-done.5), channel_id=1, source_target_pairs={{0,24},{2,26},{4,28},{6,30},{8,16},{10,18},{12,20},{14,22},{16,8},... | collective-permute-start | bytes 393224 | tf_op jit(solution)/shard_map/ppermute | solution.py:28
  74.3 8.8 %collective-permute-start.15 = (bf16[512,128]{1,0:T(8,128)(2,1)}, bf16[512,128]{1,0:T(8,128)(2,1)S(1)}, u32[]{:S(2)}, u32[]{:S(2)}) collective-permute-start(bf16[512,128]{1,0:T(8,128)(2,1)} %get-tuple-element.256), channel_id=1, source_target_pairs={{0,2},{2,0},{4,6},{6,4},{8,10},{10,8},{12,14},{14,12},{16,18},{18,... | collective-permute-start | bytes 393224 | tf_op jit(solution)/shard_map/ppermute | solution.py:28
  77.8 7.7 %collective-permute-start.17 = (bf16[512,128]{1,0:T(8,128)(2,1)}, bf16[512,128]{1,0:T(8,128)(2,1)S(1)}, u32[]{:S(2)}, u32[]{:S(2)}) collective-permute-start(bf16[512,128]{1,0:T(8,128)(2,1)} %get-tuple-element.258), channel_id=1, source_target_pairs={{0,6},{2,4},{4,2},{6,0},{8,14},{10,12},{12,10},{14,8},{16,22},{18,... | collective-permute-start | bytes 393224 | tf_op jit(solution)/shard_map/ppermute | solution.py:28
  88.6 7.5 %collective-permute-start.19 = (bf16[592,512]{1,0:T(8,128)(2,1)}, bf16[592,512]{1,0:T(8,128)(2,1)S(1)}, u32[]{:S(2)}, u32[]{:S(2)}) collective-permute-start(bf16[592,512]{1,0:T(8,128)(2,1)} %get-tuple-element.278), channel_id=1, source_target_pairs={{0,1},{1,0},{2,3},{3,2},{4,5},{5,4},{6,7},{7,6},{8,9},{9,8},{10,11... | collective-permute-start | bytes 1818632 | tf_op jit(solution)/shard_map/ppermute | solution.py:46
  89.8 23.6 %all-to-all-start.1 = ((bf16[4,192,512]{2,1,0:T(8,128)(2,1)}), bf16[4,192,512]{2,1,0:T(8,128)(2,1)S(1)}, u32[]{:S(2)}, u32[]{:S(2)}) async-start(bf16[4,192,512]{2,1,0:T(8,128)(2,1)} %shard_map.205), calls=%async_computation.1 | async-start | bytes 1572864 | tf_op jit(solution)/shard_map/all_to_all | solution.py:42
  93.6 8.9 %collective-permute-start.20 = (bf16[80,512]{1,0:T(8,128)(2,1)S(1)}, bf16[80,512]{1,0:T(8,128)(2,1)S(1)}, u32[]{:S(2)}, u32[]{:S(2)}) collective-permute-start(bf16[80,512]{1,0:T(8,128)(2,1)S(1)} %get-tuple-element.284), channel_id=1, source_target_pairs={{0,8},{2,10},{4,12},{6,14},{8,0},{10,2},{12,4},{14,6},{16,24},{18,... | collective-permute-start | bytes 245768 | tf_op jit(solution)/shard_map/ppermute | solution.py:28
  97.5 14.4 %collective-permute-start.23 = (bf16[160,512]{1,0:T(8,128)(2,1)S(1)}, bf16[160,512]{1,0:T(8,128)(2,1)S(1)}, u32[]{:S(2)}, u32[]{:S(2)}) collective-permute-start(bf16[160,512]{1,0:T(8,128)(2,1)S(1)} %get-tuple-element.288), channel_id=1, source_target_pairs={{0,2},{2,0},{4,6},{6,4},{8,10},{10,8},{12,14},{14,12},{16,18},{18,... | collective-permute-start | bytes 491528 | tf_op jit(solution)/shard_map/ppermute | solution.py:28
  99.6 8.0 %collective-permute-start.21 = (bf16[80,512]{1,0:T(8,128)(2,1)S(1)}, bf16[80,512]{1,0:T(8,128)(2,1)S(1)}, u32[]{:S(2)}, u32[]{:S(2)}) collective-permute-start(bf16[80,512]{1,0:T(8,128)(2,1)S(1)} %get-tuple-element.285), channel_id=1, source_target_pairs={{0,16},{2,18},{4,20},{6,22},{8,24},{10,26},{12,28},{14,30},{16,0},... | collective-permute-start | bytes 245768 | tf_op jit(solution)/shard_map/ppermute | solution.py:28
  101.0 12.4 %collective-permute-start.24 = (bf16[160,512]{1,0:T(8,128)(2,1)S(1)}, bf16[160,512]{1,0:T(8,128)(2,1)S(1)}, u32[]{:S(2)}, u32[]{:S(2)}) collective-permute-start(bf16[160,512]{1,0:T(8,128)(2,1)S(1)} %get-tuple-element.289), channel_id=1, source_target_pairs={{0,4},{2,6},{4,0},{6,2},{8,12},{10,14},{12,8},{14,10},{16,20},{18,... | collective-permute-start | bytes 491528 | tf_op jit(solution)/shard_map/ppermute | solution.py:28
  102.5 10.9 %collective-permute-start.25 = (bf16[160,512]{1,0:T(8,128)(2,1)S(1)}, bf16[160,512]{1,0:T(8,128)(2,1)S(1)}, u32[]{:S(2)}, u32[]{:S(2)}) collective-permute-start(bf16[160,512]{1,0:T(8,128)(2,1)S(1)} %get-tuple-element.290), channel_id=1, source_target_pairs={{0,6},{2,4},{4,2},{6,0},{8,14},{10,12},{12,10},{14,8},{16,22},{18,... | collective-permute-start | bytes 491528 | tf_op jit(solution)/shard_map/ppermute | solution.py:28
  110.9 7.8 %collective-permute-start.27 = (bf16[80,512]{1,0:T(8,128)(2,1)S(1)}, bf16[80,512]{1,0:T(8,128)(2,1)S(1)}, u32[]{:S(2)}, u32[]{:S(2)}) collective-permute-start(bf16[80,512]{1,0:T(8,128)(2,1)S(1)} %shard_map.208.refs_0_), channel_id=1, source_target_pairs={{0,16},{2,18},{4,20},{6,22},{8,24},{10,26},{12,28},{14,30},{16,0},... | collective-permute-start | bytes 245768 | tf_op jit(solution)/shard_map/ppermute | solution.py:28
  119.8 26.0 %all-to-all-start.3 = ((bf16[4,320,512]{2,1,0:T(8,128)(2,1)}), bf16[4,320,512]{2,1,0:T(8,128)(2,1)S(1)}, u32[]{:S(2)}, u32[]{:S(2)}) async-start(bf16[4,320,512]{2,1,0:T(8,128)(2,1)} %shard_map.210), calls=%async_computation.3 | async-start | bytes 2621440 | tf_op jit(solution)/shard_map/all_to_all | solution.py:42
  124.0 10.6 %collective-permute-start.30 = (bf16[88,512]{1,0:T(8,128)(2,1)S(1)}, bf16[88,512]{1,0:T(8,128)(2,1)S(1)}, u32[]{:S(2)}, u32[]{:S(2)}) collective-permute-start(bf16[88,512]{1,0:T(8,128)(2,1)S(1)} %get-tuple-element.295), channel_id=1, source_target_pairs={{0,16},{2,18},{4,20},{6,22},{8,24},{10,26},{12,28},{14,30},{16,0},... | collective-permute-start | bytes 270344 | tf_op jit(solution)/shard_map/ppermute | solution.py:28
  137.3 7.4 %collective-permute-start.33 = (bf16[88,512]{1,0:T(8,128)(2,1)S(1)}, bf16[88,512]{1,0:T(8,128)(2,1)S(1)}, u32[]{:S(2)}, u32[]{:S(2)}) collective-permute-start(bf16[88,512]{1,0:T(8,128)(2,1)S(1)} %shard_map.211.refs_0_), channel_id=1, source_target_pairs={{0,16},{2,18},{4,20},{6,22},{8,24},{10,26},{12,28},{14,30},{16,0},... | collective-permute-start | bytes 270344 | tf_op jit(solution)/shard_map/ppermute | solution.py:28
  145.9 19.4 %all-to-all-start.4 = ((bf16[4,352,512]{2,1,0:T(8,128)(2,1)}), bf16[4,352,512]{2,1,0:T(8,128)(2,1)S(1)}, u32[]{:S(2)}, u32[]{:S(2)}) async-start(bf16[4,352,512]{2,1,0:T(8,128)(2,1)} %shard_map.212), calls=%async_computation.4 | async-start | bytes 2883584 | tf_op jit(solution)/shard_map/all_to_all | solution.py:42
  149.7 8.1 %collective-permute-start.35 = (bf16[128,512]{1,0:T(8,128)(2,1)}, bf16[128,512]{1,0:T(8,128)(2,1)S(1)}, u32[]{:S(2)}, u32[]{:S(2)}) collective-permute-start(bf16[128,512]{1,0:T(8,128)(2,1)} %get-tuple-element.306), channel_id=1, source_target_pairs={{0,8},{2,10},{4,12},{6,14},{8,0},{10,2},{12,4},{14,6},{16,24},{18,... | collective-permute-start | bytes 393224 | tf_op jit(solution)/shard_map/ppermute | solution.py:28
  149.8 11.3 %collective-permute-start.36 = (bf16[128,512]{1,0:T(8,128)(2,1)S(1)}, bf16[128,512]{1,0:T(8,128)(2,1)S(1)}, u32[]{:S(2)}, u32[]{:S(2)}) collective-permute-start(bf16[128,512]{1,0:T(8,128)(2,1)S(1)} %copy-done.4), channel_id=1, source_target_pairs={{0,16},{2,18},{4,20},{6,22},{8,24},{10,26},{12,28},{14,30},{16,0},... | collective-permute-start | bytes 393224 | tf_op jit(solution)/shard_map/ppermute | solution.py:28
  152.3 8.8 %collective-permute-start.37 = (bf16[128,512]{1,0:T(8,128)(2,1)S(1)}, bf16[128,512]{1,0:T(8,128)(2,1)S(1)}, u32[]{:S(2)}, u32[]{:S(2)}) collective-permute-start(bf16[128,512]{1,0:T(8,128)(2,1)S(1)} %copy-done.3), channel_id=1, source_target_pairs={{0,24},{2,26},{4,28},{6,30},{8,16},{10,18},{12,20},{14,22},{16,8},... | collective-permute-start | bytes 393224 | tf_op jit(solution)/shard_map/ppermute | solution.py:28
  (20 other events, 142.5 us)

commit v5 on v4

--- a/solution.py
+++ b/solution.py
@@ -784,10 +784,13 @@
     at, used = 0, 0
     for height, total, (dest, many) in zip(parts, totals, dests):
         rows = height // per
-        for i in range(got.shape[0]):
+        swapped = isinstance(got, tuple)
+        digit = me % strides[0][1] if swapped else 0
+        for i in range(len(got) if swapped else got.shape[0]):
             for b in range(per):
-                begin = pl.multiple_of((i * per + (b ^ shift)) * rows, 8)
-                piece = got[i, at + b * rows : at + (b + 1) * rows, :]
+                begin = pl.multiple_of(((i ^ digit) * per + (b ^ shift)) * rows, 8)
+                source = got[i].at[0] if swapped else got.at[i]
+                piece = source[at + b * rows : at + (b + 1) * rows, :]
                 total[pl.ds(begin, rows), :] = piece.astype(F32)
         at += height
         dest(total, outs[used : used + many])
@@ -836,8 +839,9 @@
     tile[...] = total[wide : wide + tile.shape[0], :]
 
 
-def both_final_body(strides, parts, got, tile, *refs):
-    outs, totals = refs[:7], refs[7:]
+def both_final_body(strides, parts, n_in, *refs):
+    got, tile = refs[:n_in], refs[n_in]
+    outs, totals = refs[n_in + 1 : n_in + 8], refs[n_in + 8 :]
 
     def main(total, outs):
         (up,) = outs
@@ -876,6 +880,14 @@
     for k, ref in enumerate(refs[:-1]):
         begin = ref.shape[0] - local
         out[place ^ k] = ref[begin:, :].astype(F32)
+
+
+def close_body(rest, count, strides, parts, n_in, *refs):
+    main, moved = refs[: n_in + 1], refs[n_in + 1 : n_in + 1 + count]
+    outs, totals = refs[n_in + 1 + count : n_in + 9 + count], refs[n_in + 9 + count :]
+    place_body(rest, *moved, outs[7])
+    Order.leave(7)
+    both_final_body(strides, parts, n_in, *main, *outs[:7], *totals)
 
 
 def on_device(
@@ -1213,6 +1225,11 @@
         heights = [h // strides[at][1] for h in heights]
     both_terms = cut_up(chunks, heights, strides, last, size)
     heights = [h // count for h in heights]
+    (layer_out,) = call(
+        functools.partial(place_body, rest),
+        [((count, local, dim), F32, 1)],
+        [Far(layer_got[0]), *far(layer_got[1:])],
+    )
     early_last, _ = ready(early_got)
     both_got = spread(settle(both_terms), strides, last, size)
     slices = [(0, heights[0]), (heights[0], heights[1])]
@@ -1225,32 +1242,30 @@
         tops = [m[0].shape[0] for m in moved]
         slices = [(0, tops[0]), (tops[0], tops[1])]
     tall_rows = sum(h for _, h in slices) * len(both_got)
-    (copies,) = call(
+    (both_own,) = call(
         functools.partial(copies_body, slices, len(both_got)),
-        [((first, tall_rows, WIDTH), BF)],
+        [((1, tall_rows, WIDTH), BF)],
         both_got,
     )
-    both_last = exchange(copies, 1, size)
+    both_last = spread(both_own, strides, 0, size)
     input_pieces = after(tuple(input_pieces), both_got[0])
-    input_got = [input_pieces[0]] + [swap(input_pieces[k], k * rest, size) for k in range(1, count)]
-    (layer_out,) = call(
-        functools.partial(place_body, rest),
-        [((count, local, dim), F32, 1)],
-        [Far(layer_got[0]), *layer_got[1:]],
-    )
+    moved = {k: swap(input_pieces[k], k * rest, size) for k in reversed(range(1, count))}
+    input_got = [input_pieces[0]] + [moved[k] for k in range(1, count)]
     grad_down, up_tile = call(
         functools.partial(final_body, strides, [early_rows // first], [(early_dest, 2)], 2),
         [((wide, dim), F32, 1), ((tall, WIDTH), F32)],
         [early_last],
         scratch=[((early_rows, WIDTH), F32)],
     )
-    (input_grad,) = call(
-        functools.partial(place_body, rest),
-        [((count, local, dim), F32, 1)],
-        [Far(input_got[0]), *input_got[1:]],
-    )
-    grad_up, grad_out, grad_query, grad_kv, grad_router, grad_one, grad_two = call(
-        functools.partial(both_final_body, strides, [main_rows // first, late_rows // first]),
+    grad_up, grad_out, grad_query, grad_kv, grad_router, grad_one, grad_two, input_grad = call(
+        functools.partial(
+            close_body,
+            rest,
+            count,
+            strides,
+            [main_rows // first, late_rows // first],
+            len(both_last),
+        ),
         [
             ((tall, feed), F32, 1),
             ((tall, dim), F32, 1),
@@ -1259,8 +1274,9 @@
             ((experts, tall), F32, 1),
             ((1, tall), F32, 1),
             ((1, tall), F32, 1),
+            ((count, local, dim), F32, 1),
         ],
-        [both_last, up_tile],
+        [*both_last, up_tile, *input_got],
         scratch=[((main_rows, WIDTH), F32), ((late_rows, WIDTH), F32)],
     )
     return (

time: 168 us -> 165 us (0.982)
  Pallas kernels: 56.2 us -> 52.5 us
    pallas_call x22 -> x21, Pallas kernels: 56.2 us -> 52.5 us  [call(): got = list(run(*args, *moved))]
    ppermute x30 -> x33, starting transfers between devices: 48.8 us -> 52.4 us  [swap(): return lax.ppermute(values, 'ctx', [(i, i ^ mask) for i in range(size)])]
    all_to_all x5 -> x4, starting transfers between devices: 19 us -> 15.7 us  [exchange(): lax.all_to_all(parts, 'ctx', 0, 0, tiled=True, axis_index_groups=groups)]
    ppermute x30 -> x33, waiting for transfers between devices: 36.8 us -> 39.2 us  [swap(): return lax.ppermute(values, 'ctx', [(i, i ^ mask) for i in range(size)])]
    all_to_all x5 -> x4, waiting for transfers between devices: 2.2 us -> 0.01 us  [exchange(): lax.all_to_all(parts, 'ctx', 0, 0, tiled=True, axis_index_groups=groups)]
  transfers between devices with their start and end apart: 43 -> 45, of which waited for: 15 -> 13; matrix products, arithmetic and copies ran while one was open for 0% -> 0% of each run, Pallas kernels for 23% -> 21%
where the time goes in v5:
time: 165 us; the launch traced here: 164 us
  starting transfers between devices  69.9 us (42%)
  Pallas kernels  52.5 us (32%)
  waiting for transfers between devices  40.4 us (24%)
    pallas_call x21, Pallas kernels, call(): got = list(run(*args, *moved))  52.5 us
    ppermute x33, starting transfers between devices, swap(): return lax.ppermute(values, 'ctx', [(i, i ^ mask) for i in range(size)])  52.4 us
    ppermute x33, waiting for transfers between devices, swap(): return lax.ppermute(values, 'ctx', [(i, i ^ mask) for i in range(size)])  39.2 us
    all_to_all x4, starting transfers between devices, exchange(): lax.all_to_all(parts, 'ctx', 0, 0, tiled=True, axis_index_groups=groups)  15.7 us
  transfers between devices with their start and end apart: 45, of which 13 were waited for; matrix products, arithmetic and copies ran while one was open for 0% of the time, Pallas kernels for 21%

profile of v5, /device:TPU:0, one launch (start us, length us, event | category | flops | bytes accessed | tf_op | source)
XLA Modules:
  0.0 164.3 jit_solution(3670232250613187698)
XLA Ops:
  3.5 4.0 %collective-permute-start.1 = (bf16[136,512]{1,0:T(8,128)(2,1)S(1)}, bf16[136,512]{1,0:T(8,128)(2,1)S(1)}, u32[]{:S(2)}, u32[]{:S(2)}) collective-permute-start(bf16[136,512]{1,0:T(8,128)(2,1)S(1)} %get-tuple-element.167), channel_id=1, source_target_pairs={{0,16},{2,18},{4,20},{6,22},{8,24},{10,26},{12,28},{14,30},{16,0},... | collective-permute-start | bytes 417800 | tf_op jit(solution)/shard_map/ppermute | solution.py:28
  10.4 7.7 %collective-permute-done.1.refs_2_ = bf16[136,512]{1,0:T(8,128)(2,1)S(1)} collective-permute-done((bf16[136,512]{1,0:T(8,128)(2,1)S(1)}, bf16[136,512]{1,0:T(8,128)(2,1)S(1)}, u32[]{:S(2)}, u32[]{:S(2)}) %collective-permute-start.1) | collective-permute-done | bytes 139296 | tf_op jit(solution)/shard_map/ppermute | solution.py:28
  18.7 2.4 %shard_map.196 = (bf16[4,512,128]{2,1,0:T(8,128)(2,1)}, bf16[512,512]{1,0:T(8,128)(2,1)}, bf16[512,512]{1,0:T(8,128)(2,1)}, f32[8,512]{1,0:T(8,128)}, bf16[512,128]{1,0:T(8,128)(2,1)}, /*index=5*/f32[32,128]{1,0:T(8,128)S(1)}) custom-call(bf16[128,512]{1,0:T(8,128)(2,1)S(1)} %get-tuple-element.166.refs_0_, ...), custom_call_target="tpu_custom_call" | custom-call | flops 1 | bytes 1 | tf_op jit(solution)/shard_map/pallas_call | solution.py:171
  21.6 3.9 %all-to-all-start = ((bf16[4,512,128]{2,1,0:T(8,128)(2,1)}), bf16[4,512,128]{2,1,0:T(8,128)(2,1)S(1)}, u32[]{:S(2)}, u32[]{:S(2)}) async-start(bf16[4,512,128]{2,1,0:T(8,128)(2,1)} %get-tuple-element.174), calls=%async_computation | async-start | bytes 1048576 | tf_op jit(solution)/shard_map/all_to_all | solution.py:42
  25.5 2.3 %collective-permute-start.5 = (bf16[128,512]{1,0:T(8,128)(2,1)}, bf16[128,512]{1,0:T(8,128)(2,1)S(1)}, u32[]{:S(2)}, u32[]{:S(2)}) collective-permute-start(bf16[128,512]{1,0:T(8,128)(2,1)} %get-tuple-element.192), channel_id=1, source_target_pairs={{0,8},{2,10},{4,12},{6,14},{8,0},{10,2},{12,4},{14,6},{16,24},{18,... | collective-permute-start | bytes 393224 | tf_op jit(solution)/shard_map/ppermute | solution.py:28
  31.3 2.8 %shard_map.197 = (bf16[128,512]{1,0:T(8,128)(2,1)}, bf16[512,512]{1,0:T(8,128)(2,1)}, f32[2,512]{1,0:T(2,128)S(1)}, f32[2,512]{1,0:T(2,128)}, f32[8,512]{1,0:T(8...) custom-call(bf16[512,512]{1,0:T(8,128)(2,1)} %get-tuple-element.175.refs, ...), custom_call_target="tpu_custom_call" | custom-call | flops 1 | bytes 1 | tf_op jit(solution)/shard_map/pallas_call | solution.py:171
  34.1 5.7 %shard_map.198 = (f32[128,512]{1,0:T(8,128)}, f32[2,512]{1,0:T(2,128)}, bf16[512,512]{1,0:T(8,128)(2,1)}, f32[512,512]{1,0:T(8,128)S(1)}, bf16[512,512]{1,0:T(8,...) custom-call(s32[16]{0:T(128)S(1)} %copy-done.1, ...), custom_call_target="tpu_custom_call" | custom-call | flops 1 | bytes 1 | tf_op jit(solution)/shard_map/pallas_call | solution.py:171
  40.6 6.6 %shard_map.199 = (f32[512,512]{1,0:T(8,128)S(1)}, f32[512,512]{1,0:T(8,128)S(1)}, bf16[1024,512]{1,0:T(8,128)(2,1)S(1)}, bf16[512,512]{1,0:T(8,128)(2,1)}, bf16[...) custom-call(bf16[512,512]{1,0:T(8,128)(2,1)S(1)} %get-tuple-element., ...), custom_call_target="tpu_custom_call" | custom-call | flops 1 | bytes 1 | tf_op jit(solution)/shard_map/pallas_call | solution.py:171
  47.8 6.5 %shard_map.200 = (f32[128,512]{1,0:T(8,128)}, bf16[128,512]{1,0:T(8,128)(2,1)}, bf16[128,512]{1,0:T(8,128)(2,1)}, bf16[128,512]{1,0:T(8,128)(2,1)}, f32[512,512]...) custom-call(bf16[512,512]{1,0:T(8,128)(2,1)S(1)} %get-tuple-element., ...), custom_call_target="tpu_custom_call" | custom-call | flops 1 | bytes 1 | tf_op jit(solution)/shard_map/pallas_call | solution.py:171
  54.3 3.7 %shard_map.201 = (f32[512,512]{1,0:T(8,128)}, bf16[512,512]{1,0:T(8,128)(2,1)}, bf16[128,512]{1,0:T(8,128)(2,1)S(1)}, f32[2,512]{1,0:T(2,128)S(1)}, f32[8,512]{1...) custom-call(f32[512,512]{1,0:T(8,128)S(1)} %get-tuple-element.209.re, ...), custom_call_target="tpu_custom_call" | custom-call | flops 1 | bytes 1 | tf_op jit(solution)/shard_map/pallas_call | solution.py:171
  58.0 4.3 %all-to-all-start.2 = ((bf16[4,320,512]{2,1,0:T(8,128)(2,1)}), bf16[4,320,512]{2,1,0:T(8,128)(2,1)S(1)}, u32[]{:S(2)}, u32[]{:S(2)}) async-start(bf16[4,320,512]{2,1,0:T(8,128)(2,1)} %get-tuple-element.275), calls=%async_computation.2 | async-start | bytes 2621440 | tf_op jit(solution)/shard_map/all_to_all | solution.py:42
  62.4 2.5 %collective-permute-start.12 = (bf16[128,512]{1,0:T(8,128)(2,1)S(1)}, bf16[128,512]{1,0:T(8,128)(2,1)S(1)}, u32[]{:S(2)}, u32[]{:S(2)}) collective-permute-start(bf16[128,512]{1,0:T(8,128)(2,1)S(1)} %copy-done.11), channel_id=1, source_target_pairs={{0,8},{2,10},{4,12},{6,14},{8,0},{10,2},{12,4},{14,6},{16,24},{18,... | collective-permute-start | bytes 393224 | tf_op jit(solution)/shard_map/ppermute | solution.py:28
  67.9 6.5 %shard_map.202 = (bf16[128,512]{1,0:T(8,128)(2,1)S(1)}, f32[512,128]{1,0:T(8,128)}, bf16[512,128]{1,0:T(8,128)(2,1)}, bf16[512,128]{1,0:T(8,128)(2,1)}, bf16[512...) custom-call(s32[16]{0:T(128)S(1)} %copy-done.1, ...), custom_call_target="tpu_custom_call" | custom-call | flops 1 | bytes 1 | tf_op jit(solution)/shard_map/pallas_call | solution.py:171
  79.8 3.6 %shard_map.203 = (bf16[256,512]{1,0:T(8,128)(2,1)}, bf16[256,512]{1,0:T(8,128)(2,1)}, bf16[512,512]{1,0:T(8,128)(2,1)}, f32[512,512]{1,0:T(8,128)S(1)}, f32[512,...) custom-call(bf16[128,512]{1,0:T(8,128)(2,1)S(1)} %get-tuple-element., ...), custom_call_target="tpu_custom_call" | custom-call | flops 1 | bytes 1 | tf_op jit(solution)/shard_map/pallas_call | solution.py:171
  83.4 2.3 %collective-permute-done.17.refs_3_ = bf16[512,128]{1,0:T(8,128)(2,1)S(1)} collective-permute-done((bf16[512,128]{1,0:T(8,128)(2,1)}, bf16[512,128]{1,0:T(8,128)(2,1)S(1)}, u32[]{:S(2)}, u32[]{:S(2)}) %collective-permute-start.17) | collective-permute-done | bytes 131104 | tf_op jit(solution)/shard_map/ppermute | solution.py:28
  89.0 3.5 %all-to-all-start.1 = ((bf16[4,192,512]{2,1,0:T(8,128)(2,1)}), bf16[4,192,512]{2,1,0:T(8,128)(2,1)S(1)}, u32[]{:S(2)}, u32[]{:S(2)}) async-start(bf16[4,192,512]{2,1,0:T(8,128)(2,1)} %shard_map.205), calls=%async_computation.1 | async-start | bytes 1572864 | tf_op jit(solution)/shard_map/all_to_all | solution.py:42
  92.8 2.5 %collective-permute-start.20 = (bf16[80,512]{1,0:T(8,128)(2,1)S(1)}, bf16[80,512]{1,0:T(8,128)(2,1)S(1)}, u32[]{:S(2)}, u32[]{:S(2)}) collective-permute-start(bf16[80,512]{1,0:T(8,128)(2,1)S(1)} %get-tuple-element.284), channel_id=1, source_target_pairs={{0,8},{2,10},{4,12},{6,14},{8,0},{10,2},{12,4},{14,6},{16,24},{18,... | collective-permute-start | bytes 245768 | tf_op jit(solution)/shard_map/ppermute | solution.py:28
  103.2 6.0 %collective-permute-done.21.refs_2_ = bf16[80,512]{1,0:T(8,128)(2,1)S(1)} collective-permute-done((bf16[80,512]{1,0:T(8,128)(2,1)S(1)}, bf16[80,512]{1,0:T(8,128)(2,1)S(1)}, u32[]{:S(2)}, u32[]{:S(2)}) %collective-permute-start.21) | collective-permute-done | bytes 81952 | tf_op jit(solution)/shard_map/ppermute | solution.py:28
  109.3 2.2 %collective-permute-start.28 = (bf16[80,512]{1,0:T(8,128)(2,1)S(1)}, bf16[80,512]{1,0:T(8,128)(2,1)S(1)}, u32[]{:S(2)}, u32[]{:S(2)}) collective-permute-start(bf16[80,512]{1,0:T(8,128)(2,1)S(1)} %shard_map.208.refs_0_), channel_id=1, source_target_pairs={{0,24},{2,26},{4,28},{6,30},{8,16},{10,18},{12,20},{14,22},{16,8},... | collective-permute-start | bytes 245768 | tf_op jit(solution)/shard_map/ppermute | solution.py:28
  114.0 2.2 %shard_map.210 = f32[4,128,512]{2,1,0:T(8,128)} custom-call(f32[128,512]{1,0:T(8,128)} %get-tuple-element.292.refs_0_, bf16[128,512]{1,0:T(8,128)(2,1)} %copy-done.4, bf16[128,512]{1,0:T(8,128)(2,1)} %copy-done.5, bf16[128,512]{1,0:T(8,128)(2,1)} %copy-done.6), custom_call_target="tpu_custom_call" | custom-call | flops 1 | bytes 1 | tf_op jit(solution)/shard_map/pallas_call | solution.py:171
  116.2 2.9 %collective-permute-done.27.refs_2_ = bf16[80,512]{1,0:T(8,128)(2,1)S(1)} collective-permute-done((bf16[80,512]{1,0:T(8,128)(2,1)S(1)}, bf16[80,512]{1,0:T(8,128)(2,1)S(1)}, u32[]{:S(2)}, u32[]{:S(2)}) %collective-permute-start.27) | collective-permute-done | bytes 81952 | tf_op jit(solution)/shard_map/ppermute | solution.py:28
  120.3 4.0 %all-to-all-start.3 = ((bf16[4,320,512]{2,1,0:T(8,128)(2,1)}), bf16[4,320,512]{2,1,0:T(8,128)(2,1)S(1)}, u32[]{:S(2)}, u32[]{:S(2)}) async-start(bf16[4,320,512]{2,1,0:T(8,128)(2,1)} %shard_map.211), calls=%async_computation.3 | async-start | bytes 2621440 | tf_op jit(solution)/shard_map/all_to_all | solution.py:42
  124.7 3.4 %collective-permute-start.30 = (bf16[88,512]{1,0:T(8,128)(2,1)S(1)}, bf16[88,512]{1,0:T(8,128)(2,1)S(1)}, u32[]{:S(2)}, u32[]{:S(2)}) collective-permute-start(bf16[88,512]{1,0:T(8,128)(2,1)S(1)} %get-tuple-element.296), channel_id=1, source_target_pairs={{0,16},{2,18},{4,20},{6,22},{8,24},{10,26},{12,28},{14,30},{16,0},... | collective-permute-start | bytes 270344 | tf_op jit(solution)/shard_map/ppermute | solution.py:28
  129.9 5.3 %collective-permute-done.30.refs_2_ = bf16[88,512]{1,0:T(8,128)(2,1)S(1)} collective-permute-done((bf16[88,512]{1,0:T(8,128)(2,1)S(1)}, bf16[88,512]{1,0:T(8,128)(2,1)S(1)}, u32[]{:S(2)}, u32[]{:S(2)}) %collective-permute-start.30) | collective-permute-done | bytes 90144 | tf_op jit(solution)/shard_map/ppermute | solution.py:28
  135.2 2.5 %collective-permute-start.34 = (bf16[88,512]{1,0:T(8,128)(2,1)S(1)}, bf16[88,512]{1,0:T(8,128)(2,1)S(1)}, u32[]{:S(2)}, u32[]{:S(2)}) collective-permute-start(bf16[88,512]{1,0:T(8,128)(2,1)S(1)} %shard_map.212.refs_0_), channel_id=1, source_target_pairs={{0,24},{2,26},{4,28},{6,30},{8,16},{10,18},{12,20},{14,22},{16,8},... | collective-permute-start | bytes 270344 | tf_op jit(solution)/shard_map/ppermute | solution.py:28
  139.7 2.9 %collective-permute-done.34.refs_3_ = bf16[88,512]{1,0:T(8,128)(2,1)S(1)} collective-permute-done((bf16[88,512]{1,0:T(8,128)(2,1)S(1)}, bf16[88,512]{1,0:T(8,128)(2,1)S(1)}, u32[]{:S(2)}, u32[]{:S(2)}) %collective-permute-start.34) | collective-permute-done | bytes 90144 | tf_op jit(solution)/shard_map/ppermute | solution.py:28
  142.6 2.5 %collective-permute-done.33.refs_2_ = bf16[88,512]{1,0:T(8,128)(2,1)S(1)} collective-permute-done((bf16[88,512]{1,0:T(8,128)(2,1)S(1)}, bf16[88,512]{1,0:T(8,128)(2,1)S(1)}, u32[]{:S(2)}, u32[]{:S(2)}) %collective-permute-start.33) | collective-permute-done | bytes 90144 | tf_op jit(solution)/shard_map/ppermute | solution.py:28
  145.2 2.6 %collective-permute-start.37 = (bf16[1,352,512]{2,1,0:T(8,128)(2,1)S(1)}, bf16[1,352,512]{2,1,0:T(8,128)(2,1)S(1)}, u32[]{:S(2)}, u32[]{:S(2)}) collective-permute-start(bf16[1,352,512]{2,1,0:T(8,128)(2,1)S(1)} %shard_map.213.refs_0_), channel_id=1, source_target_pairs={{0,6},{2,4},{4,2},{6,0},{8,14},{10,12},{12,10},{14,8},{16,22},{18,... | collective-permute-start | bytes 1081352 | tf_op jit(solution)/shard_map/ppermute | solution.py:28
  148.7 2.4 %collective-permute-start.39 = (bf16[128,512]{1,0:T(8,128)(2,1)}, bf16[128,512]{1,0:T(8,128)(2,1)S(1)}, u32[]{:S(2)}, u32[]{:S(2)}) collective-permute-start(bf16[128,512]{1,0:T(8,128)(2,1)} %get-tuple-element.308), channel_id=1, source_target_pairs={{0,16},{2,18},{4,20},{6,22},{8,24},{10,26},{12,28},{14,30},{16,0},... | collective-permute-start | bytes 393224 | tf_op jit(solution)/shard_map/ppermute | solution.py:28
  151.1 4.0 %collective-permute-done.38.refs_6_ = bf16[128,512]{1,0:T(8,128)(2,1)S(1)} collective-permute-done((bf16[128,512]{1,0:T(8,128)(2,1)S(1)}, bf16[128,512]{1,0:T(8,128)(2,1)S(1)}, u32[]{:S(2)}, u32[]{:S(2)}) %collective-permute-start.38) | collective-permute-done | bytes 131104 | tf_op jit(solution)/shard_map/ppermute | solution.py:28
  158.8 3.1 %collective-permute-done.40.refs_8_ = bf16[128,512]{1,0:T(8,128)(2,1)S(1)} collective-permute-done((bf16[128,512]{1,0:T(8,128)(2,1)S(1)}, bf16[128,512]{1,0:T(8,128)(2,1)S(1)}, u32[]{:S(2)}, u32[]{:S(2)}) %collective-permute-start.40) | collective-permute-done | bytes 131104 | tf_op jit(solution)/shard_map/ppermute | solution.py:28
  161.9 2.2 %shard_map.215 = (f32[256,2048]{1,0:T(8,128)}, f32[256,512]{1,0:T(8,128)}, f32[256,512]{1,0:T(8,128)}, f32[256,128]{1,0:T(8,128)}, f32[8,256]{1,0:T(8,128)}, /*i...) custom-call(bf16[1,352,512]{2,1,0:T(8,128)(2,1)S(1)} %shard_map.213.refs_0_, ...), custom_call_target="tpu_custom_call" | custom-call | flops 1 | bytes 1 | tf_op jit(solution)/shard_map/pallas_call | solution.py:171
  (110 shorter events, 43.9 us)
Async XLA Ops:
  2.9 15.8 %collective-permute-start.4 = (bf16[264,1152]{1,0:T(8,128)(2,1)S(1)}, bf16[264,1152]{1,0:T(8,128)(2,1)S(1)}, u32[]{:S(2)}, u32[]{:S(2)}) collective-permute-start(bf16[264,1152]{1,0:T(8,128)(2,1)S(1)} %get-tuple-element.169), channel_id=1, source_target_pairs={{0,1},{1,0},{2,3},{3,2},{4,5},{5,4},{6,7},{7,6},{8,9},{9,8},{10,11... | collective-permute-start | bytes 1824776 | tf_op jit(solution)/shard_map/ppermute | solution.py:46
  3.5 14.5 %collective-permute-start.1 = (bf16[136,512]{1,0:T(8,128)(2,1)S(1)}, bf16[136,512]{1,0:T(8,128)(2,1)S(1)}, u32[]{:S(2)}, u32[]{:S(2)}) collective-permute-start(bf16[136,512]{1,0:T(8,128)(2,1)S(1)} %get-tuple-element.167), channel_id=1, source_target_pairs={{0,16},{2,18},{4,20},{6,22},{8,24},{10,26},{12,28},{14,30},{16,0},... | collective-permute-start | bytes 417800 | tf_op jit(solution)/shard_map/ppermute | solution.py:28
  7.5 10.5 %collective-permute-start.2 = (bf16[136,512]{1,0:T(8,128)(2,1)S(1)}, bf16[136,512]{1,0:T(8,128)(2,1)S(1)}, u32[]{:S(2)}, u32[]{:S(2)}) collective-permute-start(bf16[136,512]{1,0:T(8,128)(2,1)S(1)} %get-tuple-element.168), channel_id=1, source_target_pairs={{0,24},{2,26},{4,28},{6,30},{8,16},{10,18},{12,20},{14,22},{16,8},... | collective-permute-start | bytes 417800 | tf_op jit(solution)/shard_map/ppermute | solution.py:28
  8.9 9.8 %collective-permute-start = (bf16[136,512]{1,0:T(8,128)(2,1)S(1)}, bf16[136,512]{1,0:T(8,128)(2,1)S(1)}, u32[]{:S(2)}, u32[]{:S(2)}) collective-permute-start(bf16[136,512]{1,0:T(8,128)(2,1)S(1)} %get-tuple-element.165), channel_id=1, source_target_pairs={{0,8},{2,10},{4,12},{6,14},{8,0},{10,2},{12,4},{14,6},{16,24},{18,... | collective-permute-start | bytes 417800 | tf_op jit(solution)/shard_map/ppermute | solution.py:28
  21.1 19.5 %collective-permute-start.8 = (bf16[256,2048]{1,0:T(8,128)(2,1)}, bf16[256,2048]{1,0:T(8,128)(2,1)S(1)}, u32[]{:S(2)}, u32[]{:S(2)}) collective-permute-start(bf16[256,2048]{1,0:T(8,128)(2,1)} %refs_10_.3), channel_id=1, source_target_pairs={{0,1},{1,0},{2,3},{3,2},{4,5},{5,4},{6,7},{7,6},{8,9},{9,8},{10,11... | collective-permute-start | bytes 3145736 | tf_op jit(solution)/shard_map/ppermute | solution.py:46
  21.1 19.5 %collective-permute-start.9 = (bf16[1024,512]{1,0:T(8,128)(2,1)}, bf16[1024,512]{1,0:T(8,128)(2,1)S(1)}, u32[]{:S(2)}, u32[]{:S(2)}) collective-permute-start(bf16[1024,512]{1,0:T(8,128)(2,1)} %refs_11_.1), channel_id=1, source_target_pairs={{0,1},{1,0},{2,3},{3,2},{4,5},{5,4},{6,7},{7,6},{8,9},{9,8},{10,11... | collective-permute-start | bytes 3145736 | tf_op jit(solution)/shard_map/ppermute | solution.py:46
  21.6 12.5 %all-to-all-start = ((bf16[4,512,128]{2,1,0:T(8,128)(2,1)}), bf16[4,512,128]{2,1,0:T(8,128)(2,1)S(1)}, u32[]{:S(2)}, u32[]{:S(2)}) async-start(bf16[4,512,128]{2,1,0:T(8,128)(2,1)} %get-tuple-element.174), calls=%async_computation | async-start | bytes 1048576 | tf_op jit(solution)/shard_map/all_to_all | solution.py:42
  25.5 14.3 %collective-permute-start.5 = (bf16[128,512]{1,0:T(8,128)(2,1)}, bf16[128,512]{1,0:T(8,128)(2,1)S(1)}, u32[]{:S(2)}, u32[]{:S(2)}) collective-permute-start(bf16[128,512]{1,0:T(8,128)(2,1)} %get-tuple-element.192), channel_id=1, source_target_pairs={{0,8},{2,10},{4,12},{6,14},{8,0},{10,2},{12,4},{14,6},{16,24},{18,... | collective-permute-start | bytes 393224 | tf_op jit(solution)/shard_map/ppermute | solution.py:28
  27.9 12.0 %collective-permute-start.6 = (bf16[128,512]{1,0:T(8,128)(2,1)}, bf16[128,512]{1,0:T(8,128)(2,1)S(1)}, u32[]{:S(2)}, u32[]{:S(2)}) collective-permute-start(bf16[128,512]{1,0:T(8,128)(2,1)} %copy-done.3), channel_id=1, source_target_pairs={{0,16},{2,18},{4,20},{6,22},{8,24},{10,26},{12,28},{14,30},{16,0},... | collective-permute-start | bytes 393224 | tf_op jit(solution)/shard_map/ppermute | solution.py:28
  29.8 10.8 %collective-permute-start.7 = (bf16[128,512]{1,0:T(8,128)(2,1)}, bf16[128,512]{1,0:T(8,128)(2,1)}, u32[]{:S(2)}, u32[]{:S(2)}) collective-permute-start(bf16[128,512]{1,0:T(8,128)(2,1)} %copy-done.2), channel_id=1, source_target_pairs={{0,24},{2,26},{4,28},{6,30},{8,16},{10,18},{12,20},{14,22},{16,8},... | collective-permute-start | bytes 393224 | tf_op jit(solution)/shard_map/ppermute | solution.py:28
  58.0 31.0 %all-to-all-start.2 = ((bf16[4,320,512]{2,1,0:T(8,128)(2,1)}), bf16[4,320,512]{2,1,0:T(8,128)(2,1)S(1)}, u32[]{:S(2)}, u32[]{:S(2)}) async-start(bf16[4,320,512]{2,1,0:T(8,128)(2,1)} %get-tuple-element.275), calls=%async_computation.2 | async-start | bytes 2621440 | tf_op jit(solution)/shard_map/all_to_all | solution.py:42
  62.4 14.1 %collective-permute-start.12 = (bf16[128,512]{1,0:T(8,128)(2,1)S(1)}, bf16[128,512]{1,0:T(8,128)(2,1)S(1)}, u32[]{:S(2)}, u32[]{:S(2)}) collective-permute-start(bf16[128,512]{1,0:T(8,128)(2,1)S(1)} %copy-done.11), channel_id=1, source_target_pairs={{0,8},{2,10},{4,12},{6,14},{8,0},{10,2},{12,4},{14,6},{16,24},{18,... | collective-permute-start | bytes 393224 | tf_op jit(solution)/shard_map/ppermute | solution.py:28
  64.8 13.1 %collective-permute-start.13 = (bf16[128,512]{1,0:T(8,128)(2,1)S(1)}, bf16[128,512]{1,0:T(8,128)(2,1)S(1)}, u32[]{:S(2)}, u32[]{:S(2)}) collective-permute-start(bf16[128,512]{1,0:T(8,128)(2,1)S(1)} %copy-done.10), channel_id=1, source_target_pairs={{0,16},{2,18},{4,20},{6,22},{8,24},{10,26},{12,28},{14,30},{16,0},... | collective-permute-start | bytes 393224 | tf_op jit(solution)/shard_map/ppermute | solution.py:28
  66.4 21.5 %collective-permute-start.18 = (bf16[512,512]{1,0:T(8,128)(2,1)}, bf16[512,512]{1,0:T(8,128)(2,1)S(1)}, u32[]{:S(2)}, u32[]{:S(2)}) collective-permute-start(bf16[512,512]{1,0:T(8,128)(2,1)} %get-tuple-element.274), channel_id=1, source_target_pairs={{0,1},{1,0},{2,3},{3,2},{4,5},{5,4},{6,7},{7,6},{8,9},{9,8},{10,11... | collective-permute-start | bytes 1572872 | tf_op jit(solution)/shard_map/ppermute | solution.py:46
  66.4 13.3 %collective-permute-start.14 = (bf16[128,512]{1,0:T(8,128)(2,1)S(1)}, bf16[128,512]{1,0:T(8,128)(2,1)S(1)}, u32[]{:S(2)}, u32[]{:S(2)}) collective-permute-start(bf16[128,512]{1,0:T(8,128)(2,1)S(1)} %copy-done.9), channel_id=1, source_target_pairs={{0,24},{2,26},{4,28},{6,30},{8,16},{10,18},{12,20},{14,22},{16,8},... | collective-permute-start | bytes 393224 | tf_op jit(solution)/shard_map/ppermute | solution.py:28
  74.4 8.9 %collective-permute-start.15 = (bf16[512,128]{1,0:T(8,128)(2,1)}, bf16[512,128]{1,0:T(8,128)(2,1)S(1)}, u32[]{:S(2)}, u32[]{:S(2)}) collective-permute-start(bf16[512,128]{1,0:T(8,128)(2,1)} %get-tuple-element.256), channel_id=1, source_target_pairs={{0,2},{2,0},{4,6},{6,4},{8,10},{10,8},{12,14},{14,12},{16,18},{18,... | collective-permute-start | bytes 393224 | tf_op jit(solution)/shard_map/ppermute | solution.py:28
  78.0 7.7 %collective-permute-start.17 = (bf16[512,128]{1,0:T(8,128)(2,1)}, bf16[512,128]{1,0:T(8,128)(2,1)S(1)}, u32[]{:S(2)}, u32[]{:S(2)}) collective-permute-start(bf16[512,128]{1,0:T(8,128)(2,1)} %get-tuple-element.258), channel_id=1, source_target_pairs={{0,6},{2,4},{4,2},{6,0},{8,14},{10,12},{12,10},{14,8},{16,22},{18,... | collective-permute-start | bytes 393224 | tf_op jit(solution)/shard_map/ppermute | solution.py:28
  87.8 7.5 %collective-permute-start.19 = (bf16[592,512]{1,0:T(8,128)(2,1)S(1)}, bf16[592,512]{1,0:T(8,128)(2,1)S(1)}, u32[]{:S(2)}, u32[]{:S(2)}) collective-permute-start(bf16[592,512]{1,0:T(8,128)(2,1)S(1)} %get-tuple-element.278), channel_id=1, source_target_pairs={{0,1},{1,0},{2,3},{3,2},{4,5},{5,4},{6,7},{7,6},{8,9},{9,8},{10,11... | collective-permute-start | bytes 1818632 | tf_op jit(solution)/shard_map/ppermute | solution.py:46
  89.0 24.7 %all-to-all-start.1 = ((bf16[4,192,512]{2,1,0:T(8,128)(2,1)}), bf16[4,192,512]{2,1,0:T(8,128)(2,1)S(1)}, u32[]{:S(2)}, u32[]{:S(2)}) async-start(bf16[4,192,512]{2,1,0:T(8,128)(2,1)} %shard_map.205), calls=%async_computation.1 | async-start | bytes 1572864 | tf_op jit(solution)/shard_map/all_to_all | solution.py:42
  92.8 8.9 %collective-permute-start.20 = (bf16[80,512]{1,0:T(8,128)(2,1)S(1)}, bf16[80,512]{1,0:T(8,128)(2,1)S(1)}, u32[]{:S(2)}, u32[]{:S(2)}) collective-permute-start(bf16[80,512]{1,0:T(8,128)(2,1)S(1)} %get-tuple-element.284), channel_id=1, source_target_pairs={{0,8},{2,10},{4,12},{6,14},{8,0},{10,2},{12,4},{14,6},{16,24},{18,... | collective-permute-start | bytes 245768 | tf_op jit(solution)/shard_map/ppermute | solution.py:28
  96.7 15.6 %collective-permute-start.23 = (bf16[160,512]{1,0:T(8,128)(2,1)S(1)}, bf16[160,512]{1,0:T(8,128)(2,1)S(1)}, u32[]{:S(2)}, u32[]{:S(2)}) collective-permute-start(bf16[160,512]{1,0:T(8,128)(2,1)S(1)} %get-tuple-element.288), channel_id=1, source_target_pairs={{0,2},{2,0},{4,6},{6,4},{8,10},{10,8},{12,14},{14,12},{16,18},{18,... | collective-permute-start | bytes 491528 | tf_op jit(solution)/shard_map/ppermute | solution.py:28
  98.8 15.0 %collective-permute-start.24 = (bf16[160,512]{1,0:T(8,128)(2,1)S(1)}, bf16[160,512]{1,0:T(8,128)(2,1)S(1)}, u32[]{:S(2)}, u32[]{:S(2)}) collective-permute-start(bf16[160,512]{1,0:T(8,128)(2,1)S(1)} %get-tuple-element.289), channel_id=1, source_target_pairs={{0,4},{2,6},{4,0},{6,2},{8,12},{10,14},{12,8},{14,10},{16,20},{18,... | collective-permute-start | bytes 491528 | tf_op jit(solution)/shard_map/ppermute | solution.py:28
  100.2 13.5 %collective-permute-start.25 = (bf16[160,512]{1,0:T(8,128)(2,1)S(1)}, bf16[160,512]{1,0:T(8,128)(2,1)S(1)}, u32[]{:S(2)}, u32[]{:S(2)}) collective-permute-start(bf16[160,512]{1,0:T(8,128)(2,1)S(1)} %get-tuple-element.290), channel_id=1, source_target_pairs={{0,6},{2,4},{4,2},{6,0},{8,14},{10,12},{12,10},{14,8},{16,22},{18,... | collective-permute-start | bytes 491528 | tf_op jit(solution)/shard_map/ppermute | solution.py:28
  100.3 8.9 %collective-permute-start.21 = (bf16[80,512]{1,0:T(8,128)(2,1)S(1)}, bf16[80,512]{1,0:T(8,128)(2,1)S(1)}, u32[]{:S(2)}, u32[]{:S(2)}) collective-permute-start(bf16[80,512]{1,0:T(8,128)(2,1)S(1)} %get-tuple-element.285), channel_id=1, source_target_pairs={{0,16},{2,18},{4,20},{6,22},{8,24},{10,26},{12,28},{14,30},{16,0},... | collective-permute-start | bytes 245768 | tf_op jit(solution)/shard_map/ppermute | solution.py:28
  101.8 7.4 %collective-permute-start.22 = (bf16[80,512]{1,0:T(8,128)(2,1)S(1)}, bf16[80,512]{1,0:T(8,128)(2,1)S(1)}, u32[]{:S(2)}, u32[]{:S(2)}) collective-permute-start(bf16[80,512]{1,0:T(8,128)(2,1)S(1)} %get-tuple-element.286), channel_id=1, source_target_pairs={{0,24},{2,26},{4,28},{6,30},{8,16},{10,18},{12,20},{14,22},{16,8},... | collective-permute-start | bytes 245768 | tf_op jit(solution)/shard_map/ppermute | solution.py:28
  111.5 7.6 %collective-permute-start.27 = (bf16[80,512]{1,0:T(8,128)(2,1)S(1)}, bf16[80,512]{1,0:T(8,128)(2,1)S(1)}, u32[]{:S(2)}, u32[]{:S(2)}) collective-permute-start(bf16[80,512]{1,0:T(8,128)(2,1)S(1)} %shard_map.208.refs_0_), channel_id=1, source_target_pairs={{0,16},{2,18},{4,20},{6,22},{8,24},{10,26},{12,28},{14,30},{16,0},... | collective-permute-start | bytes 245768 | tf_op jit(solution)/shard_map/ppermute | solution.py:28
  120.3 36.8 %all-to-all-start.3 = ((bf16[4,320,512]{2,1,0:T(8,128)(2,1)}), bf16[4,320,512]{2,1,0:T(8,128)(2,1)S(1)}, u32[]{:S(2)}, u32[]{:S(2)}) async-start(bf16[4,320,512]{2,1,0:T(8,128)(2,1)} %shard_map.211), calls=%async_computation.3 | async-start | bytes 2621440 | tf_op jit(solution)/shard_map/all_to_all | solution.py:42
  124.7 10.4 %collective-permute-start.30 = (bf16[88,512]{1,0:T(8,128)(2,1)S(1)}, bf16[88,512]{1,0:T(8,128)(2,1)S(1)}, u32[]{:S(2)}, u32[]{:S(2)}) collective-permute-start(bf16[88,512]{1,0:T(8,128)(2,1)S(1)} %get-tuple-element.296), channel_id=1, source_target_pairs={{0,16},{2,18},{4,20},{6,22},{8,24},{10,26},{12,28},{14,30},{16,0},... | collective-permute-start | bytes 270344 | tf_op jit(solution)/shard_map/ppermute | solution.py:28
  145.2 16.7 %collective-permute-start.37 = (bf16[1,352,512]{2,1,0:T(8,128)(2,1)S(1)}, bf16[1,352,512]{2,1,0:T(8,128)(2,1)S(1)}, u32[]{:S(2)}, u32[]{:S(2)}) collective-permute-start(bf16[1,352,512]{2,1,0:T(8,128)(2,1)S(1)} %shard_map.213.refs_0_), channel_id=1, source_target_pairs={{0,6},{2,4},{4,2},{6,0},{8,14},{10,12},{12,10},{14,8},{16,22},{18,... | collective-permute-start | bytes 1081352 | tf_op jit(solution)/shard_map/ppermute | solution.py:28
  147.7 14.1 %collective-permute-start.36 = (bf16[1,352,512]{2,1,0:T(8,128)(2,1)S(1)}, bf16[1,352,512]{2,1,0:T(8,128)(2,1)S(1)}, u32[]{:S(2)}, u32[]{:S(2)}) collective-permute-start(bf16[1,352,512]{2,1,0:T(8,128)(2,1)S(1)} %shard_map.213.refs_0_), channel_id=1, source_target_pairs={{0,4},{2,6},{4,0},{6,2},{8,12},{10,14},{12,8},{14,10},{16,20},{18,... | collective-permute-start | bytes 1081352 | tf_op jit(solution)/shard_map/ppermute | solution.py:28
  148.3 13.6 %collective-permute-start.35 = (bf16[1,352,512]{2,1,0:T(8,128)(2,1)S(1)}, bf16[1,352,512]{2,1,0:T(8,128)(2,1)S(1)}, u32[]{:S(2)}, u32[]{:S(2)}) collective-permute-start(bf16[1,352,512]{2,1,0:T(8,128)(2,1)S(1)} %shard_map.213.refs_0_), channel_id=1, source_target_pairs={{0,2},{2,0},{4,6},{6,4},{8,10},{10,8},{12,14},{14,12},{16,18},{18,... | collective-permute-start | bytes 1081352 | tf_op jit(solution)/shard_map/ppermute | solution.py:28
  148.7 10.1 %collective-permute-start.39 = (bf16[128,512]{1,0:T(8,128)(2,1)}, bf16[128,512]{1,0:T(8,128)(2,1)S(1)}, u32[]{:S(2)}, u32[]{:S(2)}) collective-permute-start(bf16[128,512]{1,0:T(8,128)(2,1)} %get-tuple-element.308), channel_id=1, source_target_pairs={{0,16},{2,18},{4,20},{6,22},{8,24},{10,26},{12,28},{14,30},{16,0},... | collective-permute-start | bytes 393224 | tf_op jit(solution)/shard_map/ppermute | solution.py:28
  (27 other events, 268.4 us)

commit v6 on v5

--- a/solution.py
+++ b/solution.py
@@ -474,23 +474,28 @@
     dim = up.shape[0]
     per = dim // tile
 
-    def step(j, carry):
-        cols = pl.ds(pl.multiple_of(j * tile, tile), tile)
-        up_j = up[:, cols]
-        down_j = down[cols, :]
-        pre = mm(two[...], up_j)
-        back = mm(cots[...], down_j, 1, 1)
+    def products(j):
+        cols = slice(j * tile, (j + 1) * tile)
+        return mm(two[...], up[:, cols]), mm(cots[...], down[cols, :], 1, 1)
+
+    steps = width // tile
+    ready = products(0)
+    for j in range(steps):
+        cols = slice(j * tile, (j + 1) * tile)
+        pre, back = ready
+        if j + 1 < steps:
+            ready = products(j + 1)
         phi = 0.5 * (1.0 + lax.erf(pre * math.sqrt(0.5)))
         bell = jnp.exp(pre * pre * -0.5) * (1.0 / math.sqrt(2.0 * math.pi))
         act = (pre * phi).astype(BF)
         back_pre = (back * (phi + pre * bell)).astype(BF)
-        layer_out[...] += mm(act, down_j)
-        back_out[...] += mm(back_pre, up_j, 1, 1)
+        layer_out[...] += mm(act, down[cols, :])
+        back_out[...] += mm(back_pre, up[:, cols], 1, 1)
         grad = mm(act.T, cots[...]).astype(BF)
         grad_mine = mm(turned[mine, :], back_pre).astype(BF)
         grad_theirs = mm(turned[theirs, :], back_pre).astype(BF)
-        rows = pl.ds(pl.multiple_of((j // per) * half, half), half)
-        lane = pl.ds(pl.multiple_of((j % per) * tile, tile), tile)
+        rows = slice((j // per) * half, (j // per + 1) * half)
+        lane = slice((j % per) * tile, (j % per + 1) * tile)
         keep[rows, lane] = grad_mine
         if first:
             send[cols, :] = grad
@@ -498,9 +503,6 @@
         else:
             keep_down[cols, :] = grad
             send[rows, lane] = grad_theirs
-        return carry
-
-    lax.fori_loop(0, width // tile, step, 0)
     if not first:
         for k in range(count):
             layer_pieces[k][...] = slot_rows(layer_out[...], k, count).astype(layer_pieces[k].dtype)
@@ -1013,7 +1015,7 @@
         ],
     )
 
-    tile = 256
+    tile = 512
     upper = wide * tall // dim
     layer, back_two, send_one, keep_one, cots, cots_far, send_up, up_second, down_own = call(
         functools.partial(feed_body, count, rest, True, tile),

time: 165 us -> 164 us (level)
  transfers between devices with their start and end apart: 45 -> 45, of which waited for: 13 -> 13; matrix products, arithmetic and copies ran while one was open for 0% -> 0% of each run, Pallas kernels for 21% -> 20%
where the time goes in v6:
time: 164 us; the launch traced here: 163 us
  starting transfers between devices  70 us (43%)
  Pallas kernels  51.3 us (31%)
  waiting for transfers between devices  40.3 us (25%)
    ppermute x33, starting transfers between devices, swap(): return lax.ppermute(values, 'ctx', [(i, i ^ mask) for i in range(size)])  52.4 us
    pallas_call x21, Pallas kernels, call(): got = list(run(*args, *moved))  51.3 us
    ppermute x33, waiting for transfers between devices, swap(): return lax.ppermute(values, 'ctx', [(i, i ^ mask) for i in range(size)])  39.1 us
    all_to_all x4, starting transfers between devices, exchange(): lax.all_to_all(parts, 'ctx', 0, 0, tiled=True, axis_index_groups=groups)  15.8 us
  transfers between devices with their start and end apart: 45, of which 13 were waited for; matrix products, arithmetic and copies ran while one was open for 0% of the time, Pallas kernels for 20%

profile of v6, /device:TPU:0, one launch (start us, length us, event | category | flops | bytes accessed | tf_op | source)
XLA Modules:
  0.0 163.0 jit_solution(16881893519548823297)
XLA Ops:
  3.5 4.0 %collective-permute-start.1 = (bf16[136,512]{1,0:T(8,128)(2,1)S(1)}, bf16[136,512]{1,0:T(8,128)(2,1)S(1)}, u32[]{:S(2)}, u32[]{:S(2)}) collective-permute-start(bf16[136,512]{1,0:T(8,128)(2,1)S(1)} %get-tuple-element.167), channel_id=1, source_target_pairs={{0,16},{2,18},{4,20},{6,22},{8,24},{10,26},{12,28},{14,30},{16,0},... | collective-permute-start | bytes 417800 | tf_op jit(solution)/shard_map/ppermute | solution.py:28
  10.4 7.7 %collective-permute-done.1.refs_2_ = bf16[136,512]{1,0:T(8,128)(2,1)S(1)} collective-permute-done((bf16[136,512]{1,0:T(8,128)(2,1)S(1)}, bf16[136,512]{1,0:T(8,128)(2,1)S(1)}, u32[]{:S(2)}, u32[]{:S(2)}) %collective-permute-start.1) | collective-permute-done | bytes 139296 | tf_op jit(solution)/shard_map/ppermute | solution.py:28
  18.7 2.4 %shard_map.196 = (bf16[4,512,128]{2,1,0:T(8,128)(2,1)}, bf16[512,512]{1,0:T(8,128)(2,1)}, bf16[512,512]{1,0:T(8,128)(2,1)}, f32[8,512]{1,0:T(8,128)}, bf16[512,128]{1,0:T(8,128)(2,1)}, /*index=5*/f32[32,128]{1,0:T(8,128)S(1)}) custom-call(bf16[128,512]{1,0:T(8,128)(2,1)S(1)} %get-tuple-element.166.refs_0_, ...), custom_call_target="tpu_custom_call" | custom-call | flops 1 | bytes 1 | tf_op jit(solution)/shard_map/pallas_call | solution.py:171
  21.6 3.9 %all-to-all-start = ((bf16[4,512,128]{2,1,0:T(8,128)(2,1)}), bf16[4,512,128]{2,1,0:T(8,128)(2,1)S(1)}, u32[]{:S(2)}, u32[]{:S(2)}) async-start(bf16[4,512,128]{2,1,0:T(8,128)(2,1)} %get-tuple-element.174), calls=%async_computation | async-start | bytes 1048576 | tf_op jit(solution)/shard_map/all_to_all | solution.py:42
  25.5 2.3 %collective-permute-start.5 = (bf16[128,512]{1,0:T(8,128)(2,1)}, bf16[128,512]{1,0:T(8,128)(2,1)S(1)}, u32[]{:S(2)}, u32[]{:S(2)}) collective-permute-start(bf16[128,512]{1,0:T(8,128)(2,1)} %get-tuple-element.192), channel_id=1, source_target_pairs={{0,8},{2,10},{4,12},{6,14},{8,0},{10,2},{12,4},{14,6},{16,24},{18,... | collective-permute-start | bytes 393224 | tf_op jit(solution)/shard_map/ppermute | solution.py:28
  31.3 2.8 %shard_map.197 = (bf16[128,512]{1,0:T(8,128)(2,1)}, bf16[512,512]{1,0:T(8,128)(2,1)}, f32[2,512]{1,0:T(2,128)S(1)}, f32[2,512]{1,0:T(2,128)}, f32[8,512]{1,0:T(8...) custom-call(bf16[512,512]{1,0:T(8,128)(2,1)} %get-tuple-element.175.refs, ...), custom_call_target="tpu_custom_call" | custom-call | flops 1 | bytes 1 | tf_op jit(solution)/shard_map/pallas_call | solution.py:171
  34.1 5.7 %shard_map.198 = (f32[128,512]{1,0:T(8,128)}, f32[2,512]{1,0:T(2,128)}, bf16[512,512]{1,0:T(8,128)(2,1)}, f32[512,512]{1,0:T(8,128)S(1)}, bf16[512,512]{1,0:T(8,...) custom-call(s32[16]{0:T(128)S(1)} %copy-done.1, ...), custom_call_target="tpu_custom_call" | custom-call | flops 1 | bytes 1 | tf_op jit(solution)/shard_map/pallas_call | solution.py:171
  40.6 6.5 %shard_map.199 = (f32[512,512]{1,0:T(8,128)S(1)}, f32[512,512]{1,0:T(8,128)S(1)}, bf16[1024,512]{1,0:T(8,128)(2,1)S(1)}, bf16[512,512]{1,0:T(8,128)(2,1)}, bf16[...) custom-call(bf16[512,512]{1,0:T(8,128)(2,1)S(1)} %get-tuple-element., ...), custom_call_target="tpu_custom_call" | custom-call | flops 1 | bytes 1 | tf_op jit(solution)/shard_map/pallas_call | solution.py:171
  47.7 5.4 %shard_map.200 = (f32[128,512]{1,0:T(8,128)}, bf16[128,512]{1,0:T(8,128)(2,1)}, bf16[128,512]{1,0:T(8,128)(2,1)}, bf16[128,512]{1,0:T(8,128)(2,1)}, f32[512,512]...) custom-call(bf16[512,512]{1,0:T(8,128)(2,1)S(1)} %get-tuple-element., ...), custom_call_target="tpu_custom_call" | custom-call | flops 1 | bytes 1 | tf_op jit(solution)/shard_map/pallas_call | solution.py:171
  53.1 3.7 %shard_map.201 = (f32[512,512]{1,0:T(8,128)}, bf16[512,512]{1,0:T(8,128)(2,1)}, bf16[128,512]{1,0:T(8,128)(2,1)S(1)}, f32[2,512]{1,0:T(2,128)S(1)}, f32[8,512]{1...) custom-call(f32[512,512]{1,0:T(8,128)S(1)} %get-tuple-element.209.re, ...), custom_call_target="tpu_custom_call" | custom-call | flops 1 | bytes 1 | tf_op jit(solution)/shard_map/pallas_call | solution.py:171
  56.8 4.4 %all-to-all-start.2 = ((bf16[4,320,512]{2,1,0:T(8,128)(2,1)}), bf16[4,320,512]{2,1,0:T(8,128)(2,1)S(1)}, u32[]{:S(2)}, u32[]{:S(2)}) async-start(bf16[4,320,512]{2,1,0:T(8,128)(2,1)} %get-tuple-element.275), calls=%async_computation.2 | async-start | bytes 2621440 | tf_op jit(solution)/shard_map/all_to_all | solution.py:42
  61.1 2.4 %collective-permute-start.12 = (bf16[128,512]{1,0:T(8,128)(2,1)S(1)}, bf16[128,512]{1,0:T(8,128)(2,1)S(1)}, u32[]{:S(2)}, u32[]{:S(2)}) collective-permute-start(bf16[128,512]{1,0:T(8,128)(2,1)S(1)} %copy-done.11), channel_id=1, source_target_pairs={{0,8},{2,10},{4,12},{6,14},{8,0},{10,2},{12,4},{14,6},{16,24},{18,... | collective-permute-start | bytes 393224 | tf_op jit(solution)/shard_map/ppermute | solution.py:28
  66.6 6.6 %shard_map.202 = (bf16[128,512]{1,0:T(8,128)(2,1)S(1)}, f32[512,128]{1,0:T(8,128)}, bf16[512,128]{1,0:T(8,128)(2,1)}, bf16[512,128]{1,0:T(8,128)(2,1)}, bf16[512...) custom-call(s32[16]{0:T(128)S(1)} %copy-done.1, ...), custom_call_target="tpu_custom_call" | custom-call | flops 1 | bytes 1 | tf_op jit(solution)/shard_map/pallas_call | solution.py:171
  78.6 3.6 %shard_map.203 = (bf16[256,512]{1,0:T(8,128)(2,1)}, bf16[256,512]{1,0:T(8,128)(2,1)}, bf16[512,512]{1,0:T(8,128)(2,1)}, f32[512,512]{1,0:T(8,128)S(1)}, f32[512,...) custom-call(bf16[128,512]{1,0:T(8,128)(2,1)S(1)} %get-tuple-element., ...), custom_call_target="tpu_custom_call" | custom-call | flops 1 | bytes 1 | tf_op jit(solution)/shard_map/pallas_call | solution.py:171
  82.2 2.2 %collective-permute-done.17.refs_3_ = bf16[512,128]{1,0:T(8,128)(2,1)S(1)} collective-permute-done((bf16[512,128]{1,0:T(8,128)(2,1)}, bf16[512,128]{1,0:T(8,128)(2,1)S(1)}, u32[]{:S(2)}, u32[]{:S(2)}) %collective-permute-start.17) | collective-permute-done | bytes 131104 | tf_op jit(solution)/shard_map/ppermute | solution.py:28
  87.7 3.5 %all-to-all-start.1 = ((bf16[4,192,512]{2,1,0:T(8,128)(2,1)}), bf16[4,192,512]{2,1,0:T(8,128)(2,1)S(1)}, u32[]{:S(2)}, u32[]{:S(2)}) async-start(bf16[4,192,512]{2,1,0:T(8,128)(2,1)} %shard_map.205), calls=%async_computation.1 | async-start | bytes 1572864 | tf_op jit(solution)/shard_map/all_to_all | solution.py:42
  91.5 2.5 %collective-permute-start.20 = (bf16[80,512]{1,0:T(8,128)(2,1)S(1)}, bf16[80,512]{1,0:T(8,128)(2,1)S(1)}, u32[]{:S(2)}, u32[]{:S(2)}) collective-permute-start(bf16[80,512]{1,0:T(8,128)(2,1)S(1)} %get-tuple-element.284), channel_id=1, source_target_pairs={{0,8},{2,10},{4,12},{6,14},{8,0},{10,2},{12,4},{14,6},{16,24},{18,... | collective-permute-start | bytes 245768 | tf_op jit(solution)/shard_map/ppermute | solution.py:28
  101.9 6.0 %collective-permute-done.21.refs_2_ = bf16[80,512]{1,0:T(8,128)(2,1)S(1)} collective-permute-done((bf16[80,512]{1,0:T(8,128)(2,1)S(1)}, bf16[80,512]{1,0:T(8,128)(2,1)S(1)}, u32[]{:S(2)}, u32[]{:S(2)}) %collective-permute-start.21) | collective-permute-done | bytes 81952 | tf_op jit(solution)/shard_map/ppermute | solution.py:28
  108.0 2.3 %collective-permute-start.28 = (bf16[80,512]{1,0:T(8,128)(2,1)S(1)}, bf16[80,512]{1,0:T(8,128)(2,1)S(1)}, u32[]{:S(2)}, u32[]{:S(2)}) collective-permute-start(bf16[80,512]{1,0:T(8,128)(2,1)S(1)} %shard_map.208.refs_0_), channel_id=1, source_target_pairs={{0,24},{2,26},{4,28},{6,30},{8,16},{10,18},{12,20},{14,22},{16,8},... | collective-permute-start | bytes 245768 | tf_op jit(solution)/shard_map/ppermute | solution.py:28
  112.7 2.2 %shard_map.210 = f32[4,128,512]{2,1,0:T(8,128)} custom-call(f32[128,512]{1,0:T(8,128)} %get-tuple-element.292.refs_0_, bf16[128,512]{1,0:T(8,128)(2,1)} %copy-done.4, bf16[128,512]{1,0:T(8,128)(2,1)} %copy-done.5, bf16[128,512]{1,0:T(8,128)(2,1)} %copy-done.6), custom_call_target="tpu_custom_call" | custom-call | flops 1 | bytes 1 | tf_op jit(solution)/shard_map/pallas_call | solution.py:171
  114.9 2.9 %collective-permute-done.27.refs_2_ = bf16[80,512]{1,0:T(8,128)(2,1)S(1)} collective-permute-done((bf16[80,512]{1,0:T(8,128)(2,1)S(1)}, bf16[80,512]{1,0:T(8,128)(2,1)S(1)}, u32[]{:S(2)}, u32[]{:S(2)}) %collective-permute-start.27) | collective-permute-done | bytes 81952 | tf_op jit(solution)/shard_map/ppermute | solution.py:28
  119.0 4.0 %all-to-all-start.3 = ((bf16[4,320,512]{2,1,0:T(8,128)(2,1)}), bf16[4,320,512]{2,1,0:T(8,128)(2,1)S(1)}, u32[]{:S(2)}, u32[]{:S(2)}) async-start(bf16[4,320,512]{2,1,0:T(8,128)(2,1)} %shard_map.211), calls=%async_computation.3 | async-start | bytes 2621440 | tf_op jit(solution)/shard_map/all_to_all | solution.py:42
  123.5 3.4 %collective-permute-start.30 = (bf16[88,512]{1,0:T(8,128)(2,1)S(1)}, bf16[88,512]{1,0:T(8,128)(2,1)S(1)}, u32[]{:S(2)}, u32[]{:S(2)}) collective-permute-start(bf16[88,512]{1,0:T(8,128)(2,1)S(1)} %get-tuple-element.296), channel_id=1, source_target_pairs={{0,16},{2,18},{4,20},{6,22},{8,24},{10,26},{12,28},{14,30},{16,0},... | collective-permute-start | bytes 270344 | tf_op jit(solution)/shard_map/ppermute | solution.py:28
  128.5 5.4 %collective-permute-done.30.refs_2_ = bf16[88,512]{1,0:T(8,128)(2,1)S(1)} collective-permute-done((bf16[88,512]{1,0:T(8,128)(2,1)S(1)}, bf16[88,512]{1,0:T(8,128)(2,1)S(1)}, u32[]{:S(2)}, u32[]{:S(2)}) %collective-permute-start.30) | collective-permute-done | bytes 90144 | tf_op jit(solution)/shard_map/ppermute | solution.py:28
  134.0 2.5 %collective-permute-start.34 = (bf16[88,512]{1,0:T(8,128)(2,1)S(1)}, bf16[88,512]{1,0:T(8,128)(2,1)S(1)}, u32[]{:S(2)}, u32[]{:S(2)}) collective-permute-start(bf16[88,512]{1,0:T(8,128)(2,1)S(1)} %shard_map.212.refs_0_), channel_id=1, source_target_pairs={{0,24},{2,26},{4,28},{6,30},{8,16},{10,18},{12,20},{14,22},{16,8},... | collective-permute-start | bytes 270344 | tf_op jit(solution)/shard_map/ppermute | solution.py:28
  138.4 2.9 %collective-permute-done.34.refs_3_ = bf16[88,512]{1,0:T(8,128)(2,1)S(1)} collective-permute-done((bf16[88,512]{1,0:T(8,128)(2,1)S(1)}, bf16[88,512]{1,0:T(8,128)(2,1)S(1)}, u32[]{:S(2)}, u32[]{:S(2)}) %collective-permute-start.34) | collective-permute-done | bytes 90144 | tf_op jit(solution)/shard_map/ppermute | solution.py:28
  141.3 2.5 %collective-permute-done.33.refs_2_ = bf16[88,512]{1,0:T(8,128)(2,1)S(1)} collective-permute-done((bf16[88,512]{1,0:T(8,128)(2,1)S(1)}, bf16[88,512]{1,0:T(8,128)(2,1)S(1)}, u32[]{:S(2)}, u32[]{:S(2)}) %collective-permute-start.33) | collective-permute-done | bytes 90144 | tf_op jit(solution)/shard_map/ppermute | solution.py:28
  143.9 2.6 %collective-permute-start.37 = (bf16[1,352,512]{2,1,0:T(8,128)(2,1)S(1)}, bf16[1,352,512]{2,1,0:T(8,128)(2,1)S(1)}, u32[]{:S(2)}, u32[]{:S(2)}) collective-permute-start(bf16[1,352,512]{2,1,0:T(8,128)(2,1)S(1)} %shard_map.213.refs_0_), channel_id=1, source_target_pairs={{0,6},{2,4},{4,2},{6,0},{8,14},{10,12},{12,10},{14,8},{16,22},{18,... | collective-permute-start | bytes 1081352 | tf_op jit(solution)/shard_map/ppermute | solution.py:28
  147.5 2.4 %collective-permute-start.39 = (bf16[128,512]{1,0:T(8,128)(2,1)}, bf16[128,512]{1,0:T(8,128)(2,1)S(1)}, u32[]{:S(2)}, u32[]{:S(2)}) collective-permute-start(bf16[128,512]{1,0:T(8,128)(2,1)} %get-tuple-element.308), channel_id=1, source_target_pairs={{0,16},{2,18},{4,20},{6,22},{8,24},{10,26},{12,28},{14,30},{16,0},... | collective-permute-start | bytes 393224 | tf_op jit(solution)/shard_map/ppermute | solution.py:28
  149.8 4.0 %collective-permute-done.38.refs_6_ = bf16[128,512]{1,0:T(8,128)(2,1)S(1)} collective-permute-done((bf16[128,512]{1,0:T(8,128)(2,1)S(1)}, bf16[128,512]{1,0:T(8,128)(2,1)S(1)}, u32[]{:S(2)}, u32[]{:S(2)}) %collective-permute-start.38) | collective-permute-done | bytes 131104 | tf_op jit(solution)/shard_map/ppermute | solution.py:28
  157.5 3.1 %collective-permute-done.40.refs_8_ = bf16[128,512]{1,0:T(8,128)(2,1)S(1)} collective-permute-done((bf16[128,512]{1,0:T(8,128)(2,1)S(1)}, bf16[128,512]{1,0:T(8,128)(2,1)S(1)}, u32[]{:S(2)}, u32[]{:S(2)}) %collective-permute-start.40) | collective-permute-done | bytes 131104 | tf_op jit(solution)/shard_map/ppermute | solution.py:28
  160.6 2.2 %shard_map.215 = (f32[256,2048]{1,0:T(8,128)}, f32[256,512]{1,0:T(8,128)}, f32[256,512]{1,0:T(8,128)}, f32[256,128]{1,0:T(8,128)}, f32[8,256]{1,0:T(8,128)}, /*i...) custom-call(bf16[1,352,512]{2,1,0:T(8,128)(2,1)S(1)} %shard_map.213.refs_0_, ...), custom_call_target="tpu_custom_call" | custom-call | flops 1 | bytes 1 | tf_op jit(solution)/shard_map/pallas_call | solution.py:171
  (110 shorter events, 44.0 us)
Async XLA Ops:
  2.9 15.8 %collective-permute-start.4 = (bf16[264,1152]{1,0:T(8,128)(2,1)S(1)}, bf16[264,1152]{1,0:T(8,128)(2,1)S(1)}, u32[]{:S(2)}, u32[]{:S(2)}) collective-permute-start(bf16[264,1152]{1,0:T(8,128)(2,1)S(1)} %get-tuple-element.169), channel_id=1, source_target_pairs={{0,1},{1,0},{2,3},{3,2},{4,5},{5,4},{6,7},{7,6},{8,9},{9,8},{10,11... | collective-permute-start | bytes 1824776 | tf_op jit(solution)/shard_map/ppermute | solution.py:46
  3.5 14.5 %collective-permute-start.1 = (bf16[136,512]{1,0:T(8,128)(2,1)S(1)}, bf16[136,512]{1,0:T(8,128)(2,1)S(1)}, u32[]{:S(2)}, u32[]{:S(2)}) collective-permute-start(bf16[136,512]{1,0:T(8,128)(2,1)S(1)} %get-tuple-element.167), channel_id=1, source_target_pairs={{0,16},{2,18},{4,20},{6,22},{8,24},{10,26},{12,28},{14,30},{16,0},... | collective-permute-start | bytes 417800 | tf_op jit(solution)/shard_map/ppermute | solution.py:28
  7.5 10.5 %collective-permute-start.2 = (bf16[136,512]{1,0:T(8,128)(2,1)S(1)}, bf16[136,512]{1,0:T(8,128)(2,1)S(1)}, u32[]{:S(2)}, u32[]{:S(2)}) collective-permute-start(bf16[136,512]{1,0:T(8,128)(2,1)S(1)} %get-tuple-element.168), channel_id=1, source_target_pairs={{0,24},{2,26},{4,28},{6,30},{8,16},{10,18},{12,20},{14,22},{16,8},... | collective-permute-start | bytes 417800 | tf_op jit(solution)/shard_map/ppermute | solution.py:28
  8.9 9.8 %collective-permute-start = (bf16[136,512]{1,0:T(8,128)(2,1)S(1)}, bf16[136,512]{1,0:T(8,128)(2,1)S(1)}, u32[]{:S(2)}, u32[]{:S(2)}) collective-permute-start(bf16[136,512]{1,0:T(8,128)(2,1)S(1)} %get-tuple-element.165), channel_id=1, source_target_pairs={{0,8},{2,10},{4,12},{6,14},{8,0},{10,2},{12,4},{14,6},{16,24},{18,... | collective-permute-start | bytes 417800 | tf_op jit(solution)/shard_map/ppermute | solution.py:28
  21.1 19.5 %collective-permute-start.8 = (bf16[256,2048]{1,0:T(8,128)(2,1)}, bf16[256,2048]{1,0:T(8,128)(2,1)S(1)}, u32[]{:S(2)}, u32[]{:S(2)}) collective-permute-start(bf16[256,2048]{1,0:T(8,128)(2,1)} %refs_10_.3), channel_id=1, source_target_pairs={{0,1},{1,0},{2,3},{3,2},{4,5},{5,4},{6,7},{7,6},{8,9},{9,8},{10,11... | collective-permute-start | bytes 3145736 | tf_op jit(solution)/shard_map/ppermute | solution.py:46
  21.1 19.5 %collective-permute-start.9 = (bf16[1024,512]{1,0:T(8,128)(2,1)}, bf16[1024,512]{1,0:T(8,128)(2,1)S(1)}, u32[]{:S(2)}, u32[]{:S(2)}) collective-permute-start(bf16[1024,512]{1,0:T(8,128)(2,1)} %refs_11_.1), channel_id=1, source_target_pairs={{0,1},{1,0},{2,3},{3,2},{4,5},{5,4},{6,7},{7,6},{8,9},{9,8},{10,11... | collective-permute-start | bytes 3145736 | tf_op jit(solution)/shard_map/ppermute | solution.py:46
  21.6 12.5 %all-to-all-start = ((bf16[4,512,128]{2,1,0:T(8,128)(2,1)}), bf16[4,512,128]{2,1,0:T(8,128)(2,1)S(1)}, u32[]{:S(2)}, u32[]{:S(2)}) async-start(bf16[4,512,128]{2,1,0:T(8,128)(2,1)} %get-tuple-element.174), calls=%async_computation | async-start | bytes 1048576 | tf_op jit(solution)/shard_map/all_to_all | solution.py:42
  25.5 14.3 %collective-permute-start.5 = (bf16[128,512]{1,0:T(8,128)(2,1)}, bf16[128,512]{1,0:T(8,128)(2,1)S(1)}, u32[]{:S(2)}, u32[]{:S(2)}) collective-permute-start(bf16[128,512]{1,0:T(8,128)(2,1)} %get-tuple-element.192), channel_id=1, source_target_pairs={{0,8},{2,10},{4,12},{6,14},{8,0},{10,2},{12,4},{14,6},{16,24},{18,... | collective-permute-start | bytes 393224 | tf_op jit(solution)/shard_map/ppermute | solution.py:28
  27.9 12.0 %collective-permute-start.6 = (bf16[128,512]{1,0:T(8,128)(2,1)}, bf16[128,512]{1,0:T(8,128)(2,1)S(1)}, u32[]{:S(2)}, u32[]{:S(2)}) collective-permute-start(bf16[128,512]{1,0:T(8,128)(2,1)} %copy-done.3), channel_id=1, source_target_pairs={{0,16},{2,18},{4,20},{6,22},{8,24},{10,26},{12,28},{14,30},{16,0},... | collective-permute-start | bytes 393224 | tf_op jit(solution)/shard_map/ppermute | solution.py:28
  29.8 10.8 %collective-permute-start.7 = (bf16[128,512]{1,0:T(8,128)(2,1)}, bf16[128,512]{1,0:T(8,128)(2,1)}, u32[]{:S(2)}, u32[]{:S(2)}) collective-permute-start(bf16[128,512]{1,0:T(8,128)(2,1)} %copy-done.2), channel_id=1, source_target_pairs={{0,24},{2,26},{4,28},{6,30},{8,16},{10,18},{12,20},{14,22},{16,8},... | collective-permute-start | bytes 393224 | tf_op jit(solution)/shard_map/ppermute | solution.py:28
  56.8 30.9 %all-to-all-start.2 = ((bf16[4,320,512]{2,1,0:T(8,128)(2,1)}), bf16[4,320,512]{2,1,0:T(8,128)(2,1)S(1)}, u32[]{:S(2)}, u32[]{:S(2)}) async-start(bf16[4,320,512]{2,1,0:T(8,128)(2,1)} %get-tuple-element.275), calls=%async_computation.2 | async-start | bytes 2621440 | tf_op jit(solution)/shard_map/all_to_all | solution.py:42
  61.1 14.1 %collective-permute-start.12 = (bf16[128,512]{1,0:T(8,128)(2,1)S(1)}, bf16[128,512]{1,0:T(8,128)(2,1)S(1)}, u32[]{:S(2)}, u32[]{:S(2)}) collective-permute-start(bf16[128,512]{1,0:T(8,128)(2,1)S(1)} %copy-done.11), channel_id=1, source_target_pairs={{0,8},{2,10},{4,12},{6,14},{8,0},{10,2},{12,4},{14,6},{16,24},{18,... | collective-permute-start | bytes 393224 | tf_op jit(solution)/shard_map/ppermute | solution.py:28
  63.6 13.1 %collective-permute-start.13 = (bf16[128,512]{1,0:T(8,128)(2,1)S(1)}, bf16[128,512]{1,0:T(8,128)(2,1)S(1)}, u32[]{:S(2)}, u32[]{:S(2)}) collective-permute-start(bf16[128,512]{1,0:T(8,128)(2,1)S(1)} %copy-done.10), channel_id=1, source_target_pairs={{0,16},{2,18},{4,20},{6,22},{8,24},{10,26},{12,28},{14,30},{16,0},... | collective-permute-start | bytes 393224 | tf_op jit(solution)/shard_map/ppermute | solution.py:28
  65.1 21.5 %collective-permute-start.18 = (bf16[512,512]{1,0:T(8,128)(2,1)}, bf16[512,512]{1,0:T(8,128)(2,1)S(1)}, u32[]{:S(2)}, u32[]{:S(2)}) collective-permute-start(bf16[512,512]{1,0:T(8,128)(2,1)} %get-tuple-element.274), channel_id=1, source_target_pairs={{0,1},{1,0},{2,3},{3,2},{4,5},{5,4},{6,7},{7,6},{8,9},{9,8},{10,11... | collective-permute-start | bytes 1572872 | tf_op jit(solution)/shard_map/ppermute | solution.py:46
  65.1 13.5 %collective-permute-start.14 = (bf16[128,512]{1,0:T(8,128)(2,1)S(1)}, bf16[128,512]{1,0:T(8,128)(2,1)S(1)}, u32[]{:S(2)}, u32[]{:S(2)}) collective-permute-start(bf16[128,512]{1,0:T(8,128)(2,1)S(1)} %copy-done.9), channel_id=1, source_target_pairs={{0,24},{2,26},{4,28},{6,30},{8,16},{10,18},{12,20},{14,22},{16,8},... | collective-permute-start | bytes 393224 | tf_op jit(solution)/shard_map/ppermute | solution.py:28
  73.1 9.0 %collective-permute-start.15 = (bf16[512,128]{1,0:T(8,128)(2,1)}, bf16[512,128]{1,0:T(8,128)(2,1)S(1)}, u32[]{:S(2)}, u32[]{:S(2)}) collective-permute-start(bf16[512,128]{1,0:T(8,128)(2,1)} %get-tuple-element.256), channel_id=1, source_target_pairs={{0,2},{2,0},{4,6},{6,4},{8,10},{10,8},{12,14},{14,12},{16,18},{18,... | collective-permute-start | bytes 393224 | tf_op jit(solution)/shard_map/ppermute | solution.py:28
  76.7 7.7 %collective-permute-start.17 = (bf16[512,128]{1,0:T(8,128)(2,1)}, bf16[512,128]{1,0:T(8,128)(2,1)S(1)}, u32[]{:S(2)}, u32[]{:S(2)}) collective-permute-start(bf16[512,128]{1,0:T(8,128)(2,1)} %get-tuple-element.258), channel_id=1, source_target_pairs={{0,6},{2,4},{4,2},{6,0},{8,14},{10,12},{12,10},{14,8},{16,22},{18,... | collective-permute-start | bytes 393224 | tf_op jit(solution)/shard_map/ppermute | solution.py:28
  86.5 7.5 %collective-permute-start.19 = (bf16[592,512]{1,0:T(8,128)(2,1)S(1)}, bf16[592,512]{1,0:T(8,128)(2,1)S(1)}, u32[]{:S(2)}, u32[]{:S(2)}) collective-permute-start(bf16[592,512]{1,0:T(8,128)(2,1)S(1)} %get-tuple-element.278), channel_id=1, source_target_pairs={{0,1},{1,0},{2,3},{3,2},{4,5},{5,4},{6,7},{7,6},{8,9},{9,8},{10,11... | collective-permute-start | bytes 1818632 | tf_op jit(solution)/shard_map/ppermute | solution.py:46
  87.7 24.7 %all-to-all-start.1 = ((bf16[4,192,512]{2,1,0:T(8,128)(2,1)}), bf16[4,192,512]{2,1,0:T(8,128)(2,1)S(1)}, u32[]{:S(2)}, u32[]{:S(2)}) async-start(bf16[4,192,512]{2,1,0:T(8,128)(2,1)} %shard_map.205), calls=%async_computation.1 | async-start | bytes 1572864 | tf_op jit(solution)/shard_map/all_to_all | solution.py:42
  91.5 9.0 %collective-permute-start.20 = (bf16[80,512]{1,0:T(8,128)(2,1)S(1)}, bf16[80,512]{1,0:T(8,128)(2,1)S(1)}, u32[]{:S(2)}, u32[]{:S(2)}) collective-permute-start(bf16[80,512]{1,0:T(8,128)(2,1)S(1)} %get-tuple-element.284), channel_id=1, source_target_pairs={{0,8},{2,10},{4,12},{6,14},{8,0},{10,2},{12,4},{14,6},{16,24},{18,... | collective-permute-start | bytes 245768 | tf_op jit(solution)/shard_map/ppermute | solution.py:28
  95.4 15.6 %collective-permute-start.23 = (bf16[160,512]{1,0:T(8,128)(2,1)S(1)}, bf16[160,512]{1,0:T(8,128)(2,1)S(1)}, u32[]{:S(2)}, u32[]{:S(2)}) collective-permute-start(bf16[160,512]{1,0:T(8,128)(2,1)S(1)} %get-tuple-element.288), channel_id=1, source_target_pairs={{0,2},{2,0},{4,6},{6,4},{8,10},{10,8},{12,14},{14,12},{16,18},{18,... | collective-permute-start | bytes 491528 | tf_op jit(solution)/shard_map/ppermute | solution.py:28
  97.4 15.0 %collective-permute-start.24 = (bf16[160,512]{1,0:T(8,128)(2,1)S(1)}, bf16[160,512]{1,0:T(8,128)(2,1)S(1)}, u32[]{:S(2)}, u32[]{:S(2)}) collective-permute-start(bf16[160,512]{1,0:T(8,128)(2,1)S(1)} %get-tuple-element.289), channel_id=1, source_target_pairs={{0,4},{2,6},{4,0},{6,2},{8,12},{10,14},{12,8},{14,10},{16,20},{18,... | collective-permute-start | bytes 491528 | tf_op jit(solution)/shard_map/ppermute | solution.py:28
  98.9 13.5 %collective-permute-start.25 = (bf16[160,512]{1,0:T(8,128)(2,1)S(1)}, bf16[160,512]{1,0:T(8,128)(2,1)S(1)}, u32[]{:S(2)}, u32[]{:S(2)}) collective-permute-start(bf16[160,512]{1,0:T(8,128)(2,1)S(1)} %get-tuple-element.290), channel_id=1, source_target_pairs={{0,6},{2,4},{4,2},{6,0},{8,14},{10,12},{12,10},{14,8},{16,22},{18,... | collective-permute-start | bytes 491528 | tf_op jit(solution)/shard_map/ppermute | solution.py:28
  99.0 8.9 %collective-permute-start.21 = (bf16[80,512]{1,0:T(8,128)(2,1)S(1)}, bf16[80,512]{1,0:T(8,128)(2,1)S(1)}, u32[]{:S(2)}, u32[]{:S(2)}) collective-permute-start(bf16[80,512]{1,0:T(8,128)(2,1)S(1)} %get-tuple-element.285), channel_id=1, source_target_pairs={{0,16},{2,18},{4,20},{6,22},{8,24},{10,26},{12,28},{14,30},{16,0},... | collective-permute-start | bytes 245768 | tf_op jit(solution)/shard_map/ppermute | solution.py:28
  100.5 7.4 %collective-permute-start.22 = (bf16[80,512]{1,0:T(8,128)(2,1)S(1)}, bf16[80,512]{1,0:T(8,128)(2,1)S(1)}, u32[]{:S(2)}, u32[]{:S(2)}) collective-permute-start(bf16[80,512]{1,0:T(8,128)(2,1)S(1)} %get-tuple-element.286), channel_id=1, source_target_pairs={{0,24},{2,26},{4,28},{6,30},{8,16},{10,18},{12,20},{14,22},{16,8},... | collective-permute-start | bytes 245768 | tf_op jit(solution)/shard_map/ppermute | solution.py:28
  110.2 7.6 %collective-permute-start.27 = (bf16[80,512]{1,0:T(8,128)(2,1)S(1)}, bf16[80,512]{1,0:T(8,128)(2,1)S(1)}, u32[]{:S(2)}, u32[]{:S(2)}) collective-permute-start(bf16[80,512]{1,0:T(8,128)(2,1)S(1)} %shard_map.208.refs_0_), channel_id=1, source_target_pairs={{0,16},{2,18},{4,20},{6,22},{8,24},{10,26},{12,28},{14,30},{16,0},... | collective-permute-start | bytes 245768 | tf_op jit(solution)/shard_map/ppermute | solution.py:28
  119.0 36.8 %all-to-all-start.3 = ((bf16[4,320,512]{2,1,0:T(8,128)(2,1)}), bf16[4,320,512]{2,1,0:T(8,128)(2,1)S(1)}, u32[]{:S(2)}, u32[]{:S(2)}) async-start(bf16[4,320,512]{2,1,0:T(8,128)(2,1)} %shard_map.211), calls=%async_computation.3 | async-start | bytes 2621440 | tf_op jit(solution)/shard_map/all_to_all | solution.py:42
  123.5 10.4 %collective-permute-start.30 = (bf16[88,512]{1,0:T(8,128)(2,1)S(1)}, bf16[88,512]{1,0:T(8,128)(2,1)S(1)}, u32[]{:S(2)}, u32[]{:S(2)}) collective-permute-start(bf16[88,512]{1,0:T(8,128)(2,1)S(1)} %get-tuple-element.296), channel_id=1, source_target_pairs={{0,16},{2,18},{4,20},{6,22},{8,24},{10,26},{12,28},{14,30},{16,0},... | collective-permute-start | bytes 270344 | tf_op jit(solution)/shard_map/ppermute | solution.py:28
  143.9 16.7 %collective-permute-start.37 = (bf16[1,352,512]{2,1,0:T(8,128)(2,1)S(1)}, bf16[1,352,512]{2,1,0:T(8,128)(2,1)S(1)}, u32[]{:S(2)}, u32[]{:S(2)}) collective-permute-start(bf16[1,352,512]{2,1,0:T(8,128)(2,1)S(1)} %shard_map.213.refs_0_), channel_id=1, source_target_pairs={{0,6},{2,4},{4,2},{6,0},{8,14},{10,12},{12,10},{14,8},{16,22},{18,... | collective-permute-start | bytes 1081352 | tf_op jit(solution)/shard_map/ppermute | solution.py:28
  146.5 14.1 %collective-permute-start.36 = (bf16[1,352,512]{2,1,0:T(8,128)(2,1)S(1)}, bf16[1,352,512]{2,1,0:T(8,128)(2,1)S(1)}, u32[]{:S(2)}, u32[]{:S(2)}) collective-permute-start(bf16[1,352,512]{2,1,0:T(8,128)(2,1)S(1)} %shard_map.213.refs_0_), channel_id=1, source_target_pairs={{0,4},{2,6},{4,0},{6,2},{8,12},{10,14},{12,8},{14,10},{16,20},{18,... | collective-permute-start | bytes 1081352 | tf_op jit(solution)/shard_map/ppermute | solution.py:28
  147.0 13.6 %collective-permute-start.35 = (bf16[1,352,512]{2,1,0:T(8,128)(2,1)S(1)}, bf16[1,352,512]{2,1,0:T(8,128)(2,1)S(1)}, u32[]{:S(2)}, u32[]{:S(2)}) collective-permute-start(bf16[1,352,512]{2,1,0:T(8,128)(2,1)S(1)} %shard_map.213.refs_0_), channel_id=1, source_target_pairs={{0,2},{2,0},{4,6},{6,4},{8,10},{10,8},{12,14},{14,12},{16,18},{18,... | collective-permute-start | bytes 1081352 | tf_op jit(solution)/shard_map/ppermute | solution.py:28
  147.5 10.1 %collective-permute-start.39 = (bf16[128,512]{1,0:T(8,128)(2,1)}, bf16[128,512]{1,0:T(8,128)(2,1)S(1)}, u32[]{:S(2)}, u32[]{:S(2)}) collective-permute-start(bf16[128,512]{1,0:T(8,128)(2,1)} %get-tuple-element.308), channel_id=1, source_target_pairs={{0,16},{2,18},{4,20},{6,22},{8,24},{10,26},{12,28},{14,30},{16,0},... | collective-permute-start | bytes 393224 | tf_op jit(solution)/shard_map/ppermute | solution.py:28
  (27 other events, 266.3 us)

commit v7 on v6

--- a/solution.py
+++ b/solution.py
@@ -1200,7 +1200,6 @@
         ],
         main_rows,
     )
-    early_terms = inner([early], early_rows)
     pieces = call(
         functools.partial(
             start_body,
@@ -1219,6 +1218,7 @@
         scratch=[((late_rows, WIDTH), F32)],
     )
     late = pieces[:1] + [swap(pieces[j], j, size) for j in range(1, first)]
+    early_terms = inner([early], early_rows)
     early_got = outer(spread(settle(early_terms), strides, last, size))
     heights = [main_rows // first, late_rows // first]
     chunks = [[main], late]

time: 164 us -> 163 us (level)
  transfers between devices with their start and end apart: 45 -> 45, of which waited for: 13 -> 16; matrix products, arithmetic and copies ran while one was open for 0% -> 0% of each run, Pallas kernels for 20% -> 20%
where the time goes in v7:
time: 163 us
  starting transfers between devices  71.1 us (44%)
  Pallas kernels  51.3 us (31%)
  waiting for transfers between devices  38.8 us (24%)
    ppermute x33, starting transfers between devices, swap(): return lax.ppermute(values, 'ctx', [(i, i ^ mask) for i in range(size)])  53.5 us
    pallas_call x21, Pallas kernels, call(): got = list(run(*args, *moved))  51.3 us
    ppermute x33, waiting for transfers between devices, swap(): return lax.ppermute(values, 'ctx', [(i, i ^ mask) for i in range(size)])  37.7 us
    all_to_all x4, starting transfers between devices, exchange(): lax.all_to_all(parts, 'ctx', 0, 0, tiled=True, axis_index_groups=groups)  15.8 us
  transfers between devices with their start and end apart: 45, of which 16 were waited for; matrix products, arithmetic and copies ran while one was open for 0% of the time, Pallas kernels for 20%

profile of v7, /device:TPU:0, one launch (start us, length us, event | category | flops | bytes accessed | tf_op | source)
XLA Modules:
  0.0 162.6 jit_solution(16521685081835712896)
XLA Ops:
  3.5 4.0 %collective-permute-start.1 = (bf16[136,512]{1,0:T(8,128)(2,1)S(1)}, bf16[136,512]{1,0:T(8,128)(2,1)S(1)}, u32[]{:S(2)}, u32[]{:S(2)}) collective-permute-start(bf16[136,512]{1,0:T(8,128)(2,1)S(1)} %get-tuple-element.166), channel_id=1, source_target_pairs={{0,16},{2,18},{4,20},{6,22},{8,24},{10,26},{12,28},{14,30},{16,0},... | collective-permute-start | bytes 417800 | tf_op jit(solution)/shard_map/ppermute | solution.py:28
  10.4 7.7 %collective-permute-done.1.refs_2_ = bf16[136,512]{1,0:T(8,128)(2,1)S(1)} collective-permute-done((bf16[136,512]{1,0:T(8,128)(2,1)S(1)}, bf16[136,512]{1,0:T(8,128)(2,1)S(1)}, u32[]{:S(2)}, u32[]{:S(2)}) %collective-permute-start.1) | collective-permute-done | bytes 139296 | tf_op jit(solution)/shard_map/ppermute | solution.py:28
  18.7 2.4 %shard_map.196 = (bf16[4,512,128]{2,1,0:T(8,128)(2,1)}, bf16[512,512]{1,0:T(8,128)(2,1)}, bf16[512,512]{1,0:T(8,128)(2,1)}, f32[8,512]{1,0:T(8,128)}, bf16[512,128]{1,0:T(8,128)(2,1)}, /*index=5*/f32[32,128]{1,0:T(8,128)S(1)}) custom-call(bf16[128,512]{1,0:T(8,128)(2,1)S(1)} %get-tuple-element.165.refs_0_, ...), custom_call_target="tpu_custom_call" | custom-call | flops 1 | bytes 1 | tf_op jit(solution)/shard_map/pallas_call | solution.py:171
  21.6 3.9 %all-to-all-start = ((bf16[4,512,128]{2,1,0:T(8,128)(2,1)}), bf16[4,512,128]{2,1,0:T(8,128)(2,1)S(1)}, u32[]{:S(2)}, u32[]{:S(2)}) async-start(bf16[4,512,128]{2,1,0:T(8,128)(2,1)} %get-tuple-element.173), calls=%async_computation | async-start | bytes 1048576 | tf_op jit(solution)/shard_map/all_to_all | solution.py:42
  25.5 2.3 %collective-permute-start.5 = (bf16[128,512]{1,0:T(8,128)(2,1)}, bf16[128,512]{1,0:T(8,128)(2,1)S(1)}, u32[]{:S(2)}, u32[]{:S(2)}) collective-permute-start(bf16[128,512]{1,0:T(8,128)(2,1)} %get-tuple-element.191), channel_id=1, source_target_pairs={{0,8},{2,10},{4,12},{6,14},{8,0},{10,2},{12,4},{14,6},{16,24},{18,... | collective-permute-start | bytes 393224 | tf_op jit(solution)/shard_map/ppermute | solution.py:28
  31.3 2.8 %shard_map.197 = (bf16[128,512]{1,0:T(8,128)(2,1)}, bf16[512,512]{1,0:T(8,128)(2,1)}, f32[2,512]{1,0:T(2,128)S(1)}, f32[2,512]{1,0:T(2,128)}, f32[8,512]{1,0:T(8...) custom-call(bf16[512,512]{1,0:T(8,128)(2,1)} %get-tuple-element.174.refs, ...), custom_call_target="tpu_custom_call" | custom-call | flops 1 | bytes 1 | tf_op jit(solution)/shard_map/pallas_call | solution.py:171
  34.1 5.7 %shard_map.198 = (f32[128,512]{1,0:T(8,128)}, f32[2,512]{1,0:T(2,128)}, bf16[512,512]{1,0:T(8,128)(2,1)}, f32[512,512]{1,0:T(8,128)S(1)}, bf16[512,512]{1,0:T(8,...) custom-call(s32[16]{0:T(128)S(1)} %copy-done.1, ...), custom_call_target="tpu_custom_call" | custom-call | flops 1 | bytes 1 | tf_op jit(solution)/shard_map/pallas_call | solution.py:171
  40.6 6.5 %shard_map.199 = (f32[512,512]{1,0:T(8,128)S(1)}, f32[512,512]{1,0:T(8,128)S(1)}, bf16[1024,512]{1,0:T(8,128)(2,1)S(1)}, bf16[512,512]{1,0:T(8,128)(2,1)}, bf16[...) custom-call(bf16[512,512]{1,0:T(8,128)(2,1)S(1)} %get-tuple-element., ...), custom_call_target="tpu_custom_call" | custom-call | flops 1 | bytes 1 | tf_op jit(solution)/shard_map/pallas_call | solution.py:171
  47.7 5.4 %shard_map.200 = (f32[128,512]{1,0:T(8,128)}, bf16[128,512]{1,0:T(8,128)(2,1)}, bf16[128,512]{1,0:T(8,128)(2,1)}, bf16[128,512]{1,0:T(8,128)(2,1)}, f32[512,512]...) custom-call(bf16[512,512]{1,0:T(8,128)(2,1)S(1)} %get-tuple-element., ...), custom_call_target="tpu_custom_call" | custom-call | flops 1 | bytes 1 | tf_op jit(solution)/shard_map/pallas_call | solution.py:171
  53.1 3.7 %shard_map.201 = (f32[512,512]{1,0:T(8,128)}, bf16[512,512]{1,0:T(8,128)(2,1)}, bf16[128,512]{1,0:T(8,128)(2,1)S(1)}, f32[2,512]{1,0:T(2,128)S(1)}, f32[8,512]{1...) custom-call(f32[512,512]{1,0:T(8,128)S(1)} %get-tuple-element.208.re, ...), custom_call_target="tpu_custom_call" | custom-call | flops 1 | bytes 1 | tf_op jit(solution)/shard_map/pallas_call | solution.py:171
  56.8 4.4 %all-to-all-start.2 = ((bf16[4,320,512]{2,1,0:T(8,128)(2,1)}), bf16[4,320,512]{2,1,0:T(8,128)(2,1)S(1)}, u32[]{:S(2)}, u32[]{:S(2)}) async-start(bf16[4,320,512]{2,1,0:T(8,128)(2,1)} %get-tuple-element.274), calls=%async_computation.2 | async-start | bytes 2621440 | tf_op jit(solution)/shard_map/all_to_all | solution.py:42
  61.1 2.4 %collective-permute-start.12 = (bf16[128,512]{1,0:T(8,128)(2,1)S(1)}, bf16[128,512]{1,0:T(8,128)(2,1)S(1)}, u32[]{:S(2)}, u32[]{:S(2)}) collective-permute-start(bf16[128,512]{1,0:T(8,128)(2,1)S(1)} %copy-done.10), channel_id=1, source_target_pairs={{0,8},{2,10},{4,12},{6,14},{8,0},{10,2},{12,4},{14,6},{16,24},{18,... | collective-permute-start | bytes 393224 | tf_op jit(solution)/shard_map/ppermute | solution.py:28
  66.6 6.5 %shard_map.202 = (bf16[128,512]{1,0:T(8,128)(2,1)S(1)}, f32[512,128]{1,0:T(8,128)}, bf16[512,128]{1,0:T(8,128)(2,1)}, bf16[512,128]{1,0:T(8,128)(2,1)}, bf16[512...) custom-call(s32[16]{0:T(128)S(1)} %copy-done.1, ...), custom_call_target="tpu_custom_call" | custom-call | flops 1 | bytes 1 | tf_op jit(solution)/shard_map/pallas_call | solution.py:171
  78.6 3.6 %shard_map.203 = (bf16[256,512]{1,0:T(8,128)(2,1)}, bf16[256,512]{1,0:T(8,128)(2,1)}, bf16[512,512]{1,0:T(8,128)(2,1)}, f32[512,512]{1,0:T(8,128)S(1)}, f32[512,...) custom-call(bf16[128,512]{1,0:T(8,128)(2,1)S(1)} %get-tuple-element., ...), custom_call_target="tpu_custom_call" | custom-call | flops 1 | bytes 1 | tf_op jit(solution)/shard_map/pallas_call | solution.py:171
  82.2 2.2 %collective-permute-done.17.refs_3_ = bf16[512,128]{1,0:T(8,128)(2,1)S(1)} collective-permute-done((bf16[512,128]{1,0:T(8,128)(2,1)}, bf16[512,128]{1,0:T(8,128)(2,1)S(1)}, u32[]{:S(2)}, u32[]{:S(2)}) %collective-permute-start.17) | collective-permute-done | bytes 131104 | tf_op jit(solution)/shard_map/ppermute | solution.py:28
  87.7 3.5 %all-to-all-start.1 = ((bf16[4,192,512]{2,1,0:T(8,128)(2,1)}), bf16[4,192,512]{2,1,0:T(8,128)(2,1)S(1)}, u32[]{:S(2)}, u32[]{:S(2)}) async-start(bf16[4,192,512]{2,1,0:T(8,128)(2,1)} %shard_map.205), calls=%async_computation.1 | async-start | bytes 1572864 | tf_op jit(solution)/shard_map/all_to_all | solution.py:42
  92.9 2.5 %collective-permute-start.20 = (bf16[80,512]{1,0:T(8,128)(2,1)S(1)}, bf16[80,512]{1,0:T(8,128)(2,1)S(1)}, u32[]{:S(2)}, u32[]{:S(2)}) collective-permute-start(bf16[80,512]{1,0:T(8,128)(2,1)S(1)} %get-tuple-element.282), channel_id=1, source_target_pairs={{0,8},{2,10},{4,12},{6,14},{8,0},{10,2},{12,4},{14,6},{16,24},{18,... | collective-permute-start | bytes 245768 | tf_op jit(solution)/shard_map/ppermute | solution.py:28
  101.9 5.9 %collective-permute-done.21.refs_2_ = bf16[80,512]{1,0:T(8,128)(2,1)S(1)} collective-permute-done((bf16[80,512]{1,0:T(8,128)(2,1)S(1)}, bf16[80,512]{1,0:T(8,128)(2,1)S(1)}, u32[]{:S(2)}, u32[]{:S(2)}) %collective-permute-start.21) | collective-permute-done | bytes 81952 | tf_op jit(solution)/shard_map/ppermute | solution.py:28
  107.9 2.5 %collective-permute-start.28 = (bf16[80,512]{1,0:T(8,128)(2,1)S(1)}, bf16[80,512]{1,0:T(8,128)(2,1)S(1)}, u32[]{:S(2)}, u32[]{:S(2)}) collective-permute-start(bf16[80,512]{1,0:T(8,128)(2,1)S(1)} %shard_map.208.refs_0_), channel_id=1, source_target_pairs={{0,24},{2,26},{4,28},{6,30},{8,16},{10,18},{12,20},{14,22},{16,8},... | collective-permute-start | bytes 245768 | tf_op jit(solution)/shard_map/ppermute | solution.py:28
  112.6 2.2 %shard_map.210 = f32[4,128,512]{2,1,0:T(8,128)} custom-call(f32[128,512]{1,0:T(8,128)} %get-tuple-element.290.refs_0_, bf16[128,512]{1,0:T(8,128)(2,1)} %copy-done.4, bf16[128,512]{1,0:T(8,128)(2,1)} %copy-done.5, bf16[128,512]{1,0:T(8,128)(2,1)} %copy-done.6), custom_call_target="tpu_custom_call" | custom-call | flops 1 | bytes 1 | tf_op jit(solution)/shard_map/pallas_call | solution.py:171
  114.9 2.8 %collective-permute-done.27.refs_2_ = bf16[80,512]{1,0:T(8,128)(2,1)S(1)} collective-permute-done((bf16[80,512]{1,0:T(8,128)(2,1)S(1)}, bf16[80,512]{1,0:T(8,128)(2,1)S(1)}, u32[]{:S(2)}, u32[]{:S(2)}) %collective-permute-start.27) | collective-permute-done | bytes 81952 | tf_op jit(solution)/shard_map/ppermute | solution.py:28
  118.9 4.0 %all-to-all-start.3 = ((bf16[4,320,512]{2,1,0:T(8,128)(2,1)}), bf16[4,320,512]{2,1,0:T(8,128)(2,1)S(1)}, u32[]{:S(2)}, u32[]{:S(2)}) async-start(bf16[4,320,512]{2,1,0:T(8,128)(2,1)} %shard_map.211), calls=%async_computation.3 | async-start | bytes 2621440 | tf_op jit(solution)/shard_map/all_to_all | solution.py:42
  123.5 3.4 %collective-permute-start.30 = (bf16[88,512]{1,0:T(8,128)(2,1)S(1)}, bf16[88,512]{1,0:T(8,128)(2,1)S(1)}, u32[]{:S(2)}, u32[]{:S(2)}) collective-permute-start(bf16[88,512]{1,0:T(8,128)(2,1)S(1)} %get-tuple-element.294), channel_id=1, source_target_pairs={{0,16},{2,18},{4,20},{6,22},{8,24},{10,26},{12,28},{14,30},{16,0},... | collective-permute-start | bytes 270344 | tf_op jit(solution)/shard_map/ppermute | solution.py:28
  128.4 5.5 %collective-permute-done.30.refs_2_ = bf16[88,512]{1,0:T(8,128)(2,1)S(1)} collective-permute-done((bf16[88,512]{1,0:T(8,128)(2,1)S(1)}, bf16[88,512]{1,0:T(8,128)(2,1)S(1)}, u32[]{:S(2)}, u32[]{:S(2)}) %collective-permute-start.30) | collective-permute-done | bytes 90144 | tf_op jit(solution)/shard_map/ppermute | solution.py:28
  134.0 2.5 %collective-permute-start.34 = (bf16[88,512]{1,0:T(8,128)(2,1)S(1)}, bf16[88,512]{1,0:T(8,128)(2,1)S(1)}, u32[]{:S(2)}, u32[]{:S(2)}) collective-permute-start(bf16[88,512]{1,0:T(8,128)(2,1)S(1)} %shard_map.212.refs_0_), channel_id=1, source_target_pairs={{0,24},{2,26},{4,28},{6,30},{8,16},{10,18},{12,20},{14,22},{16,8},... | collective-permute-start | bytes 270344 | tf_op jit(solution)/shard_map/ppermute | solution.py:28
  138.4 2.9 %collective-permute-done.34.refs_3_ = bf16[88,512]{1,0:T(8,128)(2,1)S(1)} collective-permute-done((bf16[88,512]{1,0:T(8,128)(2,1)S(1)}, bf16[88,512]{1,0:T(8,128)(2,1)S(1)}, u32[]{:S(2)}, u32[]{:S(2)}) %collective-permute-start.34) | collective-permute-done | bytes 90144 | tf_op jit(solution)/shard_map/ppermute | solution.py:28
  141.3 2.4 %collective-permute-done.33.refs_2_ = bf16[88,512]{1,0:T(8,128)(2,1)S(1)} collective-permute-done((bf16[88,512]{1,0:T(8,128)(2,1)S(1)}, bf16[88,512]{1,0:T(8,128)(2,1)S(1)}, u32[]{:S(2)}, u32[]{:S(2)}) %collective-permute-start.33) | collective-permute-done | bytes 90144 | tf_op jit(solution)/shard_map/ppermute | solution.py:28
  143.8 2.7 %collective-permute-start.37 = (bf16[1,352,512]{2,1,0:T(8,128)(2,1)S(1)}, bf16[1,352,512]{2,1,0:T(8,128)(2,1)S(1)}, u32[]{:S(2)}, u32[]{:S(2)}) collective-permute-start(bf16[1,352,512]{2,1,0:T(8,128)(2,1)S(1)} %shard_map.213.refs_0_), channel_id=1, source_target_pairs={{0,6},{2,4},{4,2},{6,0},{8,14},{10,12},{12,10},{14,8},{16,22},{18,... | collective-permute-start | bytes 1081352 | tf_op jit(solution)/shard_map/ppermute | solution.py:28
  147.4 2.5 %collective-permute-start.39 = (bf16[128,512]{1,0:T(8,128)(2,1)}, bf16[128,512]{1,0:T(8,128)(2,1)S(1)}, u32[]{:S(2)}, u32[]{:S(2)}) collective-permute-start(bf16[128,512]{1,0:T(8,128)(2,1)} %get-tuple-element.306), channel_id=1, source_target_pairs={{0,16},{2,18},{4,20},{6,22},{8,24},{10,26},{12,28},{14,30},{16,0},... | collective-permute-start | bytes 393224 | tf_op jit(solution)/shard_map/ppermute | solution.py:28
  149.9 3.2 %collective-permute-done.38.refs_6_ = bf16[128,512]{1,0:T(8,128)(2,1)S(1)} collective-permute-done((bf16[128,512]{1,0:T(8,128)(2,1)}, bf16[128,512]{1,0:T(8,128)(2,1)S(1)}, u32[]{:S(2)}, u32[]{:S(2)}) %collective-permute-start.38) | collective-permute-done | bytes 131104 | tf_op jit(solution)/shard_map/ppermute | solution.py:28
  153.0 3.1 %collective-permute-start.40 = (bf16[128,512]{1,0:T(8,128)(2,1)S(1)}, bf16[128,512]{1,0:T(8,128)(2,1)S(1)}, u32[]{:S(2)}, u32[]{:S(2)}) collective-permute-start(bf16[128,512]{1,0:T(8,128)(2,1)S(1)} %copy-done.7), channel_id=1, source_target_pairs={{0,24},{2,26},{4,28},{6,30},{8,16},{10,18},{12,20},{14,22},{16,8},... | collective-permute-start | bytes 393224 | tf_op jit(solution)/shard_map/ppermute | solution.py:28
  160.3 2.2 %shard_map.215 = (f32[256,2048]{1,0:T(8,128)}, f32[256,512]{1,0:T(8,128)}, f32[256,512]{1,0:T(8,128)}, f32[256,128]{1,0:T(8,128)}, f32[8,256]{1,0:T(8,128)}, /*i...) custom-call(bf16[1,352,512]{2,1,0:T(8,128)(2,1)S(1)} %shard_map.213.refs_0_, ...), custom_call_target="tpu_custom_call" | custom-call | flops 1 | bytes 1 | tf_op jit(solution)/shard_map/pallas_call | solution.py:171
  (108 shorter events, 44.1 us)
Async XLA Ops:
  2.9 15.8 %collective-permute-start.4 = (bf16[264,1152]{1,0:T(8,128)(2,1)S(1)}, bf16[264,1152]{1,0:T(8,128)(2,1)S(1)}, u32[]{:S(2)}, u32[]{:S(2)}) collective-permute-start(bf16[264,1152]{1,0:T(8,128)(2,1)S(1)} %get-tuple-element.168), channel_id=1, source_target_pairs={{0,1},{1,0},{2,3},{3,2},{4,5},{5,4},{6,7},{7,6},{8,9},{9,8},{10,11... | collective-permute-start | bytes 1824776 | tf_op jit(solution)/shard_map/ppermute | solution.py:46
  3.5 14.5 %collective-permute-start.1 = (bf16[136,512]{1,0:T(8,128)(2,1)S(1)}, bf16[136,512]{1,0:T(8,128)(2,1)S(1)}, u32[]{:S(2)}, u32[]{:S(2)}) collective-permute-start(bf16[136,512]{1,0:T(8,128)(2,1)S(1)} %get-tuple-element.166), channel_id=1, source_target_pairs={{0,16},{2,18},{4,20},{6,22},{8,24},{10,26},{12,28},{14,30},{16,0},... | collective-permute-start | bytes 417800 | tf_op jit(solution)/shard_map/ppermute | solution.py:28
  7.5 10.5 %collective-permute-start.2 = (bf16[136,512]{1,0:T(8,128)(2,1)S(1)}, bf16[136,512]{1,0:T(8,128)(2,1)S(1)}, u32[]{:S(2)}, u32[]{:S(2)}) collective-permute-start(bf16[136,512]{1,0:T(8,128)(2,1)S(1)} %get-tuple-element.167), channel_id=1, source_target_pairs={{0,24},{2,26},{4,28},{6,30},{8,16},{10,18},{12,20},{14,22},{16,8},... | collective-permute-start | bytes 417800 | tf_op jit(solution)/shard_map/ppermute | solution.py:28
  8.9 9.8 %collective-permute-start = (bf16[136,512]{1,0:T(8,128)(2,1)S(1)}, bf16[136,512]{1,0:T(8,128)(2,1)S(1)}, u32[]{:S(2)}, u32[]{:S(2)}) collective-permute-start(bf16[136,512]{1,0:T(8,128)(2,1)S(1)} %get-tuple-element.164), channel_id=1, source_target_pairs={{0,8},{2,10},{4,12},{6,14},{8,0},{10,2},{12,4},{14,6},{16,24},{18,... | collective-permute-start | bytes 417800 | tf_op jit(solution)/shard_map/ppermute | solution.py:28
  21.1 19.5 %collective-permute-start.8 = (bf16[256,2048]{1,0:T(8,128)(2,1)}, bf16[256,2048]{1,0:T(8,128)(2,1)S(1)}, u32[]{:S(2)}, u32[]{:S(2)}) collective-permute-start(bf16[256,2048]{1,0:T(8,128)(2,1)} %refs_10_.3), channel_id=1, source_target_pairs={{0,1},{1,0},{2,3},{3,2},{4,5},{5,4},{6,7},{7,6},{8,9},{9,8},{10,11... | collective-permute-start | bytes 3145736 | tf_op jit(solution)/shard_map/ppermute | solution.py:46
  21.1 19.5 %collective-permute-start.9 = (bf16[1024,512]{1,0:T(8,128)(2,1)}, bf16[1024,512]{1,0:T(8,128)(2,1)S(1)}, u32[]{:S(2)}, u32[]{:S(2)}) collective-permute-start(bf16[1024,512]{1,0:T(8,128)(2,1)} %refs_11_.1), channel_id=1, source_target_pairs={{0,1},{1,0},{2,3},{3,2},{4,5},{5,4},{6,7},{7,6},{8,9},{9,8},{10,11... | collective-permute-start | bytes 3145736 | tf_op jit(solution)/shard_map/ppermute | solution.py:46
  21.6 12.5 %all-to-all-start = ((bf16[4,512,128]{2,1,0:T(8,128)(2,1)}), bf16[4,512,128]{2,1,0:T(8,128)(2,1)S(1)}, u32[]{:S(2)}, u32[]{:S(2)}) async-start(bf16[4,512,128]{2,1,0:T(8,128)(2,1)} %get-tuple-element.173), calls=%async_computation | async-start | bytes 1048576 | tf_op jit(solution)/shard_map/all_to_all | solution.py:42
  25.5 14.3 %collective-permute-start.5 = (bf16[128,512]{1,0:T(8,128)(2,1)}, bf16[128,512]{1,0:T(8,128)(2,1)S(1)}, u32[]{:S(2)}, u32[]{:S(2)}) collective-permute-start(bf16[128,512]{1,0:T(8,128)(2,1)} %get-tuple-element.191), channel_id=1, source_target_pairs={{0,8},{2,10},{4,12},{6,14},{8,0},{10,2},{12,4},{14,6},{16,24},{18,... | collective-permute-start | bytes 393224 | tf_op jit(solution)/shard_map/ppermute | solution.py:28
  27.9 12.0 %collective-permute-start.6 = (bf16[128,512]{1,0:T(8,128)(2,1)}, bf16[128,512]{1,0:T(8,128)(2,1)S(1)}, u32[]{:S(2)}, u32[]{:S(2)}) collective-permute-start(bf16[128,512]{1,0:T(8,128)(2,1)} %copy-done.3), channel_id=1, source_target_pairs={{0,16},{2,18},{4,20},{6,22},{8,24},{10,26},{12,28},{14,30},{16,0},... | collective-permute-start | bytes 393224 | tf_op jit(solution)/shard_map/ppermute | solution.py:28
  29.8 10.8 %collective-permute-start.7 = (bf16[128,512]{1,0:T(8,128)(2,1)}, bf16[128,512]{1,0:T(8,128)(2,1)}, u32[]{:S(2)}, u32[]{:S(2)}) collective-permute-start(bf16[128,512]{1,0:T(8,128)(2,1)} %copy-done.2), channel_id=1, source_target_pairs={{0,24},{2,26},{4,28},{6,30},{8,16},{10,18},{12,20},{14,22},{16,8},... | collective-permute-start | bytes 393224 | tf_op jit(solution)/shard_map/ppermute | solution.py:28
  56.8 30.9 %all-to-all-start.2 = ((bf16[4,320,512]{2,1,0:T(8,128)(2,1)}), bf16[4,320,512]{2,1,0:T(8,128)(2,1)S(1)}, u32[]{:S(2)}, u32[]{:S(2)}) async-start(bf16[4,320,512]{2,1,0:T(8,128)(2,1)} %get-tuple-element.274), calls=%async_computation.2 | async-start | bytes 2621440 | tf_op jit(solution)/shard_map/all_to_all | solution.py:42
  61.1 14.1 %collective-permute-start.12 = (bf16[128,512]{1,0:T(8,128)(2,1)S(1)}, bf16[128,512]{1,0:T(8,128)(2,1)S(1)}, u32[]{:S(2)}, u32[]{:S(2)}) collective-permute-start(bf16[128,512]{1,0:T(8,128)(2,1)S(1)} %copy-done.10), channel_id=1, source_target_pairs={{0,8},{2,10},{4,12},{6,14},{8,0},{10,2},{12,4},{14,6},{16,24},{18,... | collective-permute-start | bytes 393224 | tf_op jit(solution)/shard_map/ppermute | solution.py:28
  63.6 13.1 %collective-permute-start.13 = (bf16[128,512]{1,0:T(8,128)(2,1)S(1)}, bf16[128,512]{1,0:T(8,128)(2,1)S(1)}, u32[]{:S(2)}, u32[]{:S(2)}) collective-permute-start(bf16[128,512]{1,0:T(8,128)(2,1)S(1)} %copy-done.9), channel_id=1, source_target_pairs={{0,16},{2,18},{4,20},{6,22},{8,24},{10,26},{12,28},{14,30},{16,0},... | collective-permute-start | bytes 393224 | tf_op jit(solution)/shard_map/ppermute | solution.py:28
  65.1 21.5 %collective-permute-start.18 = (bf16[512,512]{1,0:T(8,128)(2,1)}, bf16[512,512]{1,0:T(8,128)(2,1)S(1)}, u32[]{:S(2)}, u32[]{:S(2)}) collective-permute-start(bf16[512,512]{1,0:T(8,128)(2,1)} %get-tuple-element.273), channel_id=1, source_target_pairs={{0,1},{1,0},{2,3},{3,2},{4,5},{5,4},{6,7},{7,6},{8,9},{9,8},{10,11... | collective-permute-start | bytes 1572872 | tf_op jit(solution)/shard_map/ppermute | solution.py:46
  65.1 13.5 %collective-permute-start.14 = (bf16[128,512]{1,0:T(8,128)(2,1)S(1)}, bf16[128,512]{1,0:T(8,128)(2,1)S(1)}, u32[]{:S(2)}, u32[]{:S(2)}) collective-permute-start(bf16[128,512]{1,0:T(8,128)(2,1)S(1)} %copy-done.8), channel_id=1, source_target_pairs={{0,24},{2,26},{4,28},{6,30},{8,16},{10,18},{12,20},{14,22},{16,8},... | collective-permute-start | bytes 393224 | tf_op jit(solution)/shard_map/ppermute | solution.py:28
  73.1 9.0 %collective-permute-start.15 = (bf16[512,128]{1,0:T(8,128)(2,1)}, bf16[512,128]{1,0:T(8,128)(2,1)S(1)}, u32[]{:S(2)}, u32[]{:S(2)}) collective-permute-start(bf16[512,128]{1,0:T(8,128)(2,1)} %get-tuple-element.255), channel_id=1, source_target_pairs={{0,2},{2,0},{4,6},{6,4},{8,10},{10,8},{12,14},{14,12},{16,18},{18,... | collective-permute-start | bytes 393224 | tf_op jit(solution)/shard_map/ppermute | solution.py:28
  76.7 7.7 %collective-permute-start.17 = (bf16[512,128]{1,0:T(8,128)(2,1)}, bf16[512,128]{1,0:T(8,128)(2,1)S(1)}, u32[]{:S(2)}, u32[]{:S(2)}) collective-permute-start(bf16[512,128]{1,0:T(8,128)(2,1)} %get-tuple-element.257), channel_id=1, source_target_pairs={{0,6},{2,4},{4,2},{6,0},{8,14},{10,12},{12,10},{14,8},{16,22},{18,... | collective-permute-start | bytes 393224 | tf_op jit(solution)/shard_map/ppermute | solution.py:28
  87.7 24.6 %all-to-all-start.1 = ((bf16[4,192,512]{2,1,0:T(8,128)(2,1)}), bf16[4,192,512]{2,1,0:T(8,128)(2,1)S(1)}, u32[]{:S(2)}, u32[]{:S(2)}) async-start(bf16[4,192,512]{2,1,0:T(8,128)(2,1)} %shard_map.205), calls=%async_computation.1 | async-start | bytes 1572864 | tf_op jit(solution)/shard_map/all_to_all | solution.py:42
  92.9 7.6 %collective-permute-start.20 = (bf16[80,512]{1,0:T(8,128)(2,1)S(1)}, bf16[80,512]{1,0:T(8,128)(2,1)S(1)}, u32[]{:S(2)}, u32[]{:S(2)}) collective-permute-start(bf16[80,512]{1,0:T(8,128)(2,1)S(1)} %get-tuple-element.282), channel_id=1, source_target_pairs={{0,8},{2,10},{4,12},{6,14},{8,0},{10,2},{12,4},{14,6},{16,24},{18,... | collective-permute-start | bytes 245768 | tf_op jit(solution)/shard_map/ppermute | solution.py:28
  95.4 15.5 %collective-permute-start.23 = (bf16[160,512]{1,0:T(8,128)(2,1)S(1)}, bf16[160,512]{1,0:T(8,128)(2,1)S(1)}, u32[]{:S(2)}, u32[]{:S(2)}) collective-permute-start(bf16[160,512]{1,0:T(8,128)(2,1)S(1)} %get-tuple-element.286), channel_id=1, source_target_pairs={{0,2},{2,0},{4,6},{6,4},{8,10},{10,8},{12,14},{14,12},{16,18},{18,... | collective-permute-start | bytes 491528 | tf_op jit(solution)/shard_map/ppermute | solution.py:28
  97.4 15.0 %collective-permute-start.24 = (bf16[160,512]{1,0:T(8,128)(2,1)S(1)}, bf16[160,512]{1,0:T(8,128)(2,1)S(1)}, u32[]{:S(2)}, u32[]{:S(2)}) collective-permute-start(bf16[160,512]{1,0:T(8,128)(2,1)S(1)} %get-tuple-element.287), channel_id=1, source_target_pairs={{0,4},{2,6},{4,0},{6,2},{8,12},{10,14},{12,8},{14,10},{16,20},{18,... | collective-permute-start | bytes 491528 | tf_op jit(solution)/shard_map/ppermute | solution.py:28
  98.9 13.5 %collective-permute-start.25 = (bf16[160,512]{1,0:T(8,128)(2,1)S(1)}, bf16[160,512]{1,0:T(8,128)(2,1)S(1)}, u32[]{:S(2)}, u32[]{:S(2)}) collective-permute-start(bf16[160,512]{1,0:T(8,128)(2,1)S(1)} %get-tuple-element.288), channel_id=1, source_target_pairs={{0,6},{2,4},{4,2},{6,0},{8,14},{10,12},{12,10},{14,8},{16,22},{18,... | collective-permute-start | bytes 491528 | tf_op jit(solution)/shard_map/ppermute | solution.py:28
  98.9 8.9 %collective-permute-start.21 = (bf16[80,512]{1,0:T(8,128)(2,1)S(1)}, bf16[80,512]{1,0:T(8,128)(2,1)S(1)}, u32[]{:S(2)}, u32[]{:S(2)}) collective-permute-start(bf16[80,512]{1,0:T(8,128)(2,1)S(1)} %get-tuple-element.283), channel_id=1, source_target_pairs={{0,16},{2,18},{4,20},{6,22},{8,24},{10,26},{12,28},{14,30},{16,0},... | collective-permute-start | bytes 245768 | tf_op jit(solution)/shard_map/ppermute | solution.py:28
  100.5 7.3 %collective-permute-start.22 = (bf16[80,512]{1,0:T(8,128)(2,1)S(1)}, bf16[80,512]{1,0:T(8,128)(2,1)S(1)}, u32[]{:S(2)}, u32[]{:S(2)}) collective-permute-start(bf16[80,512]{1,0:T(8,128)(2,1)S(1)} %get-tuple-element.284), channel_id=1, source_target_pairs={{0,24},{2,26},{4,28},{6,30},{8,16},{10,18},{12,20},{14,22},{16,8},... | collective-permute-start | bytes 245768 | tf_op jit(solution)/shard_map/ppermute | solution.py:28
  110.3 7.4 %collective-permute-start.27 = (bf16[80,512]{1,0:T(8,128)(2,1)S(1)}, bf16[80,512]{1,0:T(8,128)(2,1)S(1)}, u32[]{:S(2)}, u32[]{:S(2)}) collective-permute-start(bf16[80,512]{1,0:T(8,128)(2,1)S(1)} %shard_map.208.refs_0_), channel_id=1, source_target_pairs={{0,16},{2,18},{4,20},{6,22},{8,24},{10,26},{12,28},{14,30},{16,0},... | collective-permute-start | bytes 245768 | tf_op jit(solution)/shard_map/ppermute | solution.py:28
  118.9 37.2 %all-to-all-start.3 = ((bf16[4,320,512]{2,1,0:T(8,128)(2,1)}), bf16[4,320,512]{2,1,0:T(8,128)(2,1)S(1)}, u32[]{:S(2)}, u32[]{:S(2)}) async-start(bf16[4,320,512]{2,1,0:T(8,128)(2,1)} %shard_map.211), calls=%async_computation.3 | async-start | bytes 2621440 | tf_op jit(solution)/shard_map/all_to_all | solution.py:42
  123.5 10.4 %collective-permute-start.30 = (bf16[88,512]{1,0:T(8,128)(2,1)S(1)}, bf16[88,512]{1,0:T(8,128)(2,1)S(1)}, u32[]{:S(2)}, u32[]{:S(2)}) collective-permute-start(bf16[88,512]{1,0:T(8,128)(2,1)S(1)} %get-tuple-element.294), channel_id=1, source_target_pairs={{0,16},{2,18},{4,20},{6,22},{8,24},{10,26},{12,28},{14,30},{16,0},... | collective-permute-start | bytes 270344 | tf_op jit(solution)/shard_map/ppermute | solution.py:28
  134.0 7.4 %collective-permute-start.34 = (bf16[88,512]{1,0:T(8,128)(2,1)S(1)}, bf16[88,512]{1,0:T(8,128)(2,1)S(1)}, u32[]{:S(2)}, u32[]{:S(2)}) collective-permute-start(bf16[88,512]{1,0:T(8,128)(2,1)S(1)} %shard_map.212.refs_0_), channel_id=1, source_target_pairs={{0,24},{2,26},{4,28},{6,30},{8,16},{10,18},{12,20},{14,22},{16,8},... | collective-permute-start | bytes 270344 | tf_op jit(solution)/shard_map/ppermute | solution.py:28
  143.8 16.0 %collective-permute-start.37 = (bf16[1,352,512]{2,1,0:T(8,128)(2,1)S(1)}, bf16[1,352,512]{2,1,0:T(8,128)(2,1)S(1)}, u32[]{:S(2)}, u32[]{:S(2)}) collective-permute-start(bf16[1,352,512]{2,1,0:T(8,128)(2,1)S(1)} %shard_map.213.refs_0_), channel_id=1, source_target_pairs={{0,6},{2,4},{4,2},{6,0},{8,14},{10,12},{12,10},{14,8},{16,22},{18,... | collective-permute-start | bytes 1081352 | tf_op jit(solution)/shard_map/ppermute | solution.py:28
  146.5 13.6 %collective-permute-start.36 = (bf16[1,352,512]{2,1,0:T(8,128)(2,1)S(1)}, bf16[1,352,512]{2,1,0:T(8,128)(2,1)S(1)}, u32[]{:S(2)}, u32[]{:S(2)}) collective-permute-start(bf16[1,352,512]{2,1,0:T(8,128)(2,1)S(1)} %shard_map.213.refs_0_), channel_id=1, source_target_pairs={{0,4},{2,6},{4,0},{6,2},{8,12},{10,14},{12,8},{14,10},{16,20},{18,... | collective-permute-start | bytes 1081352 | tf_op jit(solution)/shard_map/ppermute | solution.py:28
  147.1 13.2 %collective-permute-start.35 = (bf16[1,352,512]{2,1,0:T(8,128)(2,1)S(1)}, bf16[1,352,512]{2,1,0:T(8,128)(2,1)S(1)}, u32[]{:S(2)}, u32[]{:S(2)}) collective-permute-start(bf16[1,352,512]{2,1,0:T(8,128)(2,1)S(1)} %shard_map.213.refs_0_), channel_id=1, source_target_pairs={{0,2},{2,0},{4,6},{6,4},{8,10},{10,8},{12,14},{14,12},{16,18},{18,... | collective-permute-start | bytes 1081352 | tf_op jit(solution)/shard_map/ppermute | solution.py:28
  147.4 10.4 %collective-permute-start.39 = (bf16[128,512]{1,0:T(8,128)(2,1)}, bf16[128,512]{1,0:T(8,128)(2,1)S(1)}, u32[]{:S(2)}, u32[]{:S(2)}) collective-permute-start(bf16[128,512]{1,0:T(8,128)(2,1)} %get-tuple-element.306), channel_id=1, source_target_pairs={{0,16},{2,18},{4,20},{6,22},{8,24},{10,26},{12,28},{14,30},{16,0},... | collective-permute-start | bytes 393224 | tf_op jit(solution)/shard_map/ppermute | solution.py:28
  (26 other events, 233.4 us)

commit v8 on v7

--- a/solution.py
+++ b/solution.py
@@ -504,6 +504,7 @@
             keep_down[cols, :] = grad
             send[rows, lane] = grad_theirs
     if not first:
+        Order.leave(count + 1, count + 2, count + 3)
         for k in range(count):
             layer_pieces[k][...] = slot_rows(layer_out[...], k, count).astype(layer_pieces[k].dtype)
 
@@ -623,6 +624,7 @@
     send[half:, :] = mm(normed_t[theirs, :], back_q).astype(BF)
     keep_out[...] = mm(mixed[mine, :], branch[...]).astype(BF)
     keep[...] = mm(normed_t[mine, :], back_q).astype(BF)
+    Order.leave(0, 1, 2)
     parts = []
     left = logit[...]
     for _ in range(3):
@@ -679,6 +681,7 @@
         out[step : step + 8, :] = jnp.concatenate([routers[:, mine], blank], axis=1).astype(out.dtype)
         gain_pair = jnp.concatenate([gains[0:1, mine], gains[1:2, mine]], axis=1)
         out[step + 8 :, :] = jnp.broadcast_to(gain_pair, (8, 2 * half)).astype(out.dtype)
+    Order.leave(count, count + 1)
     for k in range(count):
         pieces[k][...] = slot_rows(grad, k, count).astype(pieces[k].dtype)
 

time: 163 us -> 163 us (level)
  no operation moved by 1% of the time
where the time goes in v8:
time: 163 us
  starting transfers between devices  71.1 us (44%)
  Pallas kernels  51.3 us (31%)
  waiting for transfers between devices  38.8 us (24%)
    ppermute x33, starting transfers between devices, swap(): return lax.ppermute(values, 'ctx', [(i, i ^ mask) for i in range(size)])  53.5 us
    pallas_call x21, Pallas kernels, call(): got = list(run(*args, *moved))  51.3 us
    ppermute x33, waiting for transfers between devices, swap(): return lax.ppermute(values, 'ctx', [(i, i ^ mask) for i in range(size)])  37.7 us
    all_to_all x4, starting transfers between devices, exchange(): lax.all_to_all(parts, 'ctx', 0, 0, tiled=True, axis_index_groups=groups)  15.8 us
  transfers between devices with their start and end apart: 45, of which 16 were waited for; matrix products, arithmetic and copies ran while one was open for 0% of the time, Pallas kernels for 20%

profile of v8, /device:TPU:0, one launch (start us, length us, event | category | flops | bytes accessed | tf_op | source)
XLA Modules:
  0.0 162.7 jit_solution(6119233399513271177)
XLA Ops:
  3.5 4.0 %collective-permute-start.1 = (bf16[136,512]{1,0:T(8,128)(2,1)S(1)}, bf16[136,512]{1,0:T(8,128)(2,1)S(1)}, u32[]{:S(2)}, u32[]{:S(2)}) collective-permute-start(bf16[136,512]{1,0:T(8,128)(2,1)S(1)} %get-tuple-element.166), channel_id=1, source_target_pairs={{0,16},{2,18},{4,20},{6,22},{8,24},{10,26},{12,28},{14,30},{16,0},... | collective-permute-start | bytes 417800 | tf_op jit(solution)/shard_map/ppermute | solution.py:28
  10.4 7.7 %collective-permute-done.1.refs_2_ = bf16[136,512]{1,0:T(8,128)(2,1)S(1)} collective-permute-done((bf16[136,512]{1,0:T(8,128)(2,1)S(1)}, bf16[136,512]{1,0:T(8,128)(2,1)S(1)}, u32[]{:S(2)}, u32[]{:S(2)}) %collective-permute-start.1) | collective-permute-done | bytes 139296 | tf_op jit(solution)/shard_map/ppermute | solution.py:28
  18.7 2.4 %shard_map.196 = (bf16[4,512,128]{2,1,0:T(8,128)(2,1)}, bf16[512,512]{1,0:T(8,128)(2,1)}, bf16[512,512]{1,0:T(8,128)(2,1)}, f32[8,512]{1,0:T(8,128)}, bf16[512,128]{1,0:T(8,128)(2,1)}, /*index=5*/f32[32,128]{1,0:T(8,128)S(1)}) custom-call(bf16[128,512]{1,0:T(8,128)(2,1)S(1)} %get-tuple-element.165.refs_0_, ...), custom_call_target="tpu_custom_call" | custom-call | flops 1 | bytes 1 | tf_op jit(solution)/shard_map/pallas_call | solution.py:171
  21.6 3.9 %all-to-all-start = ((bf16[4,512,128]{2,1,0:T(8,128)(2,1)}), bf16[4,512,128]{2,1,0:T(8,128)(2,1)S(1)}, u32[]{:S(2)}, u32[]{:S(2)}) async-start(bf16[4,512,128]{2,1,0:T(8,128)(2,1)} %get-tuple-element.173), calls=%async_computation | async-start | bytes 1048576 | tf_op jit(solution)/shard_map/all_to_all | solution.py:42
  25.5 2.3 %collective-permute-start.5 = (bf16[128,512]{1,0:T(8,128)(2,1)}, bf16[128,512]{1,0:T(8,128)(2,1)S(1)}, u32[]{:S(2)}, u32[]{:S(2)}) collective-permute-start(bf16[128,512]{1,0:T(8,128)(2,1)} %get-tuple-element.191), channel_id=1, source_target_pairs={{0,8},{2,10},{4,12},{6,14},{8,0},{10,2},{12,4},{14,6},{16,24},{18,... | collective-permute-start | bytes 393224 | tf_op jit(solution)/shard_map/ppermute | solution.py:28
  31.3 2.8 %shard_map.197 = (bf16[128,512]{1,0:T(8,128)(2,1)}, bf16[512,512]{1,0:T(8,128)(2,1)}, f32[2,512]{1,0:T(2,128)S(1)}, f32[2,512]{1,0:T(2,128)}, f32[8,512]{1,0:T(8...) custom-call(bf16[512,512]{1,0:T(8,128)(2,1)} %get-tuple-element.174.refs, ...), custom_call_target="tpu_custom_call" | custom-call | flops 1 | bytes 1 | tf_op jit(solution)/shard_map/pallas_call | solution.py:171
  34.1 5.7 %shard_map.198 = (f32[128,512]{1,0:T(8,128)}, f32[2,512]{1,0:T(2,128)}, bf16[512,512]{1,0:T(8,128)(2,1)}, f32[512,512]{1,0:T(8,128)S(1)}, bf16[512,512]{1,0:T(8,...) custom-call(s32[16]{0:T(128)S(1)} %copy-done.1, ...), custom_call_target="tpu_custom_call" | custom-call | flops 1 | bytes 1 | tf_op jit(solution)/shard_map/pallas_call | solution.py:171
  40.6 6.5 %shard_map.199 = (f32[512,512]{1,0:T(8,128)S(1)}, f32[512,512]{1,0:T(8,128)S(1)}, bf16[1024,512]{1,0:T(8,128)(2,1)S(1)}, bf16[512,512]{1,0:T(8,128)(2,1)}, bf16[...) custom-call(bf16[512,512]{1,0:T(8,128)(2,1)S(1)} %get-tuple-element., ...), custom_call_target="tpu_custom_call" | custom-call | flops 1 | bytes 1 | tf_op jit(solution)/shard_map/pallas_call | solution.py:171
  47.7 5.3 %shard_map.200 = (f32[128,512]{1,0:T(8,128)}, bf16[128,512]{1,0:T(8,128)(2,1)}, bf16[128,512]{1,0:T(8,128)(2,1)}, bf16[128,512]{1,0:T(8,128)(2,1)}, f32[512,512]...) custom-call(bf16[512,512]{1,0:T(8,128)(2,1)S(1)} %get-tuple-element., ...), custom_call_target="tpu_custom_call" | custom-call | flops 1 | bytes 1 | tf_op jit(solution)/shard_map/pallas_call | solution.py:171
  53.1 3.7 %shard_map.201 = (f32[512,512]{1,0:T(8,128)}, bf16[512,512]{1,0:T(8,128)(2,1)}, bf16[128,512]{1,0:T(8,128)(2,1)S(1)}, f32[2,512]{1,0:T(2,128)S(1)}, f32[8,512]{1...) custom-call(f32[512,512]{1,0:T(8,128)S(1)} %get-tuple-element.208.re, ...), custom_call_target="tpu_custom_call" | custom-call | flops 1 | bytes 1 | tf_op jit(solution)/shard_map/pallas_call | solution.py:171
  56.8 4.4 %all-to-all-start.2 = ((bf16[4,320,512]{2,1,0:T(8,128)(2,1)}), bf16[4,320,512]{2,1,0:T(8,128)(2,1)S(1)}, u32[]{:S(2)}, u32[]{:S(2)}) async-start(bf16[4,320,512]{2,1,0:T(8,128)(2,1)} %get-tuple-element.274), calls=%async_computation.2 | async-start | bytes 2621440 | tf_op jit(solution)/shard_map/all_to_all | solution.py:42
  61.1 2.4 %collective-permute-start.12 = (bf16[128,512]{1,0:T(8,128)(2,1)S(1)}, bf16[128,512]{1,0:T(8,128)(2,1)S(1)}, u32[]{:S(2)}, u32[]{:S(2)}) collective-permute-start(bf16[128,512]{1,0:T(8,128)(2,1)S(1)} %copy-done.10), channel_id=1, source_target_pairs={{0,8},{2,10},{4,12},{6,14},{8,0},{10,2},{12,4},{14,6},{16,24},{18,... | collective-permute-start | bytes 393224 | tf_op jit(solution)/shard_map/ppermute | solution.py:28
  66.5 6.5 %shard_map.202 = (bf16[128,512]{1,0:T(8,128)(2,1)S(1)}, f32[512,128]{1,0:T(8,128)}, bf16[512,128]{1,0:T(8,128)(2,1)}, bf16[512,128]{1,0:T(8,128)(2,1)}, bf16[512...) custom-call(s32[16]{0:T(128)S(1)} %copy-done.1, ...), custom_call_target="tpu_custom_call" | custom-call | flops 1 | bytes 1 | tf_op jit(solution)/shard_map/pallas_call | solution.py:171
  78.5 3.6 %shard_map.203 = (bf16[256,512]{1,0:T(8,128)(2,1)}, bf16[256,512]{1,0:T(8,128)(2,1)}, bf16[512,512]{1,0:T(8,128)(2,1)}, f32[512,512]{1,0:T(8,128)S(1)}, f32[512,...) custom-call(bf16[128,512]{1,0:T(8,128)(2,1)S(1)} %get-tuple-element., ...), custom_call_target="tpu_custom_call" | custom-call | flops 1 | bytes 1 | tf_op jit(solution)/shard_map/pallas_call | solution.py:171
  84.3 2.3 %shard_map.204 = (f32[128,512]{1,0:T(8,128)}, bf16[128,512]{1,0:T(8,128)(2,1)}, bf16[128,512]{1,0:T(8,128)(2,1)}, bf16[128,512]{1,0:T(8,128)(2,1)}, f32[80,512]{...) custom-call(f32[512,128]{1,0:T(8,128)S(1)} %get-tuple-element.254.refs_0_, ...), custom_call_target="tpu_custom_call" | custom-call | flops 1 | bytes 1 | tf_op jit(solution)/shard_map/pallas_call | solution.py:171
  87.8 3.5 %all-to-all-start.1 = ((bf16[4,192,512]{2,1,0:T(8,128)(2,1)}), bf16[4,192,512]{2,1,0:T(8,128)(2,1)S(1)}, u32[]{:S(2)}, u32[]{:S(2)}) async-start(bf16[4,192,512]{2,1,0:T(8,128)(2,1)} %shard_map.205), calls=%async_computation.1 | async-start | bytes 1572864 | tf_op jit(solution)/shard_map/all_to_all | solution.py:42
  93.0 2.5 %collective-permute-start.20 = (bf16[80,512]{1,0:T(8,128)(2,1)S(1)}, bf16[80,512]{1,0:T(8,128)(2,1)S(1)}, u32[]{:S(2)}, u32[]{:S(2)}) collective-permute-start(bf16[80,512]{1,0:T(8,128)(2,1)S(1)} %get-tuple-element.282), channel_id=1, source_target_pairs={{0,8},{2,10},{4,12},{6,14},{8,0},{10,2},{12,4},{14,6},{16,24},{18,... | collective-permute-start | bytes 245768 | tf_op jit(solution)/shard_map/ppermute | solution.py:28
  101.9 5.9 %collective-permute-done.21.refs_2_ = bf16[80,512]{1,0:T(8,128)(2,1)S(1)} collective-permute-done((bf16[80,512]{1,0:T(8,128)(2,1)S(1)}, bf16[80,512]{1,0:T(8,128)(2,1)S(1)}, u32[]{:S(2)}, u32[]{:S(2)}) %collective-permute-start.21) | collective-permute-done | bytes 81952 | tf_op jit(solution)/shard_map/ppermute | solution.py:28
  107.9 2.5 %collective-permute-start.28 = (bf16[80,512]{1,0:T(8,128)(2,1)S(1)}, bf16[80,512]{1,0:T(8,128)(2,1)S(1)}, u32[]{:S(2)}, u32[]{:S(2)}) collective-permute-start(bf16[80,512]{1,0:T(8,128)(2,1)S(1)} %shard_map.208.refs_0_), channel_id=1, source_target_pairs={{0,24},{2,26},{4,28},{6,30},{8,16},{10,18},{12,20},{14,22},{16,8},... | collective-permute-start | bytes 245768 | tf_op jit(solution)/shard_map/ppermute | solution.py:28
  112.7 2.2 %shard_map.210 = f32[4,128,512]{2,1,0:T(8,128)} custom-call(f32[128,512]{1,0:T(8,128)} %get-tuple-element.290.refs_0_, bf16[128,512]{1,0:T(8,128)(2,1)} %copy-done.4, bf16[128,512]{1,0:T(8,128)(2,1)} %copy-done.5, bf16[128,512]{1,0:T(8,128)(2,1)} %copy-done.6), custom_call_target="tpu_custom_call" | custom-call | flops 1 | bytes 1 | tf_op jit(solution)/shard_map/pallas_call | solution.py:171
  114.9 2.8 %collective-permute-done.27.refs_2_ = bf16[80,512]{1,0:T(8,128)(2,1)S(1)} collective-permute-done((bf16[80,512]{1,0:T(8,128)(2,1)S(1)}, bf16[80,512]{1,0:T(8,128)(2,1)S(1)}, u32[]{:S(2)}, u32[]{:S(2)}) %collective-permute-start.27) | collective-permute-done | bytes 81952 | tf_op jit(solution)/shard_map/ppermute | solution.py:28
  119.0 4.0 %all-to-all-start.3 = ((bf16[4,320,512]{2,1,0:T(8,128)(2,1)}), bf16[4,320,512]{2,1,0:T(8,128)(2,1)S(1)}, u32[]{:S(2)}, u32[]{:S(2)}) async-start(bf16[4,320,512]{2,1,0:T(8,128)(2,1)} %shard_map.211), calls=%async_computation.3 | async-start | bytes 2621440 | tf_op jit(solution)/shard_map/all_to_all | solution.py:42
  123.6 3.4 %collective-permute-start.30 = (bf16[88,512]{1,0:T(8,128)(2,1)S(1)}, bf16[88,512]{1,0:T(8,128)(2,1)S(1)}, u32[]{:S(2)}, u32[]{:S(2)}) collective-permute-start(bf16[88,512]{1,0:T(8,128)(2,1)S(1)} %get-tuple-element.294), channel_id=1, source_target_pairs={{0,16},{2,18},{4,20},{6,22},{8,24},{10,26},{12,28},{14,30},{16,0},... | collective-permute-start | bytes 270344 | tf_op jit(solution)/shard_map/ppermute | solution.py:28
  128.5 5.5 %collective-permute-done.30.refs_2_ = bf16[88,512]{1,0:T(8,128)(2,1)S(1)} collective-permute-done((bf16[88,512]{1,0:T(8,128)(2,1)S(1)}, bf16[88,512]{1,0:T(8,128)(2,1)S(1)}, u32[]{:S(2)}, u32[]{:S(2)}) %collective-permute-start.30) | collective-permute-done | bytes 90144 | tf_op jit(solution)/shard_map/ppermute | solution.py:28
  134.0 2.5 %collective-permute-start.34 = (bf16[88,512]{1,0:T(8,128)(2,1)S(1)}, bf16[88,512]{1,0:T(8,128)(2,1)S(1)}, u32[]{:S(2)}, u32[]{:S(2)}) collective-permute-start(bf16[88,512]{1,0:T(8,128)(2,1)S(1)} %shard_map.212.refs_0_), channel_id=1, source_target_pairs={{0,24},{2,26},{4,28},{6,30},{8,16},{10,18},{12,20},{14,22},{16,8},... | collective-permute-start | bytes 270344 | tf_op jit(solution)/shard_map/ppermute | solution.py:28
  138.5 2.9 %collective-permute-done.34.refs_3_ = bf16[88,512]{1,0:T(8,128)(2,1)S(1)} collective-permute-done((bf16[88,512]{1,0:T(8,128)(2,1)S(1)}, bf16[88,512]{1,0:T(8,128)(2,1)S(1)}, u32[]{:S(2)}, u32[]{:S(2)}) %collective-permute-start.34) | collective-permute-done | bytes 90144 | tf_op jit(solution)/shard_map/ppermute | solution.py:28
  141.4 2.4 %collective-permute-done.33.refs_2_ = bf16[88,512]{1,0:T(8,128)(2,1)S(1)} collective-permute-done((bf16[88,512]{1,0:T(8,128)(2,1)S(1)}, bf16[88,512]{1,0:T(8,128)(2,1)S(1)}, u32[]{:S(2)}, u32[]{:S(2)}) %collective-permute-start.33) | collective-permute-done | bytes 90144 | tf_op jit(solution)/shard_map/ppermute | solution.py:28
  143.9 2.7 %collective-permute-start.37 = (bf16[1,352,512]{2,1,0:T(8,128)(2,1)S(1)}, bf16[1,352,512]{2,1,0:T(8,128)(2,1)S(1)}, u32[]{:S(2)}, u32[]{:S(2)}) collective-permute-start(bf16[1,352,512]{2,1,0:T(8,128)(2,1)S(1)} %shard_map.213.refs_0_), channel_id=1, source_target_pairs={{0,6},{2,4},{4,2},{6,0},{8,14},{10,12},{12,10},{14,8},{16,22},{18,... | collective-permute-start | bytes 1081352 | tf_op jit(solution)/shard_map/ppermute | solution.py:28
  147.4 2.5 %collective-permute-start.39 = (bf16[128,512]{1,0:T(8,128)(2,1)}, bf16[128,512]{1,0:T(8,128)(2,1)S(1)}, u32[]{:S(2)}, u32[]{:S(2)}) collective-permute-start(bf16[128,512]{1,0:T(8,128)(2,1)} %get-tuple-element.306), channel_id=1, source_target_pairs={{0,16},{2,18},{4,20},{6,22},{8,24},{10,26},{12,28},{14,30},{16,0},... | collective-permute-start | bytes 393224 | tf_op jit(solution)/shard_map/ppermute | solution.py:28
  149.9 3.2 %collective-permute-done.38.refs_6_ = bf16[128,512]{1,0:T(8,128)(2,1)S(1)} collective-permute-done((bf16[128,512]{1,0:T(8,128)(2,1)}, bf16[128,512]{1,0:T(8,128)(2,1)S(1)}, u32[]{:S(2)}, u32[]{:S(2)}) %collective-permute-start.38) | collective-permute-done | bytes 131104 | tf_op jit(solution)/shard_map/ppermute | solution.py:28
  153.1 3.1 %collective-permute-start.40 = (bf16[128,512]{1,0:T(8,128)(2,1)S(1)}, bf16[128,512]{1,0:T(8,128)(2,1)S(1)}, u32[]{:S(2)}, u32[]{:S(2)}) collective-permute-start(bf16[128,512]{1,0:T(8,128)(2,1)S(1)} %copy-done.7), channel_id=1, source_target_pairs={{0,24},{2,26},{4,28},{6,30},{8,16},{10,18},{12,20},{14,22},{16,8},... | collective-permute-start | bytes 393224 | tf_op jit(solution)/shard_map/ppermute | solution.py:28
  160.3 2.2 %shard_map.215 = (f32[256,2048]{1,0:T(8,128)}, f32[256,512]{1,0:T(8,128)}, f32[256,512]{1,0:T(8,128)}, f32[256,128]{1,0:T(8,128)}, f32[8,256]{1,0:T(8,128)}, /*i...) custom-call(bf16[1,352,512]{2,1,0:T(8,128)(2,1)S(1)} %shard_map.213.refs_0_, ...), custom_call_target="tpu_custom_call" | custom-call | flops 1 | bytes 1 | tf_op jit(solution)/shard_map/pallas_call | solution.py:171
  (108 shorter events, 44.1 us)
Async XLA Ops:
  2.9 15.8 %collective-permute-start.4 = (bf16[264,1152]{1,0:T(8,128)(2,1)S(1)}, bf16[264,1152]{1,0:T(8,128)(2,1)S(1)}, u32[]{:S(2)}, u32[]{:S(2)}) collective-permute-start(bf16[264,1152]{1,0:T(8,128)(2,1)S(1)} %get-tuple-element.168), channel_id=1, source_target_pairs={{0,1},{1,0},{2,3},{3,2},{4,5},{5,4},{6,7},{7,6},{8,9},{9,8},{10,11... | collective-permute-start | bytes 1824776 | tf_op jit(solution)/shard_map/ppermute | solution.py:46
  3.5 14.5 %collective-permute-start.1 = (bf16[136,512]{1,0:T(8,128)(2,1)S(1)}, bf16[136,512]{1,0:T(8,128)(2,1)S(1)}, u32[]{:S(2)}, u32[]{:S(2)}) collective-permute-start(bf16[136,512]{1,0:T(8,128)(2,1)S(1)} %get-tuple-element.166), channel_id=1, source_target_pairs={{0,16},{2,18},{4,20},{6,22},{8,24},{10,26},{12,28},{14,30},{16,0},... | collective-permute-start | bytes 417800 | tf_op jit(solution)/shard_map/ppermute | solution.py:28
  7.5 10.5 %collective-permute-start.2 = (bf16[136,512]{1,0:T(8,128)(2,1)S(1)}, bf16[136,512]{1,0:T(8,128)(2,1)S(1)}, u32[]{:S(2)}, u32[]{:S(2)}) collective-permute-start(bf16[136,512]{1,0:T(8,128)(2,1)S(1)} %get-tuple-element.167), channel_id=1, source_target_pairs={{0,24},{2,26},{4,28},{6,30},{8,16},{10,18},{12,20},{14,22},{16,8},... | collective-permute-start | bytes 417800 | tf_op jit(solution)/shard_map/ppermute | solution.py:28
  8.9 9.8 %collective-permute-start = (bf16[136,512]{1,0:T(8,128)(2,1)S(1)}, bf16[136,512]{1,0:T(8,128)(2,1)S(1)}, u32[]{:S(2)}, u32[]{:S(2)}) collective-permute-start(bf16[136,512]{1,0:T(8,128)(2,1)S(1)} %get-tuple-element.164), channel_id=1, source_target_pairs={{0,8},{2,10},{4,12},{6,14},{8,0},{10,2},{12,4},{14,6},{16,24},{18,... | collective-permute-start | bytes 417800 | tf_op jit(solution)/shard_map/ppermute | solution.py:28
  21.1 19.5 %collective-permute-start.8 = (bf16[256,2048]{1,0:T(8,128)(2,1)}, bf16[256,2048]{1,0:T(8,128)(2,1)S(1)}, u32[]{:S(2)}, u32[]{:S(2)}) collective-permute-start(bf16[256,2048]{1,0:T(8,128)(2,1)} %refs_10_.3), channel_id=1, source_target_pairs={{0,1},{1,0},{2,3},{3,2},{4,5},{5,4},{6,7},{7,6},{8,9},{9,8},{10,11... | collective-permute-start | bytes 3145736 | tf_op jit(solution)/shard_map/ppermute | solution.py:46
  21.1 19.5 %collective-permute-start.9 = (bf16[1024,512]{1,0:T(8,128)(2,1)}, bf16[1024,512]{1,0:T(8,128)(2,1)S(1)}, u32[]{:S(2)}, u32[]{:S(2)}) collective-permute-start(bf16[1024,512]{1,0:T(8,128)(2,1)} %refs_11_.1), channel_id=1, source_target_pairs={{0,1},{1,0},{2,3},{3,2},{4,5},{5,4},{6,7},{7,6},{8,9},{9,8},{10,11... | collective-permute-start | bytes 3145736 | tf_op jit(solution)/shard_map/ppermute | solution.py:46
  21.6 12.5 %all-to-all-start = ((bf16[4,512,128]{2,1,0:T(8,128)(2,1)}), bf16[4,512,128]{2,1,0:T(8,128)(2,1)S(1)}, u32[]{:S(2)}, u32[]{:S(2)}) async-start(bf16[4,512,128]{2,1,0:T(8,128)(2,1)} %get-tuple-element.173), calls=%async_computation | async-start | bytes 1048576 | tf_op jit(solution)/shard_map/all_to_all | solution.py:42
  25.5 14.3 %collective-permute-start.5 = (bf16[128,512]{1,0:T(8,128)(2,1)}, bf16[128,512]{1,0:T(8,128)(2,1)S(1)}, u32[]{:S(2)}, u32[]{:S(2)}) collective-permute-start(bf16[128,512]{1,0:T(8,128)(2,1)} %get-tuple-element.191), channel_id=1, source_target_pairs={{0,8},{2,10},{4,12},{6,14},{8,0},{10,2},{12,4},{14,6},{16,24},{18,... | collective-permute-start | bytes 393224 | tf_op jit(solution)/shard_map/ppermute | solution.py:28
  27.9 12.0 %collective-permute-start.6 = (bf16[128,512]{1,0:T(8,128)(2,1)}, bf16[128,512]{1,0:T(8,128)(2,1)S(1)}, u32[]{:S(2)}, u32[]{:S(2)}) collective-permute-start(bf16[128,512]{1,0:T(8,128)(2,1)} %copy-done.3), channel_id=1, source_target_pairs={{0,16},{2,18},{4,20},{6,22},{8,24},{10,26},{12,28},{14,30},{16,0},... | collective-permute-start | bytes 393224 | tf_op jit(solution)/shard_map/ppermute | solution.py:28
  29.8 10.8 %collective-permute-start.7 = (bf16[128,512]{1,0:T(8,128)(2,1)}, bf16[128,512]{1,0:T(8,128)(2,1)}, u32[]{:S(2)}, u32[]{:S(2)}) collective-permute-start(bf16[128,512]{1,0:T(8,128)(2,1)} %copy-done.2), channel_id=1, source_target_pairs={{0,24},{2,26},{4,28},{6,30},{8,16},{10,18},{12,20},{14,22},{16,8},... | collective-permute-start | bytes 393224 | tf_op jit(solution)/shard_map/ppermute | solution.py:28
  56.8 31.0 %all-to-all-start.2 = ((bf16[4,320,512]{2,1,0:T(8,128)(2,1)}), bf16[4,320,512]{2,1,0:T(8,128)(2,1)S(1)}, u32[]{:S(2)}, u32[]{:S(2)}) async-start(bf16[4,320,512]{2,1,0:T(8,128)(2,1)} %get-tuple-element.274), calls=%async_computation.2 | async-start | bytes 2621440 | tf_op jit(solution)/shard_map/all_to_all | solution.py:42
  61.1 14.1 %collective-permute-start.12 = (bf16[128,512]{1,0:T(8,128)(2,1)S(1)}, bf16[128,512]{1,0:T(8,128)(2,1)S(1)}, u32[]{:S(2)}, u32[]{:S(2)}) collective-permute-start(bf16[128,512]{1,0:T(8,128)(2,1)S(1)} %copy-done.10), channel_id=1, source_target_pairs={{0,8},{2,10},{4,12},{6,14},{8,0},{10,2},{12,4},{14,6},{16,24},{18,... | collective-permute-start | bytes 393224 | tf_op jit(solution)/shard_map/ppermute | solution.py:28
  63.6 13.1 %collective-permute-start.13 = (bf16[128,512]{1,0:T(8,128)(2,1)S(1)}, bf16[128,512]{1,0:T(8,128)(2,1)S(1)}, u32[]{:S(2)}, u32[]{:S(2)}) collective-permute-start(bf16[128,512]{1,0:T(8,128)(2,1)S(1)} %copy-done.9), channel_id=1, source_target_pairs={{0,16},{2,18},{4,20},{6,22},{8,24},{10,26},{12,28},{14,30},{16,0},... | collective-permute-start | bytes 393224 | tf_op jit(solution)/shard_map/ppermute | solution.py:28
  65.1 21.6 %collective-permute-start.18 = (bf16[512,512]{1,0:T(8,128)(2,1)}, bf16[512,512]{1,0:T(8,128)(2,1)S(1)}, u32[]{:S(2)}, u32[]{:S(2)}) collective-permute-start(bf16[512,512]{1,0:T(8,128)(2,1)} %get-tuple-element.273), channel_id=1, source_target_pairs={{0,1},{1,0},{2,3},{3,2},{4,5},{5,4},{6,7},{7,6},{8,9},{9,8},{10,11... | collective-permute-start | bytes 1572872 | tf_op jit(solution)/shard_map/ppermute | solution.py:46
  65.1 13.5 %collective-permute-start.14 = (bf16[128,512]{1,0:T(8,128)(2,1)S(1)}, bf16[128,512]{1,0:T(8,128)(2,1)S(1)}, u32[]{:S(2)}, u32[]{:S(2)}) collective-permute-start(bf16[128,512]{1,0:T(8,128)(2,1)S(1)} %copy-done.8), channel_id=1, source_target_pairs={{0,24},{2,26},{4,28},{6,30},{8,16},{10,18},{12,20},{14,22},{16,8},... | collective-permute-start | bytes 393224 | tf_op jit(solution)/shard_map/ppermute | solution.py:28
  73.1 9.0 %collective-permute-start.15 = (bf16[512,128]{1,0:T(8,128)(2,1)}, bf16[512,128]{1,0:T(8,128)(2,1)S(1)}, u32[]{:S(2)}, u32[]{:S(2)}) collective-permute-start(bf16[512,128]{1,0:T(8,128)(2,1)} %get-tuple-element.255), channel_id=1, source_target_pairs={{0,2},{2,0},{4,6},{6,4},{8,10},{10,8},{12,14},{14,12},{16,18},{18,... | collective-permute-start | bytes 393224 | tf_op jit(solution)/shard_map/ppermute | solution.py:28
  76.6 7.7 %collective-permute-start.17 = (bf16[512,128]{1,0:T(8,128)(2,1)}, bf16[512,128]{1,0:T(8,128)(2,1)S(1)}, u32[]{:S(2)}, u32[]{:S(2)}) collective-permute-start(bf16[512,128]{1,0:T(8,128)(2,1)} %get-tuple-element.257), channel_id=1, source_target_pairs={{0,6},{2,4},{4,2},{6,0},{8,14},{10,12},{12,10},{14,8},{16,22},{18,... | collective-permute-start | bytes 393224 | tf_op jit(solution)/shard_map/ppermute | solution.py:28
  87.8 24.6 %all-to-all-start.1 = ((bf16[4,192,512]{2,1,0:T(8,128)(2,1)}), bf16[4,192,512]{2,1,0:T(8,128)(2,1)S(1)}, u32[]{:S(2)}, u32[]{:S(2)}) async-start(bf16[4,192,512]{2,1,0:T(8,128)(2,1)} %shard_map.205), calls=%async_computation.1 | async-start | bytes 1572864 | tf_op jit(solution)/shard_map/all_to_all | solution.py:42
  93.0 7.6 %collective-permute-start.20 = (bf16[80,512]{1,0:T(8,128)(2,1)S(1)}, bf16[80,512]{1,0:T(8,128)(2,1)S(1)}, u32[]{:S(2)}, u32[]{:S(2)}) collective-permute-start(bf16[80,512]{1,0:T(8,128)(2,1)S(1)} %get-tuple-element.282), channel_id=1, source_target_pairs={{0,8},{2,10},{4,12},{6,14},{8,0},{10,2},{12,4},{14,6},{16,24},{18,... | collective-permute-start | bytes 245768 | tf_op jit(solution)/shard_map/ppermute | solution.py:28
  95.5 15.5 %collective-permute-start.23 = (bf16[160,512]{1,0:T(8,128)(2,1)S(1)}, bf16[160,512]{1,0:T(8,128)(2,1)S(1)}, u32[]{:S(2)}, u32[]{:S(2)}) collective-permute-start(bf16[160,512]{1,0:T(8,128)(2,1)S(1)} %get-tuple-element.286), channel_id=1, source_target_pairs={{0,2},{2,0},{4,6},{6,4},{8,10},{10,8},{12,14},{14,12},{16,18},{18,... | collective-permute-start | bytes 491528 | tf_op jit(solution)/shard_map/ppermute | solution.py:28
  97.4 15.0 %collective-permute-start.24 = (bf16[160,512]{1,0:T(8,128)(2,1)S(1)}, bf16[160,512]{1,0:T(8,128)(2,1)S(1)}, u32[]{:S(2)}, u32[]{:S(2)}) collective-permute-start(bf16[160,512]{1,0:T(8,128)(2,1)S(1)} %get-tuple-element.287), channel_id=1, source_target_pairs={{0,4},{2,6},{4,0},{6,2},{8,12},{10,14},{12,8},{14,10},{16,20},{18,... | collective-permute-start | bytes 491528 | tf_op jit(solution)/shard_map/ppermute | solution.py:28
  98.9 13.5 %collective-permute-start.25 = (bf16[160,512]{1,0:T(8,128)(2,1)S(1)}, bf16[160,512]{1,0:T(8,128)(2,1)S(1)}, u32[]{:S(2)}, u32[]{:S(2)}) collective-permute-start(bf16[160,512]{1,0:T(8,128)(2,1)S(1)} %get-tuple-element.288), channel_id=1, source_target_pairs={{0,6},{2,4},{4,2},{6,0},{8,14},{10,12},{12,10},{14,8},{16,22},{18,... | collective-permute-start | bytes 491528 | tf_op jit(solution)/shard_map/ppermute | solution.py:28
  99.0 8.9 %collective-permute-start.21 = (bf16[80,512]{1,0:T(8,128)(2,1)S(1)}, bf16[80,512]{1,0:T(8,128)(2,1)S(1)}, u32[]{:S(2)}, u32[]{:S(2)}) collective-permute-start(bf16[80,512]{1,0:T(8,128)(2,1)S(1)} %get-tuple-element.283), channel_id=1, source_target_pairs={{0,16},{2,18},{4,20},{6,22},{8,24},{10,26},{12,28},{14,30},{16,0},... | collective-permute-start | bytes 245768 | tf_op jit(solution)/shard_map/ppermute | solution.py:28
  100.5 7.3 %collective-permute-start.22 = (bf16[80,512]{1,0:T(8,128)(2,1)S(1)}, bf16[80,512]{1,0:T(8,128)(2,1)S(1)}, u32[]{:S(2)}, u32[]{:S(2)}) collective-permute-start(bf16[80,512]{1,0:T(8,128)(2,1)S(1)} %get-tuple-element.284), channel_id=1, source_target_pairs={{0,24},{2,26},{4,28},{6,30},{8,16},{10,18},{12,20},{14,22},{16,8},... | collective-permute-start | bytes 245768 | tf_op jit(solution)/shard_map/ppermute | solution.py:28
  110.4 7.4 %collective-permute-start.27 = (bf16[80,512]{1,0:T(8,128)(2,1)S(1)}, bf16[80,512]{1,0:T(8,128)(2,1)S(1)}, u32[]{:S(2)}, u32[]{:S(2)}) collective-permute-start(bf16[80,512]{1,0:T(8,128)(2,1)S(1)} %shard_map.208.refs_0_), channel_id=1, source_target_pairs={{0,16},{2,18},{4,20},{6,22},{8,24},{10,26},{12,28},{14,30},{16,0},... | collective-permute-start | bytes 245768 | tf_op jit(solution)/shard_map/ppermute | solution.py:28
  119.0 37.2 %all-to-all-start.3 = ((bf16[4,320,512]{2,1,0:T(8,128)(2,1)}), bf16[4,320,512]{2,1,0:T(8,128)(2,1)S(1)}, u32[]{:S(2)}, u32[]{:S(2)}) async-start(bf16[4,320,512]{2,1,0:T(8,128)(2,1)} %shard_map.211), calls=%async_computation.3 | async-start | bytes 2621440 | tf_op jit(solution)/shard_map/all_to_all | solution.py:42
  123.6 10.4 %collective-permute-start.30 = (bf16[88,512]{1,0:T(8,128)(2,1)S(1)}, bf16[88,512]{1,0:T(8,128)(2,1)S(1)}, u32[]{:S(2)}, u32[]{:S(2)}) collective-permute-start(bf16[88,512]{1,0:T(8,128)(2,1)S(1)} %get-tuple-element.294), channel_id=1, source_target_pairs={{0,16},{2,18},{4,20},{6,22},{8,24},{10,26},{12,28},{14,30},{16,0},... | collective-permute-start | bytes 270344 | tf_op jit(solution)/shard_map/ppermute | solution.py:28
  134.0 7.4 %collective-permute-start.34 = (bf16[88,512]{1,0:T(8,128)(2,1)S(1)}, bf16[88,512]{1,0:T(8,128)(2,1)S(1)}, u32[]{:S(2)}, u32[]{:S(2)}) collective-permute-start(bf16[88,512]{1,0:T(8,128)(2,1)S(1)} %shard_map.212.refs_0_), channel_id=1, source_target_pairs={{0,24},{2,26},{4,28},{6,30},{8,16},{10,18},{12,20},{14,22},{16,8},... | collective-permute-start | bytes 270344 | tf_op jit(solution)/shard_map/ppermute | solution.py:28
  143.9 16.0 %collective-permute-start.37 = (bf16[1,352,512]{2,1,0:T(8,128)(2,1)S(1)}, bf16[1,352,512]{2,1,0:T(8,128)(2,1)S(1)}, u32[]{:S(2)}, u32[]{:S(2)}) collective-permute-start(bf16[1,352,512]{2,1,0:T(8,128)(2,1)S(1)} %shard_map.213.refs_0_), channel_id=1, source_target_pairs={{0,6},{2,4},{4,2},{6,0},{8,14},{10,12},{12,10},{14,8},{16,22},{18,... | collective-permute-start | bytes 1081352 | tf_op jit(solution)/shard_map/ppermute | solution.py:28
  146.6 13.6 %collective-permute-start.36 = (bf16[1,352,512]{2,1,0:T(8,128)(2,1)S(1)}, bf16[1,352,512]{2,1,0:T(8,128)(2,1)S(1)}, u32[]{:S(2)}, u32[]{:S(2)}) collective-permute-start(bf16[1,352,512]{2,1,0:T(8,128)(2,1)S(1)} %shard_map.213.refs_0_), channel_id=1, source_target_pairs={{0,4},{2,6},{4,0},{6,2},{8,12},{10,14},{12,8},{14,10},{16,20},{18,... | collective-permute-start | bytes 1081352 | tf_op jit(solution)/shard_map/ppermute | solution.py:28
  147.1 13.2 %collective-permute-start.35 = (bf16[1,352,512]{2,1,0:T(8,128)(2,1)S(1)}, bf16[1,352,512]{2,1,0:T(8,128)(2,1)S(1)}, u32[]{:S(2)}, u32[]{:S(2)}) collective-permute-start(bf16[1,352,512]{2,1,0:T(8,128)(2,1)S(1)} %shard_map.213.refs_0_), channel_id=1, source_target_pairs={{0,2},{2,0},{4,6},{6,4},{8,10},{10,8},{12,14},{14,12},{16,18},{18,... | collective-permute-start | bytes 1081352 | tf_op jit(solution)/shard_map/ppermute | solution.py:28
  147.4 10.4 %collective-permute-start.39 = (bf16[128,512]{1,0:T(8,128)(2,1)}, bf16[128,512]{1,0:T(8,128)(2,1)S(1)}, u32[]{:S(2)}, u32[]{:S(2)}) collective-permute-start(bf16[128,512]{1,0:T(8,128)(2,1)} %get-tuple-element.306), channel_id=1, source_target_pairs={{0,16},{2,18},{4,20},{6,22},{8,24},{10,26},{12,28},{14,30},{16,0},... | collective-permute-start | bytes 393224 | tf_op jit(solution)/shard_map/ppermute | solution.py:28
  (26 other events, 233.3 us)

commit v9 on v8

--- a/solution.py
+++ b/solution.py
@@ -594,15 +594,16 @@
         return carry
 
     lax.fori_loop(0, rest, step, 0, unroll=rest <= 4)
-    for h in range(2):
-        for s in range(TWO):
-            here, cols = slice(h * half, (h + 1) * half), slice(s * half, (s + 1) * half)
-            grad_q_out[s * head : (s + 1) * head, here] = grad_q[h, :, cols].astype(BF)
     rows = outs[0].shape[0]
     digit = (lax.axis_index("ctx") % rest) // (rest // split)
     for i, out in enumerate(outs):
         begin = pl.multiple_of((digit ^ i) * rows, rows)
         out[...] = grad_kv[pl.ds(begin, rows), :].astype(out.dtype)
+        Order.leave(i + 1)
+    for h in range(2):
+        for s in range(TWO):
+            here, cols = slice(h * half, (h + 1) * half), slice(s * half, (s + 1) * half)
+            grad_q_out[s * head : (s + 1) * head, here] = grad_q[h, :, cols].astype(BF)
 
 
 def query_body(experts, head, *refs):

time: 163 us -> 163 us (level)
  no operation moved by 1% of the time
where the time goes in v9:
time: 163 us
  starting transfers between devices  71.1 us (44%)
  Pallas kernels  51.3 us (31%)
  waiting for transfers between devices  38.8 us (24%)
    ppermute x33, starting transfers between devices, swap(): return lax.ppermute(values, 'ctx', [(i, i ^ mask) for i in range(size)])  53.5 us
    pallas_call x21, Pallas kernels, call(): got = list(run(*args, *moved))  51.3 us
    ppermute x33, waiting for transfers between devices, swap(): return lax.ppermute(values, 'ctx', [(i, i ^ mask) for i in range(size)])  37.7 us
    all_to_all x4, starting transfers between devices, exchange(): lax.all_to_all(parts, 'ctx', 0, 0, tiled=True, axis_index_groups=groups)  15.8 us
  transfers between devices with their start and end apart: 45, of which 16 were waited for; matrix products, arithmetic and copies ran while one was open for 0% of the time, Pallas kernels for 20%

profile of v9, /device:TPU:0, one launch (start us, length us, event | category | flops | bytes accessed | tf_op | source)
XLA Modules:
  0.0 162.7 jit_solution(6119233399513271177)
XLA Ops:
  3.5 4.0 %collective-permute-start.1 = (bf16[136,512]{1,0:T(8,128)(2,1)S(1)}, bf16[136,512]{1,0:T(8,128)(2,1)S(1)}, u32[]{:S(2)}, u32[]{:S(2)}) collective-permute-start(bf16[136,512]{1,0:T(8,128)(2,1)S(1)} %get-tuple-element.166), channel_id=1, source_target_pairs={{0,16},{2,18},{4,20},{6,22},{8,24},{10,26},{12,28},{14,30},{16,0},... | collective-permute-start | bytes 417800 | tf_op jit(solution)/shard_map/ppermute | solution.py:28
  10.4 7.7 %collective-permute-done.1.refs_2_ = bf16[136,512]{1,0:T(8,128)(2,1)S(1)} collective-permute-done((bf16[136,512]{1,0:T(8,128)(2,1)S(1)}, bf16[136,512]{1,0:T(8,128)(2,1)S(1)}, u32[]{:S(2)}, u32[]{:S(2)}) %collective-permute-start.1) | collective-permute-done | bytes 139296 | tf_op jit(solution)/shard_map/ppermute | solution.py:28
  18.7 2.4 %shard_map.196 = (bf16[4,512,128]{2,1,0:T(8,128)(2,1)}, bf16[512,512]{1,0:T(8,128)(2,1)}, bf16[512,512]{1,0:T(8,128)(2,1)}, f32[8,512]{1,0:T(8,128)}, bf16[512,128]{1,0:T(8,128)(2,1)}, /*index=5*/f32[32,128]{1,0:T(8,128)S(1)}) custom-call(bf16[128,512]{1,0:T(8,128)(2,1)S(1)} %get-tuple-element.165.refs_0_, ...), custom_call_target="tpu_custom_call" | custom-call | flops 1 | bytes 1 | tf_op jit(solution)/shard_map/pallas_call | solution.py:171
  21.6 3.9 %all-to-all-start = ((bf16[4,512,128]{2,1,0:T(8,128)(2,1)}), bf16[4,512,128]{2,1,0:T(8,128)(2,1)S(1)}, u32[]{:S(2)}, u32[]{:S(2)}) async-start(bf16[4,512,128]{2,1,0:T(8,128)(2,1)} %get-tuple-element.173), calls=%async_computation | async-start | bytes 1048576 | tf_op jit(solution)/shard_map/all_to_all | solution.py:42
  25.5 2.3 %collective-permute-start.5 = (bf16[128,512]{1,0:T(8,128)(2,1)}, bf16[128,512]{1,0:T(8,128)(2,1)S(1)}, u32[]{:S(2)}, u32[]{:S(2)}) collective-permute-start(bf16[128,512]{1,0:T(8,128)(2,1)} %get-tuple-element.191), channel_id=1, source_target_pairs={{0,8},{2,10},{4,12},{6,14},{8,0},{10,2},{12,4},{14,6},{16,24},{18,... | collective-permute-start | bytes 393224 | tf_op jit(solution)/shard_map/ppermute | solution.py:28
  31.3 2.8 %shard_map.197 = (bf16[128,512]{1,0:T(8,128)(2,1)}, bf16[512,512]{1,0:T(8,128)(2,1)}, f32[2,512]{1,0:T(2,128)S(1)}, f32[2,512]{1,0:T(2,128)}, f32[8,512]{1,0:T(8...) custom-call(bf16[512,512]{1,0:T(8,128)(2,1)} %get-tuple-element.174.refs, ...), custom_call_target="tpu_custom_call" | custom-call | flops 1 | bytes 1 | tf_op jit(solution)/shard_map/pallas_call | solution.py:171
  34.1 5.7 %shard_map.198 = (f32[128,512]{1,0:T(8,128)}, f32[2,512]{1,0:T(2,128)}, bf16[512,512]{1,0:T(8,128)(2,1)}, f32[512,512]{1,0:T(8,128)S(1)}, bf16[512,512]{1,0:T(8,...) custom-call(s32[16]{0:T(128)S(1)} %copy-done.1, ...), custom_call_target="tpu_custom_call" | custom-call | flops 1 | bytes 1 | tf_op jit(solution)/shard_map/pallas_call | solution.py:171
  40.6 6.5 %shard_map.199 = (f32[512,512]{1,0:T(8,128)S(1)}, f32[512,512]{1,0:T(8,128)S(1)}, bf16[1024,512]{1,0:T(8,128)(2,1)S(1)}, bf16[512,512]{1,0:T(8,128)(2,1)}, bf16[...) custom-call(bf16[512,512]{1,0:T(8,128)(2,1)S(1)} %get-tuple-element., ...), custom_call_target="tpu_custom_call" | custom-call | flops 1 | bytes 1 | tf_op jit(solution)/shard_map/pallas_call | solution.py:171
  47.7 5.3 %shard_map.200 = (f32[128,512]{1,0:T(8,128)}, bf16[128,512]{1,0:T(8,128)(2,1)}, bf16[128,512]{1,0:T(8,128)(2,1)}, bf16[128,512]{1,0:T(8,128)(2,1)}, f32[512,512]...) custom-call(bf16[512,512]{1,0:T(8,128)(2,1)S(1)} %get-tuple-element., ...), custom_call_target="tpu_custom_call" | custom-call | flops 1 | bytes 1 | tf_op jit(solution)/shard_map/pallas_call | solution.py:171
  53.1 3.7 %shard_map.201 = (f32[512,512]{1,0:T(8,128)}, bf16[512,512]{1,0:T(8,128)(2,1)}, bf16[128,512]{1,0:T(8,128)(2,1)S(1)}, f32[2,512]{1,0:T(2,128)S(1)}, f32[8,512]{1...) custom-call(f32[512,512]{1,0:T(8,128)S(1)} %get-tuple-element.208.re, ...), custom_call_target="tpu_custom_call" | custom-call | flops 1 | bytes 1 | tf_op jit(solution)/shard_map/pallas_call | solution.py:171
  56.8 4.4 %all-to-all-start.2 = ((bf16[4,320,512]{2,1,0:T(8,128)(2,1)}), bf16[4,320,512]{2,1,0:T(8,128)(2,1)S(1)}, u32[]{:S(2)}, u32[]{:S(2)}) async-start(bf16[4,320,512]{2,1,0:T(8,128)(2,1)} %get-tuple-element.274), calls=%async_computation.2 | async-start | bytes 2621440 | tf_op jit(solution)/shard_map/all_to_all | solution.py:42
  61.1 2.4 %collective-permute-start.12 = (bf16[128,512]{1,0:T(8,128)(2,1)S(1)}, bf16[128,512]{1,0:T(8,128)(2,1)S(1)}, u32[]{:S(2)}, u32[]{:S(2)}) collective-permute-start(bf16[128,512]{1,0:T(8,128)(2,1)S(1)} %copy-done.10), channel_id=1, source_target_pairs={{0,8},{2,10},{4,12},{6,14},{8,0},{10,2},{12,4},{14,6},{16,24},{18,... | collective-permute-start | bytes 393224 | tf_op jit(solution)/shard_map/ppermute | solution.py:28
  66.5 6.5 %shard_map.202 = (bf16[128,512]{1,0:T(8,128)(2,1)S(1)}, f32[512,128]{1,0:T(8,128)}, bf16[512,128]{1,0:T(8,128)(2,1)}, bf16[512,128]{1,0:T(8,128)(2,1)}, bf16[512...) custom-call(s32[16]{0:T(128)S(1)} %copy-done.1, ...), custom_call_target="tpu_custom_call" | custom-call | flops 1 | bytes 1 | tf_op jit(solution)/shard_map/pallas_call | solution.py:171
  78.5 3.6 %shard_map.203 = (bf16[256,512]{1,0:T(8,128)(2,1)}, bf16[256,512]{1,0:T(8,128)(2,1)}, bf16[512,512]{1,0:T(8,128)(2,1)}, f32[512,512]{1,0:T(8,128)S(1)}, f32[512,...) custom-call(bf16[128,512]{1,0:T(8,128)(2,1)S(1)} %get-tuple-element., ...), custom_call_target="tpu_custom_call" | custom-call | flops 1 | bytes 1 | tf_op jit(solution)/shard_map/pallas_call | solution.py:171
  84.3 2.3 %shard_map.204 = (f32[128,512]{1,0:T(8,128)}, bf16[128,512]{1,0:T(8,128)(2,1)}, bf16[128,512]{1,0:T(8,128)(2,1)}, bf16[128,512]{1,0:T(8,128)(2,1)}, f32[80,512]{...) custom-call(f32[512,128]{1,0:T(8,128)S(1)} %get-tuple-element.254.refs_0_, ...), custom_call_target="tpu_custom_call" | custom-call | flops 1 | bytes 1 | tf_op jit(solution)/shard_map/pallas_call | solution.py:171
  87.8 3.5 %all-to-all-start.1 = ((bf16[4,192,512]{2,1,0:T(8,128)(2,1)}), bf16[4,192,512]{2,1,0:T(8,128)(2,1)S(1)}, u32[]{:S(2)}, u32[]{:S(2)}) async-start(bf16[4,192,512]{2,1,0:T(8,128)(2,1)} %shard_map.205), calls=%async_computation.1 | async-start | bytes 1572864 | tf_op jit(solution)/shard_map/all_to_all | solution.py:42
  93.0 2.5 %collective-permute-start.20 = (bf16[80,512]{1,0:T(8,128)(2,1)S(1)}, bf16[80,512]{1,0:T(8,128)(2,1)S(1)}, u32[]{:S(2)}, u32[]{:S(2)}) collective-permute-start(bf16[80,512]{1,0:T(8,128)(2,1)S(1)} %get-tuple-element.282), channel_id=1, source_target_pairs={{0,8},{2,10},{4,12},{6,14},{8,0},{10,2},{12,4},{14,6},{16,24},{18,... | collective-permute-start | bytes 245768 | tf_op jit(solution)/shard_map/ppermute | solution.py:28
  101.9 5.9 %collective-permute-done.21.refs_2_ = bf16[80,512]{1,0:T(8,128)(2,1)S(1)} collective-permute-done((bf16[80,512]{1,0:T(8,128)(2,1)S(1)}, bf16[80,512]{1,0:T(8,128)(2,1)S(1)}, u32[]{:S(2)}, u32[]{:S(2)}) %collective-permute-start.21) | collective-permute-done | bytes 81952 | tf_op jit(solution)/shard_map/ppermute | solution.py:28
  107.9 2.5 %collective-permute-start.28 = (bf16[80,512]{1,0:T(8,128)(2,1)S(1)}, bf16[80,512]{1,0:T(8,128)(2,1)S(1)}, u32[]{:S(2)}, u32[]{:S(2)}) collective-permute-start(bf16[80,512]{1,0:T(8,128)(2,1)S(1)} %shard_map.208.refs_0_), channel_id=1, source_target_pairs={{0,24},{2,26},{4,28},{6,30},{8,16},{10,18},{12,20},{14,22},{16,8},... | collective-permute-start | bytes 245768 | tf_op jit(solution)/shard_map/ppermute | solution.py:28
  112.7 2.2 %shard_map.210 = f32[4,128,512]{2,1,0:T(8,128)} custom-call(f32[128,512]{1,0:T(8,128)} %get-tuple-element.290.refs_0_, bf16[128,512]{1,0:T(8,128)(2,1)} %copy-done.4, bf16[128,512]{1,0:T(8,128)(2,1)} %copy-done.5, bf16[128,512]{1,0:T(8,128)(2,1)} %copy-done.6), custom_call_target="tpu_custom_call" | custom-call | flops 1 | bytes 1 | tf_op jit(solution)/shard_map/pallas_call | solution.py:171
  114.9 2.8 %collective-permute-done.27.refs_2_ = bf16[80,512]{1,0:T(8,128)(2,1)S(1)} collective-permute-done((bf16[80,512]{1,0:T(8,128)(2,1)S(1)}, bf16[80,512]{1,0:T(8,128)(2,1)S(1)}, u32[]{:S(2)}, u32[]{:S(2)}) %collective-permute-start.27) | collective-permute-done | bytes 81952 | tf_op jit(solution)/shard_map/ppermute | solution.py:28
  119.0 4.0 %all-to-all-start.3 = ((bf16[4,320,512]{2,1,0:T(8,128)(2,1)}), bf16[4,320,512]{2,1,0:T(8,128)(2,1)S(1)}, u32[]{:S(2)}, u32[]{:S(2)}) async-start(bf16[4,320,512]{2,1,0:T(8,128)(2,1)} %shard_map.211), calls=%async_computation.3 | async-start | bytes 2621440 | tf_op jit(solution)/shard_map/all_to_all | solution.py:42
  123.6 3.4 %collective-permute-start.30 = (bf16[88,512]{1,0:T(8,128)(2,1)S(1)}, bf16[88,512]{1,0:T(8,128)(2,1)S(1)}, u32[]{:S(2)}, u32[]{:S(2)}) collective-permute-start(bf16[88,512]{1,0:T(8,128)(2,1)S(1)} %get-tuple-element.294), channel_id=1, source_target_pairs={{0,16},{2,18},{4,20},{6,22},{8,24},{10,26},{12,28},{14,30},{16,0},... | collective-permute-start | bytes 270344 | tf_op jit(solution)/shard_map/ppermute | solution.py:28
  128.5 5.5 %collective-permute-done.30.refs_2_ = bf16[88,512]{1,0:T(8,128)(2,1)S(1)} collective-permute-done((bf16[88,512]{1,0:T(8,128)(2,1)S(1)}, bf16[88,512]{1,0:T(8,128)(2,1)S(1)}, u32[]{:S(2)}, u32[]{:S(2)}) %collective-permute-start.30) | collective-permute-done | bytes 90144 | tf_op jit(solution)/shard_map/ppermute | solution.py:28
  134.0 2.5 %collective-permute-start.34 = (bf16[88,512]{1,0:T(8,128)(2,1)S(1)}, bf16[88,512]{1,0:T(8,128)(2,1)S(1)}, u32[]{:S(2)}, u32[]{:S(2)}) collective-permute-start(bf16[88,512]{1,0:T(8,128)(2,1)S(1)} %shard_map.212.refs_0_), channel_id=1, source_target_pairs={{0,24},{2,26},{4,28},{6,30},{8,16},{10,18},{12,20},{14,22},{16,8},... | collective-permute-start | bytes 270344 | tf_op jit(solution)/shard_map/ppermute | solution.py:28
  138.5 2.9 %collective-permute-done.34.refs_3_ = bf16[88,512]{1,0:T(8,128)(2,1)S(1)} collective-permute-done((bf16[88,512]{1,0:T(8,128)(2,1)S(1)}, bf16[88,512]{1,0:T(8,128)(2,1)S(1)}, u32[]{:S(2)}, u32[]{:S(2)}) %collective-permute-start.34) | collective-permute-done | bytes 90144 | tf_op jit(solution)/shard_map/ppermute | solution.py:28
  141.4 2.4 %collective-permute-done.33.refs_2_ = bf16[88,512]{1,0:T(8,128)(2,1)S(1)} collective-permute-done((bf16[88,512]{1,0:T(8,128)(2,1)S(1)}, bf16[88,512]{1,0:T(8,128)(2,1)S(1)}, u32[]{:S(2)}, u32[]{:S(2)}) %collective-permute-start.33) | collective-permute-done | bytes 90144 | tf_op jit(solution)/shard_map/ppermute | solution.py:28
  143.9 2.7 %collective-permute-start.37 = (bf16[1,352,512]{2,1,0:T(8,128)(2,1)S(1)}, bf16[1,352,512]{2,1,0:T(8,128)(2,1)S(1)}, u32[]{:S(2)}, u32[]{:S(2)}) collective-permute-start(bf16[1,352,512]{2,1,0:T(8,128)(2,1)S(1)} %shard_map.213.refs_0_), channel_id=1, source_target_pairs={{0,6},{2,4},{4,2},{6,0},{8,14},{10,12},{12,10},{14,8},{16,22},{18,... | collective-permute-start | bytes 1081352 | tf_op jit(solution)/shard_map/ppermute | solution.py:28
  147.4 2.5 %collective-permute-start.39 = (bf16[128,512]{1,0:T(8,128)(2,1)}, bf16[128,512]{1,0:T(8,128)(2,1)S(1)}, u32[]{:S(2)}, u32[]{:S(2)}) collective-permute-start(bf16[128,512]{1,0:T(8,128)(2,1)} %get-tuple-element.306), channel_id=1, source_target_pairs={{0,16},{2,18},{4,20},{6,22},{8,24},{10,26},{12,28},{14,30},{16,0},... | collective-permute-start | bytes 393224 | tf_op jit(solution)/shard_map/ppermute | solution.py:28
  149.9 3.2 %collective-permute-done.38.refs_6_ = bf16[128,512]{1,0:T(8,128)(2,1)S(1)} collective-permute-done((bf16[128,512]{1,0:T(8,128)(2,1)}, bf16[128,512]{1,0:T(8,128)(2,1)S(1)}, u32[]{:S(2)}, u32[]{:S(2)}) %collective-permute-start.38) | collective-permute-done | bytes 131104 | tf_op jit(solution)/shard_map/ppermute | solution.py:28
  153.1 3.1 %collective-permute-start.40 = (bf16[128,512]{1,0:T(8,128)(2,1)S(1)}, bf16[128,512]{1,0:T(8,128)(2,1)S(1)}, u32[]{:S(2)}, u32[]{:S(2)}) collective-permute-start(bf16[128,512]{1,0:T(8,128)(2,1)S(1)} %copy-done.7), channel_id=1, source_target_pairs={{0,24},{2,26},{4,28},{6,30},{8,16},{10,18},{12,20},{14,22},{16,8},... | collective-permute-start | bytes 393224 | tf_op jit(solution)/shard_map/ppermute | solution.py:28
  160.3 2.2 %shard_map.215 = (f32[256,2048]{1,0:T(8,128)}, f32[256,512]{1,0:T(8,128)}, f32[256,512]{1,0:T(8,128)}, f32[256,128]{1,0:T(8,128)}, f32[8,256]{1,0:T(8,128)}, /*i...) custom-call(bf16[1,352,512]{2,1,0:T(8,128)(2,1)S(1)} %shard_map.213.refs_0_, ...), custom_call_target="tpu_custom_call" | custom-call | flops 1 | bytes 1 | tf_op jit(solution)/shard_map/pallas_call | solution.py:171
  (108 shorter events, 44.1 us)
Async XLA Ops:
  2.9 15.8 %collective-permute-start.4 = (bf16[264,1152]{1,0:T(8,128)(2,1)S(1)}, bf16[264,1152]{1,0:T(8,128)(2,1)S(1)}, u32[]{:S(2)}, u32[]{:S(2)}) collective-permute-start(bf16[264,1152]{1,0:T(8,128)(2,1)S(1)} %get-tuple-element.168), channel_id=1, source_target_pairs={{0,1},{1,0},{2,3},{3,2},{4,5},{5,4},{6,7},{7,6},{8,9},{9,8},{10,11... | collective-permute-start | bytes 1824776 | tf_op jit(solution)/shard_map/ppermute | solution.py:46
  3.5 14.5 %collective-permute-start.1 = (bf16[136,512]{1,0:T(8,128)(2,1)S(1)}, bf16[136,512]{1,0:T(8,128)(2,1)S(1)}, u32[]{:S(2)}, u32[]{:S(2)}) collective-permute-start(bf16[136,512]{1,0:T(8,128)(2,1)S(1)} %get-tuple-element.166), channel_id=1, source_target_pairs={{0,16},{2,18},{4,20},{6,22},{8,24},{10,26},{12,28},{14,30},{16,0},... | collective-permute-start | bytes 417800 | tf_op jit(solution)/shard_map/ppermute | solution.py:28
  7.5 10.5 %collective-permute-start.2 = (bf16[136,512]{1,0:T(8,128)(2,1)S(1)}, bf16[136,512]{1,0:T(8,128)(2,1)S(1)}, u32[]{:S(2)}, u32[]{:S(2)}) collective-permute-start(bf16[136,512]{1,0:T(8,128)(2,1)S(1)} %get-tuple-element.167), channel_id=1, source_target_pairs={{0,24},{2,26},{4,28},{6,30},{8,16},{10,18},{12,20},{14,22},{16,8},... | collective-permute-start | bytes 417800 | tf_op jit(solution)/shard_map/ppermute | solution.py:28
  8.9 9.8 %collective-permute-start = (bf16[136,512]{1,0:T(8,128)(2,1)S(1)}, bf16[136,512]{1,0:T(8,128)(2,1)S(1)}, u32[]{:S(2)}, u32[]{:S(2)}) collective-permute-start(bf16[136,512]{1,0:T(8,128)(2,1)S(1)} %get-tuple-element.164), channel_id=1, source_target_pairs={{0,8},{2,10},{4,12},{6,14},{8,0},{10,2},{12,4},{14,6},{16,24},{18,... | collective-permute-start | bytes 417800 | tf_op jit(solution)/shard_map/ppermute | solution.py:28
  21.1 19.5 %collective-permute-start.8 = (bf16[256,2048]{1,0:T(8,128)(2,1)}, bf16[256,2048]{1,0:T(8,128)(2,1)S(1)}, u32[]{:S(2)}, u32[]{:S(2)}) collective-permute-start(bf16[256,2048]{1,0:T(8,128)(2,1)} %refs_10_.3), channel_id=1, source_target_pairs={{0,1},{1,0},{2,3},{3,2},{4,5},{5,4},{6,7},{7,6},{8,9},{9,8},{10,11... | collective-permute-start | bytes 3145736 | tf_op jit(solution)/shard_map/ppermute | solution.py:46
  21.1 19.5 %collective-permute-start.9 = (bf16[1024,512]{1,0:T(8,128)(2,1)}, bf16[1024,512]{1,0:T(8,128)(2,1)S(1)}, u32[]{:S(2)}, u32[]{:S(2)}) collective-permute-start(bf16[1024,512]{1,0:T(8,128)(2,1)} %refs_11_.1), channel_id=1, source_target_pairs={{0,1},{1,0},{2,3},{3,2},{4,5},{5,4},{6,7},{7,6},{8,9},{9,8},{10,11... | collective-permute-start | bytes 3145736 | tf_op jit(solution)/shard_map/ppermute | solution.py:46
  21.6 12.5 %all-to-all-start = ((bf16[4,512,128]{2,1,0:T(8,128)(2,1)}), bf16[4,512,128]{2,1,0:T(8,128)(2,1)S(1)}, u32[]{:S(2)}, u32[]{:S(2)}) async-start(bf16[4,512,128]{2,1,0:T(8,128)(2,1)} %get-tuple-element.173), calls=%async_computation | async-start | bytes 1048576 | tf_op jit(solution)/shard_map/all_to_all | solution.py:42
  25.5 14.3 %collective-permute-start.5 = (bf16[128,512]{1,0:T(8,128)(2,1)}, bf16[128,512]{1,0:T(8,128)(2,1)S(1)}, u32[]{:S(2)}, u32[]{:S(2)}) collective-permute-start(bf16[128,512]{1,0:T(8,128)(2,1)} %get-tuple-element.191), channel_id=1, source_target_pairs={{0,8},{2,10},{4,12},{6,14},{8,0},{10,2},{12,4},{14,6},{16,24},{18,... | collective-permute-start | bytes 393224 | tf_op jit(solution)/shard_map/ppermute | solution.py:28
  27.9 12.0 %collective-permute-start.6 = (bf16[128,512]{1,0:T(8,128)(2,1)}, bf16[128,512]{1,0:T(8,128)(2,1)S(1)}, u32[]{:S(2)}, u32[]{:S(2)}) collective-permute-start(bf16[128,512]{1,0:T(8,128)(2,1)} %copy-done.3), channel_id=1, source_target_pairs={{0,16},{2,18},{4,20},{6,22},{8,24},{10,26},{12,28},{14,30},{16,0},... | collective-permute-start | bytes 393224 | tf_op jit(solution)/shard_map/ppermute | solution.py:28
  29.8 10.8 %collective-permute-start.7 = (bf16[128,512]{1,0:T(8,128)(2,1)}, bf16[128,512]{1,0:T(8,128)(2,1)}, u32[]{:S(2)}, u32[]{:S(2)}) collective-permute-start(bf16[128,512]{1,0:T(8,128)(2,1)} %copy-done.2), channel_id=1, source_target_pairs={{0,24},{2,26},{4,28},{6,30},{8,16},{10,18},{12,20},{14,22},{16,8},... | collective-permute-start | bytes 393224 | tf_op jit(solution)/shard_map/ppermute | solution.py:28
  56.8 31.0 %all-to-all-start.2 = ((bf16[4,320,512]{2,1,0:T(8,128)(2,1)}), bf16[4,320,512]{2,1,0:T(8,128)(2,1)S(1)}, u32[]{:S(2)}, u32[]{:S(2)}) async-start(bf16[4,320,512]{2,1,0:T(8,128)(2,1)} %get-tuple-element.274), calls=%async_computation.2 | async-start | bytes 2621440 | tf_op jit(solution)/shard_map/all_to_all | solution.py:42
  61.1 14.1 %collective-permute-start.12 = (bf16[128,512]{1,0:T(8,128)(2,1)S(1)}, bf16[128,512]{1,0:T(8,128)(2,1)S(1)}, u32[]{:S(2)}, u32[]{:S(2)}) collective-permute-start(bf16[128,512]{1,0:T(8,128)(2,1)S(1)} %copy-done.10), channel_id=1, source_target_pairs={{0,8},{2,10},{4,12},{6,14},{8,0},{10,2},{12,4},{14,6},{16,24},{18,... | collective-permute-start | bytes 393224 | tf_op jit(solution)/shard_map/ppermute | solution.py:28
  63.6 13.1 %collective-permute-start.13 = (bf16[128,512]{1,0:T(8,128)(2,1)S(1)}, bf16[128,512]{1,0:T(8,128)(2,1)S(1)}, u32[]{:S(2)}, u32[]{:S(2)}) collective-permute-start(bf16[128,512]{1,0:T(8,128)(2,1)S(1)} %copy-done.9), channel_id=1, source_target_pairs={{0,16},{2,18},{4,20},{6,22},{8,24},{10,26},{12,28},{14,30},{16,0},... | collective-permute-start | bytes 393224 | tf_op jit(solution)/shard_map/ppermute | solution.py:28
  65.1 21.6 %collective-permute-start.18 = (bf16[512,512]{1,0:T(8,128)(2,1)}, bf16[512,512]{1,0:T(8,128)(2,1)S(1)}, u32[]{:S(2)}, u32[]{:S(2)}) collective-permute-start(bf16[512,512]{1,0:T(8,128)(2,1)} %get-tuple-element.273), channel_id=1, source_target_pairs={{0,1},{1,0},{2,3},{3,2},{4,5},{5,4},{6,7},{7,6},{8,9},{9,8},{10,11... | collective-permute-start | bytes 1572872 | tf_op jit(solution)/shard_map/ppermute | solution.py:46
  65.1 13.5 %collective-permute-start.14 = (bf16[128,512]{1,0:T(8,128)(2,1)S(1)}, bf16[128,512]{1,0:T(8,128)(2,1)S(1)}, u32[]{:S(2)}, u32[]{:S(2)}) collective-permute-start(bf16[128,512]{1,0:T(8,128)(2,1)S(1)} %copy-done.8), channel_id=1, source_target_pairs={{0,24},{2,26},{4,28},{6,30},{8,16},{10,18},{12,20},{14,22},{16,8},... | collective-permute-start | bytes 393224 | tf_op jit(solution)/shard_map/ppermute | solution.py:28
  73.1 9.0 %collective-permute-start.15 = (bf16[512,128]{1,0:T(8,128)(2,1)}, bf16[512,128]{1,0:T(8,128)(2,1)S(1)}, u32[]{:S(2)}, u32[]{:S(2)}) collective-permute-start(bf16[512,128]{1,0:T(8,128)(2,1)} %get-tuple-element.255), channel_id=1, source_target_pairs={{0,2},{2,0},{4,6},{6,4},{8,10},{10,8},{12,14},{14,12},{16,18},{18,... | collective-permute-start | bytes 393224 | tf_op jit(solution)/shard_map/ppermute | solution.py:28
  76.6 7.7 %collective-permute-start.17 = (bf16[512,128]{1,0:T(8,128)(2,1)}, bf16[512,128]{1,0:T(8,128)(2,1)S(1)}, u32[]{:S(2)}, u32[]{:S(2)}) collective-permute-start(bf16[512,128]{1,0:T(8,128)(2,1)} %get-tuple-element.257), channel_id=1, source_target_pairs={{0,6},{2,4},{4,2},{6,0},{8,14},{10,12},{12,10},{14,8},{16,22},{18,... | collective-permute-start | bytes 393224 | tf_op jit(solution)/shard_map/ppermute | solution.py:28
  87.8 24.6 %all-to-all-start.1 = ((bf16[4,192,512]{2,1,0:T(8,128)(2,1)}), bf16[4,192,512]{2,1,0:T(8,128)(2,1)S(1)}, u32[]{:S(2)}, u32[]{:S(2)}) async-start(bf16[4,192,512]{2,1,0:T(8,128)(2,1)} %shard_map.205), calls=%async_computation.1 | async-start | bytes 1572864 | tf_op jit(solution)/shard_map/all_to_all | solution.py:42
  93.0 7.6 %collective-permute-start.20 = (bf16[80,512]{1,0:T(8,128)(2,1)S(1)}, bf16[80,512]{1,0:T(8,128)(2,1)S(1)}, u32[]{:S(2)}, u32[]{:S(2)}) collective-permute-start(bf16[80,512]{1,0:T(8,128)(2,1)S(1)} %get-tuple-element.282), channel_id=1, source_target_pairs={{0,8},{2,10},{4,12},{6,14},{8,0},{10,2},{12,4},{14,6},{16,24},{18,... | collective-permute-start | bytes 245768 | tf_op jit(solution)/shard_map/ppermute | solution.py:28
  95.5 15.5 %collective-permute-start.23 = (bf16[160,512]{1,0:T(8,128)(2,1)S(1)}, bf16[160,512]{1,0:T(8,128)(2,1)S(1)}, u32[]{:S(2)}, u32[]{:S(2)}) collective-permute-start(bf16[160,512]{1,0:T(8,128)(2,1)S(1)} %get-tuple-element.286), channel_id=1, source_target_pairs={{0,2},{2,0},{4,6},{6,4},{8,10},{10,8},{12,14},{14,12},{16,18},{18,... | collective-permute-start | bytes 491528 | tf_op jit(solution)/shard_map/ppermute | solution.py:28
  97.4 15.0 %collective-permute-start.24 = (bf16[160,512]{1,0:T(8,128)(2,1)S(1)}, bf16[160,512]{1,0:T(8,128)(2,1)S(1)}, u32[]{:S(2)}, u32[]{:S(2)}) collective-permute-start(bf16[160,512]{1,0:T(8,128)(2,1)S(1)} %get-tuple-element.287), channel_id=1, source_target_pairs={{0,4},{2,6},{4,0},{6,2},{8,12},{10,14},{12,8},{14,10},{16,20},{18,... | collective-permute-start | bytes 491528 | tf_op jit(solution)/shard_map/ppermute | solution.py:28
  98.9 13.5 %collective-permute-start.25 = (bf16[160,512]{1,0:T(8,128)(2,1)S(1)}, bf16[160,512]{1,0:T(8,128)(2,1)S(1)}, u32[]{:S(2)}, u32[]{:S(2)}) collective-permute-start(bf16[160,512]{1,0:T(8,128)(2,1)S(1)} %get-tuple-element.288), channel_id=1, source_target_pairs={{0,6},{2,4},{4,2},{6,0},{8,14},{10,12},{12,10},{14,8},{16,22},{18,... | collective-permute-start | bytes 491528 | tf_op jit(solution)/shard_map/ppermute | solution.py:28
  99.0 8.9 %collective-permute-start.21 = (bf16[80,512]{1,0:T(8,128)(2,1)S(1)}, bf16[80,512]{1,0:T(8,128)(2,1)S(1)}, u32[]{:S(2)}, u32[]{:S(2)}) collective-permute-start(bf16[80,512]{1,0:T(8,128)(2,1)S(1)} %get-tuple-element.283), channel_id=1, source_target_pairs={{0,16},{2,18},{4,20},{6,22},{8,24},{10,26},{12,28},{14,30},{16,0},... | collective-permute-start | bytes 245768 | tf_op jit(solution)/shard_map/ppermute | solution.py:28
  100.5 7.3 %collective-permute-start.22 = (bf16[80,512]{1,0:T(8,128)(2,1)S(1)}, bf16[80,512]{1,0:T(8,128)(2,1)S(1)}, u32[]{:S(2)}, u32[]{:S(2)}) collective-permute-start(bf16[80,512]{1,0:T(8,128)(2,1)S(1)} %get-tuple-element.284), channel_id=1, source_target_pairs={{0,24},{2,26},{4,28},{6,30},{8,16},{10,18},{12,20},{14,22},{16,8},... | collective-permute-start | bytes 245768 | tf_op jit(solution)/shard_map/ppermute | solution.py:28
  110.4 7.4 %collective-permute-start.27 = (bf16[80,512]{1,0:T(8,128)(2,1)S(1)}, bf16[80,512]{1,0:T(8,128)(2,1)S(1)}, u32[]{:S(2)}, u32[]{:S(2)}) collective-permute-start(bf16[80,512]{1,0:T(8,128)(2,1)S(1)} %shard_map.208.refs_0_), channel_id=1, source_target_pairs={{0,16},{2,18},{4,20},{6,22},{8,24},{10,26},{12,28},{14,30},{16,0},... | collective-permute-start | bytes 245768 | tf_op jit(solution)/shard_map/ppermute | solution.py:28
  119.0 37.2 %all-to-all-start.3 = ((bf16[4,320,512]{2,1,0:T(8,128)(2,1)}), bf16[4,320,512]{2,1,0:T(8,128)(2,1)S(1)}, u32[]{:S(2)}, u32[]{:S(2)}) async-start(bf16[4,320,512]{2,1,0:T(8,128)(2,1)} %shard_map.211), calls=%async_computation.3 | async-start | bytes 2621440 | tf_op jit(solution)/shard_map/all_to_all | solution.py:42
  123.6 10.4 %collective-permute-start.30 = (bf16[88,512]{1,0:T(8,128)(2,1)S(1)}, bf16[88,512]{1,0:T(8,128)(2,1)S(1)}, u32[]{:S(2)}, u32[]{:S(2)}) collective-permute-start(bf16[88,512]{1,0:T(8,128)(2,1)S(1)} %get-tuple-element.294), channel_id=1, source_target_pairs={{0,16},{2,18},{4,20},{6,22},{8,24},{10,26},{12,28},{14,30},{16,0},... | collective-permute-start | bytes 270344 | tf_op jit(solution)/shard_map/ppermute | solution.py:28
  134.0 7.4 %collective-permute-start.34 = (bf16[88,512]{1,0:T(8,128)(2,1)S(1)}, bf16[88,512]{1,0:T(8,128)(2,1)S(1)}, u32[]{:S(2)}, u32[]{:S(2)}) collective-permute-start(bf16[88,512]{1,0:T(8,128)(2,1)S(1)} %shard_map.212.refs_0_), channel_id=1, source_target_pairs={{0,24},{2,26},{4,28},{6,30},{8,16},{10,18},{12,20},{14,22},{16,8},... | collective-permute-start | bytes 270344 | tf_op jit(solution)/shard_map/ppermute | solution.py:28
  143.9 16.0 %collective-permute-start.37 = (bf16[1,352,512]{2,1,0:T(8,128)(2,1)S(1)}, bf16[1,352,512]{2,1,0:T(8,128)(2,1)S(1)}, u32[]{:S(2)}, u32[]{:S(2)}) collective-permute-start(bf16[1,352,512]{2,1,0:T(8,128)(2,1)S(1)} %shard_map.213.refs_0_), channel_id=1, source_target_pairs={{0,6},{2,4},{4,2},{6,0},{8,14},{10,12},{12,10},{14,8},{16,22},{18,... | collective-permute-start | bytes 1081352 | tf_op jit(solution)/shard_map/ppermute | solution.py:28
  146.6 13.6 %collective-permute-start.36 = (bf16[1,352,512]{2,1,0:T(8,128)(2,1)S(1)}, bf16[1,352,512]{2,1,0:T(8,128)(2,1)S(1)}, u32[]{:S(2)}, u32[]{:S(2)}) collective-permute-start(bf16[1,352,512]{2,1,0:T(8,128)(2,1)S(1)} %shard_map.213.refs_0_), channel_id=1, source_target_pairs={{0,4},{2,6},{4,0},{6,2},{8,12},{10,14},{12,8},{14,10},{16,20},{18,... | collective-permute-start | bytes 1081352 | tf_op jit(solution)/shard_map/ppermute | solution.py:28
  147.1 13.2 %collective-permute-start.35 = (bf16[1,352,512]{2,1,0:T(8,128)(2,1)S(1)}, bf16[1,352,512]{2,1,0:T(8,128)(2,1)S(1)}, u32[]{:S(2)}, u32[]{:S(2)}) collective-permute-start(bf16[1,352,512]{2,1,0:T(8,128)(2,1)S(1)} %shard_map.213.refs_0_), channel_id=1, source_target_pairs={{0,2},{2,0},{4,6},{6,4},{8,10},{10,8},{12,14},{14,12},{16,18},{18,... | collective-permute-start | bytes 1081352 | tf_op jit(solution)/shard_map/ppermute | solution.py:28
  147.4 10.4 %collective-permute-start.39 = (bf16[128,512]{1,0:T(8,128)(2,1)}, bf16[128,512]{1,0:T(8,128)(2,1)S(1)}, u32[]{:S(2)}, u32[]{:S(2)}) collective-permute-start(bf16[128,512]{1,0:T(8,128)(2,1)} %get-tuple-element.306), channel_id=1, source_target_pairs={{0,16},{2,18},{4,20},{6,22},{8,24},{10,26},{12,28},{14,30},{16,0},... | collective-permute-start | bytes 393224 | tf_op jit(solution)/shard_map/ppermute | solution.py:28
  (26 other events, 233.3 us)

commit v10 on v8

--- a/solution.py
+++ b/solution.py
@@ -387,6 +387,7 @@
     half = total // 2
     block = half // count
     turn_keys(kv_ref, kv_turned)
+    Order.rest()
     sides, gaps = [], []
     for h in range(2):
         side = both_slots(qt, head, slice(h * half, (h + 1) * half))
@@ -425,7 +426,6 @@
             here, cols = slice(h * half, (h + 1) * half), slice(s * half, (s + 1) * half)
             log_out[s : s + 1, here] = logs[:, cols]
             att_out[s * head : (s + 1) * head, here] = attended[:, cols]
-    Order.rest()
     Order.leave(0, 1)
     for e in range(experts):
         part = jnp.zeros((head, total), F32)
@@ -1011,7 +1011,7 @@
         [block_order, kv, Far(qt), gates, route, *far([tok, gain_rows, wo])],
         scratch=[((keys, span), BF)],
         smem=(0,),
-        late=(5, 6, 7),
+        late=(2, 5, 6, 7),
         ahead=[
             Ahead(cotangent, (local, dim), lambda r: r.at[here()]),
             Ahead(up_w, (tall, wide), lanes(lambda: 1 - core())),

time: 163 us -> 163 us (level)
  transfers between devices with their start and end apart: 45 -> 45, of which waited for: 16 -> 16; matrix products, arithmetic and copies ran while one was open for 0% -> 0% of each run, Pallas kernels for 20% -> 21%
where the time goes in v10:
time: 163 us
  starting transfers between devices  71.1 us (44%)
  Pallas kernels  51.9 us (32%)
  waiting for transfers between devices  38.2 us (23%)
    ppermute x33, starting transfers between devices, swap(): return lax.ppermute(values, 'ctx', [(i, i ^ mask) for i in range(size)])  53.5 us
    pallas_call x21, Pallas kernels, call(): got = list(run(*args, *moved))  51.9 us
    ppermute x33, waiting for transfers between devices, swap(): return lax.ppermute(values, 'ctx', [(i, i ^ mask) for i in range(size)])  37.1 us
    all_to_all x4, starting transfers between devices, exchange(): lax.all_to_all(parts, 'ctx', 0, 0, tiled=True, axis_index_groups=groups)  15.8 us
  transfers between devices with their start and end apart: 45, of which 16 were waited for; matrix products, arithmetic and copies ran while one was open for 0% of the time, Pallas kernels for 21%

profile of v10, /device:TPU:0, one launch (start us, length us, event | category | flops | bytes accessed | tf_op | source)
XLA Modules:
  0.0 162.7 jit_solution(14006458304895761298)
XLA Ops:
  3.5 4.0 %collective-permute-start.1 = (bf16[136,512]{1,0:T(8,128)(2,1)S(1)}, bf16[136,512]{1,0:T(8,128)(2,1)S(1)}, u32[]{:S(2)}, u32[]{:S(2)}) collective-permute-start(bf16[136,512]{1,0:T(8,128)(2,1)S(1)} %get-tuple-element.166), channel_id=1, source_target_pairs={{0,16},{2,18},{4,20},{6,22},{8,24},{10,26},{12,28},{14,30},{16,0},... | collective-permute-start | bytes 417800 | tf_op jit(solution)/shard_map/ppermute | solution.py:28
  10.4 7.7 %collective-permute-done.1.refs_2_ = bf16[136,512]{1,0:T(8,128)(2,1)S(1)} collective-permute-done((bf16[136,512]{1,0:T(8,128)(2,1)S(1)}, bf16[136,512]{1,0:T(8,128)(2,1)S(1)}, u32[]{:S(2)}, u32[]{:S(2)}) %collective-permute-start.1) | collective-permute-done | bytes 139296 | tf_op jit(solution)/shard_map/ppermute | solution.py:28
  18.7 2.4 %shard_map.196 = (bf16[4,512,128]{2,1,0:T(8,128)(2,1)}, bf16[512,512]{1,0:T(8,128)(2,1)}, bf16[512,512]{1,0:T(8,128)(2,1)}, f32[8,512]{1,0:T(8,128)}, bf16[512,128]{1,0:T(8,128)(2,1)}, /*index=5*/f32[32,128]{1,0:T(8,128)S(1)}) custom-call(bf16[128,512]{1,0:T(8,128)(2,1)S(1)} %get-tuple-element.165.refs_0_, ...), custom_call_target="tpu_custom_call" | custom-call | flops 1 | bytes 1 | tf_op jit(solution)/shard_map/pallas_call | solution.py:171
  21.6 3.9 %all-to-all-start = ((bf16[4,512,128]{2,1,0:T(8,128)(2,1)}), bf16[4,512,128]{2,1,0:T(8,128)(2,1)S(1)}, u32[]{:S(2)}, u32[]{:S(2)}) async-start(bf16[4,512,128]{2,1,0:T(8,128)(2,1)} %get-tuple-element.173), calls=%async_computation | async-start | bytes 1048576 | tf_op jit(solution)/shard_map/all_to_all | solution.py:42
  25.5 2.3 %collective-permute-start.5 = (bf16[128,512]{1,0:T(8,128)(2,1)}, bf16[128,512]{1,0:T(8,128)(2,1)S(1)}, u32[]{:S(2)}, u32[]{:S(2)}) collective-permute-start(bf16[128,512]{1,0:T(8,128)(2,1)} %get-tuple-element.191), channel_id=1, source_target_pairs={{0,8},{2,10},{4,12},{6,14},{8,0},{10,2},{12,4},{14,6},{16,24},{18,... | collective-permute-start | bytes 393224 | tf_op jit(solution)/shard_map/ppermute | solution.py:28
  31.3 2.8 %shard_map.197 = (bf16[128,512]{1,0:T(8,128)(2,1)}, bf16[512,512]{1,0:T(8,128)(2,1)}, f32[2,512]{1,0:T(2,128)S(1)}, f32[2,512]{1,0:T(2,128)}, f32[8,512]{1,0:T(8...) custom-call(bf16[512,512]{1,0:T(8,128)(2,1)} %get-tuple-element.174.refs, ...), custom_call_target="tpu_custom_call" | custom-call | flops 1 | bytes 1 | tf_op jit(solution)/shard_map/pallas_call | solution.py:171
  34.1 6.3 %shard_map.198 = (f32[128,512]{1,0:T(8,128)}, f32[2,512]{1,0:T(2,128)}, bf16[512,512]{1,0:T(8,128)(2,1)}, f32[512,512]{1,0:T(8,128)S(1)}, bf16[512,512]{1,0:T(8,...) custom-call(s32[16]{0:T(128)S(1)} %copy-done.1, ...), custom_call_target="tpu_custom_call" | custom-call | flops 1 | bytes 1 | tf_op jit(solution)/shard_map/pallas_call | solution.py:171
  40.6 6.5 %shard_map.199 = (f32[512,512]{1,0:T(8,128)S(1)}, f32[512,512]{1,0:T(8,128)S(1)}, bf16[1024,512]{1,0:T(8,128)(2,1)S(1)}, bf16[512,512]{1,0:T(8,128)(2,1)}, bf16[...) custom-call(bf16[512,512]{1,0:T(8,128)(2,1)S(1)} %get-tuple-element., ...), custom_call_target="tpu_custom_call" | custom-call | flops 1 | bytes 1 | tf_op jit(solution)/shard_map/pallas_call | solution.py:171
  47.7 5.3 %shard_map.200 = (f32[128,512]{1,0:T(8,128)}, bf16[128,512]{1,0:T(8,128)(2,1)}, bf16[128,512]{1,0:T(8,128)(2,1)}, bf16[128,512]{1,0:T(8,128)(2,1)}, f32[512,512]...) custom-call(bf16[512,512]{1,0:T(8,128)(2,1)S(1)} %get-tuple-element., ...), custom_call_target="tpu_custom_call" | custom-call | flops 1 | bytes 1 | tf_op jit(solution)/shard_map/pallas_call | solution.py:171
  53.1 3.7 %shard_map.201 = (f32[512,512]{1,0:T(8,128)}, bf16[512,512]{1,0:T(8,128)(2,1)}, bf16[128,512]{1,0:T(8,128)(2,1)S(1)}, f32[2,512]{1,0:T(2,128)S(1)}, f32[8,512]{1...) custom-call(f32[512,512]{1,0:T(8,128)S(1)} %get-tuple-element.208.re, ...), custom_call_target="tpu_custom_call" | custom-call | flops 1 | bytes 1 | tf_op jit(solution)/shard_map/pallas_call | solution.py:171
  56.8 4.4 %all-to-all-start.2 = ((bf16[4,320,512]{2,1,0:T(8,128)(2,1)}), bf16[4,320,512]{2,1,0:T(8,128)(2,1)S(1)}, u32[]{:S(2)}, u32[]{:S(2)}) async-start(bf16[4,320,512]{2,1,0:T(8,128)(2,1)} %get-tuple-element.274), calls=%async_computation.2 | async-start | bytes 2621440 | tf_op jit(solution)/shard_map/all_to_all | solution.py:42
  61.1 2.4 %collective-permute-start.12 = (bf16[128,512]{1,0:T(8,128)(2,1)S(1)}, bf16[128,512]{1,0:T(8,128)(2,1)S(1)}, u32[]{:S(2)}, u32[]{:S(2)}) collective-permute-start(bf16[128,512]{1,0:T(8,128)(2,1)S(1)} %copy-done.10), channel_id=1, source_target_pairs={{0,8},{2,10},{4,12},{6,14},{8,0},{10,2},{12,4},{14,6},{16,24},{18,... | collective-permute-start | bytes 393224 | tf_op jit(solution)/shard_map/ppermute | solution.py:28
  66.5 6.5 %shard_map.202 = (bf16[128,512]{1,0:T(8,128)(2,1)S(1)}, f32[512,128]{1,0:T(8,128)}, bf16[512,128]{1,0:T(8,128)(2,1)}, bf16[512,128]{1,0:T(8,128)(2,1)}, bf16[512...) custom-call(s32[16]{0:T(128)S(1)} %copy-done.1, ...), custom_call_target="tpu_custom_call" | custom-call | flops 1 | bytes 1 | tf_op jit(solution)/shard_map/pallas_call | solution.py:171
  78.5 3.6 %shard_map.203 = (bf16[256,512]{1,0:T(8,128)(2,1)}, bf16[256,512]{1,0:T(8,128)(2,1)}, bf16[512,512]{1,0:T(8,128)(2,1)}, f32[512,512]{1,0:T(8,128)S(1)}, f32[512,...) custom-call(bf16[128,512]{1,0:T(8,128)(2,1)S(1)} %get-tuple-element., ...), custom_call_target="tpu_custom_call" | custom-call | flops 1 | bytes 1 | tf_op jit(solution)/shard_map/pallas_call | solution.py:171
  84.3 2.3 %shard_map.204 = (f32[128,512]{1,0:T(8,128)}, bf16[128,512]{1,0:T(8,128)(2,1)}, bf16[128,512]{1,0:T(8,128)(2,1)}, bf16[128,512]{1,0:T(8,128)(2,1)}, f32[80,512]{...) custom-call(f32[512,128]{1,0:T(8,128)S(1)} %get-tuple-element.254.refs_0_, ...), custom_call_target="tpu_custom_call" | custom-call | flops 1 | bytes 1 | tf_op jit(solution)/shard_map/pallas_call | solution.py:171
  87.8 3.5 %all-to-all-start.1 = ((bf16[4,192,512]{2,1,0:T(8,128)(2,1)}), bf16[4,192,512]{2,1,0:T(8,128)(2,1)S(1)}, u32[]{:S(2)}, u32[]{:S(2)}) async-start(bf16[4,192,512]{2,1,0:T(8,128)(2,1)} %shard_map.205), calls=%async_computation.1 | async-start | bytes 1572864 | tf_op jit(solution)/shard_map/all_to_all | solution.py:42
  93.0 2.5 %collective-permute-start.20 = (bf16[80,512]{1,0:T(8,128)(2,1)S(1)}, bf16[80,512]{1,0:T(8,128)(2,1)S(1)}, u32[]{:S(2)}, u32[]{:S(2)}) collective-permute-start(bf16[80,512]{1,0:T(8,128)(2,1)S(1)} %get-tuple-element.282), channel_id=1, source_target_pairs={{0,8},{2,10},{4,12},{6,14},{8,0},{10,2},{12,4},{14,6},{16,24},{18,... | collective-permute-start | bytes 245768 | tf_op jit(solution)/shard_map/ppermute | solution.py:28
  101.9 5.9 %collective-permute-done.21.refs_2_ = bf16[80,512]{1,0:T(8,128)(2,1)S(1)} collective-permute-done((bf16[80,512]{1,0:T(8,128)(2,1)S(1)}, bf16[80,512]{1,0:T(8,128)(2,1)S(1)}, u32[]{:S(2)}, u32[]{:S(2)}) %collective-permute-start.21) | collective-permute-done | bytes 81952 | tf_op jit(solution)/shard_map/ppermute | solution.py:28
  107.9 2.5 %collective-permute-start.28 = (bf16[80,512]{1,0:T(8,128)(2,1)S(1)}, bf16[80,512]{1,0:T(8,128)(2,1)S(1)}, u32[]{:S(2)}, u32[]{:S(2)}) collective-permute-start(bf16[80,512]{1,0:T(8,128)(2,1)S(1)} %shard_map.208.refs_0_), channel_id=1, source_target_pairs={{0,24},{2,26},{4,28},{6,30},{8,16},{10,18},{12,20},{14,22},{16,8},... | collective-permute-start | bytes 245768 | tf_op jit(solution)/shard_map/ppermute | solution.py:28
  112.7 2.2 %shard_map.210 = f32[4,128,512]{2,1,0:T(8,128)} custom-call(f32[128,512]{1,0:T(8,128)} %get-tuple-element.290.refs_0_, bf16[128,512]{1,0:T(8,128)(2,1)} %copy-done.4, bf16[128,512]{1,0:T(8,128)(2,1)} %copy-done.5, bf16[128,512]{1,0:T(8,128)(2,1)} %copy-done.6), custom_call_target="tpu_custom_call" | custom-call | flops 1 | bytes 1 | tf_op jit(solution)/shard_map/pallas_call | solution.py:171
  114.9 2.8 %collective-permute-done.27.refs_2_ = bf16[80,512]{1,0:T(8,128)(2,1)S(1)} collective-permute-done((bf16[80,512]{1,0:T(8,128)(2,1)S(1)}, bf16[80,512]{1,0:T(8,128)(2,1)S(1)}, u32[]{:S(2)}, u32[]{:S(2)}) %collective-permute-start.27) | collective-permute-done | bytes 81952 | tf_op jit(solution)/shard_map/ppermute | solution.py:28
  119.0 4.0 %all-to-all-start.3 = ((bf16[4,320,512]{2,1,0:T(8,128)(2,1)}), bf16[4,320,512]{2,1,0:T(8,128)(2,1)S(1)}, u32[]{:S(2)}, u32[]{:S(2)}) async-start(bf16[4,320,512]{2,1,0:T(8,128)(2,1)} %shard_map.211), calls=%async_computation.3 | async-start | bytes 2621440 | tf_op jit(solution)/shard_map/all_to_all | solution.py:42
  123.6 3.4 %collective-permute-start.30 = (bf16[88,512]{1,0:T(8,128)(2,1)S(1)}, bf16[88,512]{1,0:T(8,128)(2,1)S(1)}, u32[]{:S(2)}, u32[]{:S(2)}) collective-permute-start(bf16[88,512]{1,0:T(8,128)(2,1)S(1)} %get-tuple-element.294), channel_id=1, source_target_pairs={{0,16},{2,18},{4,20},{6,22},{8,24},{10,26},{12,28},{14,30},{16,0},... | collective-permute-start | bytes 270344 | tf_op jit(solution)/shard_map/ppermute | solution.py:28
  128.5 5.5 %collective-permute-done.30.refs_2_ = bf16[88,512]{1,0:T(8,128)(2,1)S(1)} collective-permute-done((bf16[88,512]{1,0:T(8,128)(2,1)S(1)}, bf16[88,512]{1,0:T(8,128)(2,1)S(1)}, u32[]{:S(2)}, u32[]{:S(2)}) %collective-permute-start.30) | collective-permute-done | bytes 90144 | tf_op jit(solution)/shard_map/ppermute | solution.py:28
  134.0 2.5 %collective-permute-start.34 = (bf16[88,512]{1,0:T(8,128)(2,1)S(1)}, bf16[88,512]{1,0:T(8,128)(2,1)S(1)}, u32[]{:S(2)}, u32[]{:S(2)}) collective-permute-start(bf16[88,512]{1,0:T(8,128)(2,1)S(1)} %shard_map.212.refs_0_), channel_id=1, source_target_pairs={{0,24},{2,26},{4,28},{6,30},{8,16},{10,18},{12,20},{14,22},{16,8},... | collective-permute-start | bytes 270344 | tf_op jit(solution)/shard_map/ppermute | solution.py:28
  138.5 2.9 %collective-permute-done.34.refs_3_ = bf16[88,512]{1,0:T(8,128)(2,1)S(1)} collective-permute-done((bf16[88,512]{1,0:T(8,128)(2,1)S(1)}, bf16[88,512]{1,0:T(8,128)(2,1)S(1)}, u32[]{:S(2)}, u32[]{:S(2)}) %collective-permute-start.34) | collective-permute-done | bytes 90144 | tf_op jit(solution)/shard_map/ppermute | solution.py:28
  141.4 2.4 %collective-permute-done.33.refs_2_ = bf16[88,512]{1,0:T(8,128)(2,1)S(1)} collective-permute-done((bf16[88,512]{1,0:T(8,128)(2,1)S(1)}, bf16[88,512]{1,0:T(8,128)(2,1)S(1)}, u32[]{:S(2)}, u32[]{:S(2)}) %collective-permute-start.33) | collective-permute-done | bytes 90144 | tf_op jit(solution)/shard_map/ppermute | solution.py:28
  143.9 2.7 %collective-permute-start.37 = (bf16[1,352,512]{2,1,0:T(8,128)(2,1)S(1)}, bf16[1,352,512]{2,1,0:T(8,128)(2,1)S(1)}, u32[]{:S(2)}, u32[]{:S(2)}) collective-permute-start(bf16[1,352,512]{2,1,0:T(8,128)(2,1)S(1)} %shard_map.213.refs_0_), channel_id=1, source_target_pairs={{0,6},{2,4},{4,2},{6,0},{8,14},{10,12},{12,10},{14,8},{16,22},{18,... | collective-permute-start | bytes 1081352 | tf_op jit(solution)/shard_map/ppermute | solution.py:28
  147.4 2.5 %collective-permute-start.39 = (bf16[128,512]{1,0:T(8,128)(2,1)}, bf16[128,512]{1,0:T(8,128)(2,1)S(1)}, u32[]{:S(2)}, u32[]{:S(2)}) collective-permute-start(bf16[128,512]{1,0:T(8,128)(2,1)} %get-tuple-element.306), channel_id=1, source_target_pairs={{0,16},{2,18},{4,20},{6,22},{8,24},{10,26},{12,28},{14,30},{16,0},... | collective-permute-start | bytes 393224 | tf_op jit(solution)/shard_map/ppermute | solution.py:28
  149.9 3.2 %collective-permute-done.38.refs_6_ = bf16[128,512]{1,0:T(8,128)(2,1)S(1)} collective-permute-done((bf16[128,512]{1,0:T(8,128)(2,1)}, bf16[128,512]{1,0:T(8,128)(2,1)S(1)}, u32[]{:S(2)}, u32[]{:S(2)}) %collective-permute-start.38) | collective-permute-done | bytes 131104 | tf_op jit(solution)/shard_map/ppermute | solution.py:28
  153.1 3.1 %collective-permute-start.40 = (bf16[128,512]{1,0:T(8,128)(2,1)S(1)}, bf16[128,512]{1,0:T(8,128)(2,1)S(1)}, u32[]{:S(2)}, u32[]{:S(2)}) collective-permute-start(bf16[128,512]{1,0:T(8,128)(2,1)S(1)} %copy-done.7), channel_id=1, source_target_pairs={{0,24},{2,26},{4,28},{6,30},{8,16},{10,18},{12,20},{14,22},{16,8},... | collective-permute-start | bytes 393224 | tf_op jit(solution)/shard_map/ppermute | solution.py:28
  160.3 2.2 %shard_map.215 = (f32[256,2048]{1,0:T(8,128)}, f32[256,512]{1,0:T(8,128)}, f32[256,512]{1,0:T(8,128)}, f32[256,128]{1,0:T(8,128)}, f32[8,256]{1,0:T(8,128)}, /*i...) custom-call(bf16[1,352,512]{2,1,0:T(8,128)(2,1)S(1)} %shard_map.213.refs_0_, ...), custom_call_target="tpu_custom_call" | custom-call | flops 1 | bytes 1 | tf_op jit(solution)/shard_map/pallas_call | solution.py:171
  (108 shorter events, 43.5 us)
Async XLA Ops:
  2.9 15.8 %collective-permute-start.4 = (bf16[264,1152]{1,0:T(8,128)(2,1)S(1)}, bf16[264,1152]{1,0:T(8,128)(2,1)S(1)}, u32[]{:S(2)}, u32[]{:S(2)}) collective-permute-start(bf16[264,1152]{1,0:T(8,128)(2,1)S(1)} %get-tuple-element.168), channel_id=1, source_target_pairs={{0,1},{1,0},{2,3},{3,2},{4,5},{5,4},{6,7},{7,6},{8,9},{9,8},{10,11... | collective-permute-start | bytes 1824776 | tf_op jit(solution)/shard_map/ppermute | solution.py:46
  3.5 14.5 %collective-permute-start.1 = (bf16[136,512]{1,0:T(8,128)(2,1)S(1)}, bf16[136,512]{1,0:T(8,128)(2,1)S(1)}, u32[]{:S(2)}, u32[]{:S(2)}) collective-permute-start(bf16[136,512]{1,0:T(8,128)(2,1)S(1)} %get-tuple-element.166), channel_id=1, source_target_pairs={{0,16},{2,18},{4,20},{6,22},{8,24},{10,26},{12,28},{14,30},{16,0},... | collective-permute-start | bytes 417800 | tf_op jit(solution)/shard_map/ppermute | solution.py:28
  7.5 10.5 %collective-permute-start.2 = (bf16[136,512]{1,0:T(8,128)(2,1)S(1)}, bf16[136,512]{1,0:T(8,128)(2,1)S(1)}, u32[]{:S(2)}, u32[]{:S(2)}) collective-permute-start(bf16[136,512]{1,0:T(8,128)(2,1)S(1)} %get-tuple-element.167), channel_id=1, source_target_pairs={{0,24},{2,26},{4,28},{6,30},{8,16},{10,18},{12,20},{14,22},{16,8},... | collective-permute-start | bytes 417800 | tf_op jit(solution)/shard_map/ppermute | solution.py:28
  8.9 9.8 %collective-permute-start = (bf16[136,512]{1,0:T(8,128)(2,1)S(1)}, bf16[136,512]{1,0:T(8,128)(2,1)S(1)}, u32[]{:S(2)}, u32[]{:S(2)}) collective-permute-start(bf16[136,512]{1,0:T(8,128)(2,1)S(1)} %get-tuple-element.164), channel_id=1, source_target_pairs={{0,8},{2,10},{4,12},{6,14},{8,0},{10,2},{12,4},{14,6},{16,24},{18,... | collective-permute-start | bytes 417800 | tf_op jit(solution)/shard_map/ppermute | solution.py:28
  21.1 19.5 %collective-permute-start.8 = (bf16[256,2048]{1,0:T(8,128)(2,1)}, bf16[256,2048]{1,0:T(8,128)(2,1)S(1)}, u32[]{:S(2)}, u32[]{:S(2)}) collective-permute-start(bf16[256,2048]{1,0:T(8,128)(2,1)} %refs_10_.3), channel_id=1, source_target_pairs={{0,1},{1,0},{2,3},{3,2},{4,5},{5,4},{6,7},{7,6},{8,9},{9,8},{10,11... | collective-permute-start | bytes 3145736 | tf_op jit(solution)/shard_map/ppermute | solution.py:46
  21.1 19.5 %collective-permute-start.9 = (bf16[1024,512]{1,0:T(8,128)(2,1)}, bf16[1024,512]{1,0:T(8,128)(2,1)S(1)}, u32[]{:S(2)}, u32[]{:S(2)}) collective-permute-start(bf16[1024,512]{1,0:T(8,128)(2,1)} %refs_11_.1), channel_id=1, source_target_pairs={{0,1},{1,0},{2,3},{3,2},{4,5},{5,4},{6,7},{7,6},{8,9},{9,8},{10,11... | collective-permute-start | bytes 3145736 | tf_op jit(solution)/shard_map/ppermute | solution.py:46
  21.6 12.5 %all-to-all-start = ((bf16[4,512,128]{2,1,0:T(8,128)(2,1)}), bf16[4,512,128]{2,1,0:T(8,128)(2,1)S(1)}, u32[]{:S(2)}, u32[]{:S(2)}) async-start(bf16[4,512,128]{2,1,0:T(8,128)(2,1)} %get-tuple-element.173), calls=%async_computation | async-start | bytes 1048576 | tf_op jit(solution)/shard_map/all_to_all | solution.py:42
  25.5 14.9 %collective-permute-start.5 = (bf16[128,512]{1,0:T(8,128)(2,1)}, bf16[128,512]{1,0:T(8,128)(2,1)S(1)}, u32[]{:S(2)}, u32[]{:S(2)}) collective-permute-start(bf16[128,512]{1,0:T(8,128)(2,1)} %get-tuple-element.191), channel_id=1, source_target_pairs={{0,8},{2,10},{4,12},{6,14},{8,0},{10,2},{12,4},{14,6},{16,24},{18,... | collective-permute-start | bytes 393224 | tf_op jit(solution)/shard_map/ppermute | solution.py:28
  27.9 12.6 %collective-permute-start.6 = (bf16[128,512]{1,0:T(8,128)(2,1)}, bf16[128,512]{1,0:T(8,128)(2,1)S(1)}, u32[]{:S(2)}, u32[]{:S(2)}) collective-permute-start(bf16[128,512]{1,0:T(8,128)(2,1)} %copy-done.3), channel_id=1, source_target_pairs={{0,16},{2,18},{4,20},{6,22},{8,24},{10,26},{12,28},{14,30},{16,0},... | collective-permute-start | bytes 393224 | tf_op jit(solution)/shard_map/ppermute | solution.py:28
  29.8 10.8 %collective-permute-start.7 = (bf16[128,512]{1,0:T(8,128)(2,1)}, bf16[128,512]{1,0:T(8,128)(2,1)}, u32[]{:S(2)}, u32[]{:S(2)}) collective-permute-start(bf16[128,512]{1,0:T(8,128)(2,1)} %copy-done.2), channel_id=1, source_target_pairs={{0,24},{2,26},{4,28},{6,30},{8,16},{10,18},{12,20},{14,22},{16,8},... | collective-permute-start | bytes 393224 | tf_op jit(solution)/shard_map/ppermute | solution.py:28
  56.8 31.0 %all-to-all-start.2 = ((bf16[4,320,512]{2,1,0:T(8,128)(2,1)}), bf16[4,320,512]{2,1,0:T(8,128)(2,1)S(1)}, u32[]{:S(2)}, u32[]{:S(2)}) async-start(bf16[4,320,512]{2,1,0:T(8,128)(2,1)} %get-tuple-element.274), calls=%async_computation.2 | async-start | bytes 2621440 | tf_op jit(solution)/shard_map/all_to_all | solution.py:42
  61.1 14.1 %collective-permute-start.12 = (bf16[128,512]{1,0:T(8,128)(2,1)S(1)}, bf16[128,512]{1,0:T(8,128)(2,1)S(1)}, u32[]{:S(2)}, u32[]{:S(2)}) collective-permute-start(bf16[128,512]{1,0:T(8,128)(2,1)S(1)} %copy-done.10), channel_id=1, source_target_pairs={{0,8},{2,10},{4,12},{6,14},{8,0},{10,2},{12,4},{14,6},{16,24},{18,... | collective-permute-start | bytes 393224 | tf_op jit(solution)/shard_map/ppermute | solution.py:28
  63.6 13.1 %collective-permute-start.13 = (bf16[128,512]{1,0:T(8,128)(2,1)S(1)}, bf16[128,512]{1,0:T(8,128)(2,1)S(1)}, u32[]{:S(2)}, u32[]{:S(2)}) collective-permute-start(bf16[128,512]{1,0:T(8,128)(2,1)S(1)} %copy-done.9), channel_id=1, source_target_pairs={{0,16},{2,18},{4,20},{6,22},{8,24},{10,26},{12,28},{14,30},{16,0},... | collective-permute-start | bytes 393224 | tf_op jit(solution)/shard_map/ppermute | solution.py:28
  65.1 21.6 %collective-permute-start.18 = (bf16[512,512]{1,0:T(8,128)(2,1)}, bf16[512,512]{1,0:T(8,128)(2,1)S(1)}, u32[]{:S(2)}, u32[]{:S(2)}) collective-permute-start(bf16[512,512]{1,0:T(8,128)(2,1)} %get-tuple-element.273), channel_id=1, source_target_pairs={{0,1},{1,0},{2,3},{3,2},{4,5},{5,4},{6,7},{7,6},{8,9},{9,8},{10,11... | collective-permute-start | bytes 1572872 | tf_op jit(solution)/shard_map/ppermute | solution.py:46
  65.1 13.5 %collective-permute-start.14 = (bf16[128,512]{1,0:T(8,128)(2,1)S(1)}, bf16[128,512]{1,0:T(8,128)(2,1)S(1)}, u32[]{:S(2)}, u32[]{:S(2)}) collective-permute-start(bf16[128,512]{1,0:T(8,128)(2,1)S(1)} %copy-done.8), channel_id=1, source_target_pairs={{0,24},{2,26},{4,28},{6,30},{8,16},{10,18},{12,20},{14,22},{16,8},... | collective-permute-start | bytes 393224 | tf_op jit(solution)/shard_map/ppermute | solution.py:28
  73.1 9.0 %collective-permute-start.15 = (bf16[512,128]{1,0:T(8,128)(2,1)}, bf16[512,128]{1,0:T(8,128)(2,1)S(1)}, u32[]{:S(2)}, u32[]{:S(2)}) collective-permute-start(bf16[512,128]{1,0:T(8,128)(2,1)} %get-tuple-element.255), channel_id=1, source_target_pairs={{0,2},{2,0},{4,6},{6,4},{8,10},{10,8},{12,14},{14,12},{16,18},{18,... | collective-permute-start | bytes 393224 | tf_op jit(solution)/shard_map/ppermute | solution.py:28
  76.6 7.7 %collective-permute-start.17 = (bf16[512,128]{1,0:T(8,128)(2,1)}, bf16[512,128]{1,0:T(8,128)(2,1)S(1)}, u32[]{:S(2)}, u32[]{:S(2)}) collective-permute-start(bf16[512,128]{1,0:T(8,128)(2,1)} %get-tuple-element.257), channel_id=1, source_target_pairs={{0,6},{2,4},{4,2},{6,0},{8,14},{10,12},{12,10},{14,8},{16,22},{18,... | collective-permute-start | bytes 393224 | tf_op jit(solution)/shard_map/ppermute | solution.py:28
  87.8 24.6 %all-to-all-start.1 = ((bf16[4,192,512]{2,1,0:T(8,128)(2,1)}), bf16[4,192,512]{2,1,0:T(8,128)(2,1)S(1)}, u32[]{:S(2)}, u32[]{:S(2)}) async-start(bf16[4,192,512]{2,1,0:T(8,128)(2,1)} %shard_map.205), calls=%async_computation.1 | async-start | bytes 1572864 | tf_op jit(solution)/shard_map/all_to_all | solution.py:42
  93.0 7.6 %collective-permute-start.20 = (bf16[80,512]{1,0:T(8,128)(2,1)S(1)}, bf16[80,512]{1,0:T(8,128)(2,1)S(1)}, u32[]{:S(2)}, u32[]{:S(2)}) collective-permute-start(bf16[80,512]{1,0:T(8,128)(2,1)S(1)} %get-tuple-element.282), channel_id=1, source_target_pairs={{0,8},{2,10},{4,12},{6,14},{8,0},{10,2},{12,4},{14,6},{16,24},{18,... | collective-permute-start | bytes 245768 | tf_op jit(solution)/shard_map/ppermute | solution.py:28
  95.5 15.5 %collective-permute-start.23 = (bf16[160,512]{1,0:T(8,128)(2,1)S(1)}, bf16[160,512]{1,0:T(8,128)(2,1)S(1)}, u32[]{:S(2)}, u32[]{:S(2)}) collective-permute-start(bf16[160,512]{1,0:T(8,128)(2,1)S(1)} %get-tuple-element.286), channel_id=1, source_target_pairs={{0,2},{2,0},{4,6},{6,4},{8,10},{10,8},{12,14},{14,12},{16,18},{18,... | collective-permute-start | bytes 491528 | tf_op jit(solution)/shard_map/ppermute | solution.py:28
  97.4 15.0 %collective-permute-start.24 = (bf16[160,512]{1,0:T(8,128)(2,1)S(1)}, bf16[160,512]{1,0:T(8,128)(2,1)S(1)}, u32[]{:S(2)}, u32[]{:S(2)}) collective-permute-start(bf16[160,512]{1,0:T(8,128)(2,1)S(1)} %get-tuple-element.287), channel_id=1, source_target_pairs={{0,4},{2,6},{4,0},{6,2},{8,12},{10,14},{12,8},{14,10},{16,20},{18,... | collective-permute-start | bytes 491528 | tf_op jit(solution)/shard_map/ppermute | solution.py:28
  98.9 13.5 %collective-permute-start.25 = (bf16[160,512]{1,0:T(8,128)(2,1)S(1)}, bf16[160,512]{1,0:T(8,128)(2,1)S(1)}, u32[]{:S(2)}, u32[]{:S(2)}) collective-permute-start(bf16[160,512]{1,0:T(8,128)(2,1)S(1)} %get-tuple-element.288), channel_id=1, source_target_pairs={{0,6},{2,4},{4,2},{6,0},{8,14},{10,12},{12,10},{14,8},{16,22},{18,... | collective-permute-start | bytes 491528 | tf_op jit(solution)/shard_map/ppermute | solution.py:28
  99.0 8.9 %collective-permute-start.21 = (bf16[80,512]{1,0:T(8,128)(2,1)S(1)}, bf16[80,512]{1,0:T(8,128)(2,1)S(1)}, u32[]{:S(2)}, u32[]{:S(2)}) collective-permute-start(bf16[80,512]{1,0:T(8,128)(2,1)S(1)} %get-tuple-element.283), channel_id=1, source_target_pairs={{0,16},{2,18},{4,20},{6,22},{8,24},{10,26},{12,28},{14,30},{16,0},... | collective-permute-start | bytes 245768 | tf_op jit(solution)/shard_map/ppermute | solution.py:28
  100.5 7.3 %collective-permute-start.22 = (bf16[80,512]{1,0:T(8,128)(2,1)S(1)}, bf16[80,512]{1,0:T(8,128)(2,1)S(1)}, u32[]{:S(2)}, u32[]{:S(2)}) collective-permute-start(bf16[80,512]{1,0:T(8,128)(2,1)S(1)} %get-tuple-element.284), channel_id=1, source_target_pairs={{0,24},{2,26},{4,28},{6,30},{8,16},{10,18},{12,20},{14,22},{16,8},... | collective-permute-start | bytes 245768 | tf_op jit(solution)/shard_map/ppermute | solution.py:28
  110.4 7.4 %collective-permute-start.27 = (bf16[80,512]{1,0:T(8,128)(2,1)S(1)}, bf16[80,512]{1,0:T(8,128)(2,1)S(1)}, u32[]{:S(2)}, u32[]{:S(2)}) collective-permute-start(bf16[80,512]{1,0:T(8,128)(2,1)S(1)} %shard_map.208.refs_0_), channel_id=1, source_target_pairs={{0,16},{2,18},{4,20},{6,22},{8,24},{10,26},{12,28},{14,30},{16,0},... | collective-permute-start | bytes 245768 | tf_op jit(solution)/shard_map/ppermute | solution.py:28
  119.0 37.2 %all-to-all-start.3 = ((bf16[4,320,512]{2,1,0:T(8,128)(2,1)}), bf16[4,320,512]{2,1,0:T(8,128)(2,1)S(1)}, u32[]{:S(2)}, u32[]{:S(2)}) async-start(bf16[4,320,512]{2,1,0:T(8,128)(2,1)} %shard_map.211), calls=%async_computation.3 | async-start | bytes 2621440 | tf_op jit(solution)/shard_map/all_to_all | solution.py:42
  123.6 10.4 %collective-permute-start.30 = (bf16[88,512]{1,0:T(8,128)(2,1)S(1)}, bf16[88,512]{1,0:T(8,128)(2,1)S(1)}, u32[]{:S(2)}, u32[]{:S(2)}) collective-permute-start(bf16[88,512]{1,0:T(8,128)(2,1)S(1)} %get-tuple-element.294), channel_id=1, source_target_pairs={{0,16},{2,18},{4,20},{6,22},{8,24},{10,26},{12,28},{14,30},{16,0},... | collective-permute-start | bytes 270344 | tf_op jit(solution)/shard_map/ppermute | solution.py:28
  134.0 7.4 %collective-permute-start.34 = (bf16[88,512]{1,0:T(8,128)(2,1)S(1)}, bf16[88,512]{1,0:T(8,128)(2,1)S(1)}, u32[]{:S(2)}, u32[]{:S(2)}) collective-permute-start(bf16[88,512]{1,0:T(8,128)(2,1)S(1)} %shard_map.212.refs_0_), channel_id=1, source_target_pairs={{0,24},{2,26},{4,28},{6,30},{8,16},{10,18},{12,20},{14,22},{16,8},... | collective-permute-start | bytes 270344 | tf_op jit(solution)/shard_map/ppermute | solution.py:28
  143.9 16.0 %collective-permute-start.37 = (bf16[1,352,512]{2,1,0:T(8,128)(2,1)S(1)}, bf16[1,352,512]{2,1,0:T(8,128)(2,1)S(1)}, u32[]{:S(2)}, u32[]{:S(2)}) collective-permute-start(bf16[1,352,512]{2,1,0:T(8,128)(2,1)S(1)} %shard_map.213.refs_0_), channel_id=1, source_target_pairs={{0,6},{2,4},{4,2},{6,0},{8,14},{10,12},{12,10},{14,8},{16,22},{18,... | collective-permute-start | bytes 1081352 | tf_op jit(solution)/shard_map/ppermute | solution.py:28
  146.6 13.6 %collective-permute-start.36 = (bf16[1,352,512]{2,1,0:T(8,128)(2,1)S(1)}, bf16[1,352,512]{2,1,0:T(8,128)(2,1)S(1)}, u32[]{:S(2)}, u32[]{:S(2)}) collective-permute-start(bf16[1,352,512]{2,1,0:T(8,128)(2,1)S(1)} %shard_map.213.refs_0_), channel_id=1, source_target_pairs={{0,4},{2,6},{4,0},{6,2},{8,12},{10,14},{12,8},{14,10},{16,20},{18,... | collective-permute-start | bytes 1081352 | tf_op jit(solution)/shard_map/ppermute | solution.py:28
  147.1 13.2 %collective-permute-start.35 = (bf16[1,352,512]{2,1,0:T(8,128)(2,1)S(1)}, bf16[1,352,512]{2,1,0:T(8,128)(2,1)S(1)}, u32[]{:S(2)}, u32[]{:S(2)}) collective-permute-start(bf16[1,352,512]{2,1,0:T(8,128)(2,1)S(1)} %shard_map.213.refs_0_), channel_id=1, source_target_pairs={{0,2},{2,0},{4,6},{6,4},{8,10},{10,8},{12,14},{14,12},{16,18},{18,... | collective-permute-start | bytes 1081352 | tf_op jit(solution)/shard_map/ppermute | solution.py:28
  147.4 10.4 %collective-permute-start.39 = (bf16[128,512]{1,0:T(8,128)(2,1)}, bf16[128,512]{1,0:T(8,128)(2,1)S(1)}, u32[]{:S(2)}, u32[]{:S(2)}) collective-permute-start(bf16[128,512]{1,0:T(8,128)(2,1)} %get-tuple-element.306), channel_id=1, source_target_pairs={{0,16},{2,18},{4,20},{6,22},{8,24},{10,26},{12,28},{14,30},{16,0},... | collective-permute-start | bytes 393224 | tf_op jit(solution)/shard_map/ppermute | solution.py:28
  (26 other events, 233.3 us)
